TPU v7x, 128 devices: a whole 4x4x4 slice. The times are simulated.
128 devices in a mesh: gx: 8 (over z, x_hi), gy: 8 (over y, core), gz: 2 (over x_lo).
Axes of the slice: x: 4 (x_hi: 2, x_lo: 2; x = x_hi * 2 + x_lo), y: 4, z: 4, core: 2. Of those that a mesh axis runs over, the one named last changes fastest.
Arguments:
- volume: bfloat16 [64, 128, 32, 128], P('gx', 'gy', 'gz'), may hold values from -6 to 6
- w_full: bfloat16 [3, 3, 3, 128, 128], replicated, may hold values from -0.15625 to 0.15625
- w_half: bfloat16 [3, 3, 3, 128, 256], replicated, may hold values from -0.15625 to 0.15625
- w_bottom_in: bfloat16 [3, 3, 3, 256, 512], P(None, None, None, None, 'gx'), may hold values from -0.109375 to 0.109375
- w_bottom_out: bfloat16 [3, 3, 3, 512, 512], P(None, None, None, None, 'gx'), may hold values from -0.078125 to 0.078125
- w_up: bfloat16 [3, 3, 3, 768, 256], replicated, may hold values from -0.0625 to 0.0625
Outputs:
- decoded: bfloat16 [32, 64, 16, 256], P('gx', 'gy', 'gz')
All inputs are finite; a program needn't handle non-finite values.
Results may differ from a plain program's by a relative error of at most 0.009.
Values may be sent and summed in bfloat16 or wider, within the bound.
No kernel may reach another device: no remote copies, remote signals or barrier semaphores. Data moves between devices by JAX's collectives and lax.ppermute only.
A program may use at most 64 MiB of HBM per device.

v0:
```python
import jax
import jax.numpy as jnp
from jax import lax
from jax.sharding import PartitionSpec as P


def conv(field, kernel):
    result = lax.conv_general_dilated(
        field[None],
        kernel,
        (1, 1, 1),
        "VALID",
        dimension_numbers=("NDHWC", "DHWIO", "NDHWC"),
        preferred_element_type=jnp.float32,
    )
    return result[0]


def rectify(total):
    return jnp.maximum(total, 0.0).astype(jnp.bfloat16)


def shrink(field):
    size_x, size_y, size_z, channels = field.shape
    blocks = field.reshape(size_x // 2, 2, size_y // 2, 2, size_z // 2, 2, channels)
    return jnp.max(blocks, axis=(1, 3, 5))


def enlarge(field):
    size_x, size_y, size_z, channels = field.shape
    spread = jnp.broadcast_to(
        field[:, None, :, None, :, None, :], (size_x, 2, size_y, 2, size_z, 2, channels)
    )
    return spread.reshape(2 * size_x, 2 * size_y, 2 * size_z, channels)


def halo(field, axis, count, dim, width):
    place = lax.axis_index(axis)
    size = field.shape[dim]
    low = lax.slice_in_dim(field, 0, width, axis=dim)
    high = lax.slice_in_dim(field, size - width, size, axis=dim)
    zero = jnp.zeros_like(low)
    if count == 2:
        got = lax.ppermute(jnp.where(place == 0, high, low), axis, [(0, 1), (1, 0)])
        below = jnp.where(place == 1, got, zero)
        above = jnp.where(place == 0, got, zero)
        return below, above
    even = place % 2 == 0
    inner = [(i, i ^ 1) for i in range(count)]
    outer = [(i, (((i + 1) ^ 1) - 1) % count) for i in range(count)]
    got_in = lax.ppermute(jnp.where(even, high, low), axis, inner)
    got_out = lax.ppermute(jnp.where(even, low, high), axis, outer)
    below = jnp.where(place > 0, jnp.where(even, got_out, got_in), zero)
    above = jnp.where(place < count - 1, jnp.where(even, got_in, got_out), zero)
    return below, above


def extend(field, axis, count, dim, width):
    below, above = halo(field, axis, count, dim, width)
    return jnp.concatenate([below, field, above], axis=dim)


def clear_outside(field, axis, count, dim, width):
    place = lax.axis_index(axis)
    size = field.shape[dim]
    index = lax.broadcasted_iota(jnp.int32, field.shape, dim)
    inside = ((index >= width) | (place > 0)) & ((index < size - width) | (place < count - 1))
    return jnp.where(inside, field, jnp.zeros_like(field))


def solution(mesh):
    gx, gy, gz = mesh.shape["gx"], mesh.shape["gy"], mesh.shape["gz"]

    def local(volume, w_full, w_half, w_bottom_in, w_bottom_out, w_up):
        place_z = lax.axis_index("gz")
        field = extend(volume, "gx", gx, 0, 3)
        field = extend(field, "gy", gy, 1, 3)
        field = extend(field, "gz", gz, 2, 1)
        pooled = shrink(rectify(conv(field, w_full)))
        pooled = clear_outside(pooled, "gx", gx, 0, 1)
        pooled = clear_outside(pooled, "gy", gy, 1, 1)
        pooled = extend(pooled, "gz", gz, 2, 1)
        skip = rectify(conv(pooled, w_half))
        coarse = shrink(skip)
        own_x, own_y, own_z, ch1 = coarse.shape

        column = extend(coarse, "gy", gy, 1, 1)
        column = jnp.broadcast_to(column[None], (gx * gz,) + column.shape)
        column = lax.all_to_all(column, ("gx", "gz"), 0, 0)
        column = column.reshape(gx, gz, own_x, own_y + 2, own_z, ch1)
        column = column.transpose(0, 2, 3, 1, 4, 5).reshape(gx * own_x, own_y + 2, gz * own_z, ch1)
        first = rectify(conv(jnp.pad(column, ((1, 1), (0, 0), (1, 1), (0, 0))), w_bottom_in))

        part = first.shape[-1]
        first = jnp.broadcast_to(first[None], (gx,) + first.shape)
        first = lax.all_to_all(first, "gx", 0, 0)
        first = first.transpose(1, 2, 3, 0, 4).reshape(first.shape[1:4] + (gx * part,))
        first = extend(first, "gy", gy, 1, 2)
        first = jnp.pad(first, ((1, 1), (0, 0), (1, 1), (0, 0)))
        second = rectify(conv(first, w_bottom_out))
        second = clear_outside(second, "gy", gy, 1, 1)
        second = jnp.pad(second, ((1, 1), (0, 0), (1, 1), (0, 0)))
        second = lax.dynamic_slice_in_dim(second, place_z * own_z, own_z + 2, axis=2)
        second = jnp.stack([second[own_x * i : own_x * i + own_x + 2] for i in range(gx)])
        second = lax.all_to_all(second, "gx", 0, 0)
        second = second.transpose(1, 2, 3, 0, 4).reshape(second.shape[1:4] + (gx * part,))

        around = extend(skip, "gx", gx, 0, 1)
        around = extend(around, "gy", gy, 1, 1)
        around = extend(around, "gz", gz, 2, 1)
        spread = enlarge(second)[1:-1, 1:-1, 1:-1]
        joined = jnp.concatenate([spread, around], axis=3)
        return conv(joined, w_up).astype(jnp.bfloat16)

    space = P("gx", "gy", "gz", None)
    filters = P(None, None, None, None, "gx")
    return jax.shard_map(
        local,
        mesh=mesh,
        in_specs=(space, P(), P(), filters, filters, P()),
        out_specs=space,
        check_vma=False,
    )
```

profile of v0, /device:TPU:0, one launch (start us, length us, event | category | flops | bytes accessed | tf_op | source)
XLA Modules:
  0.0 162.6 jit_solution(1502687871316534538)
XLA Ops:
  0.0 1.3 copy.58
  1.4 6.7 %collective-permute-start = (bf16[3,16,16,128]{3,1,2,0:T(8,128)(2,1)S(1)}, bf16[3,16,16,128]{3,1,2,0:T(8,128)(2,1)S(1)}, u32[]{:S(2)}, u32[]{:S(2)}) collective-permute-start(bf16[3,16,16,128]{3,1,2,0:T(8,128)(2,1)S(1)} %get-tuple-element.15), channel_id=1, source_target_pairs={{0,112},{16,32},{32,16},{48,64},{64,48},{80,96},{96,80},{112,0},{1... | collective-permute-start | bytes 589832 | tf_op jit(solution)/shard_map/ppermute | solution.py:52
  8.0 5.7 %collective-permute-done = bf16[3,16,16,128]{3,1,2,0:T(8,128)(2,1)S(1)} collective-permute-done((bf16[3,16,16,128]{3,1,2,0:T(8,128)(2,1)S(1)}, bf16[3,16,16,128]{3,1,2,0:T(8,128)(2,1)S(1)}, u32[]{:S(2)}, u32[]{:S(2)}) %collective-permute-start) | collective-permute-done | bytes 196640 | tf_op jit(solution)/shard_map/ppermute | solution.py:52
  13.7 2.6 %collective-permute-done.1 = bf16[3,16,16,128]{3,1,2,0:T(8,128)(2,1)S(1)} collective-permute-done((bf16[3,16,16,128]{3,1,2,0:T(8,128)(2,1)S(1)}, bf16[3,16,16,128]{3,1,2,0:T(8,128)(2,1)S(1)}, u32[]{:S(2)}, u32[]{:S(2)}) %collective-permute-start.1) | collective-permute-done | bytes 196640 | tf_op jit(solution)/shard_map/ppermute | solution.py:51
  17.0 3.1 %collective-permute-start.2 = (bf16[14,3,16,128]{3,1,2,0:T(4,128)(2,1)S(1)}, bf16[14,3,16,128]{3,1,2,0:T(4,128)(2,1)}, u32[]{:S(2)}, u32[]{:S(2)}) collective-permute-start(bf16[14,3,16,128]{3,1,2,0:T(4,128)(2,1)S(1)} %get-tuple-element.8), channel_id=1, source_target_pairs={{0,14},{2,4},{4,2},{6,8},{8,6},{10,12},{12,10},{14,0},{1,15},{3,5}... | collective-permute-start | bytes 516104 | tf_op jit(solution)/shard_map/ppermute | solution.py:52
  20.1 3.8 %collective-permute-done.2 = bf16[14,3,16,128]{3,1,2,0:T(4,128)(2,1)} collective-permute-done((bf16[14,3,16,128]{3,1,2,0:T(4,128)(2,1)S(1)}, bf16[14,3,16,128]{3,1,2,0:T(4,128)(2,1)}, u32[]{:S(2)}, u32[]{:S(2)}) %collective-permute-start.2) | collective-permute-done | bytes 172064 | tf_op jit(solution)/shard_map/ppermute | solution.py:52
  23.9 1.1 select_select_fusion.1
  25.2 0.9 collective-permute-start.4
  26.1 3.9 %collective-permute-done.4 = bf16[14,22,1,128]{3,1,2,0:T(8,128)(2,1)S(1)} collective-permute-done((bf16[14,22,1,128]{3,1,2,0:T(8,128)(2,1)S(1)}, bf16[14,22,1,128]{3,1,2,0:T(8,128)(2,1)S(1)}, u32[]{:S(2)}, u32[]{:S(2)}) %collective-permute-start.4) | collective-permute-done | bytes 78880 | tf_op jit(solution)/shard_map/ppermute | solution.py:44
  30.0 0.8 maximum_bitcast_fusion
  31.9 0.6 copy-done.4
  32.4 10.7 %maximum_convert_fusion = bf16[12,20,8,3,128]{4,2,3,1,0:T(8,128)(2,1)S(1)} fusion(bf16[3,3,3,128,128]{4,3,2,1,0:T(8,128)(2,1)S(1)} %copy-done.4, bf16[14,22,1,7,2,128]{5,3,4,1,0,2:T(8,128)(2,1)S(1)} %slice.114, bf16[14,22,1,8,3,128]{5,3,4,1,0,2:T(8,128)(2,1)S(1)} %copy.62, pred[8,3]{0,1:T(4,128)(4,1)S(1)} %copy-done.5), kind=kOutput, calls=%fused_computation.12 | convolution fusion | flops 5107752960 | bytes 5355544 | tf_op jit(solution)/shard_map/conv_general_dilated | solution.py:8
  44.0 1.4 reduce_max.18
  45.5 0.7 collective-permute-start.5
  46.2 3.3 %collective-permute-done.5 = bf16[6,10,1,128]{3,2,1,0:T(2,128)(2,1)S(1)} collective-permute-done((bf16[6,10,1,128]{3,2,1,0:T(2,128)(2,1)S(1)}, bf16[6,10,1,128]{3,2,1,0:T(2,128)(2,1)S(1)}, u32[]{:S(2)}, u32[]{:S(2)}) %collective-permute-start.5) | collective-permute-done | bytes 15392 | tf_op jit(solution)/shard_map/ppermute | solution.py:44
  49.7 3.1 %fusion.42 = (bf16[4,8,8,256]{3,2,1,0:T(8,128)(2,1)S(1)}, bf16[1,4,8,8,256]{4,0,3,2,1:T(2,128)(2,1)S(1)}) fusion(bf16[3,3,3,128,256]{4,3,2,1,0:T(8,128)(2,1)S(1)} %copy-done, bf16[1,6,10,10,128]{4,3,2,1,0:T(8,128)(2,1)S(1)} %maximum_bitcast_fusion.2), kind=kOutput, calls=%fused_computation.121 | convolution fusion | flops 453115904 | bytes 2185216 | tf_op jit(solution)/shard_map/conv_general_dilated | solution.py:8
  53.1 1.0 collective-permute-start.6
  54.2 3.3 %collective-permute-done.6 = bf16[2,1,4,256]{3,2,1,0:T(4,128)(2,1)S(1)} collective-permute-done((bf16[2,1,4,256]{3,2,1,0:T(4,128)(2,1)S(1)}, bf16[2,1,4,256]{3,2,1,0:T(4,128)(2,1)S(1)}, u32[]{:S(2)}, u32[]{:S(2)}) %collective-permute-start.6) | collective-permute-done | bytes 4128 | tf_op jit(solution)/shard_map/ppermute | solution.py:52
  57.5 0.8 broadcast_in_dim.73
  58.3 5.4 %all-to-all-start = ((bf16[16,2,6,4,256]{4,3,2,1,0:T(4,128)(2,1)}), bf16[16,2,6,4,256]{4,3,2,1,0:T(4,128)(2,1)S(1)}, u32[]{:S(2)}, u32[]{:S(2)}) async-start(bf16[16,2,6,4,256]{4,3,2,1,0:T(4,128)(2,1)} %broadcast_in_dim.73), calls=%async_computation | async-start | bytes 786432 | tf_op jit(solution)/shard_map/all_to_all | solution.py:89
  64.1 5.6 %collective-permute-start.10 = (bf16[1,8,8,256]{3,0,2,1:T(2,128)(2,1)S(1)}, bf16[1,8,8,256]{3,0,2,1:T(2,128)(2,1)S(1)}, u32[]{:S(2)}, u32[]{:S(2)}) collective-permute-start(bf16[1,8,8,256]{3,0,2,1:T(2,128)(2,1)S(1)} %get-tuple-element.21), channel_id=1, source_target_pairs={{0,112},{16,32},{32,16},{48,64},{64,48},{80,96},{96,80},{112,0},{1... | collective-permute-start | bytes 98312 | tf_op jit(solution)/shard_map/ppermute | solution.py:52
  70.1 3.7 %all-to-all-done = bf16[16,2,6,4,256]{4,3,2,1,0:T(4,128)(2,1)S(1)} async-done(((bf16[16,2,6,4,256]{4,3,2,1,0:T(4,128)(2,1)}), bf16[16,2,6,4,256]{4,3,2,1,0:T(4,128)(2,1)S(1)}, u32[]{:S(2)}, u32[]{:S(2)}) %all-to-all-start) | async-done | bytes 393248 | tf_op jit(solution)/shard_map/all_to_all | solution.py:89
  74.3 6.6 %fusion.28 = bf16[1,16,4,8,64]{4,0,3,2,1:T(2,128)(2,1)S(1)} fusion(bf16[3,3,3,256,64]{3,4,2,1,0:T(8,128)(2,1)} %param.9, bf16[1,18,6,10,256]{4,3,2,1,0:T(8,128)(2,1)S(1)} %pad_bitcast_fusion), kind=kOutput, calls=%fused_computation.32 | convolution fusion | flops 453050368 | bytes 1503232 | tf_op jit(solution)/shard_map/conv_general_dilated | solution.py:8
  81.4 1.5 reshape.56
  82.9 3.5 %all-to-all-start.1 = ((bf16[8,2,16384]{2,1,0:T(2,128)(2,1)}), bf16[8,2,16384]{2,1,0:T(2,128)(2,1)S(1)}, u32[]{:S(2)}, u32[]{:S(2)}) async-start(bf16[8,2,16384]{2,1,0:T(2,128)(2,1)} %reshape.56), calls=%async_computation.1 | async-start | bytes 1048576 | tf_op jit(solution)/shard_map/all_to_all | solution.py:96
  86.6 0.7 broadcast_select_fusion.24
  87.2 0.6 broadcast_select_fusion.23
  87.9 2.3 %collective-permute-start.12 = (bf16[6,1,8,256]{3,0,2,1:T(8,128)(2,1)}, bf16[6,1,8,256]{3,0,2,1:T(8,128)(2,1)}, u32[]{:S(2)}, u32[]{:S(2)}) collective-permute-start(bf16[6,1,8,256]{3,0,2,1:T(8,128)(2,1)} %get-tuple-element.5), channel_id=1, source_target_pairs={{0,14},{2,4},{4,2},{6,8},{8,6},{10,12},{12,10},{14,0},{1,15},{3,5}... | collective-permute-start | bytes 73736 | tf_op jit(solution)/shard_map/ppermute | solution.py:52
  90.2 6.3 %all-to-all-done.1 = bf16[8,2,16384]{2,1,0:T(2,128)(2,1)S(1)} async-done(((bf16[8,2,16384]{2,1,0:T(2,128)(2,1)}), bf16[8,2,16384]{2,1,0:T(2,128)(2,1)S(1)}, u32[]{:S(2)}, u32[]{:S(2)}) %all-to-all-start.1) | async-done | bytes 524320 | tf_op jit(solution)/shard_map/all_to_all | solution.py:96
  96.5 0.7 reshape.57
  97.5 1.2 copy.71
  98.8 0.6 reshape.39
  99.4 0.6 broadcast_select_fusion.4
  100.1 1.0 collective-permute-start.9
  101.1 0.8 select_select_fusion.6
  101.8 0.8 fusion.38
  102.6 0.8 collective-permute-start.14
  103.4 3.6 %collective-permute-done.8 = bf16[16,2,8,512]{3,1,2,0:T(2,128)(2,1)S(1)} collective-permute-done((bf16[16,2,8,512]{3,1,2,0:T(2,128)(2,1)S(1)}, bf16[16,2,8,512]{3,1,2,0:T(2,128)(2,1)S(1)}, u32[]{:S(2)}, u32[]{:S(2)}) %collective-permute-start.8) | collective-permute-done | bytes 262176 | tf_op jit(solution)/shard_map/ppermute | solution.py:52
  107.6 0.9 fusion.18
  108.5 16.1 %fusion.25 = bf16[1,16,6,8,64]{4,0,3,2,1:T(2,128)(2,1)S(1)} fusion(bf16[3,3,3,512,64]{3,4,2,1,0:T(8,128)(2,1)S(1)} %copy-done.3, bf16[1,18,8,10,512]{4,2,3,1,0:T(8,128)(2,1)S(1)} %fusion.18), kind=kOutput, calls=%fused_computation.30 | convolution fusion | flops 1359052800 | bytes 3342336 | tf_op jit(solution)/shard_map/conv_general_dilated | solution.py:8
  125.4 0.9 reshape.58
  126.2 3.4 %all-to-all-start.2 = ((bf16[8,2,4608]{2,1,0:T(2,128)(2,1)}), bf16[8,2,4608]{2,1,0:T(2,128)(2,1)S(1)}, u32[]{:S(2)}, u32[]{:S(2)}) async-start(bf16[8,2,4608]{2,1,0:T(2,128)(2,1)} %reshape.58), calls=%async_computation.2 | async-start | bytes 294912 | tf_op jit(solution)/shard_map/all_to_all | solution.py:105
  129.6 8.2 %all-to-all-done.2 = bf16[8,2,4608]{2,1,0:T(2,128)(2,1)S(1)} async-done(((bf16[8,2,4608]{2,1,0:T(2,128)(2,1)}), bf16[8,2,4608]{2,1,0:T(2,128)(2,1)S(1)}, u32[]{:S(2)}, u32[]{:S(2)}) %all-to-all-start.2) | async-done | bytes 147488 | tf_op jit(solution)/shard_map/all_to_all | solution.py:105
  138.4 0.8 broadcast_in_dim.81
  139.2 1.3 reshape.40
  140.5 1.3 slice.122
  142.3 19.2 %fusion.29 = bf16[1,4,8,8,256]{4,0,3,2,1:T(2,128)(2,1)S(1)} fusion(bf16[3,3,3,768,256]{4,3,2,1,0:T(8,128)(2,1)} %param.11, bf16[1,6,10,10,768]{4,1,3,2,0:T(8,128)(2,1)S(1)} %maximum_bitcast_fusion.1), kind=kOutput, calls=%fused_computation.33 | convolution fusion | flops 2717974528 | bytes 11669504 | tf_op jit(solution)/shard_map/conv_general_dilated | solution.py:8
  161.5 0.7 copy.109
  (75 shorter events, 7.7 us)
Async XLA Ops:
  0.0 49.7 %copy-start = (bf16[3,3,3,128,256]{4,3,2,1,0:T(8,128)(2,1)S(1)}, bf16[3,3,3,128,256]{4,3,2,1,0:T(8,128)(2,1)}, u32[]{:S(2)}) copy-start(bf16[3,3,3,128,256]{4,3,2,1,0:T(8,128)(2,1)} %param.8) | copy-start | bytes 5308420
  1.4 12.4 %collective-permute-start = (bf16[3,16,16,128]{3,1,2,0:T(8,128)(2,1)S(1)}, bf16[3,16,16,128]{3,1,2,0:T(8,128)(2,1)S(1)}, u32[]{:S(2)}, u32[]{:S(2)}) collective-permute-start(bf16[3,16,16,128]{3,1,2,0:T(8,128)(2,1)S(1)} %get-tuple-element.15), channel_id=1, source_target_pairs={{0,112},{16,32},{32,16},{48,64},{64,48},{80,96},{96,80},{112,0},{1... | collective-permute-start | bytes 589832 | tf_op jit(solution)/shard_map/ppermute | solution.py:52
  8.0 8.4 %collective-permute-start.1 = (bf16[3,16,16,128]{3,1,2,0:T(8,128)(2,1)S(1)}, bf16[3,16,16,128]{3,1,2,0:T(8,128)(2,1)S(1)}, u32[]{:S(2)}, u32[]{:S(2)}) collective-permute-start(bf16[3,16,16,128]{3,1,2,0:T(8,128)(2,1)S(1)} %get-tuple-element.16), channel_id=1, source_target_pairs={{0,16},{16,0},{32,48},{48,32},{64,80},{80,64},{96,112},{112,96},{1... | collective-permute-start | bytes 589832 | tf_op jit(solution)/shard_map/ppermute | solution.py:51
  16.9 3.2 %collective-permute-start.3 = (bf16[14,3,16,128]{3,1,2,0:T(4,128)(2,1)S(1)}, bf16[14,3,16,128]{3,1,2,0:T(4,128)(2,1)S(1)}, u32[]{:S(2)}, u32[]{:S(2)}) collective-permute-start(bf16[14,3,16,128]{3,1,2,0:T(4,128)(2,1)S(1)} %broadcast_select_fusion.6), channel_id=1, source_target_pairs={{0,2},{2,0},{4,6},{6,4},{8,10},{10,8},{12,14},{14,12},{1,3},{3,1},... | collective-permute-start | bytes 516104 | tf_op jit(solution)/shard_map/ppermute | solution.py:51
  17.0 6.9 %collective-permute-start.2 = (bf16[14,3,16,128]{3,1,2,0:T(4,128)(2,1)S(1)}, bf16[14,3,16,128]{3,1,2,0:T(4,128)(2,1)}, u32[]{:S(2)}, u32[]{:S(2)}) collective-permute-start(bf16[14,3,16,128]{3,1,2,0:T(4,128)(2,1)S(1)} %get-tuple-element.8), channel_id=1, source_target_pairs={{0,14},{2,4},{4,2},{6,8},{8,6},{10,12},{12,10},{14,0},{1,15},{3,5}... | collective-permute-start | bytes 516104 | tf_op jit(solution)/shard_map/ppermute | solution.py:52
  25.2 4.8 %collective-permute-start.4 = (bf16[14,22,1,128]{3,1,2,0:T(8,128)(2,1)S(1)}, bf16[14,22,1,128]{3,1,2,0:T(8,128)(2,1)S(1)}, u32[]{:S(2)}, u32[]{:S(2)}) collective-permute-start(bf16[14,22,1,128]{3,1,2,0:T(8,128)(2,1)S(1)} %fusion.35), channel_id=1, source_target_pairs={{0,1},{1,0},{2,3},{3,2},{4,5},{5,4},{6,7},{7,6},{8,9},{9,8},{10,11... | collective-permute-start | bytes 236552 | tf_op jit(solution)/shard_map/ppermute | solution.py:44
  31.3 1.2 copy-start.4
  31.3 1.2 copy-start.5
  45.5 4.0 %collective-permute-start.5 = (bf16[6,10,1,128]{3,2,1,0:T(2,128)(2,1)S(1)}, bf16[6,10,1,128]{3,2,1,0:T(2,128)(2,1)S(1)}, u32[]{:S(2)}, u32[]{:S(2)}) collective-permute-start(bf16[6,10,1,128]{3,2,1,0:T(2,128)(2,1)S(1)} %broadcast_select_fusion.19), channel_id=1, source_target_pairs={{0,1},{1,0},{2,3},{3,2},{4,5},{5,4},{6,7},{7,6},{8,9},{9,8},{10,11... | collective-permute-start | bytes 46088 | tf_op jit(solution)/shard_map/ppermute | solution.py:44
  53.1 4.3 %collective-permute-start.6 = (bf16[2,1,4,256]{3,2,1,0:T(4,128)(2,1)S(1)}, bf16[2,1,4,256]{3,2,1,0:T(4,128)(2,1)S(1)}, u32[]{:S(2)}, u32[]{:S(2)}) collective-permute-start(bf16[2,1,4,256]{3,2,1,0:T(4,128)(2,1)S(1)} %get-tuple-element.33), channel_id=1, source_target_pairs={{0,14},{2,4},{4,2},{6,8},{8,6},{10,12},{12,10},{14,0},{1,15},{3,5}... | collective-permute-start | bytes 12296 | tf_op jit(solution)/shard_map/ppermute | solution.py:52
  54.1 3.3 %collective-permute-start.7 = (bf16[2,1,4,256]{3,2,1,0:T(4,128)(2,1)S(1)}, bf16[2,1,4,256]{3,2,1,0:T(4,128)(2,1)S(1)}, u32[]{:S(2)}, u32[]{:S(2)}) collective-permute-start(bf16[2,1,4,256]{3,2,1,0:T(4,128)(2,1)S(1)} %get-tuple-element.34), channel_id=1, source_target_pairs={{0,2},{2,0},{4,6},{6,4},{8,10},{10,8},{12,14},{14,12},{1,3},{3,1},... | collective-permute-start | bytes 12296 | tf_op jit(solution)/shard_map/ppermute | solution.py:51
  58.3 15.5 %all-to-all-start = ((bf16[16,2,6,4,256]{4,3,2,1,0:T(4,128)(2,1)}), bf16[16,2,6,4,256]{4,3,2,1,0:T(4,128)(2,1)S(1)}, u32[]{:S(2)}, u32[]{:S(2)}) async-start(bf16[16,2,6,4,256]{4,3,2,1,0:T(4,128)(2,1)} %broadcast_in_dim.73), calls=%async_computation | async-start | bytes 786432 | tf_op jit(solution)/shard_map/all_to_all | solution.py:89
  64.1 22.3 %collective-permute-start.10 = (bf16[1,8,8,256]{3,0,2,1:T(2,128)(2,1)S(1)}, bf16[1,8,8,256]{3,0,2,1:T(2,128)(2,1)S(1)}, u32[]{:S(2)}, u32[]{:S(2)}) collective-permute-start(bf16[1,8,8,256]{3,0,2,1:T(2,128)(2,1)S(1)} %get-tuple-element.21), channel_id=1, source_target_pairs={{0,112},{16,32},{32,16},{48,64},{64,48},{80,96},{96,80},{112,0},{1... | collective-permute-start | bytes 98312 | tf_op jit(solution)/shard_map/ppermute | solution.py:52
  69.7 16.7 %collective-permute-start.11 = (bf16[1,8,8,256]{3,0,2,1:T(2,128)(2,1)S(1)}, bf16[1,8,8,256]{3,0,2,1:T(2,128)(2,1)S(1)}, u32[]{:S(2)}, u32[]{:S(2)}) collective-permute-start(bf16[1,8,8,256]{3,0,2,1:T(2,128)(2,1)S(1)} %get-tuple-element.22), channel_id=1, source_target_pairs={{0,16},{16,0},{32,48},{48,32},{64,80},{80,64},{96,112},{112,96},{1... | collective-permute-start | bytes 98312 | tf_op jit(solution)/shard_map/ppermute | solution.py:51
  82.9 13.6 %all-to-all-start.1 = ((bf16[8,2,16384]{2,1,0:T(2,128)(2,1)}), bf16[8,2,16384]{2,1,0:T(2,128)(2,1)S(1)}, u32[]{:S(2)}, u32[]{:S(2)}) async-start(bf16[8,2,16384]{2,1,0:T(2,128)(2,1)} %reshape.56), calls=%async_computation.1 | async-start | bytes 1048576 | tf_op jit(solution)/shard_map/all_to_all | solution.py:96
  86.5 1.3 copy-start.1
  87.9 13.2 %collective-permute-start.13 = (bf16[6,1,8,256]{3,0,2,1:T(8,128)(2,1)}, bf16[6,1,8,256]{3,0,2,1:T(8,128)(2,1)}, u32[]{:S(2)}, u32[]{:S(2)}) collective-permute-start(bf16[6,1,8,256]{3,0,2,1:T(8,128)(2,1)} %broadcast_select_fusion.23), channel_id=1, source_target_pairs={{0,2},{2,0},{4,6},{6,4},{8,10},{10,8},{12,14},{14,12},{1,3},{3,1},... | collective-permute-start | bytes 73736 | tf_op jit(solution)/shard_map/ppermute | solution.py:51
  87.9 13.2 %collective-permute-start.12 = (bf16[6,1,8,256]{3,0,2,1:T(8,128)(2,1)}, bf16[6,1,8,256]{3,0,2,1:T(8,128)(2,1)}, u32[]{:S(2)}, u32[]{:S(2)}) collective-permute-start(bf16[6,1,8,256]{3,0,2,1:T(8,128)(2,1)} %get-tuple-element.5), channel_id=1, source_target_pairs={{0,14},{2,4},{4,2},{6,8},{8,6},{10,12},{12,10},{14,0},{1,15},{3,5}... | collective-permute-start | bytes 73736 | tf_op jit(solution)/shard_map/ppermute | solution.py:52
  99.3 9.2 %copy-start.3 = (bf16[3,3,3,512,64]{3,4,2,1,0:T(8,128)(2,1)S(1)}, bf16[3,3,3,512,64]{3,4,2,1,0:T(8,128)(2,1)}, u32[]{:S(2)}) copy-start(bf16[3,3,3,512,64]{3,4,2,1,0:T(8,128)(2,1)} %param.10) | copy-start | bytes 5308420
  100.0 7.1 %collective-permute-start.8 = (bf16[16,2,8,512]{3,1,2,0:T(2,128)(2,1)S(1)}, bf16[16,2,8,512]{3,1,2,0:T(2,128)(2,1)S(1)}, u32[]{:S(2)}, u32[]{:S(2)}) collective-permute-start(bf16[16,2,8,512]{3,1,2,0:T(2,128)(2,1)S(1)} %get-tuple-element.13), channel_id=1, source_target_pairs={{0,14},{2,4},{4,2},{6,8},{8,6},{10,12},{12,10},{14,0},{1,15},{3,5}... | collective-permute-start | bytes 786440 | tf_op jit(solution)/shard_map/ppermute | solution.py:52
  100.1 7.0 %collective-permute-start.9 = (bf16[16,2,8,512]{3,1,2,0:T(2,128)(2,1)S(1)}, bf16[16,2,8,512]{3,1,2,0:T(2,128)(2,1)S(1)}, u32[]{:S(2)}, u32[]{:S(2)}) collective-permute-start(bf16[16,2,8,512]{3,1,2,0:T(2,128)(2,1)S(1)} %get-tuple-element.14), channel_id=1, source_target_pairs={{0,2},{2,0},{4,6},{6,4},{8,10},{10,8},{12,14},{14,12},{1,3},{3,1},... | collective-permute-start | bytes 786440 | tf_op jit(solution)/shard_map/ppermute | solution.py:51
  102.6 27.0 %collective-permute-start.14 = (bf16[6,10,1,256]{3,0,2,1:T(8,128)(2,1)S(1)}, bf16[6,10,1,256]{3,0,2,1:T(8,128)(2,1)S(1)}, u32[]{:S(2)}, u32[]{:S(2)}) collective-permute-start(bf16[6,10,1,256]{3,0,2,1:T(8,128)(2,1)S(1)} %fusion.38), channel_id=1, source_target_pairs={{0,1},{1,0},{2,3},{3,2},{4,5},{5,4},{6,7},{7,6},{8,9},{9,8},{10,11... | collective-permute-start | bytes 92168 | tf_op jit(solution)/shard_map/ppermute | solution.py:44
  126.2 11.6 %all-to-all-start.2 = ((bf16[8,2,4608]{2,1,0:T(2,128)(2,1)}), bf16[8,2,4608]{2,1,0:T(2,128)(2,1)S(1)}, u32[]{:S(2)}, u32[]{:S(2)}) async-start(bf16[8,2,4608]{2,1,0:T(2,128)(2,1)} %reshape.58), calls=%async_computation.2 | async-start | bytes 294912 | tf_op jit(solution)/shard_map/all_to_all | solution.py:105
  138.4 3.5 %copy-start.2 = (bf16[1,8,8,256]{3,0,2,1:T(2,128)(2,1)S(1)}, bf16[1,8,8,256]{3,0,2,1:T(2,128)(2,1)}, u32[]{:S(2)}) copy-start(bf16[1,8,8,256]{3,0,2,1:T(2,128)(2,1)} %copy-done.1) | copy-start | bytes 98308
where the time goes:
time: 166 us; the launch traced here: 163 us
  matrix products  55.9 us (34%)
  waiting for transfers between devices  44.5 us (27%)
  starting transfers between devices  34.9 us (21%)
  local copies, waits for them, and re-layouts  16.1 us (10%)
  other arithmetic  10.3 us (6%)
    conv_general_dilated x5, matrix products, conv(): lax.conv_general_dilated(field[None], kernel, (1, 1, 1), 'VALID', dimensi...  55.9 us
    ppermute x6, starting transfers between devices, halo(): got_out = lax.ppermute(jnp.where(even, low, high), axis, outer)  18.8 us
    ppermute x6, waiting for transfers between devices, halo(): got_out = lax.ppermute(jnp.where(even, low, high), axis, outer)  16.5 us
    all_to_all x1, waiting for transfers between devices, local(): second = lax.all_to_all(second, 'gx', 0, 0)  8.16 us
    ppermute x3, waiting for transfers between devices, halo(): got = lax.ppermute(jnp.where(place == 0, high, low), axis, [(0, 1), (1, 0)])  7.18 us
    unnamed x26, local copies, waits for them, and re-layouts  6.56 us
    all_to_all x1, waiting for transfers between devices, local(): first = lax.all_to_all(first, 'gx', 0, 0)  6.33 us
    all_to_all x1, starting transfers between devices, local(): column = lax.all_to_all(column, ('gx', 'gz'), 0, 0)  5.37 us
  transfers between devices with their start and end apart: 18, of which 10 were waited for; matrix products, arithmetic and copies ran while one was open for 21% of the time, Pallas kernels for 0%

commit v1 on v0

--- a/solution.py
+++ b/solution.py
@@ -1,6 +1,8 @@
 import jax
 import jax.numpy as jnp
 from jax import lax
+from jax.experimental import pallas as pl
+from jax.experimental.pallas import tpu as pltpu
 from jax.sharding import PartitionSpec as P
 
 
@@ -68,6 +70,122 @@
     return jnp.where(inside, field, jnp.zeros_like(field))
 
 
+def roll_rows(block, shift):
+    return pltpu.roll(block, shift % block.shape[1], 1)
+
+
+def tile_conv(field, weights, name):
+    size_a, size_b, size_s, channels = field.shape
+    size_a, size_b = size_a - 2, size_b - 2
+    steps, taps, _, width = weights.shape
+    filters = width if taps == 3 else 64
+    wide = width if taps == 3 else 128
+    part = max(1, 256 // (size_b * size_s))
+
+    def body(field_ref, weights_ref, out_ref):
+        for first in range(0, size_a, part):
+            rows = part * size_b * size_s
+            groups = part * size_b
+            blocks = []
+            for step in range(steps):
+                da, db = step // 3, step % 3
+                block = field_ref[first + da : first + da + part, db : db + size_b]
+                if size_s % 16:
+                    block = block.astype(jnp.float32)
+                blocks.append(block.reshape(rows, channels).astype(jnp.bfloat16))
+            block = jnp.concatenate(blocks, axis=1)
+            sums = []
+            for tap in range(taps):
+                kernel = weights_ref[:, tap].reshape(steps * channels, width)
+                sums.append(jnp.dot(block, kernel, preferred_element_type=jnp.float32))
+            if taps == 3:
+                low, mid, high = [total.reshape(groups, size_s, width) for total in sums]
+            else:
+                low = sums[0][:, :128].reshape(groups, size_s, 128)
+                mid = pltpu.roll(sums[0][:, :128], 64, 1).reshape(groups, size_s, 128)
+                high = sums[0][:, 128:].reshape(groups, size_s, 128)
+            if size_s == 8:
+                total = roll_rows(low, 1) + mid + roll_rows(high, -1)
+            else:
+                index = lax.broadcasted_iota(jnp.int32, (groups, 8, wide), 1)
+                down = jnp.where(index == 0, roll_rows(low[:, 8:], 1), roll_rows(low[:, :8], 1))
+                up = jnp.where(index == 7, roll_rows(high[:, 8:], -1), roll_rows(high[:, :8], -1))
+                total = down + mid[:, :8] + up
+            total = jnp.maximum(total, 0.0).reshape(part, size_b, 8, wide)
+            out_ref[first : first + part] = total[..., :filters].astype(out_ref.dtype)
+
+    return pl.pallas_call(
+        body,
+        in_specs=[pl.BlockSpec(memory_space=pltpu.VMEM)] * 2,
+        out_specs=pl.BlockSpec(memory_space=pltpu.VMEM),
+        out_shape=jax.ShapeDtypeStruct((size_a, size_b, 8, filters), jnp.bfloat16),
+        compiler_params=pltpu.CompilerParams(vmem_limit_bytes=40 << 20),
+        name=name,
+    )(field, weights)
+
+
+def decode(place_z, field, edge, weights):
+    size_x, size_y, size_z, channels = field.shape
+    size_x, size_y = size_x - 2, size_y - 2
+    filters = weights.shape[-1]
+    rows, extra = size_x * size_y * size_z, size_x * size_y
+    weights = weights.reshape(9, 3, channels, filters)
+
+    def body(place_ref, field_ref, edge_ref, weights_hbm, out_ref, weights_ref, sums_ref, sems):
+        copies = [pltpu.make_async_copy(weights_hbm.at[step], weights_ref.at[step], sems.at[step]) for step in range(9)]
+        for copy in copies:
+            copy.start()
+        for dx in range(3):
+            blocks = []
+            for dy in range(3):
+                main = field_ref[dx : dx + size_x, dy : dy + size_y].astype(jnp.float32).reshape(rows, channels)
+                side = edge_ref[dy, dx : dx + size_x].astype(jnp.float32).reshape(extra, channels)
+                blocks.append(jnp.concatenate([main, side], axis=0).astype(jnp.bfloat16))
+                copies[3 * dx + dy].wait()
+            block = jnp.concatenate(blocks, axis=1)
+            for tap in range(3):
+                kernel = weights_ref[3 * dx : 3 * dx + 3, tap].reshape(3 * channels, filters)
+                product = jnp.dot(block, kernel, preferred_element_type=jnp.float32)
+                if dx == 0:
+                    sums_ref[tap] = product
+                else:
+                    sums_ref[tap] += product
+        first = place_ref[0] == 0
+        low, mid, high = [sums_ref[tap, :rows].reshape(extra, size_z, filters) for tap in range(3)]
+        zero = jnp.zeros((extra, filters), jnp.float32)
+        below = jnp.where(first, zero, sums_ref[0, rows:])
+        above = jnp.where(first, sums_ref[2, rows:], zero)
+        index = lax.broadcasted_iota(jnp.int32, (extra, size_z, filters), 1)
+        down = jnp.where(index == 0, below[:, None, :], roll_rows(low, 1))
+        up = jnp.where(index == size_z - 1, above[:, None, :], roll_rows(high, -1))
+        out_ref[...] = (down + mid + up).reshape(size_x, size_y, size_z, filters).astype(out_ref.dtype)
+
+    return pl.pallas_call(
+        body,
+        in_specs=[
+            pl.BlockSpec(memory_space=pltpu.SMEM),
+            pl.BlockSpec(memory_space=pltpu.VMEM),
+            pl.BlockSpec(memory_space=pltpu.VMEM),
+            pl.BlockSpec(memory_space=pl.ANY),
+        ],
+        out_specs=pl.BlockSpec(memory_space=pltpu.VMEM),
+        out_shape=jax.ShapeDtypeStruct((size_x, size_y, size_z, filters), jnp.bfloat16),
+        scratch_shapes=[
+            pltpu.VMEM(weights.shape, weights.dtype),
+            pltpu.VMEM((3, rows + extra, filters), jnp.float32),
+            pltpu.SemaphoreType.DMA((9,)),
+        ],
+        compiler_params=pltpu.CompilerParams(vmem_limit_bytes=48 << 20),
+        name="decode",
+    )(place_z, field, edge, weights)
+
+
+def beside(weights):
+    channels, filters = weights.shape[3:]
+    weights = weights.transpose(0, 2, 3, 1, 4).reshape(9, 1, channels, 3 * filters)
+    return jnp.pad(weights, ((0, 0), (0, 0), (0, 0), (0, 256 - 3 * filters)))
+
+
 def solution(mesh):
     gx, gy, gz = mesh.shape["gx"], mesh.shape["gy"], mesh.shape["gz"]
 
@@ -79,8 +197,9 @@
         pooled = shrink(rectify(conv(field, w_full)))
         pooled = clear_outside(pooled, "gx", gx, 0, 1)
         pooled = clear_outside(pooled, "gy", gy, 1, 1)
-        pooled = extend(pooled, "gz", gz, 2, 1)
-        skip = rectify(conv(pooled, w_half))
+        below, above = halo(pooled, "gz", gz, 2, 1)
+        pooled = jnp.concatenate([pooled, above, jnp.zeros_like(pooled)[:, :, :6], below], axis=2)
+        skip = tile_conv(pooled, w_half.reshape(9, 3, w_half.shape[3], w_half.shape[4]), "half")
         coarse = shrink(skip)
         own_x, own_y, own_z, ch1 = coarse.shape
 
@@ -88,29 +207,33 @@
         column = jnp.broadcast_to(column[None], (gx * gz,) + column.shape)
         column = lax.all_to_all(column, ("gx", "gz"), 0, 0)
         column = column.reshape(gx, gz, own_x, own_y + 2, own_z, ch1)
-        column = column.transpose(0, 2, 3, 1, 4, 5).reshape(gx * own_x, own_y + 2, gz * own_z, ch1)
-        first = rectify(conv(jnp.pad(column, ((1, 1), (0, 0), (1, 1), (0, 0))), w_bottom_in))
+        column = column.transpose(0, 2, 1, 4, 3, 5).reshape(gx * own_x, gz * own_z, own_y + 2, ch1)
+        column = jnp.pad(column, ((1, 1), (1, 1), (0, 2), (0, 0)))
+        first = tile_conv(column, beside(w_bottom_in), "bottom_in")[:, :, 1 : own_y + 1]
 
         part = first.shape[-1]
         first = jnp.broadcast_to(first[None], (gx,) + first.shape)
         first = lax.all_to_all(first, "gx", 0, 0)
         first = first.transpose(1, 2, 3, 0, 4).reshape(first.shape[1:4] + (gx * part,))
-        first = extend(first, "gy", gy, 1, 2)
-        first = jnp.pad(first, ((1, 1), (0, 0), (1, 1), (0, 0)))
-        second = rectify(conv(first, w_bottom_out))
-        second = clear_outside(second, "gy", gy, 1, 1)
-        second = jnp.pad(second, ((1, 1), (0, 0), (1, 1), (0, 0)))
-        second = lax.dynamic_slice_in_dim(second, place_z * own_z, own_z + 2, axis=2)
+        first = extend(first, "gy", gy, 2, 2)
+        first = jnp.pad(first, ((1, 1), (1, 1), (0, 0), (0, 0)))
+        second = tile_conv(first, beside(w_bottom_out), "bottom_out")[:, :, 1 : own_y + 3]
+        second = clear_outside(second, "gy", gy, 2, 1)
+        second = jnp.pad(second, ((1, 1), (1, 1), (0, 0), (0, 0)))
+        second = lax.dynamic_slice_in_dim(second, place_z * own_z, own_z + 2, axis=1)
         second = jnp.stack([second[own_x * i : own_x * i + own_x + 2] for i in range(gx)])
         second = lax.all_to_all(second, "gx", 0, 0)
-        second = second.transpose(1, 2, 3, 0, 4).reshape(second.shape[1:4] + (gx * part,))
+        second = second.transpose(1, 3, 2, 0, 4).reshape(own_x + 2, own_y + 2, own_z + 2, gx * part)
 
         around = extend(skip, "gx", gx, 0, 1)
         around = extend(around, "gy", gy, 1, 1)
-        around = extend(around, "gz", gz, 2, 1)
-        spread = enlarge(second)[1:-1, 1:-1, 1:-1]
-        joined = jnp.concatenate([spread, around], axis=3)
-        return conv(joined, w_up).astype(jnp.bfloat16)
+        got = lax.ppermute(jnp.where(place_z == 0, around[:, :, -1], around[:, :, 0]), "gz", [(0, 1), (1, 0)])
+        spread = enlarge(second)[1:-1, 1:-1]
+        side = jnp.where(place_z == 0, spread[:, :, -2], spread[:, :, 1])
+        joined = jnp.concatenate([spread[:, :, 2:-2], around], axis=3)
+        side = jnp.concatenate([side, got], axis=2)
+        side = jnp.stack([side[:, dy : dy + skip.shape[1]] for dy in range(3)])
+        return decode(place_z[None], joined, side, w_up)
 
     space = P("gx", "gy", "gz", None)
     filters = P(None, None, None, None, "gx")

time: 166 us -> 153 us (0.922); the launches traced: 163 us -> 153 us
  matrix products: 55.9 us -> 19.8 us
  local copies, waits for them, and re-layouts: 16.1 us -> 30.9 us
  Pallas kernels: 0 us -> 13.1 us
  waiting for transfers between devices: 44.5 us -> 42.7 us
    conv_general_dilated x5 -> x1, matrix products: 55.9 us -> 19.8 us  [conv(): lax.conv_general_dilated(field[None], kernel, (1, 1, 1), 'VALID', dimensi...]
    pallas_call x0 -> x4, Pallas kernels: none -> 13.1 us  [the longest x1 7.77 us: decode(): pl.pallas_call(body, in_specs=[pl.BlockSpec(memory_space=pltpu.SMEM), pl....]
    unnamed x26 -> x30, local copies, waits for them, and re-layouts: 6.56 us -> 12.6 us
    all_to_all x1, waiting for transfers between devices: 3.68 us -> 0.01 us  [local(): column = lax.all_to_all(column, ('gx', 'gz'), 0, 0)]
    pad x0 -> x3, local copies, waits for them, and re-layouts: none -> 3.39 us  [the longest x2 3.29 us: beside(): return jnp.pad(weights, ((0, 0), (0, 0), (0, 0), (0, 256 - 3 * filters)))]
    reshape x1 -> x3, local copies, waits for them, and re-layouts: 0.1 us -> 3.16 us  [the longest x2 3.1 us: beside(): weights.transpose(0, 2, 3, 1, 4).reshape(9, 1, channels, 3 * filters)]
    reshape x1, local copies, waits for them, and re-layouts: 0.57 us -> 2.66 us  [local(): first.transpose(1, 2, 3, 0, 4).reshape(first.shape[1:4] + (gx * part,))]
    ppermute x6, waiting for transfers between devices: 16.5 us -> 18.3 us  [halo(): got_out = lax.ppermute(jnp.where(even, low, high), axis, outer)]
  transfers between devices with their start and end apart: 18 -> 18, of which waited for: 10 -> 9; matrix products, arithmetic and copies ran while one was open for 21% -> 19% of each run, Pallas kernels for 0% -> 1%
where the time goes in v1:
time: 153 us
  waiting for transfers between devices  42.7 us (28%)
  starting transfers between devices  33.7 us (22%)
  local copies, waits for them, and re-layouts  30.9 us (20%)
  matrix products  19.8 us (13%)
  Pallas kernels  13.1 us (9%)
  other arithmetic  11.8 us (8%)
    conv_general_dilated x1, matrix products, conv(): lax.conv_general_dilated(field[None], kernel, (1, 1, 1), 'VALID', dimensi...  19.8 us
    ppermute x6, waiting for transfers between devices, halo(): got_out = lax.ppermute(jnp.where(even, low, high), axis, outer)  18.3 us
    ppermute x6, starting transfers between devices, halo(): got_out = lax.ppermute(jnp.where(even, low, high), axis, outer)  17.4 us
    unnamed x30, local copies, waits for them, and re-layouts  12.6 us
    all_to_all x1, waiting for transfers between devices, local(): first = lax.all_to_all(first, 'gx', 0, 0)  7.91 us
    pallas_call x1, Pallas kernels, decode(): pl.pallas_call(body, in_specs=[pl.BlockSpec(memory_space=pltpu.SMEM), pl....  7.77 us
    ppermute x2, waiting for transfers between devices, halo(): got = lax.ppermute(jnp.where(place == 0, high, low), axis, [(0, 1), (1, 0)])  7.1 us
    all_to_all x1, waiting for transfers between devices, local(): second = lax.all_to_all(second, 'gx', 0, 0)  6.7 us
  transfers between devices with their start and end apart: 18, of which 9 were waited for; matrix products, arithmetic and copies ran while one was open for 19% of the time, Pallas kernels for 1%

profile of v1, /device:TPU:0, one launch (start us, length us, event | category | flops | bytes accessed | tf_op | source)
XLA Modules:
  0.0 152.6 jit_solution(8378977732260515420)
XLA Ops:
  0.0 1.3 copy.30
  1.3 6.7 %collective-permute-start = (bf16[3,16,16,128]{3,1,2,0:T(8,128)(2,1)S(1)}, bf16[3,16,16,128]{3,1,2,0:T(8,128)(2,1)S(1)}, u32[]{:S(2)}, u32[]{:S(2)}) collective-permute-start(bf16[3,16,16,128]{3,1,2,0:T(8,128)(2,1)S(1)} %get-tuple-element.17), channel_id=1, source_target_pairs={{0,112},{16,32},{32,16},{48,64},{64,48},{80,96},{96,80},{112,0},{1... | collective-permute-start | bytes 589832 | tf_op jit(solution)/shard_map/ppermute | solution.py:54
  8.0 5.7 %collective-permute-done = bf16[3,16,16,128]{3,1,2,0:T(8,128)(2,1)S(1)} collective-permute-done((bf16[3,16,16,128]{3,1,2,0:T(8,128)(2,1)S(1)}, bf16[3,16,16,128]{3,1,2,0:T(8,128)(2,1)S(1)}, u32[]{:S(2)}, u32[]{:S(2)}) %collective-permute-start) | collective-permute-done | bytes 196640 | tf_op jit(solution)/shard_map/ppermute | solution.py:54
  13.7 2.6 %collective-permute-done.1 = bf16[3,16,16,128]{3,1,2,0:T(8,128)(2,1)S(1)} collective-permute-done((bf16[3,16,16,128]{3,1,2,0:T(8,128)(2,1)S(1)}, bf16[3,16,16,128]{3,1,2,0:T(8,128)(2,1)S(1)}, u32[]{:S(2)}, u32[]{:S(2)}) %collective-permute-start.1) | collective-permute-done | bytes 196640 | tf_op jit(solution)/shard_map/ppermute | solution.py:53
  17.0 3.1 %collective-permute-start.2 = (bf16[14,3,16,128]{3,1,2,0:T(4,128)(2,1)S(1)}, bf16[14,3,16,128]{3,1,2,0:T(4,128)(2,1)S(1)}, u32[]{:S(2)}, u32[]{:S(2)}) collective-permute-start(bf16[14,3,16,128]{3,1,2,0:T(4,128)(2,1)S(1)} %get-tuple-element.8), channel_id=1, source_target_pairs={{0,14},{2,4},{4,2},{6,8},{8,6},{10,12},{12,10},{14,0},{1,15},{3,5}... | collective-permute-start | bytes 516104 | tf_op jit(solution)/shard_map/ppermute | solution.py:54
  20.1 3.7 %collective-permute-done.2 = bf16[14,3,16,128]{3,1,2,0:T(4,128)(2,1)S(1)} collective-permute-done((bf16[14,3,16,128]{3,1,2,0:T(4,128)(2,1)S(1)}, bf16[14,3,16,128]{3,1,2,0:T(4,128)(2,1)S(1)}, u32[]{:S(2)}, u32[]{:S(2)}) %collective-permute-start.2) | collective-permute-done | bytes 172064 | tf_op jit(solution)/shard_map/ppermute | solution.py:54
  24.8 3.9 %collective-permute-done.4 = bf16[14,22,1,128]{3,1,2,0:T(8,128)(2,1)S(1)} collective-permute-done((bf16[14,22,1,128]{3,1,2,0:T(8,128)(2,1)S(1)}, bf16[14,22,1,128]{3,1,2,0:T(8,128)(2,1)S(1)}, u32[]{:S(2)}, u32[]{:S(2)}) %collective-permute-start.4) | collective-permute-done | bytes 78880 | tf_op jit(solution)/shard_map/ppermute | solution.py:46
  28.7 0.8 maximum_bitcast_fusion
  29.5 19.8 %fusion.3 = bf16[1,12,20,16,128]{4,0,3,2,1:T(2,128)(2,1)S(1)} fusion(bf16[3,3,3,128,128]{4,3,2,1,0:T(8,128)(2,1)S(1)} %copy-done, bf16[1,14,22,18,128]{4,2,3,1,0:T(8,128)(2,1)S(1)} %maximum_bitcast_fusion), kind=kOutput, calls=%fused_computation.8 | convolution fusion | flops 3398369280 | bytes 3287040 | tf_op jit(solution)/shard_map/conv_general_dilated | solution.py:10
  49.3 1.1 copy.49
  50.5 2.4 %reduce_max.18 = bf16[6,10,8,128]{3,2,1,0:T(8,128)(2,1)S(1)} reduce(bf16[6,2,10,2,8,2,128]{6,5,4,3,2,1,0:T(2,128)(2,1)} %bitcast.65, bf16[]{:T(256)} %constant.66.clone.1), dimensions={1,3,5}, to_apply=%region_0.1 | reduce | flops 430080 | bytes 1105922 | tf_op jit(solution)/shard_map/reduce_max | solution.py:28
  53.0 0.9 collective-permute-start.5
  54.0 3.2 %collective-permute-done.5 = bf16[6,10,1,128]{3,2,1,0:T(2,128)(2,1)S(1)} collective-permute-done((bf16[6,10,1,128]{3,2,1,0:T(2,128)(2,1)S(1)}, bf16[6,10,1,128]{3,2,1,0:T(2,128)(2,1)S(1)}, u32[]{:S(2)}, u32[]{:S(2)}) %collective-permute-start.5) | collective-permute-done | bytes 15392 | tf_op jit(solution)/shard_map/ppermute | solution.py:46
  57.4 1.2 half.1
  58.9 1.0 collective-permute-start.6
  59.9 3.3 %collective-permute-done.6 = bf16[2,1,4,256]{3,2,1,0:T(4,128)(2,1)S(1)} collective-permute-done((bf16[2,1,4,256]{3,2,1,0:T(4,128)(2,1)S(1)}, bf16[2,1,4,256]{3,2,1,0:T(4,128)(2,1)S(1)}, u32[]{:S(2)}, u32[]{:S(2)}) %collective-permute-start.6) | collective-permute-done | bytes 4128 | tf_op jit(solution)/shard_map/ppermute | solution.py:54
  63.2 0.9 broadcast_in_dim.59
  64.1 5.4 %all-to-all-start = ((bf16[16,2,6,4,256]{4,3,2,1,0:T(4,128)(2,1)}), bf16[16,2,6,4,256]{4,3,2,1,0:T(4,128)(2,1)}, u32[]{:S(2)}, u32[]{:S(2)}) async-start(bf16[16,2,6,4,256]{4,3,2,1,0:T(4,128)(2,1)} %broadcast_in_dim.59), calls=%async_computation | async-start | bytes 786432 | tf_op jit(solution)/shard_map/all_to_all | solution.py:208
  69.6 5.6 %collective-permute-start.10 = (bf16[1,8,8,256]{3,1,0,2:T(8,128)(2,1)S(1)}, bf16[1,8,8,256]{3,1,0,2:T(8,128)(2,1)S(1)}, u32[]{:S(2)}, u32[]{:S(2)}) collective-permute-start(bf16[1,8,8,256]{3,1,0,2:T(8,128)(2,1)S(1)} %get-tuple-element.26), channel_id=1, source_target_pairs={{0,112},{16,32},{32,16},{48,64},{64,48},{80,96},{96,80},{112,0},{1... | collective-permute-start | bytes 98312 | tf_op jit(solution)/shard_map/ppermute | solution.py:54
  75.3 0.7 copy.36
  76.0 1.2 pad.21.weights_ref
  77.2 0.7 copy-done.5
  78.0 2.4 %copy.39 = bf16[9,1,512,192]{3,2,1,0:T(8,128)(2,1)} copy(bf16[9,1,512,192]{2,3,0,1:T(8,128)(2,1)S(1)} %bitcast.63) | data formatting | bytes 3538944 | tf_op jit(solution)/shard_map/reshape | solution.py:185
  80.5 2.1 %pad.23.weights_ref = bf16[9,1,512,256]{3,2,1,0:T(8,128)(2,1)S(1)} pad(bf16[9,1,512,192]{3,2,1,0:T(8,128)(2,1)} %copy.39, bf16[]{:T(256)} %constant.64.clone.1), padding=0_0x0_0x0_0x0_64 | pad | bytes 4128770 | tf_op jit(solution)/shard_map/jit(_pad)/pad | solution.py:186
  82.6 1.2 copy.34
  83.9 1.5 bottom_in.1
  85.5 1.3 broadcast_in_dim.60
  86.8 3.4 %reshape.48 = bf16[8,2,16384]{2,1,0:T(2,128)(2,1)} reshape(bf16[8,16,8,4,64]{4,3,2,1,0:T(4,128)(2,1)} %broadcast_in_dim.60) | data formatting | bytes 1048576
  90.2 5.1 %all-to-all-start.1 = ((bf16[8,2,16384]{2,1,0:T(2,128)(2,1)}), bf16[8,2,16384]{2,1,0:T(2,128)(2,1)}, u32[]{:S(2)}, u32[]{:S(2)}) async-start(bf16[8,2,16384]{2,1,0:T(2,128)(2,1)} %reshape.48), calls=%async_computation.1 | async-start | bytes 1048576 | tf_op jit(solution)/shard_map/all_to_all | solution.py:216
  95.3 0.7 broadcast_select_fusion.14
  96.0 0.7 broadcast_select_fusion.13
  96.7 0.9 collective-permute-start.12
  97.6 7.9 %all-to-all-done.1 = bf16[8,2,16384]{2,1,0:T(2,128)(2,1)} async-done(((bf16[8,2,16384]{2,1,0:T(2,128)(2,1)}), bf16[8,2,16384]{2,1,0:T(2,128)(2,1)}, u32[]{:S(2)}, u32[]{:S(2)}) %all-to-all-start.1) | async-done | bytes 524320 | tf_op jit(solution)/shard_map/all_to_all | solution.py:216
  105.5 3.5 %reshape.49 = bf16[8,16,8,4,64]{4,3,2,1,0:T(4,128)(2,1)} reshape(bf16[8,2,16384]{2,1,0:T(2,128)(2,1)} %all-to-all-done.1) | data formatting | bytes 1048576
  109.0 3.4 %copy.37 = bf16[16,8,4,8,64]{4,3,2,1,0:T(8,128)(2,1)} copy(bf16[16,8,4,8,64]{4,2,1,0,3:T(4,128)(2,1)} %bitcast.64) | data formatting | bytes 1048576 | tf_op jit(solution)/shard_map/transpose | solution.py:217
  112.5 2.7 %reshape.44 = bf16[16,8,4,512]{3,2,1,0:T(4,128)(2,1)} reshape(bf16[16,8,4,8,64]{4,3,2,1,0:T(8,128)(2,1)} %copy.37) | data formatting | bytes 1048576 | tf_op jit(solution)/shard_map/reshape | solution.py:217
  115.1 1.9 %broadcast_select_fusion.4 = (bf16[16,8,2,512]{3,2,1,0:T(2,128)(2,1)S(1)}, bf16[16,8,2,512]{3,2,1,0:T(2,128)(2,1)S(1)}) fusion(pred[]{:T(512)S(6)} %eq.15, bf16[16,8,4,512]{3,2,1,0:T(4,128)(2,1)} %reshape.44), kind=kLoop, calls=%fused_computation.21 | loop fusion | flops 262144 | bytes 1048577 | tf_op jit(solution)/shard_map/jit(_where)/select_n | solution.py:54
  117.6 0.8 copy-done.4
  118.5 5.6 %collective-permute-done.8 = bf16[16,8,2,512]{3,2,1,0:T(2,128)(2,1)S(1)} collective-permute-done((bf16[16,8,2,512]{3,2,1,0:T(2,128)(2,1)S(1)}, bf16[16,8,2,512]{3,2,1,0:T(2,128)(2,1)S(1)}, u32[]{:S(2)}, u32[]{:S(2)}) %collective-permute-start.8) | collective-permute-done | bytes 262176 | tf_op jit(solution)/shard_map/ppermute | solution.py:54
  124.6 0.9 select_maximum_fusion.field_ref
  125.5 2.7 %bottom_out.1 = bf16[16,8,8,64]{3,2,1,0:T(8,128)(2,1)S(1)} custom-call(bf16[18,10,8,512]{3,2,1,0:T(8,128)(2,1)S(1)} %select_maximum_fusion.field_ref, bf16[9,1,512,256]{3,2,1,0:T(8,128)(2,1)S(1)} %pad.23.weights_ref), custom_call_target="tpu_custom_call" | custom-call | tf_op jit(solution)/shard_map/bottom_out/pallas_call | solution.py:117
  128.9 0.9 reshape.50
  129.7 3.4 %all-to-all-start.2 = ((bf16[8,2,4608]{2,1,0:T(2,128)(2,1)}), bf16[8,2,4608]{2,1,0:T(2,128)(2,1)S(1)}, u32[]{:S(2)}, u32[]{:S(2)}) async-start(bf16[8,2,4608]{2,1,0:T(2,128)(2,1)} %reshape.50), calls=%async_computation.2 | async-start | bytes 294912 | tf_op jit(solution)/shard_map/all_to_all | solution.py:225
  133.1 0.8 fusion.15
  134.6 6.7 %all-to-all-done.2 = bf16[8,2,4608]{2,1,0:T(2,128)(2,1)S(1)} async-done(((bf16[8,2,4608]{2,1,0:T(2,128)(2,1)}), bf16[8,2,4608]{2,1,0:T(2,128)(2,1)S(1)}, u32[]{:S(2)}, u32[]{:S(2)}) %all-to-all-start.2) | async-done | bytes 147488 | tf_op jit(solution)/shard_map/all_to_all | solution.py:225
  141.9 0.8 broadcast_in_dim.64
  143.7 1.0 fusion.13
  144.7 7.8 %decode.1 = bf16[4,8,8,256]{3,2,1,0:T(8,128)(2,1)} custom-call(s32[1]{0:T(128)} %bitcast.place_ref, bf16[6,10,8,768]{3,2,1,0:T(8,128)(2,1)S(1)} %pad_maximum_fusion.field_ref, bf16[3,6,8,768]{3,2,1,0:T(8,128)(2,1)S(1)} %pad_maximum_fusion.6.edge_ref, bf16[9,3,768,256]{3,2,1,0:T(8,128)(2,1)} %bitcast.62), custom_call_target="tpu_custom_call" | custom-call | tf_op jit(solution)/shard_map/decode/pallas_call | solution.py:163
  (83 shorter events, 7.0 us)
Async XLA Ops:
  0.0 29.5 %copy-start = (bf16[3,3,3,128,128]{4,3,2,1,0:T(8,128)(2,1)S(1)}, bf16[3,3,3,128,128]{4,3,2,1,0:T(8,128)(2,1)}, u32[]{:S(2)}) copy-start(bf16[3,3,3,128,128]{4,3,2,1,0:T(8,128)(2,1)} %param.7) | copy-start | bytes 2654212
  1.3 12.4 %collective-permute-start = (bf16[3,16,16,128]{3,1,2,0:T(8,128)(2,1)S(1)}, bf16[3,16,16,128]{3,1,2,0:T(8,128)(2,1)S(1)}, u32[]{:S(2)}, u32[]{:S(2)}) collective-permute-start(bf16[3,16,16,128]{3,1,2,0:T(8,128)(2,1)S(1)} %get-tuple-element.17), channel_id=1, source_target_pairs={{0,112},{16,32},{32,16},{48,64},{64,48},{80,96},{96,80},{112,0},{1... | collective-permute-start | bytes 589832 | tf_op jit(solution)/shard_map/ppermute | solution.py:54
  8.0 8.4 %collective-permute-start.1 = (bf16[3,16,16,128]{3,1,2,0:T(8,128)(2,1)S(1)}, bf16[3,16,16,128]{3,1,2,0:T(8,128)(2,1)S(1)}, u32[]{:S(2)}, u32[]{:S(2)}) collective-permute-start(bf16[3,16,16,128]{3,1,2,0:T(8,128)(2,1)S(1)} %get-tuple-element.18), channel_id=1, source_target_pairs={{0,16},{16,0},{32,48},{48,32},{64,80},{80,64},{96,112},{112,96},{1... | collective-permute-start | bytes 589832 | tf_op jit(solution)/shard_map/ppermute | solution.py:53
  16.9 3.2 %collective-permute-start.3 = (bf16[14,3,16,128]{3,1,2,0:T(4,128)(2,1)S(1)}, bf16[14,3,16,128]{3,1,2,0:T(4,128)(2,1)S(1)}, u32[]{:S(2)}, u32[]{:S(2)}) collective-permute-start(bf16[14,3,16,128]{3,1,2,0:T(4,128)(2,1)S(1)} %broadcast_select_fusion.6), channel_id=1, source_target_pairs={{0,2},{2,0},{4,6},{6,4},{8,10},{10,8},{12,14},{14,12},{1,3},{3,1},... | collective-permute-start | bytes 516104 | tf_op jit(solution)/shard_map/ppermute | solution.py:53
  17.0 6.8 %collective-permute-start.2 = (bf16[14,3,16,128]{3,1,2,0:T(4,128)(2,1)S(1)}, bf16[14,3,16,128]{3,1,2,0:T(4,128)(2,1)S(1)}, u32[]{:S(2)}, u32[]{:S(2)}) collective-permute-start(bf16[14,3,16,128]{3,1,2,0:T(4,128)(2,1)S(1)} %get-tuple-element.8), channel_id=1, source_target_pairs={{0,14},{2,4},{4,2},{6,8},{8,6},{10,12},{12,10},{14,0},{1,15},{3,5}... | collective-permute-start | bytes 516104 | tf_op jit(solution)/shard_map/ppermute | solution.py:54
  24.1 4.6 %collective-permute-start.4 = (bf16[14,22,1,128]{3,1,2,0:T(8,128)(2,1)S(1)}, bf16[14,22,1,128]{3,1,2,0:T(8,128)(2,1)S(1)}, u32[]{:S(2)}, u32[]{:S(2)}) collective-permute-start(bf16[14,22,1,128]{3,1,2,0:T(8,128)(2,1)S(1)} %fusion.9), channel_id=1, source_target_pairs={{0,1},{1,0},{2,3},{3,2},{4,5},{5,4},{6,7},{7,6},{8,9},{9,8},{10,11... | collective-permute-start | bytes 236552 | tf_op jit(solution)/shard_map/ppermute | solution.py:46
  49.3 8.1 %copy-start.2 = (bf16[3,3,3,128,256]{4,3,2,1,0:T(8,128)(2,1)S(1)}, bf16[3,3,3,128,256]{4,3,2,1,0:T(8,128)(2,1)}, u32[]{:S(2)}) copy-start(bf16[3,3,3,128,256]{4,3,2,1,0:T(8,128)(2,1)} %param.8) | copy-start | bytes 5308420
  53.0 4.2 %collective-permute-start.5 = (bf16[6,10,1,128]{3,2,1,0:T(2,128)(2,1)S(1)}, bf16[6,10,1,128]{3,2,1,0:T(2,128)(2,1)S(1)}, u32[]{:S(2)}, u32[]{:S(2)}) collective-permute-start(bf16[6,10,1,128]{3,2,1,0:T(2,128)(2,1)S(1)} %broadcast_select_fusion.20), channel_id=1, source_target_pairs={{0,1},{1,0},{2,3},{3,2},{4,5},{5,4},{6,7},{7,6},{8,9},{9,8},{10,11... | collective-permute-start | bytes 46088 | tf_op jit(solution)/shard_map/ppermute | solution.py:46
  58.6 16.6 %copy-start.6 = (bf16[3,3,3,256,64]{3,4,2,1,0:T(8,128)(2,1)S(1)}, bf16[3,3,3,256,64]{3,4,2,1,0:T(8,128)(2,1)}, u32[]{:S(2)}) copy-start(bf16[3,3,3,256,64]{3,4,2,1,0:T(8,128)(2,1)} %param.9) | copy-start | bytes 2654212
  58.9 4.3 %collective-permute-start.6 = (bf16[2,1,4,256]{3,2,1,0:T(4,128)(2,1)S(1)}, bf16[2,1,4,256]{3,2,1,0:T(4,128)(2,1)S(1)}, u32[]{:S(2)}, u32[]{:S(2)}) collective-permute-start(bf16[2,1,4,256]{3,2,1,0:T(4,128)(2,1)S(1)} %get-tuple-element.36), channel_id=1, source_target_pairs={{0,14},{2,4},{4,2},{6,8},{8,6},{10,12},{12,10},{14,0},{1,15},{3,5}... | collective-permute-start | bytes 12296 | tf_op jit(solution)/shard_map/ppermute | solution.py:54
  59.9 3.3 %collective-permute-start.7 = (bf16[2,1,4,256]{3,2,1,0:T(4,128)(2,1)S(1)}, bf16[2,1,4,256]{3,2,1,0:T(4,128)(2,1)S(1)}, u32[]{:S(2)}, u32[]{:S(2)}) collective-permute-start(bf16[2,1,4,256]{3,2,1,0:T(4,128)(2,1)S(1)} %get-tuple-element.37), channel_id=1, source_target_pairs={{0,2},{2,0},{4,6},{6,4},{8,10},{10,8},{12,14},{14,12},{1,3},{3,1},... | collective-permute-start | bytes 12296 | tf_op jit(solution)/shard_map/ppermute | solution.py:53
  64.1 18.4 %all-to-all-start = ((bf16[16,2,6,4,256]{4,3,2,1,0:T(4,128)(2,1)}), bf16[16,2,6,4,256]{4,3,2,1,0:T(4,128)(2,1)}, u32[]{:S(2)}, u32[]{:S(2)}) async-start(bf16[16,2,6,4,256]{4,3,2,1,0:T(4,128)(2,1)} %broadcast_in_dim.59), calls=%async_computation | async-start | bytes 786432 | tf_op jit(solution)/shard_map/all_to_all | solution.py:208
  69.6 25.7 %collective-permute-start.10 = (bf16[1,8,8,256]{3,1,0,2:T(8,128)(2,1)S(1)}, bf16[1,8,8,256]{3,1,0,2:T(8,128)(2,1)S(1)}, u32[]{:S(2)}, u32[]{:S(2)}) collective-permute-start(bf16[1,8,8,256]{3,1,0,2:T(8,128)(2,1)S(1)} %get-tuple-element.26), channel_id=1, source_target_pairs={{0,112},{16,32},{32,16},{48,64},{64,48},{80,96},{96,80},{112,0},{1... | collective-permute-start | bytes 98312 | tf_op jit(solution)/shard_map/ppermute | solution.py:54
  75.1 20.1 %collective-permute-start.11 = (bf16[1,8,8,256]{3,1,0,2:T(8,128)(2,1)S(1)}, bf16[1,8,8,256]{3,1,0,2:T(8,128)(2,1)S(1)}, u32[]{:S(2)}, u32[]{:S(2)}) collective-permute-start(bf16[1,8,8,256]{3,1,0,2:T(8,128)(2,1)S(1)} %get-tuple-element.27), channel_id=1, source_target_pairs={{0,16},{16,0},{32,48},{48,32},{64,80},{80,64},{96,112},{112,96},{1... | collective-permute-start | bytes 98312 | tf_op jit(solution)/shard_map/ppermute | solution.py:53
  75.9 1.9 %copy-start.5 = (bf16[3,3,3,512,64]{3,4,2,1,0:T(8,128)(2,1)S(1)}, bf16[3,3,3,512,64]{3,4,2,1,0:T(8,128)(2,1)}, u32[]{:S(2)}) copy-start(bf16[3,3,3,512,64]{3,4,2,1,0:T(8,128)(2,1)} %param.10) | copy-start | bytes 5308420
  82.5 1.4 copy-start.1
  90.2 15.4 %all-to-all-start.1 = ((bf16[8,2,16384]{2,1,0:T(2,128)(2,1)}), bf16[8,2,16384]{2,1,0:T(2,128)(2,1)}, u32[]{:S(2)}, u32[]{:S(2)}) async-start(bf16[8,2,16384]{2,1,0:T(2,128)(2,1)} %reshape.48), calls=%async_computation.1 | async-start | bytes 1048576 | tf_op jit(solution)/shard_map/all_to_all | solution.py:216
  96.7 20.5 %collective-permute-start.13 = (bf16[6,1,8,256]{3,1,0,2:T(2,128)(2,1)}, bf16[6,1,8,256]{3,1,0,2:T(2,128)(2,1)S(1)}, u32[]{:S(2)}, u32[]{:S(2)}) collective-permute-start(bf16[6,1,8,256]{3,1,0,2:T(2,128)(2,1)} %broadcast_select_fusion.13), channel_id=1, source_target_pairs={{0,2},{2,0},{4,6},{6,4},{8,10},{10,8},{12,14},{14,12},{1,3},{3,1},... | collective-permute-start | bytes 73736 | tf_op jit(solution)/shard_map/ppermute | solution.py:53
  96.7 20.5 %collective-permute-start.12 = (bf16[6,1,8,256]{3,1,0,2:T(2,128)(2,1)}, bf16[6,1,8,256]{3,1,0,2:T(2,128)(2,1)S(1)}, u32[]{:S(2)}, u32[]{:S(2)}) collective-permute-start(bf16[6,1,8,256]{3,1,0,2:T(2,128)(2,1)} %get-tuple-element.5), channel_id=1, source_target_pairs={{0,14},{2,4},{4,2},{6,8},{8,6},{10,12},{12,10},{14,0},{1,15},{3,5}... | collective-permute-start | bytes 73736 | tf_op jit(solution)/shard_map/ppermute | solution.py:54
  115.1 9.5 %copy-start.3 = (bf16[16,8,4,512]{3,2,1,0:T(4,128)(2,1)S(1)}, bf16[16,8,4,512]{3,2,1,0:T(4,128)(2,1)}, u32[]{:S(2)}) copy-start(bf16[16,8,4,512]{3,2,1,0:T(4,128)(2,1)} %reshape.44) | copy-start | bytes 1572868
  117.0 7.1 %collective-permute-start.8 = (bf16[16,8,2,512]{3,2,1,0:T(2,128)(2,1)S(1)}, bf16[16,8,2,512]{3,2,1,0:T(2,128)(2,1)S(1)}, u32[]{:S(2)}, u32[]{:S(2)}) collective-permute-start(bf16[16,8,2,512]{3,2,1,0:T(2,128)(2,1)S(1)} %get-tuple-element.15), channel_id=1, source_target_pairs={{0,14},{2,4},{4,2},{6,8},{8,6},{10,12},{12,10},{14,0},{1,15},{3,5}... | collective-permute-start | bytes 786440 | tf_op jit(solution)/shard_map/ppermute | solution.py:54
  117.1 7.0 %collective-permute-start.9 = (bf16[16,8,2,512]{3,2,1,0:T(2,128)(2,1)S(1)}, bf16[16,8,2,512]{3,2,1,0:T(2,128)(2,1)S(1)}, u32[]{:S(2)}, u32[]{:S(2)}) collective-permute-start(bf16[16,8,2,512]{3,2,1,0:T(2,128)(2,1)S(1)} %get-tuple-element.16), channel_id=1, source_target_pairs={{0,2},{2,0},{4,6},{6,4},{8,10},{10,8},{12,14},{14,12},{1,3},{3,1},... | collective-permute-start | bytes 786440 | tf_op jit(solution)/shard_map/ppermute | solution.py:53
  117.6 0.8 copy-start.4
  129.7 11.6 %all-to-all-start.2 = ((bf16[8,2,4608]{2,1,0:T(2,128)(2,1)}), bf16[8,2,4608]{2,1,0:T(2,128)(2,1)S(1)}, u32[]{:S(2)}, u32[]{:S(2)}) async-start(bf16[8,2,4608]{2,1,0:T(2,128)(2,1)} %reshape.50), calls=%async_computation.2 | async-start | bytes 294912 | tf_op jit(solution)/shard_map/all_to_all | solution.py:225
  133.9 9.7 %collective-permute-start.14 = (bf16[6,10,256]{2,1,0:T(8,128)(2,1)S(1)}, bf16[6,10,256]{2,1,0:T(8,128)(2,1)}, u32[]{:S(2)}, u32[]{:S(2)}) collective-permute-start(bf16[6,10,256]{2,1,0:T(8,128)(2,1)S(1)} %fusion.15), channel_id=1, source_target_pairs={{0,1},{1,0},{2,3},{3,2},{4,5},{5,4},{6,7},{7,6},{8,9},{9,8},{10,11... | collective-permute-start | bytes 92168 | tf_op jit(solution)/shard_map/ppermute | solution.py:230

commit v2 on v1

v2 whole, which is shorter than its diff:
```python
import jax
import jax.numpy as jnp
from jax import lax
from jax.experimental import pallas as pl
from jax.experimental.pallas import tpu as pltpu
from jax.sharding import PartitionSpec as P


def shrink(field):
    size_x, size_y, size_z, channels = field.shape
    blocks = field.reshape(size_x // 2, 2, size_y // 2, 2, size_z // 2, 2, channels)
    return jnp.max(blocks, axis=(1, 3, 5))


def halo(field, axis, count, dim, width):
    place = lax.axis_index(axis)
    size = field.shape[dim]
    low = lax.slice_in_dim(field, 0, width, axis=dim)
    high = lax.slice_in_dim(field, size - width, size, axis=dim)
    zero = jnp.zeros_like(low)
    if count == 2:
        got = lax.ppermute(jnp.where(place == 0, high, low), axis, [(0, 1), (1, 0)])
        below = jnp.where(place == 1, got, zero)
        above = jnp.where(place == 0, got, zero)
        return below, above
    even = place % 2 == 0
    inner = [(i, i ^ 1) for i in range(count)]
    outer = [(i, (((i + 1) ^ 1) - 1) % count) for i in range(count)]
    got_in = lax.ppermute(jnp.where(even, high, low), axis, inner)
    got_out = lax.ppermute(jnp.where(even, low, high), axis, outer)
    below = jnp.where(place > 0, jnp.where(even, got_out, got_in), zero)
    above = jnp.where(place < count - 1, jnp.where(even, got_in, got_out), zero)
    return below, above


def extend(field, axis, count, dim, width):
    below, above = halo(field, axis, count, dim, width)
    return jnp.concatenate([below, field, above], axis=dim)


def roll_rows(block, shift):
    return pltpu.roll(block, shift % block.shape[1], 1)


def tile_conv(field, weights, name):
    size_a, size_b, size_s, channels = field.shape
    size_a, size_b = size_a - 2, size_b - 2
    steps, taps, _, width = weights.shape
    filters = width if taps == 3 else 64
    wide = width if taps == 3 else 128
    part = max(1, 256 // (size_b * size_s))

    def body(field_ref, weights_ref, out_ref):
        for first in range(0, size_a, part):
            rows = part * size_b * size_s
            groups = part * size_b
            blocks = []
            for step in range(steps):
                da, db = step // 3, step % 3
                block = field_ref[first + da : first + da + part, db : db + size_b]
                if size_s % 16:
                    block = block.astype(jnp.float32)
                blocks.append(block.reshape(rows, channels).astype(jnp.bfloat16))
            block = jnp.concatenate(blocks, axis=1)
            sums = []
            for tap in range(taps):
                kernel = weights_ref[:, tap].reshape(steps * channels, width)
                sums.append(jnp.dot(block, kernel, preferred_element_type=jnp.float32))
            if taps == 3:
                low, mid, high = [total.reshape(groups, size_s, width) for total in sums]
            else:
                low = sums[0][:, :128].reshape(groups, size_s, 128)
                mid = pltpu.roll(sums[0][:, :128], 64, 1).reshape(groups, size_s, 128)
                high = sums[0][:, 128:].reshape(groups, size_s, 128)
            if size_s == 8:
                total = roll_rows(low, 1) + mid + roll_rows(high, -1)
            else:
                index = lax.broadcasted_iota(jnp.int32, (groups, 8, wide), 1)
                down = jnp.where(index == 0, roll_rows(low[:, 8:], 1), roll_rows(low[:, :8], 1))
                up = jnp.where(index == 7, roll_rows(high[:, 8:], -1), roll_rows(high[:, :8], -1))
                total = down + mid[:, :8] + up
            total = jnp.maximum(total, 0.0).reshape(part, size_b, 8, wide)
            out_ref[first : first + part] = total[..., :filters].astype(out_ref.dtype)

    return pl.pallas_call(
        body,
        in_specs=[pl.BlockSpec(memory_space=pltpu.VMEM)] * 2,
        out_specs=pl.BlockSpec(memory_space=pltpu.VMEM),
        out_shape=jax.ShapeDtypeStruct((size_a, size_b, 8, filters), jnp.bfloat16),
        compiler_params=pltpu.CompilerParams(vmem_limit_bytes=40 << 20),
        name=name,
    )(field, weights)


def encode(place, field, edge, weights):
    size_x, size_y, size_z, channels = field.shape
    size_x, size_y = size_x - 2, size_y - 2
    filters = weights.shape[-1] // 2
    rows, extra = size_y * size_z, edge.shape[2]
    pool_y, pool_z = size_y // 2, size_z // 2

    def body(place_ref, field_ref, edge_ref, weights_ref, out_ref, rows_ref):
        index = lax.broadcasted_iota(jnp.int32, (size_y, size_z, 2 * filters), 1)
        first = place_ref[2] == 0
        line = lax.broadcasted_iota(jnp.int32, (pool_y, pool_z, filters), 0)
        inside_y = ((line > 0) | (place_ref[1] > 0)) & ((line < pool_y - 1) | (place_ref[1] < place_ref[4]))
        for pair in range(size_x // 2):
            blocks = []
            for plane in range(4):
                for dy in range(3):
                    main = field_ref[2 * pair + plane, dy : dy + size_y].reshape(rows, channels)
                    blocks.append(jnp.concatenate([main, edge_ref[dy, 2 * pair + plane]], axis=0))
            block = jnp.concatenate(blocks, axis=1)
            sums = []
            for tap in range(3):
                kernel = weights_ref[:, :, tap].reshape(12 * channels, 2 * filters)
                sums.append(jnp.dot(block, kernel, preferred_element_type=jnp.float32))
            low, mid, high = [total[:rows].reshape(size_y, size_z, 2 * filters) for total in sums]
            below = jnp.where(first, 0.0, sums[0][rows : rows + size_y])
            above = jnp.where(first, sums[2][rows : rows + size_y], 0.0)
            down = jnp.where(index == 0, below[:, None, :], pltpu.roll(low, 1, 1))
            up = jnp.where(index == size_z - 1, above[:, None, :], pltpu.roll(high, size_z - 1, 1))
            total = jnp.maximum(down + mid + up, 0.0)
            total = jnp.maximum(total[..., :filters], total[..., filters:])
            total = jnp.max(total.reshape(pool_y, 2, size_z, filters), axis=1)
            rows_ref[...] = total.reshape(pool_y * size_z, filters)
            total = jnp.maximum(
                rows_ref[pl.ds(0, pool_y * pool_z, stride=2), :], rows_ref[pl.ds(1, pool_y * pool_z, stride=2), :]
            ).reshape(pool_y, pool_z, filters)
            inside = inside_y
            if pair == 0:
                inside = inside & (place_ref[0] > 0)
            if pair == size_x // 2 - 1:
                inside = inside & (place_ref[0] < place_ref[3])
            out_ref[pair] = jnp.where(inside, total, 0.0).astype(out_ref.dtype)

    return pl.pallas_call(
        body,
        in_specs=[pl.BlockSpec(memory_space=pltpu.SMEM)] + [pl.BlockSpec(memory_space=pltpu.VMEM)] * 3,
        out_specs=pl.BlockSpec(memory_space=pltpu.VMEM),
        out_shape=jax.ShapeDtypeStruct((size_x // 2, pool_y, pool_z, filters), jnp.bfloat16),
        scratch_shapes=[pltpu.VMEM((pool_y * size_z, filters), jnp.float32)],
        compiler_params=pltpu.CompilerParams(vmem_limit_bytes=32 << 20),
        name="encode",
    )(place, field, edge, weights)


def paired(weights):
    grow = [(0, 0)] * 4
    return jnp.concatenate([jnp.pad(weights, [(0, 1)] + grow), jnp.pad(weights, [(1, 0)] + grow)], axis=4)


def halves(pair_low, pair_high):
    lane = lax.broadcasted_iota(jnp.int32, pair_low.shape, pair_low.ndim - 1)
    axis = pair_low.ndim - 1
    even = jnp.where(lane < 64, pair_low, pltpu.roll(pair_high, 64, axis))
    odd = jnp.where(lane < 64, pltpu.roll(pair_low, 64, axis), pair_high)
    return even, odd


def side_by_side(even, odd):
    lane = lax.broadcasted_iota(jnp.int32, even.shape, even.ndim - 1)
    return jnp.where(lane < 64, even, pltpu.roll(odd, 64, even.ndim - 1))


def column_product(pad_ref, weights_ref, first, start, planes, size_z):
    channels = pad_ref.shape[-1]
    rows = planes * size_z * 8
    blocks = []
    for dx in range(3):
        for dz in range(3):
            block = pad_ref[first + dx : first + dx + planes, pl.ds(start + dz, size_z)]
            blocks.append(block.reshape(rows, channels).astype(jnp.bfloat16))
    block = jnp.concatenate(blocks, axis=1)
    total = jnp.dot(block, weights_ref[...].reshape(9 * channels, 256), preferred_element_type=jnp.float32)
    low = total[:, :128].reshape(planes * size_z, 8, 128)
    mid = pltpu.roll(total[:, :128], 64, 1).reshape(planes * size_z, 8, 128)
    high = total[:, 128:].reshape(planes * size_z, 8, 128)
    total = pltpu.roll(low, 1, 1) + mid + pltpu.roll(high, 7, 1)
    return jnp.maximum(total, 0.0).reshape(planes, size_z, 8, 128)


def bottom_in(place, field, weights):
    count, own_x, own_z, _, channels = field.shape
    devices = count // 2
    size_x, all_z, size_z, size_y = devices * own_x, 2 * own_z, own_z + 2, own_z

    def body(place_ref, field_ref, weights_ref, out_ref, pad_ref):
        zero = jnp.zeros((all_z + 2, 8, channels), jnp.float32)
        pad_ref[0] = zero
        pad_ref[size_x + 1] = zero
        for x in range(size_x):
            pad_ref[x + 1, 0] = zero[0]
            pad_ref[x + 1, all_z + 1] = zero[0]
        for i in range(devices):
            for half in range(2):
                block = field_ref[2 * i + half].astype(jnp.float32)
                pad_ref[1 + own_x * i : 1 + own_x * i + own_x, 1 + own_z * half : 1 + own_z * half + own_z] = block
        start = 2 * place_ref[2]
        for first in range(0, size_x, 4):
            total = column_product(pad_ref, weights_ref, first, start, 4, size_z)
            for pair in range(2):
                both = side_by_side(total[2 * pair], total[2 * pair + 1])[:, 1 : size_y + 1].astype(out_ref.dtype)
                for i in range(devices):
                    out_ref[i, first // 2 + pair] = both

    return pl.pallas_call(
        body,
        in_specs=[pl.BlockSpec(memory_space=pltpu.SMEM)] + [pl.BlockSpec(memory_space=pltpu.VMEM)] * 2,
        out_specs=pl.BlockSpec(memory_space=pltpu.VMEM),
        out_shape=jax.ShapeDtypeStruct((devices, size_x // 2, size_z, size_y, 128), jnp.bfloat16),
        scratch_shapes=[pltpu.VMEM((size_x + 2, all_z + 2, 8, channels), jnp.float32)],
        compiler_params=pltpu.CompilerParams(vmem_limit_bytes=16 << 20),
        name="bottom_in",
    )(place, field, weights)


def bottom_out(place, field, weights):
    devices, pairs, size_z, _, _ = field.shape
    size_x, channels = 2 * pairs, 64 * devices
    own_x = size_x // devices

    def body(place_ref, field_ref, weights_ref, out_ref, pad_ref, total_ref):
        zero = jnp.zeros((size_z + 2, 8, channels), jnp.float32)
        for ref in (pad_ref, total_ref):
            wide = ref.shape[-1]
            ref[0] = zero[..., :wide]
            ref[size_x + 1] = zero[..., :wide]
            for x in range(size_x):
                ref[x + 1, 0] = zero[0, :, :wide]
                ref[x + 1, size_z + 1] = zero[0, :, :wide]
        for k in range(devices // 2):
            for pair in range(pairs):
                low, high = [field_ref[2 * k + i, pair].astype(jnp.float32) for i in range(2)]
                even, odd = halves(low, high)
                pad_ref[1 + 2 * pair, 1 : size_z + 1, :, 128 * k : 128 * k + 128] = even
                pad_ref[2 + 2 * pair, 1 : size_z + 1, :, 128 * k : 128 * k + 128] = odd
        for first in range(0, size_x, 4):
            total = column_product(pad_ref, weights_ref, first, 0, 4, size_z)
            total_ref[1 + first : 5 + first, 1 : size_z + 1] = total
        start = 2 * place_ref[2]
        for i in range(size_x // 2 + 1):
            low, high = [total_ref[2 * i + n, pl.ds(start, size_z)] for n in range(2)]
            both = side_by_side(low, high).astype(out_ref.dtype)
            if i < devices:
                out_ref[i, 0] = both
            if i > 0:
                out_ref[i - 1, 1] = both

    return pl.pallas_call(
        body,
        in_specs=[pl.BlockSpec(memory_space=pltpu.SMEM)] + [pl.BlockSpec(memory_space=pltpu.VMEM)] * 2,
        out_specs=pl.BlockSpec(memory_space=pltpu.VMEM),
        out_shape=jax.ShapeDtypeStruct((devices, own_x, size_z, 8, 128), jnp.bfloat16),
        scratch_shapes=[
            pltpu.VMEM((size_x + 2, size_z + 2, 8, channels), jnp.float32),
            pltpu.VMEM((size_x + 2, size_z + 2, 8, 128), jnp.float32),
        ],
        compiler_params=pltpu.CompilerParams(vmem_limit_bytes=24 << 20),
        name="bottom_out",
    )(place, field, weights)


def decode(place, bottom, skip, edge, weights):
    devices, pairs, coarse_z, _, _ = bottom.shape
    full_x, full_y, size_z, skip_channels = skip.shape
    size_x, size_y = full_x - 2, full_y - 2
    channels = 64 * devices + skip_channels
    filters = weights.shape[-1]
    rows, extra = size_x * size_y * size_z, size_x * size_y
    weights = weights.reshape(9, 3, channels, filters)

    def body(place_ref, bottom_ref, skip_ref, edge_ref, weights_hbm, out_ref, weights_ref, main_ref, side_ref, sums_ref, sems):
        copies = [pltpu.make_async_copy(weights_hbm.at[step], weights_ref.at[step], sems.at[step]) for step in range(9)]
        for copy in copies:
            copy.start()
        first = place_ref[2] == 0
        planes = [[] for _ in range(2 * pairs)]
        for k in range(devices // 2):
            for pair in range(pairs):
                low, high = [bottom_ref[2 * k + i, pair].astype(jnp.float32) for i in range(2)]
                even, odd = halves(low, high)
                planes[2 * pair].append(even.reshape(coarse_z * 8, 128))
                planes[2 * pair + 1].append(odd.reshape(coarse_z * 8, 128))

        def choice(y, z, source):
            line = (y + 1) // 2 + 1
            inside = ((line > 1) | (place_ref[1] > 0)) & ((line < coarse_z) | (place_ref[1] < place_ref[4]))
            return jnp.where((source == z * 8 + line) & inside, 1.0, 0.0).astype(jnp.bfloat16)

        shape = (full_y * size_z, coarse_z * 8)
        row = lax.broadcasted_iota(jnp.int32, shape, 0)
        spread = choice(row // size_z, row % size_z // 2 + 1, lax.broadcasted_iota(jnp.int32, shape, 1))
        shape = (16, coarse_z * 8)
        row = lax.broadcasted_iota(jnp.int32, shape, 0)
        other = jnp.where(first, coarse_z - 1, 0)
        spread_edge = choice(row, other, lax.broadcasted_iota(jnp.int32, shape, 1))
        for plane in range(2 * pairs):
            coarse = jnp.concatenate(planes[plane], axis=1).astype(jnp.bfloat16)
            fine = jnp.dot(spread, coarse, preferred_element_type=jnp.float32)
            fine_edge = jnp.dot(spread_edge, coarse, preferred_element_type=jnp.float32)
            for x in range(full_x):
                if (x + 1) // 2 != plane:
                    continue
                joined = jnp.concatenate([fine, skip_ref[x].astype(jnp.float32).reshape(full_y * size_z, skip_channels)], axis=1)
                joined_edge = jnp.concatenate([fine_edge, edge_ref[x].astype(jnp.float32)], axis=1)
                for dy in range(3):
                    main_ref[dy, x] = joined[8 * dy : 8 * dy + size_y * size_z].astype(jnp.bfloat16)
                    side_ref[dy, x] = joined_edge[dy : dy + size_y]
        for dx in range(3):
            blocks = []
            for dy in range(3):
                main = main_ref[dy, dx : dx + size_x].reshape(rows, channels)
                side = side_ref[dy, dx : dx + size_x].reshape(extra, channels).astype(jnp.bfloat16)
                blocks.append(jnp.concatenate([main, side], axis=0))
                copies[3 * dx + dy].wait()
            block = jnp.concatenate(blocks, axis=1)
            for tap in range(3):
                kernel = weights_ref[3 * dx : 3 * dx + 3, tap].reshape(3 * channels, filters)
                product = jnp.dot(block, kernel, preferred_element_type=jnp.float32)
                if dx == 0:
                    sums_ref[tap] = product
                else:
                    sums_ref[tap] += product
        low, mid, high = [sums_ref[tap, :rows].reshape(extra, size_z, filters) for tap in range(3)]
        below = jnp.where(first, 0.0, sums_ref[0, rows:])
        above = jnp.where(first, sums_ref[2, rows:], 0.0)
        index = lax.broadcasted_iota(jnp.int32, (extra, size_z, filters), 1)
        down = jnp.where(index == 0, below[:, None, :], roll_rows(low, 1))
        up = jnp.where(index == size_z - 1, above[:, None, :], roll_rows(high, -1))
        out_ref[...] = (down + mid + up).reshape(size_x, size_y, size_z, filters).astype(out_ref.dtype)

    return pl.pallas_call(
        body,
        in_specs=[pl.BlockSpec(memory_space=pltpu.SMEM)]
        + [pl.BlockSpec(memory_space=pltpu.VMEM)] * 3
        + [pl.BlockSpec(memory_space=pl.ANY)],
        out_specs=pl.BlockSpec(memory_space=pltpu.VMEM),
        out_shape=jax.ShapeDtypeStruct((size_x, size_y, size_z, filters), jnp.bfloat16),
        scratch_shapes=[
            pltpu.VMEM(weights.shape, weights.dtype),
            pltpu.VMEM((3, full_x, size_y * size_z, channels), jnp.bfloat16),
            pltpu.VMEM((3, full_x, size_y, channels), jnp.float32),
            pltpu.VMEM((3, rows + extra, filters), jnp.float32),
            pltpu.SemaphoreType.DMA((9,)),
        ],
        compiler_params=pltpu.CompilerParams(vmem_limit_bytes=32 << 20),
        name="decode",
    )(place, bottom, skip, edge, weights)


def beside(weights):
    channels, filters = weights.shape[3:]
    weights = weights.transpose(0, 2, 3, 1, 4).reshape(9, channels, 3 * filters)
    return jnp.pad(weights, ((0, 0), (0, 0), (0, 256 - 3 * filters)))


def solution(mesh):
    gx, gy, gz = mesh.shape["gx"], mesh.shape["gy"], mesh.shape["gz"]

    def local(volume, w_full, w_half, w_bottom_in, w_bottom_out, w_up):
        place_z = lax.axis_index("gz")
        place = jnp.stack([lax.axis_index("gx"), lax.axis_index("gy"), place_z, jnp.int32(gx - 1), jnp.int32(gy - 1)])
        swap = [(0, 1), (1, 0)]

        def edge_of(plane_low, plane_high):
            return lax.ppermute(jnp.where(place_z == 0, plane_high, plane_low), "gz", swap)

        below, above = halo(volume, "gx", gx, 0, 3)
        w_pair, w_in, w_out = paired(w_full), beside(w_bottom_in), beside(w_bottom_out)
        below, above, w_pair, w_in, w_out = lax.optimization_barrier((below, above, w_pair, w_in, w_out))
        field = jnp.concatenate([below, volume, above], axis=0)
        field = extend(field, "gy", gy, 1, 3)
        edge = edge_of(field[:, :, 0], field[:, :, -1])
        rows = field.shape[1] - 2
        edge = jnp.stack([jnp.pad(edge[:, dy : dy + rows], ((0, 0), (0, -rows % 16), (0, 0))) for dy in range(3)])
        pooled = encode(place, field, edge, w_pair)

        got = edge_of(pooled[:, :, 0], pooled[:, :, -1])[:, :, None]
        zero = jnp.zeros_like(got)
        above, below = jnp.where(place_z == 0, got, zero), jnp.where(place_z == 0, zero, got)
        pooled = jnp.concatenate([pooled, above, jnp.zeros_like(pooled)[:, :, :6], below], axis=2)
        skip = tile_conv(pooled, w_half.reshape(9, 3, w_half.shape[3], w_half.shape[4]), "half")
        coarse = shrink(skip).transpose(0, 2, 1, 3)
        own_y = coarse.shape[2]

        column = jnp.pad(extend(coarse, "gy", gy, 2, 1), ((0, 0), (0, 0), (0, 6 - own_y), (0, 0)))
        column = jnp.broadcast_to(column[None], (gx * gz,) + column.shape)
        column = lax.all_to_all(column, ("gx", "gz"), 0, 0)
        first = bottom_in(place, column, w_in)
        first = lax.all_to_all(first, "gx", 0, 0)
        first = extend(first, "gy", gy, 3, 2)
        second = bottom_out(place, first, w_out)
        second = lax.all_to_all(second, "gx", 0, 0)

        around = extend(skip, "gx", gx, 0, 1)
        around = extend(around, "gy", gy, 1, 1)
        side = edge_of(around[:, :, 0], around[:, :, -1])
        side = jnp.pad(side, ((0, 0), (0, -side.shape[1] % 16), (0, 0)))
        return decode(place, second, around, side, w_up)

    space = P("gx", "gy", "gz", None)
    filters = P(None, None, None, None, "gx")
    return jax.shard_map(
        local,
        mesh=mesh,
        in_specs=(space, P(), P(), filters, filters, P()),
        out_specs=space,
        check_vma=False,
    )
```

time: 153 us -> 128 us (0.84)
  matrix products: 19.8 us -> 0 us
  local copies, waits for them, and re-layouts: 30.9 us -> 20 us
  Pallas kernels: 13.1 us -> 21.7 us
  waiting for transfers between devices: 42.7 us -> 34.3 us
  other arithmetic: 11.8 us -> 15.8 us
    conv_general_dilated x1 -> x0, matrix products: 19.8 us -> none  [conv(): lax.conv_general_dilated(field[None], kernel, (1, 1, 1), 'VALID', dimensi...]
    pallas_call x1 -> x4, Pallas kernels: 7.77 us -> 20.5 us  [the longest x1 8.74 us: decode(): pl.pallas_call(body, in_specs=[pl.BlockSpec(memory_space=pltpu.SMEM)] + [...]
    ppermute x6, starting transfers between devices: 0.21 us -> 5.85 us  [halo(): got_in = lax.ppermute(jnp.where(even, high, low), axis, inner)]
    ppermute x6, starting transfers between devices: 17.4 us -> 12.2 us  [halo(): got_out = lax.ppermute(jnp.where(even, low, high), axis, outer)]
    ppermute x6, waiting for transfers between devices: 18.3 us -> 13.3 us  [halo(): got_out = lax.ppermute(jnp.where(even, low, high), axis, outer)]
    transpose x4 -> x0, local copies, waits for them, and re-layouts: 4.79 us -> none  [the longest x1 3.42 us: local(): first.transpose(1, 2, 3, 0, 4).reshape(first.shape[1:4] + (gx * part,))]
    pallas_call x3 -> x1, Pallas kernels: 5.31 us -> 1.19 us  [tile_conv(): pl.pallas_call(body, in_specs=[pl.BlockSpec(memory_space=pltpu.VMEM)] * 2...]
    all_to_all x1, waiting for transfers between devices: 0.01 us -> 2.82 us  [local(): column = lax.all_to_all(column, ('gx', 'gz'), 0, 0)]
  transfers between devices with their start and end apart: 18 -> 18, of which waited for: 9 -> 9; matrix products, arithmetic and copies ran while one was open for 19% -> 10% of each run, Pallas kernels for 1% -> 2%
where the time goes in v2:
time: 128 us; the launch traced here: 127 us
  starting transfers between devices  34.3 us (27%)
  waiting for transfers between devices  34.3 us (27%)
  Pallas kernels  21.7 us (17%)
  local copies, waits for them, and re-layouts  20 us (16%)
  other arithmetic  15.8 us (12%)
    ppermute x6, waiting for transfers between devices, halo(): got_out = lax.ppermute(jnp.where(even, low, high), axis, outer)  13.3 us
    ppermute x6, starting transfers between devices, halo(): got_out = lax.ppermute(jnp.where(even, low, high), axis, outer)  12.2 us
    unnamed x32, local copies, waits for them, and re-layouts  9.85 us
    pallas_call x1, Pallas kernels, decode(): pl.pallas_call(body, in_specs=[pl.BlockSpec(memory_space=pltpu.SMEM)] + [...  8.74 us
    ppermute x3, waiting for transfers between devices, edge_of(): lax.ppermute(jnp.where(place_z == 0, plane_high, plane_low), 'gz', swap)  8.04 us
    pallas_call x1, Pallas kernels, encode(): pl.pallas_call(body, in_specs=[pl.BlockSpec(memory_space=pltpu.SMEM)] + [...  5.93 us
    all_to_all x1, waiting for transfers between devices, local(): first = lax.all_to_all(first, 'gx', 0, 0)  5.92 us
    ppermute x6, starting transfers between devices, halo(): got_in = lax.ppermute(jnp.where(even, high, low), axis, inner)  5.85 us
  transfers between devices with their start and end apart: 18, of which 9 were waited for; matrix products, arithmetic and copies ran while one was open for 10% of the time, Pallas kernels for 2%

profile of v2, /device:TPU:0, one launch (start us, length us, event | category | flops | bytes accessed | tf_op | source)
XLA Modules:
  0.0 126.7 jit_solution(7171266636728946758)
XLA Ops:
  0.0 1.3 copy.67
  1.3 0.8 broadcast_select_fusion.8
  2.1 3.1 %collective-permute-start.1 = (bf16[3,16,16,128]{3,1,0,2:T(8,128)(2,1)}, bf16[3,16,16,128]{3,1,0,2:T(8,128)(2,1)}, u32[]{:S(2)}, u32[]{:S(2)}) collective-permute-start(bf16[3,16,16,128]{3,1,0,2:T(8,128)(2,1)} %get-tuple-element.20), channel_id=1, source_target_pairs={{0,16},{16,0},{32,48},{48,32},{64,80},{80,64},{96,112},{112,96},{1... | collective-permute-start | bytes 589832 | tf_op jit(solution)/shard_map/ppermute | solution.py:29
  5.2 4.0 %collective-permute-start = (bf16[3,16,16,128]{3,1,0,2:T(8,128)(2,1)}, bf16[3,16,16,128]{3,1,0,2:T(8,128)(2,1)}, u32[]{:S(2)}, u32[]{:S(2)}) collective-permute-start(bf16[3,16,16,128]{3,1,0,2:T(8,128)(2,1)} %get-tuple-element.21), channel_id=1, source_target_pairs={{0,112},{16,32},{32,16},{48,64},{64,48},{80,96},{96,80},{112,0},{1... | collective-permute-start | bytes 589832 | tf_op jit(solution)/shard_map/ppermute | solution.py:30
  9.2 1.5 %copy.70 = bf16[9,256,192]{2,1,0:T(8,128)(2,1)} copy(bf16[9,256,192]{1,2,0:T(8,128)(2,1)S(1)} %bitcast.34) | data formatting | bytes 1769472 | tf_op jit(solution)/shard_map/reshape | solution.py:354
  10.9 2.4 %copy.72 = bf16[9,512,192]{2,1,0:T(8,128)(2,1)} copy(bf16[9,512,192]{1,2,0:T(8,128)(2,1)S(1)} %bitcast.33) | data formatting | bytes 3538944 | tf_op jit(solution)/shard_map/reshape | solution.py:354
  13.4 1.6 %pad.36.weights_ref = bf16[9,256,256]{2,1,0:T(8,128)(2,1)S(1)} pad(bf16[9,256,192]{2,1,0:T(8,128)(2,1)} %copy.70, bf16[]{:T(256)} %constant.51.clone.1), padding=0_0x0_0x0_64 | pad | bytes 2064386 | tf_op jit(solution)/shard_map/jit(_pad)/pad | solution.py:355
  15.8 0.7 copy-done.12
  16.6 1.8 %fusion.2.weights_ref = bf16[4,3,3,128,256]{4,3,2,1,0:T(8,128)(2,1)} fusion(bf16[3,3,3,128,128]{4,3,2,1,0:T(8,128)(2,1)S(1)} %copy-done.12), kind=kLoop, calls=%fused_computation.4 | loop fusion | flops 9437184 | bytes 3244032 | tf_op jit(solution)/shard_map/concatenate | solution.py:150
  18.3 1.1 select_select_fusion.2
  19.7 0.9 copy-done.6
  20.6 1.0 broadcast_select_fusion.7
  21.6 1.9 %collective-permute-start.2 = (bf16[14,3,16,128]{3,1,0,2:T(4,128)(2,1)}, bf16[14,3,16,128]{3,1,0,2:T(4,128)(2,1)}, u32[]{:S(2)}, u32[]{:S(2)}) collective-permute-start(bf16[14,3,16,128]{3,1,0,2:T(4,128)(2,1)} %get-tuple-element.18), channel_id=1, source_target_pairs={{0,14},{2,4},{4,2},{6,8},{8,6},{10,12},{12,10},{14,0},{1,15},{3,5}... | collective-permute-start | bytes 516104 | tf_op jit(solution)/shard_map/ppermute | solution.py:30
  23.5 5.1 %collective-permute-done.2 = bf16[14,3,16,128]{3,1,0,2:T(4,128)(2,1)} collective-permute-done((bf16[14,3,16,128]{3,1,0,2:T(4,128)(2,1)}, bf16[14,3,16,128]{3,1,0,2:T(4,128)(2,1)}, u32[]{:S(2)}, u32[]{:S(2)}) %collective-permute-start.2) | collective-permute-done | bytes 172064 | tf_op jit(solution)/shard_map/ppermute | solution.py:30
  28.6 1.3 select_select_fusion.1
  29.8 2.0 %pad_maximum_fusion = bf16[14,22,16,128]{3,1,0,2:T(8,128)(2,1)S(1)} fusion(bf16[14,3,16,128]{3,1,0,2:T(4,128)(2,1)S(1)} %get-tuple-element.23, bf16[14,16,16,128]{3,1,0,2:T(8,128)(2,1)} %copy-done.6, bf16[14,3,16,128]{3,1,0,2:T(4,128)(2,1)S(1)} %get-tuple-element.22), kind=kLoop, calls=%fused_computation.5 | loop fusion | flops 3784704 | bytes 2523136 | tf_op jit(solution)/shard_map/concatenate | solution.py:38
  31.9 1.6 %collective-permute-start.4 = (bf16[14,22,128]{2,1,0:T(8,128)(2,1)S(1)}, bf16[14,22,128]{2,1,0:T(8,128)(2,1)S(1)}, u32[]{:S(2)}, u32[]{:S(2)}) collective-permute-start(bf16[14,22,128]{2,1,0:T(8,128)(2,1)S(1)} %fusion.3), channel_id=1, source_target_pairs={{0,1},{1,0},{2,3},{3,2},{4,5},{5,4},{6,7},{7,6},{8,9},{9,8},{10,11... | collective-permute-start | bytes 236552 | tf_op jit(solution)/shard_map/ppermute | solution.py:367
  33.8 2.6 %collective-permute-done.4 = bf16[14,22,128]{2,1,0:T(8,128)(2,1)S(1)} collective-permute-done((bf16[14,22,128]{2,1,0:T(8,128)(2,1)S(1)}, bf16[14,22,128]{2,1,0:T(8,128)(2,1)S(1)}, u32[]{:S(2)}, u32[]{:S(2)}) %collective-permute-start.4) | collective-permute-done | bytes 78880 | tf_op jit(solution)/shard_map/ppermute | solution.py:367
  36.6 5.9 %encode.1 = bf16[6,10,8,128]{3,2,1,0:T(8,128)(2,1)S(1)} custom-call(s32[5]{0:T(128)S(1)} %pad_add_fusion.place_ref, bf16[14,22,16,128]{3,2,1,0:T(8,128)(2,1)S(1)} %copy.74.field_ref, bf16[3,14,32,128]{3,2,1,0:T(8,128)(2,1)S(1)} %pad_maximum_fusion.3.edge_ref, bf16[4,3,3,128,256]{4,3,2,1,0:T(8,128)(2,1)S(1)} %copy-done.1), custom_call_target="tpu_custom_call" | custom-call | tf_op jit(solution)/shard_map/encode/pallas_call | solution.py:137
  42.6 1.6 %collective-permute-start.5 = (bf16[6,10,128]{2,0,1:T(8,128)(2,1)S(1)}, bf16[6,10,128]{2,0,1:T(8,128)(2,1)S(1)}, u32[]{:S(2)}, u32[]{:S(2)}) collective-permute-start(bf16[6,10,128]{2,0,1:T(8,128)(2,1)S(1)} %bitcast.37), channel_id=1, source_target_pairs={{0,1},{1,0},{2,3},{3,2},{4,5},{5,4},{6,7},{7,6},{8,9},{9,8},{10,11... | collective-permute-start | bytes 46088 | tf_op jit(solution)/shard_map/ppermute | solution.py:367
  44.3 2.2 %collective-permute-done.5 = bf16[6,10,128]{2,0,1:T(8,128)(2,1)S(1)} collective-permute-done((bf16[6,10,128]{2,0,1:T(8,128)(2,1)S(1)}, bf16[6,10,128]{2,0,1:T(8,128)(2,1)S(1)}, u32[]{:S(2)}, u32[]{:S(2)}) %collective-permute-start.5) | collective-permute-done | bytes 15392 | tf_op jit(solution)/shard_map/ppermute | solution.py:367
  46.7 1.2 half.1
  48.6 1.6 %reshape.27 = bf16[2,2,4,2,4,2,256]{6,5,4,3,2,1,0:T(2,128)(2,1)} reshape(bf16[4,8,8,256]{3,2,1,0:T(8,128)(2,1)} %copy-done.4) | data formatting | bytes 262144 | tf_op jit(solution)/shard_map/reshape | solution.py:11
  50.2 1.7 %reduce_max.9 = bf16[2,4,4,256]{3,2,1,0:T(4,128)(2,1)} reduce(bf16[2,2,4,2,4,2,256]{6,5,4,3,2,1,0:T(2,128)(2,1)} %reshape.27, bf16[]{:T(256)} %constant.52.clone.1), dimensions={1,3,5}, to_apply=%region_0.1 | reduce | flops 57344 | bytes 147458 | tf_op jit(solution)/shard_map/reduce_max | solution.py:12
  51.8 0.7 broadcast_select_fusion.20
  53.2 3.7 %collective-permute-done.6 = bf16[2,4,1,256]{3,1,2,0:T(4,128)(2,1)S(1)} collective-permute-done((bf16[2,4,1,256]{3,1,2,0:T(4,128)(2,1)S(1)}, bf16[2,4,1,256]{3,1,2,0:T(4,128)(2,1)S(1)}, u32[]{:S(2)}, u32[]{:S(2)}) %collective-permute-start.6) | collective-permute-done | bytes 4128 | tf_op jit(solution)/shard_map/ppermute | solution.py:30
  56.9 0.7 pad_maximum_fusion.8
  57.6 0.9 broadcast_in_dim.32
  58.5 5.4 %all-to-all-start = ((bf16[16,2,4,8,256]{4,3,2,1,0:T(8,128)(2,1)}), bf16[16,2,4,8,256]{4,3,2,1,0:T(8,128)(2,1)}, u32[]{:S(2)}, u32[]{:S(2)}) async-start(bf16[16,2,4,8,256]{4,3,2,1,0:T(8,128)(2,1)} %broadcast_in_dim.32), calls=%async_computation | async-start | bytes 1048576 | tf_op jit(solution)/shard_map/all_to_all | solution.py:389
  63.9 0.9 copy.79
  66.1 5.5 %collective-permute-start.10 = (bf16[1,8,8,256]{3,1,0,2:T(8,128)(2,1)}, bf16[1,8,8,256]{3,1,0,2:T(8,128)(2,1)}, u32[]{:S(2)}, u32[]{:S(2)}) collective-permute-start(bf16[1,8,8,256]{3,1,0,2:T(8,128)(2,1)} %get-tuple-element.30), channel_id=1, source_target_pairs={{0,112},{16,32},{32,16},{48,64},{64,48},{80,96},{96,80},{112,0},{1... | collective-permute-start | bytes 98312 | tf_op jit(solution)/shard_map/ppermute | solution.py:30
  71.6 2.8 %all-to-all-done.field_ref = bf16[16,2,4,8,256]{4,3,2,1,0:T(8,128)(2,1)} async-done(((bf16[16,2,4,8,256]{4,3,2,1,0:T(8,128)(2,1)}), bf16[16,2,4,8,256]{4,3,2,1,0:T(8,128)(2,1)}, u32[]{:S(2)}, u32[]{:S(2)}) %all-to-all-start) | async-done | bytes 524320 | tf_op jit(solution)/shard_map/all_to_all | solution.py:389
  74.5 2.4 %bottom_in.1 = bf16[8,8,6,4,128]{4,3,2,1,0:T(4,128)(2,1)S(1)} custom-call(s32[5]{0:T(128)S(1)} %pad_add_fusion.place_ref, bf16[16,2,4,8,256]{4,3,2,1,0:T(8,128)(2,1)} %all-to-all-done.field_ref, bf16[9,256,256]{2,1,0:T(8,128)(2,1)S(1)} %pad.36.weights_ref), custom_call_target="tpu_custom_call" | custom-call | tf_op jit(solution)/shard_map/bottom_in/pallas_call | solution.py:207
  76.9 0.7 copy-done.3
  77.6 3.6 %all-to-all-start.1 = ((bf16[8,8,6,4,128]{4,3,2,1,0:T(4,128)(2,1)}), bf16[8,8,6,4,128]{4,3,2,1,0:T(4,128)(2,1)S(1)}, u32[]{:S(2)}, u32[]{:S(2)}) async-start(bf16[8,8,6,4,128]{4,3,2,1,0:T(4,128)(2,1)} %copy-done.3), calls=%async_computation.1 | async-start | bytes 786432 | tf_op jit(solution)/shard_map/all_to_all | solution.py:391
  81.2 0.8 select_select_fusion.5
  82.0 1.1 broadcast_select_fusion.14
  83.5 1.2 collective-permute-start.13
  84.7 5.9 %all-to-all-done.1 = bf16[8,8,6,4,128]{4,3,2,1,0:T(4,128)(2,1)S(1)} async-done(((bf16[8,8,6,4,128]{4,3,2,1,0:T(4,128)(2,1)}), bf16[8,8,6,4,128]{4,3,2,1,0:T(4,128)(2,1)S(1)}, u32[]{:S(2)}, u32[]{:S(2)}) %all-to-all-start.1) | async-done | bytes 393248 | tf_op jit(solution)/shard_map/all_to_all | solution.py:391
  91.2 1.4 %collective-permute-start.9 = (bf16[8,8,6,2,128]{4,3,2,1,0:T(2,128)(2,1)S(1)}, bf16[8,8,6,2,128]{4,3,2,1,0:T(2,128)(2,1)S(1)}, u32[]{:S(2)}, u32[]{:S(2)}) collective-permute-start(bf16[8,8,6,2,128]{4,3,2,1,0:T(2,128)(2,1)S(1)} %get-tuple-element.27), channel_id=1, source_target_pairs={{0,2},{2,0},{4,6},{6,4},{8,10},{10,8},{12,14},{14,12},{1,3},{3,1},... | collective-permute-start | bytes 589832 | tf_op jit(solution)/shard_map/ppermute | solution.py:29
  92.9 4.6 %collective-permute-done.8 = bf16[8,8,6,2,128]{4,3,2,1,0:T(2,128)(2,1)S(1)} collective-permute-done((bf16[8,8,6,2,128]{4,3,2,1,0:T(2,128)(2,1)S(1)}, bf16[8,8,6,2,128]{4,3,2,1,0:T(2,128)(2,1)S(1)}, u32[]{:S(2)}, u32[]{:S(2)}) %collective-permute-start.8) | collective-permute-done | bytes 196640 | tf_op jit(solution)/shard_map/ppermute | solution.py:30
  98.6 3.4 %bottom_out.1 = bf16[8,2,6,8,128]{4,3,2,1,0:T(8,128)(2,1)} custom-call(s32[5]{0:T(128)S(1)} %pad_add_fusion.place_ref, bf16[8,8,6,8,128]{4,3,2,1,0:T(8,128)(2,1)S(1)} %pad_maximum_fusion.1.field_ref, bf16[9,512,256]{2,1,0:T(8,128)(2,1)S(1)} %pad.37.weights_ref), custom_call_target="tpu_custom_call" | custom-call | tf_op jit(solution)/shard_map/bottom_out/pallas_call | solution.py:250
  102.0 3.4 %all-to-all-start.2 = ((bf16[8,2,6,8,128]{4,3,2,1,0:T(8,128)(2,1)}), bf16[8,2,6,8,128]{4,3,2,1,0:T(8,128)(2,1)S(1)}, u32[]{:S(2)}, u32[]{:S(2)}) async-start(bf16[8,2,6,8,128]{4,3,2,1,0:T(8,128)(2,1)} %bottom_out.1), calls=%async_computation.2 | async-start | bytes 393216 | tf_op jit(solution)/shard_map/all_to_all | solution.py:394
  105.4 0.8 collective-permute-start.14
  106.3 3.3 %collective-permute-done.14 = bf16[6,10,256]{2,1,0:T(8,128)(2,1)S(1)} collective-permute-done((bf16[6,10,256]{2,1,0:T(8,128)(2,1)S(1)}, bf16[6,10,256]{2,1,0:T(8,128)(2,1)S(1)}, u32[]{:S(2)}, u32[]{:S(2)}) %collective-permute-start.14) | collective-permute-done | bytes 30752 | tf_op jit(solution)/shard_map/ppermute | solution.py:367
  109.6 4.2 %all-to-all-done.2.bottom_ref = bf16[8,2,6,8,128]{4,3,2,1,0:T(8,128)(2,1)S(1)} async-done(((bf16[8,2,6,8,128]{4,3,2,1,0:T(8,128)(2,1)}), bf16[8,2,6,8,128]{4,3,2,1,0:T(8,128)(2,1)S(1)}, u32[]{:S(2)}, u32[]{:S(2)}) %all-to-all-start.2) | async-done | bytes 196640 | tf_op jit(solution)/shard_map/all_to_all | solution.py:394
  113.8 4.0 %copy-done = bf16[3,3,3,768,256]{4,3,2,1,0:T(8,128)(2,1)S(1)} copy-done((bf16[3,3,3,768,256]{4,3,2,1,0:T(8,128)(2,1)S(1)}, bf16[3,3,3,768,256]{4,3,2,1,0:T(8,128)(2,1)}, u32[]{:S(2)}) %copy-start) | copy-done | bytes 10616856
  117.8 8.7 %decode.1 = bf16[4,8,8,256]{3,2,1,0:T(8,128)(2,1)} custom-call(s32[5]{0:T(128)S(1)} %pad_add_fusion.place_ref, bf16[8,2,6,8,128]{4,3,2,1,0:T(8,128)(2,1)S(1)} %all-to-all-done.2.bottom_ref, bf16[6,10,8,256]{3,2,1,0:T(8,128)(2,1)S(1)} %copy.82.skip_ref, bf16[6,16,256]{2,1,0:T(8,128)(2,1)S(1)} %pad.42.edge_ref, bf16[9,3,768,256]{3,2,1,0:T(8,128)(2,1)S(1)} %bitcast.31), custom_call_target="tpu_custom_call" | custom-call | tf_op jit(solution)/shard_map/decode/pallas_call | solution.py:333
  (72 shorter events, 7.3 us)
Async XLA Ops:
  0.0 9.2 %copy-start.11 = (bf16[3,3,3,256,64]{3,4,2,1,0:T(8,128)(2,1)S(1)}, bf16[3,3,3,256,64]{3,4,2,1,0:T(8,128)(2,1)}, u32[]{:S(2)}) copy-start(bf16[3,3,3,256,64]{3,4,2,1,0:T(8,128)(2,1)} %param.9) | copy-start | bytes 2654212
  1.3 9.5 %copy-start.8 = (bf16[3,3,3,512,64]{3,4,2,1,0:T(8,128)(2,1)S(1)}, bf16[3,3,3,512,64]{3,4,2,1,0:T(8,128)(2,1)}, u32[]{:S(2)}) copy-start(bf16[3,3,3,512,64]{3,4,2,1,0:T(8,128)(2,1)} %param.10) | copy-start | bytes 5308420
  2.1 16.3 %collective-permute-start.1 = (bf16[3,16,16,128]{3,1,0,2:T(8,128)(2,1)}, bf16[3,16,16,128]{3,1,0,2:T(8,128)(2,1)}, u32[]{:S(2)}, u32[]{:S(2)}) collective-permute-start(bf16[3,16,16,128]{3,1,0,2:T(8,128)(2,1)} %get-tuple-element.20), channel_id=1, source_target_pairs={{0,16},{16,0},{32,48},{48,32},{64,80},{80,64},{96,112},{112,96},{1... | collective-permute-start | bytes 589832 | tf_op jit(solution)/shard_map/ppermute | solution.py:29
  5.2 13.2 %collective-permute-start = (bf16[3,16,16,128]{3,1,0,2:T(8,128)(2,1)}, bf16[3,16,16,128]{3,1,0,2:T(8,128)(2,1)}, u32[]{:S(2)}, u32[]{:S(2)}) collective-permute-start(bf16[3,16,16,128]{3,1,0,2:T(8,128)(2,1)} %get-tuple-element.21), channel_id=1, source_target_pairs={{0,112},{16,32},{32,16},{48,64},{64,48},{80,96},{96,80},{112,0},{1... | collective-permute-start | bytes 589832 | tf_op jit(solution)/shard_map/ppermute | solution.py:30
  13.4 2.0 %copy-start.5 = (bf16[9,512,192]{2,1,0:T(8,128)(2,1)S(1)}, bf16[9,512,192]{2,1,0:T(8,128)(2,1)}, u32[]{:S(2)}) copy-start(bf16[9,512,192]{2,1,0:T(8,128)(2,1)} %copy.72) | copy-start | bytes 5308420
  15.4 1.2 copy-start.12
  16.6 2.9 %copy-start.7 = (bf16[8,16,16,128]{3,2,1,0:T(8,128)(2,1)S(1)}, bf16[8,16,16,128]{3,2,1,0:T(8,128)(2,1)}, u32[]{:S(2)}) copy-start(bf16[8,16,16,128]{3,2,1,0:T(8,128)(2,1)} %param.6) | copy-start | bytes 1572868
  19.6 0.9 copy-start.6
  21.6 7.0 %collective-permute-start.2 = (bf16[14,3,16,128]{3,1,0,2:T(4,128)(2,1)}, bf16[14,3,16,128]{3,1,0,2:T(4,128)(2,1)}, u32[]{:S(2)}, u32[]{:S(2)}) collective-permute-start(bf16[14,3,16,128]{3,1,0,2:T(4,128)(2,1)} %get-tuple-element.18), channel_id=1, source_target_pairs={{0,14},{2,4},{4,2},{6,8},{8,6},{10,12},{12,10},{14,0},{1,15},{3,5}... | collective-permute-start | bytes 516104 | tf_op jit(solution)/shard_map/ppermute | solution.py:30
  23.5 5.1 %collective-permute-start.3 = (bf16[14,3,16,128]{3,1,0,2:T(4,128)(2,1)}, bf16[14,3,16,128]{3,1,0,2:T(4,128)(2,1)}, u32[]{:S(2)}, u32[]{:S(2)}) collective-permute-start(bf16[14,3,16,128]{3,1,0,2:T(4,128)(2,1)} %get-tuple-element.19), channel_id=1, source_target_pairs={{0,2},{2,0},{4,6},{6,4},{8,10},{10,8},{12,14},{14,12},{1,3},{3,1},... | collective-permute-start | bytes 516104 | tf_op jit(solution)/shard_map/ppermute | solution.py:29
  31.8 4.8 %copy-start.1 = (bf16[4,3,3,128,256]{4,3,2,1,0:T(8,128)(2,1)S(1)}, bf16[4,3,3,128,256]{4,3,2,1,0:T(8,128)(2,1)}, u32[]{:S(2)}) copy-start(bf16[4,3,3,128,256]{4,3,2,1,0:T(8,128)(2,1)} %fusion.2.weights_ref) | copy-start | bytes 7077892
  31.9 4.6 %collective-permute-start.4 = (bf16[14,22,128]{2,1,0:T(8,128)(2,1)S(1)}, bf16[14,22,128]{2,1,0:T(8,128)(2,1)S(1)}, u32[]{:S(2)}, u32[]{:S(2)}) collective-permute-start(bf16[14,22,128]{2,1,0:T(8,128)(2,1)S(1)} %fusion.3), channel_id=1, source_target_pairs={{0,1},{1,0},{2,3},{3,2},{4,5},{5,4},{6,7},{7,6},{8,9},{9,8},{10,11... | collective-permute-start | bytes 236552 | tf_op jit(solution)/shard_map/ppermute | solution.py:367
  36.6 10.1 %copy-start.2 = (bf16[3,3,3,128,256]{4,3,2,1,0:T(8,128)(2,1)S(1)}, bf16[3,3,3,128,256]{4,3,2,1,0:T(8,128)(2,1)}, u32[]{:S(2)}) copy-start(bf16[3,3,3,128,256]{4,3,2,1,0:T(8,128)(2,1)} %param.8) | copy-start | bytes 5308420
  42.6 3.9 %collective-permute-start.5 = (bf16[6,10,128]{2,0,1:T(8,128)(2,1)S(1)}, bf16[6,10,128]{2,0,1:T(8,128)(2,1)S(1)}, u32[]{:S(2)}, u32[]{:S(2)}) collective-permute-start(bf16[6,10,128]{2,0,1:T(8,128)(2,1)S(1)} %bitcast.37), channel_id=1, source_target_pairs={{0,1},{1,0},{2,3},{3,2},{4,5},{5,4},{6,7},{7,6},{8,9},{9,8},{10,11... | collective-permute-start | bytes 46088 | tf_op jit(solution)/shard_map/ppermute | solution.py:367
  47.9 0.7 copy-start.4
  52.5 4.3 %collective-permute-start.6 = (bf16[2,4,1,256]{3,1,2,0:T(4,128)(2,1)S(1)}, bf16[2,4,1,256]{3,1,2,0:T(4,128)(2,1)S(1)}, u32[]{:S(2)}, u32[]{:S(2)}) collective-permute-start(bf16[2,4,1,256]{3,1,2,0:T(4,128)(2,1)S(1)} %get-tuple-element.41), channel_id=1, source_target_pairs={{0,14},{2,4},{4,2},{6,8},{8,6},{10,12},{12,10},{14,0},{1,15},{3,5}... | collective-permute-start | bytes 12296 | tf_op jit(solution)/shard_map/ppermute | solution.py:30
  53.0 3.8 %collective-permute-start.7 = (bf16[2,4,1,256]{3,1,2,0:T(4,128)(2,1)S(1)}, bf16[2,4,1,256]{3,1,2,0:T(4,128)(2,1)S(1)}, u32[]{:S(2)}, u32[]{:S(2)}) collective-permute-start(bf16[2,4,1,256]{3,1,2,0:T(4,128)(2,1)S(1)} %get-tuple-element.42), channel_id=1, source_target_pairs={{0,2},{2,0},{4,6},{6,4},{8,10},{10,8},{12,14},{14,12},{1,3},{3,1},... | collective-permute-start | bytes 12296 | tf_op jit(solution)/shard_map/ppermute | solution.py:29
  58.5 15.9 %all-to-all-start = ((bf16[16,2,4,8,256]{4,3,2,1,0:T(8,128)(2,1)}), bf16[16,2,4,8,256]{4,3,2,1,0:T(8,128)(2,1)}, u32[]{:S(2)}, u32[]{:S(2)}) async-start(bf16[16,2,4,8,256]{4,3,2,1,0:T(8,128)(2,1)} %broadcast_in_dim.32), calls=%async_computation | async-start | bytes 1048576 | tf_op jit(solution)/shard_map/all_to_all | solution.py:389
  64.8 0.7 copy-start.9
  66.1 15.1 %collective-permute-start.10 = (bf16[1,8,8,256]{3,1,0,2:T(8,128)(2,1)}, bf16[1,8,8,256]{3,1,0,2:T(8,128)(2,1)}, u32[]{:S(2)}, u32[]{:S(2)}) collective-permute-start(bf16[1,8,8,256]{3,1,0,2:T(8,128)(2,1)} %get-tuple-element.30), channel_id=1, source_target_pairs={{0,112},{16,32},{32,16},{48,64},{64,48},{80,96},{96,80},{112,0},{1... | collective-permute-start | bytes 98312 | tf_op jit(solution)/shard_map/ppermute | solution.py:30
  71.6 9.6 %collective-permute-start.11 = (bf16[1,8,8,256]{3,1,0,2:T(8,128)(2,1)}, bf16[1,8,8,256]{3,1,0,2:T(8,128)(2,1)}, u32[]{:S(2)}, u32[]{:S(2)}) collective-permute-start(bf16[1,8,8,256]{3,1,0,2:T(8,128)(2,1)} %get-tuple-element.31), channel_id=1, source_target_pairs={{0,16},{16,0},{32,48},{48,32},{64,80},{80,64},{96,112},{112,96},{1... | collective-permute-start | bytes 98312 | tf_op jit(solution)/shard_map/ppermute | solution.py:29
  76.9 0.8 copy-start.3
  77.6 15.1 %copy-start.10 = (bf16[4,8,8,256]{3,1,0,2:T(8,128)(2,1)S(1)}, bf16[4,8,8,256]{3,1,0,2:T(8,128)(2,1)}, u32[]{:S(2)}) copy-start(bf16[4,8,8,256]{3,1,0,2:T(8,128)(2,1)} %copy-done.9) | copy-start | bytes 393220
  77.6 13.0 %all-to-all-start.1 = ((bf16[8,8,6,4,128]{4,3,2,1,0:T(4,128)(2,1)}), bf16[8,8,6,4,128]{4,3,2,1,0:T(4,128)(2,1)S(1)}, u32[]{:S(2)}, u32[]{:S(2)}) async-start(bf16[8,8,6,4,128]{4,3,2,1,0:T(4,128)(2,1)} %copy-done.3), calls=%async_computation.1 | async-start | bytes 786432 | tf_op jit(solution)/shard_map/all_to_all | solution.py:391
  83.1 9.4 %collective-permute-start.12 = (bf16[6,1,8,256]{3,1,0,2:T(2,128)(2,1)S(1)}, bf16[6,1,8,256]{3,1,0,2:T(2,128)(2,1)S(1)}, u32[]{:S(2)}, u32[]{:S(2)}) collective-permute-start(bf16[6,1,8,256]{3,1,0,2:T(2,128)(2,1)S(1)} %get-tuple-element.15), channel_id=1, source_target_pairs={{0,14},{2,4},{4,2},{6,8},{8,6},{10,12},{12,10},{14,0},{1,15},{3,5}... | collective-permute-start | bytes 73736 | tf_op jit(solution)/shard_map/ppermute | solution.py:30
  83.5 9.1 %collective-permute-start.13 = (bf16[6,1,8,256]{3,1,0,2:T(2,128)(2,1)S(1)}, bf16[6,1,8,256]{3,1,0,2:T(2,128)(2,1)S(1)}, u32[]{:S(2)}, u32[]{:S(2)}) collective-permute-start(bf16[6,1,8,256]{3,1,0,2:T(2,128)(2,1)S(1)} %broadcast_select_fusion.13), channel_id=1, source_target_pairs={{0,2},{2,0},{4,6},{6,4},{8,10},{10,8},{12,14},{14,12},{1,3},{3,1},... | collective-permute-start | bytes 73736 | tf_op jit(solution)/shard_map/ppermute | solution.py:29
  91.1 6.4 %collective-permute-start.8 = (bf16[8,8,6,2,128]{4,3,2,1,0:T(2,128)(2,1)S(1)}, bf16[8,8,6,2,128]{4,3,2,1,0:T(2,128)(2,1)S(1)}, u32[]{:S(2)}, u32[]{:S(2)}) collective-permute-start(bf16[8,8,6,2,128]{4,3,2,1,0:T(2,128)(2,1)S(1)} %get-tuple-element.26), channel_id=1, source_target_pairs={{0,14},{2,4},{4,2},{6,8},{8,6},{10,12},{12,10},{14,0},{1,15},{3,5}... | collective-permute-start | bytes 589832 | tf_op jit(solution)/shard_map/ppermute | solution.py:30
  91.2 6.3 %collective-permute-start.9 = (bf16[8,8,6,2,128]{4,3,2,1,0:T(2,128)(2,1)S(1)}, bf16[8,8,6,2,128]{4,3,2,1,0:T(2,128)(2,1)S(1)}, u32[]{:S(2)}, u32[]{:S(2)}) collective-permute-start(bf16[8,8,6,2,128]{4,3,2,1,0:T(2,128)(2,1)S(1)} %get-tuple-element.27), channel_id=1, source_target_pairs={{0,2},{2,0},{4,6},{6,4},{8,10},{10,8},{12,14},{14,12},{1,3},{3,1},... | collective-permute-start | bytes 589832 | tf_op jit(solution)/shard_map/ppermute | solution.py:29
  102.0 11.8 %all-to-all-start.2 = ((bf16[8,2,6,8,128]{4,3,2,1,0:T(8,128)(2,1)}), bf16[8,2,6,8,128]{4,3,2,1,0:T(8,128)(2,1)S(1)}, u32[]{:S(2)}, u32[]{:S(2)}) async-start(bf16[8,2,6,8,128]{4,3,2,1,0:T(8,128)(2,1)} %bottom_out.1), calls=%async_computation.2 | async-start | bytes 393216 | tf_op jit(solution)/shard_map/all_to_all | solution.py:394
  105.4 4.2 %collective-permute-start.14 = (bf16[6,10,256]{2,1,0:T(8,128)(2,1)S(1)}, bf16[6,10,256]{2,1,0:T(8,128)(2,1)S(1)}, u32[]{:S(2)}, u32[]{:S(2)}) collective-permute-start(bf16[6,10,256]{2,1,0:T(8,128)(2,1)S(1)} %fusion.4), channel_id=1, source_target_pairs={{0,1},{1,0},{2,3},{3,2},{4,5},{5,4},{6,7},{7,6},{8,9},{9,8},{10,11... | collective-permute-start | bytes 92168 | tf_op jit(solution)/shard_map/ppermute | solution.py:367
  113.8 4.0 %copy-start = (bf16[3,3,3,768,256]{4,3,2,1,0:T(8,128)(2,1)S(1)}, bf16[3,3,3,768,256]{4,3,2,1,0:T(8,128)(2,1)}, u32[]{:S(2)}) copy-start(bf16[3,3,3,768,256]{4,3,2,1,0:T(8,128)(2,1)} %param.11) | copy-start | bytes 31850500

commit v3 on v2

--- a/solution.py
+++ b/solution.py
@@ -6,10 +6,18 @@
 from jax.sharding import PartitionSpec as P
 
 
-def shrink(field):
-    size_x, size_y, size_z, channels = field.shape
-    blocks = field.reshape(size_x // 2, 2, size_y // 2, 2, size_z // 2, 2, channels)
-    return jnp.max(blocks, axis=(1, 3, 5))
+def swaps(low, high, axis, count):
+    even = lax.axis_index(axis) % 2 == 0
+    inner = [(i, i ^ 1) for i in range(count)]
+    outer = [(i, (((i + 1) ^ 1) - 1) % count) for i in range(count)]
+    got_in = lax.ppermute(jnp.where(even, high, low), axis, inner)
+    got_out = lax.ppermute(jnp.where(even, low, high), axis, outer)
+    return got_in, got_out
+
+
+def ordered(got_in, got_out, axis):
+    even = lax.axis_index(axis) % 2 == 0
+    return jnp.where(even, got_out, got_in), jnp.where(even, got_in, got_out)
 
 
 def halo(field, axis, count, dim, width):
@@ -17,20 +25,9 @@
     size = field.shape[dim]
     low = lax.slice_in_dim(field, 0, width, axis=dim)
     high = lax.slice_in_dim(field, size - width, size, axis=dim)
+    below, above = ordered(*swaps(low, high, axis, count), axis)
     zero = jnp.zeros_like(low)
-    if count == 2:
-        got = lax.ppermute(jnp.where(place == 0, high, low), axis, [(0, 1), (1, 0)])
-        below = jnp.where(place == 1, got, zero)
-        above = jnp.where(place == 0, got, zero)
-        return below, above
-    even = place % 2 == 0
-    inner = [(i, i ^ 1) for i in range(count)]
-    outer = [(i, (((i + 1) ^ 1) - 1) % count) for i in range(count)]
-    got_in = lax.ppermute(jnp.where(even, high, low), axis, inner)
-    got_out = lax.ppermute(jnp.where(even, low, high), axis, outer)
-    below = jnp.where(place > 0, jnp.where(even, got_out, got_in), zero)
-    above = jnp.where(place < count - 1, jnp.where(even, got_in, got_out), zero)
-    return below, above
+    return jnp.where(place > 0, below, zero), jnp.where(place < count - 1, above, zero)
 
 
 def extend(field, axis, count, dim, width):
@@ -38,89 +35,122 @@
     return jnp.concatenate([below, field, above], axis=dim)
 
 
-def roll_rows(block, shift):
-    return pltpu.roll(block, shift % block.shape[1], 1)
-
-
-def tile_conv(field, weights, name):
-    size_a, size_b, size_s, channels = field.shape
-    size_a, size_b = size_a - 2, size_b - 2
-    steps, taps, _, width = weights.shape
-    filters = width if taps == 3 else 64
-    wide = width if taps == 3 else 128
-    part = max(1, 256 // (size_b * size_s))
-
-    def body(field_ref, weights_ref, out_ref):
-        for first in range(0, size_a, part):
-            rows = part * size_b * size_s
-            groups = part * size_b
-            blocks = []
-            for step in range(steps):
-                da, db = step // 3, step % 3
-                block = field_ref[first + da : first + da + part, db : db + size_b]
-                if size_s % 16:
-                    block = block.astype(jnp.float32)
-                blocks.append(block.reshape(rows, channels).astype(jnp.bfloat16))
-            block = jnp.concatenate(blocks, axis=1)
-            sums = []
-            for tap in range(taps):
-                kernel = weights_ref[:, tap].reshape(steps * channels, width)
-                sums.append(jnp.dot(block, kernel, preferred_element_type=jnp.float32))
-            if taps == 3:
-                low, mid, high = [total.reshape(groups, size_s, width) for total in sums]
-            else:
-                low = sums[0][:, :128].reshape(groups, size_s, 128)
-                mid = pltpu.roll(sums[0][:, :128], 64, 1).reshape(groups, size_s, 128)
-                high = sums[0][:, 128:].reshape(groups, size_s, 128)
-            if size_s == 8:
-                total = roll_rows(low, 1) + mid + roll_rows(high, -1)
-            else:
-                index = lax.broadcasted_iota(jnp.int32, (groups, 8, wide), 1)
-                down = jnp.where(index == 0, roll_rows(low[:, 8:], 1), roll_rows(low[:, :8], 1))
-                up = jnp.where(index == 7, roll_rows(high[:, 8:], -1), roll_rows(high[:, :8], -1))
-                total = down + mid[:, :8] + up
-            total = jnp.maximum(total, 0.0).reshape(part, size_b, 8, wide)
-            out_ref[first : first + part] = total[..., :filters].astype(out_ref.dtype)
+def half_level(place, field, edge, weights):
+    full_x, full_y, size_z, channels = field.shape
+    size_x, size_y = full_x - 2, full_y - 2
+    filters = weights.shape[-1]
+    rows, extra = size_x * size_y * size_z, size_x * size_y
+
+    def body(place_ref, field_ref, edge_ref, weights_ref, out_ref, coarse_ref, rows_ref):
+        first = place_ref[2] == 0
+        edge_plane = edge_ref[...].astype(jnp.float32)
+        blocks = []
+        for dx in range(3):
+            for dy in range(3):
+                main = field_ref[dx : dx + size_x, dy : dy + size_y].astype(jnp.float32).reshape(rows, channels)
+                side = edge_plane[dx : dx + size_x, dy : dy + size_y].reshape(extra, channels)
+                blocks.append(jnp.concatenate([main, side], axis=0).astype(jnp.bfloat16))
+        block = jnp.concatenate(blocks, axis=1)
+        sums = []
+        for tap in range(3):
+            kernel = weights_ref[:, tap].reshape(9 * channels, filters)
+            sums.append(jnp.dot(block, kernel, preferred_element_type=jnp.float32))
+        total = jnp.maximum(join_taps(first, sums, extra, size_z), 0.0)
+        out_ref[...] = total.reshape(size_x, size_y, size_z, filters).astype(out_ref.dtype)
+        total = jnp.max(total.reshape(size_x // 2, 2, size_y // 2, 2, size_z, filters), axis=(1, 3))
+        count = size_y // 2
+        for part in range(filters // 128):
+            rows_ref[...] = total[..., 128 * part : 128 * part + 128].reshape(rows // 4, 128)
+            for x in range(size_x // 2):
+                for z in range(size_z // 2):
+                    start = x * count * size_z + 2 * z
+                    pooled = jnp.maximum(
+                        rows_ref[pl.ds(start, count, stride=size_z), :], rows_ref[pl.ds(start + 1, count, stride=size_z), :]
+                    )
+                    coarse_ref[x, z, :, 128 * part : 128 * part + 128] = pooled.astype(coarse_ref.dtype)
 
     return pl.pallas_call(
         body,
-        in_specs=[pl.BlockSpec(memory_space=pltpu.VMEM)] * 2,
-        out_specs=pl.BlockSpec(memory_space=pltpu.VMEM),
-        out_shape=jax.ShapeDtypeStruct((size_a, size_b, 8, filters), jnp.bfloat16),
-        compiler_params=pltpu.CompilerParams(vmem_limit_bytes=40 << 20),
-        name=name,
-    )(field, weights)
-
-
-def encode(place, field, edge, weights):
-    size_x, size_y, size_z, channels = field.shape
-    size_x, size_y = size_x - 2, size_y - 2
+        in_specs=[pl.BlockSpec(memory_space=pltpu.SMEM)] + [pl.BlockSpec(memory_space=pltpu.VMEM)] * 3,
+        out_specs=[pl.BlockSpec(memory_space=pltpu.VMEM)] * 2,
+        out_shape=[
+            jax.ShapeDtypeStruct((size_x, size_y, size_z, filters), jnp.bfloat16),
+            jax.ShapeDtypeStruct((size_x // 2, size_z // 2, size_y // 2, filters), jnp.bfloat16),
+        ],
+        scratch_shapes=[pltpu.VMEM((rows // 4, 128), jnp.float32)],
+        compiler_params=pltpu.CompilerParams(vmem_limit_bytes=12 << 20),
+        name="half_level",
+    )(place, field, edge, weights)
+
+
+def join_taps(first, sums, groups, size_z):
+    rows, filters = groups * size_z, sums[0].shape[-1]
+    low, mid, high = [total[:rows].reshape(groups, size_z, filters) for total in sums]
+    below = jnp.where(first, 0.0, sums[0][rows : rows + groups])
+    above = jnp.where(first, sums[2][rows : rows + groups], 0.0)
+    index = lax.broadcasted_iota(jnp.int32, (groups, size_z, filters), 1)
+    down = jnp.where(index == 0, below[:, None, :], pltpu.roll(low, 1, 1))
+    up = jnp.where(index == size_z - 1, above[:, None, :], pltpu.roll(high, size_z - 1, 1))
+    return down + mid + up
+
+
+def encode(place, own, x_in, x_out, y_in, y_out, edge, weights):
+    own_x, own_y, size_z, channels = own.shape
+    reach = x_in.shape[0]
+    full_x, full_y = own_x + 2 * reach, own_y + 2 * reach
+    size_x, size_y = full_x - 2, full_y - 2
     filters = weights.shape[-1] // 2
-    rows, extra = size_y * size_z, edge.shape[2]
+    rows, extra = size_y * size_z, size_y + (-size_y % 16)
     pool_y, pool_z = size_y // 2, size_z // 2
 
-    def body(place_ref, field_ref, edge_ref, weights_ref, out_ref, rows_ref):
-        index = lax.broadcasted_iota(jnp.int32, (size_y, size_z, 2 * filters), 1)
+    def body(
+        place_ref, own_ref, x_in_ref, x_out_ref, y_in_ref, y_out_ref, edge_ref, weights_ref, out_ref, field_ref, side_ref, rows_ref
+    ):
+        even_x, even_y = place_ref[0] % 2 == 0, place_ref[1] % 2 == 0
+        low_x, high_x = place_ref[0] > 0, place_ref[0] < place_ref[3]
+        low_y, high_y = place_ref[1] > 0, place_ref[1] < place_ref[4]
+        nil = jnp.bfloat16(0)
+        inner_y = slice(reach, reach + own_y)
+        below, above = jnp.where(even_x, x_out_ref[...], x_in_ref[...]), jnp.where(even_x, x_in_ref[...], x_out_ref[...])
+        field_ref[:reach, inner_y] = jnp.where(low_x, below, nil)
+        field_ref[reach + own_x :, inner_y] = jnp.where(high_x, above, nil)
+        field_ref[reach : reach + own_x, inner_y] = own_ref[...]
+        for x in range(full_x):
+            here_low, here_high = low_y, high_y
+            if x < reach:
+                here_low, here_high = low_y & low_x, high_y & low_x
+            if x >= reach + own_x:
+                here_low, here_high = low_y & high_x, high_y & high_x
+            below, above = jnp.where(even_y, y_out_ref[x], y_in_ref[x]), jnp.where(even_y, y_in_ref[x], y_out_ref[x])
+            field_ref[x, :reach] = jnp.where(here_low, below, nil)
+            field_ref[x, reach + own_y :] = jnp.where(here_high, above, nil)
+            line = lax.broadcasted_iota(jnp.int32, (full_y, channels), 0)
+            inside = ((line >= reach) | low_y) & ((line < reach + own_y) | high_y)
+            if x < reach:
+                inside = inside & low_x
+            if x >= reach + own_x:
+                inside = inside & high_x
+            plane = jnp.where(inside, edge_ref[x].astype(jnp.float32), 0.0)
+            for dy in range(3):
+                side_ref[dy, x, :size_y] = plane[dy : dy + size_y]
+                side_ref[dy, x, size_y:] = jnp.zeros((extra - size_y, channels), jnp.float32)
+
         first = place_ref[2] == 0
         line = lax.broadcasted_iota(jnp.int32, (pool_y, pool_z, filters), 0)
-        inside_y = ((line > 0) | (place_ref[1] > 0)) & ((line < pool_y - 1) | (place_ref[1] < place_ref[4]))
+        inside_y = ((line > 0) | low_y) & ((line < pool_y - 1) | high_y)
         for pair in range(size_x // 2):
             blocks = []
             for plane in range(4):
                 for dy in range(3):
                     main = field_ref[2 * pair + plane, dy : dy + size_y].reshape(rows, channels)
-                    blocks.append(jnp.concatenate([main, edge_ref[dy, 2 * pair + plane]], axis=0))
+                    side = side_ref[dy, 2 * pair + plane].astype(jnp.bfloat16)
+                    blocks.append(jnp.concatenate([main, side], axis=0))
             block = jnp.concatenate(blocks, axis=1)
             sums = []
             for tap in range(3):
                 kernel = weights_ref[:, :, tap].reshape(12 * channels, 2 * filters)
                 sums.append(jnp.dot(block, kernel, preferred_element_type=jnp.float32))
-            low, mid, high = [total[:rows].reshape(size_y, size_z, 2 * filters) for total in sums]
-            below = jnp.where(first, 0.0, sums[0][rows : rows + size_y])
-            above = jnp.where(first, sums[2][rows : rows + size_y], 0.0)
-            down = jnp.where(index == 0, below[:, None, :], pltpu.roll(low, 1, 1))
-            up = jnp.where(index == size_z - 1, above[:, None, :], pltpu.roll(high, size_z - 1, 1))
-            total = jnp.maximum(down + mid + up, 0.0)
+            total = jnp.maximum(join_taps(first, sums, size_y, size_z), 0.0)
             total = jnp.maximum(total[..., :filters], total[..., filters:])
             total = jnp.max(total.reshape(pool_y, 2, size_z, filters), axis=1)
             rows_ref[...] = total.reshape(pool_y * size_z, filters)
@@ -129,20 +159,24 @@
             ).reshape(pool_y, pool_z, filters)
             inside = inside_y
             if pair == 0:
-                inside = inside & (place_ref[0] > 0)
+                inside = inside & low_x
             if pair == size_x // 2 - 1:
-                inside = inside & (place_ref[0] < place_ref[3])
+                inside = inside & high_x
             out_ref[pair] = jnp.where(inside, total, 0.0).astype(out_ref.dtype)
 
     return pl.pallas_call(
         body,
-        in_specs=[pl.BlockSpec(memory_space=pltpu.SMEM)] + [pl.BlockSpec(memory_space=pltpu.VMEM)] * 3,
+        in_specs=[pl.BlockSpec(memory_space=pltpu.SMEM)] + [pl.BlockSpec(memory_space=pltpu.VMEM)] * 7,
         out_specs=pl.BlockSpec(memory_space=pltpu.VMEM),
         out_shape=jax.ShapeDtypeStruct((size_x // 2, pool_y, pool_z, filters), jnp.bfloat16),
-        scratch_shapes=[pltpu.VMEM((pool_y * size_z, filters), jnp.float32)],
-        compiler_params=pltpu.CompilerParams(vmem_limit_bytes=32 << 20),
+        scratch_shapes=[
+            pltpu.VMEM((full_x, full_y, size_z, channels), jnp.bfloat16),
+            pltpu.VMEM((3, full_x, extra, channels), jnp.float32),
+            pltpu.VMEM((pool_y * size_z, filters), jnp.float32),
+        ],
+        compiler_params=pltpu.CompilerParams(vmem_limit_bytes=16 << 20),
         name="encode",
-    )(place, field, edge, weights)
+    )(place, own, x_in, x_out, y_in, y_out, edge, weights)
 
 
 def paired(weights):
@@ -210,7 +244,7 @@
         out_specs=pl.BlockSpec(memory_space=pltpu.VMEM),
         out_shape=jax.ShapeDtypeStruct((devices, size_x // 2, size_z, size_y, 128), jnp.bfloat16),
         scratch_shapes=[pltpu.VMEM((size_x + 2, all_z + 2, 8, channels), jnp.float32)],
-        compiler_params=pltpu.CompilerParams(vmem_limit_bytes=16 << 20),
+        compiler_params=pltpu.CompilerParams(vmem_limit_bytes=12 << 20),
         name="bottom_in",
     )(place, field, weights)
 
@@ -256,7 +290,7 @@
             pltpu.VMEM((size_x + 2, size_z + 2, 8, channels), jnp.float32),
             pltpu.VMEM((size_x + 2, size_z + 2, 8, 128), jnp.float32),
         ],
-        compiler_params=pltpu.CompilerParams(vmem_limit_bytes=24 << 20),
+        compiler_params=pltpu.CompilerParams(vmem_limit_bytes=16 << 20),
         name="bottom_out",
     )(place, field, weights)
 
@@ -270,10 +304,7 @@
     rows, extra = size_x * size_y * size_z, size_x * size_y
     weights = weights.reshape(9, 3, channels, filters)
 
-    def body(place_ref, bottom_ref, skip_ref, edge_ref, weights_hbm, out_ref, weights_ref, main_ref, side_ref, sums_ref, sems):
-        copies = [pltpu.make_async_copy(weights_hbm.at[step], weights_ref.at[step], sems.at[step]) for step in range(9)]
-        for copy in copies:
-            copy.start()
+    def body(place_ref, bottom_ref, skip_ref, edge_ref, weights_ref, out_ref, main_ref, side_ref, sums_ref):
         first = place_ref[2] == 0
         planes = [[] for _ in range(2 * pairs)]
         for k in range(devices // 2):
@@ -313,7 +344,6 @@
                 main = main_ref[dy, dx : dx + size_x].reshape(rows, channels)
                 side = side_ref[dy, dx : dx + size_x].reshape(extra, channels).astype(jnp.bfloat16)
                 blocks.append(jnp.concatenate([main, side], axis=0))
-                copies[3 * dx + dy].wait()
             block = jnp.concatenate(blocks, axis=1)
             for tap in range(3):
                 kernel = weights_ref[3 * dx : 3 * dx + 3, tap].reshape(3 * channels, filters)
@@ -322,29 +352,21 @@
                     sums_ref[tap] = product
                 else:
                     sums_ref[tap] += product
-        low, mid, high = [sums_ref[tap, :rows].reshape(extra, size_z, filters) for tap in range(3)]
-        below = jnp.where(first, 0.0, sums_ref[0, rows:])
-        above = jnp.where(first, sums_ref[2, rows:], 0.0)
-        index = lax.broadcasted_iota(jnp.int32, (extra, size_z, filters), 1)
-        down = jnp.where(index == 0, below[:, None, :], roll_rows(low, 1))
-        up = jnp.where(index == size_z - 1, above[:, None, :], roll_rows(high, -1))
-        out_ref[...] = (down + mid + up).reshape(size_x, size_y, size_z, filters).astype(out_ref.dtype)
+        total = join_taps(first, [sums_ref[tap] for tap in range(3)], extra, size_z)
+        out_ref[...] = total.reshape(size_x, size_y, size_z, filters).astype(out_ref.dtype)
 
     return pl.pallas_call(
         body,
         in_specs=[pl.BlockSpec(memory_space=pltpu.SMEM)]
-        + [pl.BlockSpec(memory_space=pltpu.VMEM)] * 3
-        + [pl.BlockSpec(memory_space=pl.ANY)],
+        + [pl.BlockSpec(memory_space=pltpu.VMEM)] * 4,
         out_specs=pl.BlockSpec(memory_space=pltpu.VMEM),
         out_shape=jax.ShapeDtypeStruct((size_x, size_y, size_z, filters), jnp.bfloat16),
         scratch_shapes=[
-            pltpu.VMEM(weights.shape, weights.dtype),
             pltpu.VMEM((3, full_x, size_y * size_z, channels), jnp.bfloat16),
             pltpu.VMEM((3, full_x, size_y, channels), jnp.float32),
             pltpu.VMEM((3, rows + extra, filters), jnp.float32),
-            pltpu.SemaphoreType.DMA((9,)),
         ],
-        compiler_params=pltpu.CompilerParams(vmem_limit_bytes=32 << 20),
+        compiler_params=pltpu.CompilerParams(vmem_limit_bytes=16 << 20),
         name="decode",
     )(place, bottom, skip, edge, weights)
 
@@ -366,22 +388,25 @@
         def edge_of(plane_low, plane_high):
             return lax.ppermute(jnp.where(place_z == 0, plane_high, plane_low), "gz", swap)
 
-        below, above = halo(volume, "gx", gx, 0, 3)
-        w_pair, w_in, w_out = paired(w_full), beside(w_bottom_in), beside(w_bottom_out)
-        below, above, w_pair, w_in, w_out = lax.optimization_barrier((below, above, w_pair, w_in, w_out))
-        field = jnp.concatenate([below, volume, above], axis=0)
-        field = extend(field, "gy", gy, 1, 3)
-        edge = edge_of(field[:, :, 0], field[:, :, -1])
-        rows = field.shape[1] - 2
-        edge = jnp.stack([jnp.pad(edge[:, dy : dy + rows], ((0, 0), (0, -rows % 16), (0, 0))) for dy in range(3)])
-        pooled = encode(place, field, edge, w_pair)
-
-        got = edge_of(pooled[:, :, 0], pooled[:, :, -1])[:, :, None]
-        zero = jnp.zeros_like(got)
-        above, below = jnp.where(place_z == 0, got, zero), jnp.where(place_z == 0, zero, got)
-        pooled = jnp.concatenate([pooled, above, jnp.zeros_like(pooled)[:, :, :6], below], axis=2)
-        skip = tile_conv(pooled, w_half.reshape(9, 3, w_half.shape[3], w_half.shape[4]), "half")
-        coarse = shrink(skip).transpose(0, 2, 1, 3)
+        x_in, x_out = swaps(volume[:3], volume[-3:], "gx", gx)
+        w_pair, w_out = paired(w_full), beside(w_bottom_out)
+        x_in, x_out, w_pair, w_out = lax.optimization_barrier((x_in, x_out, w_pair, w_out))
+        below, above = ordered(x_in, x_out, "gx")
+        y_low = jnp.concatenate([below[:, :3], volume[:, :3], above[:, :3]], axis=0)
+        y_high = jnp.concatenate([below[:, -3:], volume[:, -3:], above[:, -3:]], axis=0)
+        y_in, y_out = swaps(y_low, y_high, "gy", gy)
+        low, high = ordered(y_in, y_out, "gy")
+
+        def plane(z):
+            middle = jnp.concatenate([below[:, :, z], volume[:, :, z], above[:, :, z]], axis=0)
+            return jnp.concatenate([low[:, :, z], middle, high[:, :, z]], axis=1)
+
+        edge = edge_of(plane(0), plane(-1))
+        edge, w_in = lax.optimization_barrier((edge, beside(w_bottom_in)))
+        pooled = encode(place, volume, x_in, x_out, y_in, y_out, edge, w_pair)
+
+        edge = edge_of(pooled[:, :, 0], pooled[:, :, -1])
+        skip, coarse = half_level(place, pooled, edge, w_half.reshape(9, 3, w_half.shape[3], w_half.shape[4]))
         own_y = coarse.shape[2]
 
         column = jnp.pad(extend(coarse, "gy", gy, 2, 1), ((0, 0), (0, 0), (0, 6 - own_y), (0, 0)))

time: 128 us -> 118 us (0.922)
  other arithmetic: 15.8 us -> 8.83 us
  local copies, waits for them, and re-layouts: 20 us -> 24.2 us
  Pallas kernels: 21.7 us -> 17.9 us
  waiting for transfers between devices: 34.3 us -> 32.6 us
    slice x2 -> x5, local copies, waits for them, and re-layouts: 0.05 us -> 4.11 us  [the longest x1 1.78 us: plane(): volume[:, :, z]]
    pallas_call x1, Pallas kernels: 8.74 us -> 4.72 us  [decode(): pl.pallas_call(body, in_specs=[pl.BlockSpec(memory_space=pltpu.SMEM)] + [...]
    concatenate x4 -> x3, other arithmetic: 3.64 us -> 0.95 us  [extend(): return jnp.concatenate([below, field, above], axis=dim)]
    optimization_barrier x0 -> x2, local copies, waits for them, and re-layouts: none -> 1.96 us  [local(): lax.optimization_barrier((x_in, x_out, w_pair, w_out))]
    ppermute x3, starting transfers between devices: 3.92 us -> 2.08 us  [edge_of(): lax.ppermute(jnp.where(place_z == 0, plane_high, plane_low), 'gz', swap)]
    reduce_max x1 -> x0, other arithmetic: 1.68 us -> none  [shrink(): return jnp.max(blocks, axis=(1, 3, 5))]
    reshape x1 -> x0, local copies, waits for them, and re-layouts: 1.61 us -> none  [shrink(): field.reshape(size_x // 2, 2, size_y // 2, 2, size_z // 2, 2, channels)]
    ppermute x12, starting transfers between devices: 18.1 us -> 19.6 us  [the longest x6 18.1 us: swaps(): got_out = lax.ppermute(jnp.where(even, low, high), axis, outer)]
  transfers between devices with their start and end apart: 18 -> 18, of which waited for: 9 -> 9; matrix products, arithmetic and copies ran while one was open for 10% -> 15% of each run, Pallas kernels for 2% -> 2%
where the time goes in v3:
time: 118 us; the launch traced here: 117 us
  starting transfers between devices  33.6 us (28%)
  waiting for transfers between devices  32.6 us (28%)
  local copies, waits for them, and re-layouts  24.2 us (21%)
  Pallas kernels  17.9 us (15%)
  other arithmetic  8.83 us (7%)
    ppermute x6, starting transfers between devices, swaps(): got_out = lax.ppermute(jnp.where(even, low, high), axis, outer)  18.1 us
    ppermute x6, waiting for transfers between devices, swaps(): got_out = lax.ppermute(jnp.where(even, low, high), axis, outer)  12.8 us
    unnamed x40, local copies, waits for them, and re-layouts  10.1 us
    ppermute x3, waiting for transfers between devices, edge_of(): lax.ppermute(jnp.where(place_z == 0, plane_high, plane_low), 'gz', swap)  8.28 us
    pallas_call x1, Pallas kernels, encode(): pl.pallas_call(body, in_specs=[pl.BlockSpec(memory_space=pltpu.SMEM)] + [...  5.97 us
    all_to_all x1, starting transfers between devices, local(): column = lax.all_to_all(column, ('gx', 'gz'), 0, 0)  4.95 us
    pallas_call x1, Pallas kernels, decode(): pl.pallas_call(body, in_specs=[pl.BlockSpec(memory_space=pltpu.SMEM)] + [...  4.72 us
    all_to_all x1, waiting for transfers between devices, local(): first = lax.all_to_all(first, 'gx', 0, 0)  4.53 us
  transfers between devices with their start and end apart: 18, of which 9 were waited for; matrix products, arithmetic and copies ran while one was open for 15% of the time, Pallas kernels for 2%

profile of v3, /device:TPU:0, one launch (start us, length us, event | category | flops | bytes accessed | tf_op | source)
XLA Modules:
  0.0 117.5 jit_solution(556887393624910183)
XLA Ops:
  0.0 1.1 fusion.12
  1.1 0.8 broadcast_select_fusion.12
  2.0 6.6 %collective-permute-start.1 = (bf16[3,16,16,128]{3,1,0,2:T(8,128)(2,1)}, bf16[3,16,16,128]{3,1,0,2:T(8,128)(2,1)}, u32[]{:S(2)}, u32[]{:S(2)}) collective-permute-start(bf16[3,16,16,128]{3,1,0,2:T(8,128)(2,1)} %get-tuple-element.40), channel_id=1, source_target_pairs={{0,112},{16,32},{32,16},{48,64},{64,48},{80,96},{96,80},{112,0},{1... | collective-permute-start | bytes 589832 | tf_op jit(solution)/shard_map/ppermute | solution.py:14
  8.6 1.8 %fusion.10 = (bf16[8,16,1,128]{3,2,1,0:T(2,128)(2,1)}, bf16[8,16,1,128]{3,2,1,0:T(2,128)(2,1)}) fusion(bf16[8,16,16,128]{3,2,1,0:T(8,128)(2,1)} %own_ref.1), kind=kLoop, calls=%fused_computation.64 | loop fusion | bytes 131072 | tf_op jit(solution)/shard_map/slice | solution.py:401
  10.3 1.1 fusion.11
  11.4 0.7 copy.47
  12.1 0.7 copy.48
  12.9 1.5 %copy.34 = bf16[9,256,192]{2,1,0:T(8,128)(2,1)} copy(bf16[9,256,192]{1,2,0:T(8,128)(2,1)S(1)} %bitcast.38) | data formatting | bytes 1769472 | tf_op jit(solution)/shard_map/reshape | solution.py:376
  14.6 2.4 %copy.28 = bf16[9,512,192]{2,1,0:T(8,128)(2,1)} copy(bf16[9,512,192]{1,2,0:T(8,128)(2,1)S(1)} %bitcast.37) | data formatting | bytes 3538944 | tf_op jit(solution)/shard_map/reshape | solution.py:376
  17.1 1.6 %pad.27.weights_ref = bf16[9,256,256]{2,1,0:T(8,128)(2,1)S(1)} pad(bf16[9,256,192]{2,1,0:T(8,128)(2,1)} %copy.34, bf16[]{:T(256)} %constant.58.clone.1), padding=0_0x0_0x0_64 | pad | bytes 2064386 | tf_op jit(solution)/shard_map/jit(_pad)/pad | solution.py:377
  19.5 0.7 copy-done.13
  21.2 1.1 broadcast_select_fusion.11
  22.7 2.3 %collective-permute-start.3 = (bf16[14,3,16,128]{3,1,0,2:T(4,128)(2,1)S(1)}, bf16[14,3,16,128]{3,1,0,2:T(4,128)(2,1)S(1)}, u32[]{:S(2)}, u32[]{:S(2)}) collective-permute-start(bf16[14,3,16,128]{3,1,0,2:T(4,128)(2,1)S(1)} %get-tuple-element.32), channel_id=1, source_target_pairs={{0,14},{2,4},{4,2},{6,8},{8,6},{10,12},{12,10},{14,0},{1,15},{3,5}... | collective-permute-start | bytes 516104 | tf_op jit(solution)/shard_map/ppermute | solution.py:14
  25.0 4.5 %collective-permute-done.3 = bf16[14,3,16,128]{3,1,0,2:T(4,128)(2,1)S(1)} collective-permute-done((bf16[14,3,16,128]{3,1,0,2:T(4,128)(2,1)S(1)}, bf16[14,3,16,128]{3,1,0,2:T(4,128)(2,1)S(1)}, u32[]{:S(2)}, u32[]{:S(2)}) %collective-permute-start.3) | collective-permute-done | bytes 172064 | tf_op jit(solution)/shard_map/ppermute | solution.py:14
  29.8 0.7 collective-permute-start.4
  30.5 1.0 copy.35.x_in_ref
  31.5 1.0 copy.36.x_out_ref
  32.6 1.8 %collective-permute-done.4.edge_ref = bf16[14,22,128]{2,1,0:T(8,128)(2,1)S(1)} collective-permute-done((bf16[14,22,128]{2,1,0:T(8,128)(2,1)S(1)}, bf16[14,22,128]{2,1,0:T(8,128)(2,1)S(1)}, u32[]{:S(2)}, u32[]{:S(2)}) %collective-permute-start.4) | collective-permute-done | bytes 78880 | tf_op jit(solution)/shard_map/ppermute | solution.py:389
  34.4 6.0 %encode.1.field_ref = bf16[6,10,8,128]{3,2,1,0:T(8,128)(2,1)S(1)} custom-call(s32[5]{0:T(128)S(1)} %pad_add_fusion.place_ref, bf16[8,16,16,128]{3,2,1,0:T(8,128)(2,1)S(1)} %copy-done.1, bf16[3,16,16,128]{3,2,1,0:T(8,128)(2,1)S(1)} %copy.35.x_in_ref, bf16[3,16,16,128]{3,2,1,0:T(8,128)(2,1)S(1)} %copy.36.x_out_ref, ...), custom_call_target="tpu_custom_call" | custom-call | tf_op jit(solution)/shard_map/encode/pallas_call | solution.py:167
  40.4 0.7 collective-permute-start.5
  41.1 3.2 %collective-permute-done.5.edge_ref = bf16[6,10,128]{2,1,0:T(8,128)(2,1)S(1)} collective-permute-done((bf16[6,10,128]{2,1,0:T(8,128)(2,1)S(1)}, bf16[6,10,128]{2,1,0:T(8,128)(2,1)S(1)}, u32[]{:S(2)}, u32[]{:S(2)}) %collective-permute-start.5) | collective-permute-done | bytes 15392 | tf_op jit(solution)/shard_map/ppermute | solution.py:389
  44.3 1.4 %half_level.1 = (bf16[4,8,8,256]{3,2,1,0:T(8,128)(2,1)S(1)}, bf16[2,4,4,256]{3,2,1,0:T(4,128)(2,1)S(1)}) custom-call(s32[5]{0:T(128)S(1)} %pad_add_fusion.place_ref, bf16[6,10,8,128]{3,2,1,0:T(8,128)(2,1)S(1)} %encode.1.field_ref, bf16[6,10,128]{2,1,0:T(8,128)(2,1)S(1)} %collective-permute-done.5.edge_ref, bf16[9,3,128,256]{3,2,1,0:T(8,128)(2,1)S(1)} %bitcast.36), custom_call_target="tpu_custom_call" | custom-call | tf_op jit(solution)/shard_map/half_level/pallas_call | solution.py:72
  47.0 0.9 collective-permute-start.6
  47.9 3.7 %collective-permute-done.6 = bf16[2,4,1,256]{3,2,1,0:T(2,128)(2,1)} collective-permute-done((bf16[2,4,1,256]{3,2,1,0:T(2,128)(2,1)}, bf16[2,4,1,256]{3,2,1,0:T(2,128)(2,1)}, u32[]{:S(2)}, u32[]{:S(2)}) %collective-permute-start.6) | collective-permute-done | bytes 4128 | tf_op jit(solution)/shard_map/ppermute | solution.py:14
  51.6 0.7 broadcast_select_fusion.27
  52.4 0.9 broadcast_in_dim.19
  53.2 5.0 %all-to-all-start = ((bf16[16,2,4,8,256]{4,3,2,1,0:T(8,128)(2,1)}), bf16[16,2,4,8,256]{4,3,2,1,0:T(8,128)(2,1)}, u32[]{:S(2)}, u32[]{:S(2)}) async-start(bf16[16,2,4,8,256]{4,3,2,1,0:T(8,128)(2,1)} %broadcast_in_dim.19), calls=%async_computation | async-start | bytes 1048576 | tf_op jit(solution)/shard_map/all_to_all | solution.py:414
  58.2 0.9 copy.41
  60.4 5.5 %collective-permute-start.10 = (bf16[1,8,8,256]{3,1,0,2:T(8,128)(2,1)}, bf16[1,8,8,256]{3,1,0,2:T(8,128)(2,1)}, u32[]{:S(2)}, u32[]{:S(2)}) collective-permute-start(bf16[1,8,8,256]{3,1,0,2:T(8,128)(2,1)} %get-tuple-element.54), channel_id=1, source_target_pairs={{0,112},{16,32},{32,16},{48,64},{64,48},{80,96},{96,80},{112,0},{1... | collective-permute-start | bytes 98312 | tf_op jit(solution)/shard_map/ppermute | solution.py:14
  65.9 2.8 %all-to-all-done.field_ref = bf16[16,2,4,8,256]{4,3,2,1,0:T(8,128)(2,1)} async-done(((bf16[16,2,4,8,256]{4,3,2,1,0:T(8,128)(2,1)}), bf16[16,2,4,8,256]{4,3,2,1,0:T(8,128)(2,1)}, u32[]{:S(2)}, u32[]{:S(2)}) %all-to-all-start) | async-done | bytes 524320 | tf_op jit(solution)/shard_map/all_to_all | solution.py:414
  68.7 0.7 copy-done.6
  69.4 2.4 %bottom_in.1 = bf16[8,8,6,4,128]{4,3,2,1,0:T(4,128)(2,1)S(1)} custom-call(s32[5]{0:T(128)S(1)} %copy-done.6, bf16[16,2,4,8,256]{4,3,2,1,0:T(8,128)(2,1)} %all-to-all-done.field_ref, bf16[9,256,256]{2,1,0:T(8,128)(2,1)S(1)} %pad.27.weights_ref), custom_call_target="tpu_custom_call" | custom-call | tf_op jit(solution)/shard_map/bottom_in/pallas_call | solution.py:241
  71.8 0.7 copy-done.3
  72.6 3.6 %all-to-all-start.1 = ((bf16[8,8,6,4,128]{4,3,2,1,0:T(4,128)(2,1)}), bf16[8,8,6,4,128]{4,3,2,1,0:T(4,128)(2,1)S(1)}, u32[]{:S(2)}, u32[]{:S(2)}) async-start(bf16[8,8,6,4,128]{4,3,2,1,0:T(4,128)(2,1)} %copy-done.3), calls=%async_computation.1 | async-start | bytes 786432 | tf_op jit(solution)/shard_map/all_to_all | solution.py:416
  76.2 0.8 select_select_fusion.1
  77.0 1.1 broadcast_select_fusion.18
  78.2 2.8 %collective-permute-start.12 = (bf16[6,1,8,256]{3,1,0,2:T(2,128)(2,1)S(1)}, bf16[6,1,8,256]{3,1,0,2:T(2,128)(2,1)S(1)}, u32[]{:S(2)}, u32[]{:S(2)}) collective-permute-start(bf16[6,1,8,256]{3,1,0,2:T(2,128)(2,1)S(1)} %get-tuple-element.21), channel_id=1, source_target_pairs={{0,14},{2,4},{4,2},{6,8},{8,6},{10,12},{12,10},{14,0},{1,15},{3,5}... | collective-permute-start | bytes 73736 | tf_op jit(solution)/shard_map/ppermute | solution.py:14
  81.0 4.5 %all-to-all-done.1 = bf16[8,8,6,4,128]{4,3,2,1,0:T(4,128)(2,1)S(1)} async-done(((bf16[8,8,6,4,128]{4,3,2,1,0:T(4,128)(2,1)}), bf16[8,8,6,4,128]{4,3,2,1,0:T(4,128)(2,1)S(1)}, u32[]{:S(2)}, u32[]{:S(2)}) %all-to-all-start.1) | async-done | bytes 393248 | tf_op jit(solution)/shard_map/all_to_all | solution.py:416
  86.1 1.4 %collective-permute-start.9 = (bf16[8,8,6,2,128]{4,3,2,1,0:T(2,128)(2,1)S(1)}, bf16[8,8,6,2,128]{4,3,2,1,0:T(2,128)(2,1)S(1)}, u32[]{:S(2)}, u32[]{:S(2)}) collective-permute-start(bf16[8,8,6,2,128]{4,3,2,1,0:T(2,128)(2,1)S(1)} %get-tuple-element.37), channel_id=1, source_target_pairs={{0,2},{2,0},{4,6},{6,4},{8,10},{10,8},{12,14},{14,12},{1,3},{3,1},... | collective-permute-start | bytes 589832 | tf_op jit(solution)/shard_map/ppermute | solution.py:13
  87.9 4.6 %collective-permute-done.8 = bf16[8,8,6,2,128]{4,3,2,1,0:T(2,128)(2,1)S(1)} collective-permute-done((bf16[8,8,6,2,128]{4,3,2,1,0:T(2,128)(2,1)S(1)}, bf16[8,8,6,2,128]{4,3,2,1,0:T(2,128)(2,1)S(1)}, u32[]{:S(2)}, u32[]{:S(2)}) %collective-permute-start.8) | collective-permute-done | bytes 196640 | tf_op jit(solution)/shard_map/ppermute | solution.py:14
  92.8 0.7 pad_maximum_fusion.field_ref
  93.5 3.4 %bottom_out.1 = bf16[8,2,6,8,128]{4,3,2,1,0:T(8,128)(2,1)} custom-call(s32[5]{0:T(128)S(1)} %copy-done.7, bf16[8,8,6,8,128]{4,3,2,1,0:T(8,128)(2,1)S(1)} %pad_maximum_fusion.field_ref, bf16[9,512,256]{2,1,0:T(8,128)(2,1)S(1)} %pad.26.weights_ref), custom_call_target="tpu_custom_call" | custom-call | tf_op jit(solution)/shard_map/bottom_out/pallas_call | solution.py:284
  96.9 3.4 %all-to-all-start.2 = ((bf16[8,2,6,8,128]{4,3,2,1,0:T(8,128)(2,1)}), bf16[8,2,6,8,128]{4,3,2,1,0:T(8,128)(2,1)S(1)}, u32[]{:S(2)}, u32[]{:S(2)}) async-start(bf16[8,2,6,8,128]{4,3,2,1,0:T(8,128)(2,1)} %bottom_out.1), calls=%async_computation.2 | async-start | bytes 393216 | tf_op jit(solution)/shard_map/all_to_all | solution.py:419
  100.3 0.7 collective-permute-start.14
  101.2 3.3 %collective-permute-done.14 = bf16[6,10,256]{2,1,0:T(8,128)(2,1)S(1)} collective-permute-done((bf16[6,10,256]{2,1,0:T(8,128)(2,1)S(1)}, bf16[6,10,256]{2,1,0:T(8,128)(2,1)S(1)}, u32[]{:S(2)}, u32[]{:S(2)}) %collective-permute-start.14) | collective-permute-done | bytes 30752 | tf_op jit(solution)/shard_map/ppermute | solution.py:389
  104.5 4.2 %all-to-all-done.2.bottom_ref = bf16[8,2,6,8,128]{4,3,2,1,0:T(8,128)(2,1)S(1)} async-done(((bf16[8,2,6,8,128]{4,3,2,1,0:T(8,128)(2,1)}), bf16[8,2,6,8,128]{4,3,2,1,0:T(8,128)(2,1)S(1)}, u32[]{:S(2)}, u32[]{:S(2)}) %all-to-all-start.2) | async-done | bytes 196640 | tf_op jit(solution)/shard_map/all_to_all | solution.py:419
  108.7 4.0 %copy-done = bf16[3,3,3,768,256]{4,3,2,1,0:T(8,128)(2,1)S(1)} copy-done((bf16[3,3,3,768,256]{4,3,2,1,0:T(8,128)(2,1)S(1)}, bf16[3,3,3,768,256]{4,3,2,1,0:T(8,128)(2,1)}, u32[]{:S(2)}) %copy-start) | copy-done | bytes 10616856
  112.7 4.7 %decode.1 = bf16[4,8,8,256]{3,2,1,0:T(8,128)(2,1)} custom-call(s32[5]{0:T(128)S(1)} %copy-done.7, bf16[8,2,6,8,128]{4,3,2,1,0:T(8,128)(2,1)S(1)} %all-to-all-done.2.bottom_ref, bf16[6,10,8,256]{3,2,1,0:T(8,128)(2,1)S(1)} %copy.44.skip_ref, bf16[6,16,256]{2,1,0:T(8,128)(2,1)S(1)} %pad.29.edge_ref, bf16[9,3,768,256]{3,2,1,0:T(8,128)(2,1)S(1)} %bitcast.35), custom_call_target="tpu_custom_call" | custom-call | tf_op jit(solution)/shard_map/decode/pallas_call | solution.py:358
  (76 shorter events, 7.2 us)
Async XLA Ops:
  0.0 12.8 %copy-start.12 = (bf16[3,3,3,256,64]{3,4,2,1,0:T(8,128)(2,1)S(1)}, bf16[3,3,3,256,64]{3,4,2,1,0:T(8,128)(2,1)}, u32[]{:S(2)}) copy-start(bf16[3,3,3,256,64]{3,4,2,1,0:T(8,128)(2,1)} %param.9) | copy-start | bytes 2654212
  2.0 19.2 %collective-permute-start.1 = (bf16[3,16,16,128]{3,1,0,2:T(8,128)(2,1)}, bf16[3,16,16,128]{3,1,0,2:T(8,128)(2,1)}, u32[]{:S(2)}, u32[]{:S(2)}) collective-permute-start(bf16[3,16,16,128]{3,1,0,2:T(8,128)(2,1)} %get-tuple-element.40), channel_id=1, source_target_pairs={{0,112},{16,32},{32,16},{48,64},{64,48},{80,96},{96,80},{112,0},{1... | collective-permute-start | bytes 589832 | tf_op jit(solution)/shard_map/ppermute | solution.py:14
  8.6 12.6 %collective-permute-start = (bf16[3,16,16,128]{3,1,0,2:T(8,128)(2,1)}, bf16[3,16,16,128]{3,1,0,2:T(8,128)(2,1)}, u32[]{:S(2)}, u32[]{:S(2)}) collective-permute-start(bf16[3,16,16,128]{3,1,0,2:T(8,128)(2,1)} %get-tuple-element.41), channel_id=1, source_target_pairs={{0,16},{16,0},{32,48},{48,32},{64,80},{80,64},{96,112},{112,96},{1... | collective-permute-start | bytes 589832 | tf_op jit(solution)/shard_map/ppermute | solution.py:13
  10.3 4.1 %copy-start.9 = (bf16[3,3,3,512,64]{3,4,2,1,0:T(8,128)(2,1)S(1)}, bf16[3,3,3,512,64]{3,4,2,1,0:T(8,128)(2,1)}, u32[]{:S(2)}) copy-start(bf16[3,3,3,512,64]{3,4,2,1,0:T(8,128)(2,1)} %param.10) | copy-start | bytes 5308420
  17.1 2.0 %copy-start.8 = (bf16[9,512,192]{2,1,0:T(8,128)(2,1)S(1)}, bf16[9,512,192]{2,1,0:T(8,128)(2,1)}, u32[]{:S(2)}) copy-start(bf16[9,512,192]{2,1,0:T(8,128)(2,1)} %copy.28) | copy-start | bytes 5308420
  19.1 1.2 copy-start.13
  20.3 0.8 copy-start.16
  20.3 0.9 copy-start.17
  20.3 2.1 %copy-start.14 = (bf16[8,3,16,128]{3,1,0,2:T(4,128)(2,1)S(1)}, bf16[8,3,16,128]{3,1,0,2:T(4,128)(2,1)}, u32[]{:S(2)}) copy-start(bf16[8,3,16,128]{3,1,0,2:T(4,128)(2,1)} %copy.47) | copy-start | bytes 294916
  20.3 2.1 %copy-start.15 = (bf16[8,3,16,128]{3,1,0,2:T(4,128)(2,1)S(1)}, bf16[8,3,16,128]{3,1,0,2:T(4,128)(2,1)}, u32[]{:S(2)}) copy-start(bf16[8,3,16,128]{3,1,0,2:T(4,128)(2,1)} %copy.48) | copy-start | bytes 294916
  22.2 12.1 %copy-start.1 = (bf16[8,16,16,128]{3,2,1,0:T(8,128)(2,1)S(1)}, bf16[8,16,16,128]{3,2,1,0:T(8,128)(2,1)}, u32[]{:S(2)}) copy-start(bf16[8,16,16,128]{3,2,1,0:T(8,128)(2,1)} %own_ref.1) | copy-start | bytes 1572868
  22.7 6.7 %collective-permute-start.3 = (bf16[14,3,16,128]{3,1,0,2:T(4,128)(2,1)S(1)}, bf16[14,3,16,128]{3,1,0,2:T(4,128)(2,1)S(1)}, u32[]{:S(2)}, u32[]{:S(2)}) collective-permute-start(bf16[14,3,16,128]{3,1,0,2:T(4,128)(2,1)S(1)} %get-tuple-element.32), channel_id=1, source_target_pairs={{0,14},{2,4},{4,2},{6,8},{8,6},{10,12},{12,10},{14,0},{1,15},{3,5}... | collective-permute-start | bytes 516104 | tf_op jit(solution)/shard_map/ppermute | solution.py:14
  25.0 4.5 %collective-permute-start.2 = (bf16[14,3,16,128]{3,1,0,2:T(4,128)(2,1)S(1)}, bf16[14,3,16,128]{3,1,0,2:T(4,128)(2,1)S(1)}, u32[]{:S(2)}, u32[]{:S(2)}) collective-permute-start(bf16[14,3,16,128]{3,1,0,2:T(4,128)(2,1)S(1)} %get-tuple-element.33), channel_id=1, source_target_pairs={{0,2},{2,0},{4,6},{6,4},{8,10},{10,8},{12,14},{14,12},{1,3},{3,1},... | collective-permute-start | bytes 516104 | tf_op jit(solution)/shard_map/ppermute | solution.py:13
  29.8 4.6 %collective-permute-start.4 = (bf16[14,22,128]{2,1,0:T(8,128)(2,1)S(1)}, bf16[14,22,128]{2,1,0:T(8,128)(2,1)S(1)}, u32[]{:S(2)}, u32[]{:S(2)}) collective-permute-start(bf16[14,22,128]{2,1,0:T(8,128)(2,1)S(1)} %maximum_select_fusion), channel_id=1, source_target_pairs={{0,1},{1,0},{2,3},{3,2},{4,5},{5,4},{6,7},{7,6},{8,9},{9,8},{10,11... | collective-permute-start | bytes 236552 | tf_op jit(solution)/shard_map/ppermute | solution.py:389
  30.5 13.8 %copy-start.5 = (s32[5]{0:T(128)}, s32[5]{0:T(128)S(1)}, u32[]{:S(2)}) copy-start(s32[5]{0:T(128)S(1)} %pad_add_fusion.place_ref) | copy-start | bytes 64
  32.5 11.8 %copy-start.2 = (bf16[3,3,3,128,256]{4,3,2,1,0:T(8,128)(2,1)S(1)}, bf16[3,3,3,128,256]{4,3,2,1,0:T(8,128)(2,1)}, u32[]{:S(2)}) copy-start(bf16[3,3,3,128,256]{4,3,2,1,0:T(8,128)(2,1)} %param.8) | copy-start | bytes 5308420
  40.4 3.9 %collective-permute-start.5 = (bf16[6,10,128]{2,1,0:T(8,128)(2,1)S(1)}, bf16[6,10,128]{2,1,0:T(8,128)(2,1)S(1)}, u32[]{:S(2)}, u32[]{:S(2)}) collective-permute-start(bf16[6,10,128]{2,1,0:T(8,128)(2,1)S(1)} %fusion.9), channel_id=1, source_target_pairs={{0,1},{1,0},{2,3},{3,2},{4,5},{5,4},{6,7},{7,6},{8,9},{9,8},{10,11... | collective-permute-start | bytes 46088 | tf_op jit(solution)/shard_map/ppermute | solution.py:389
  45.7 0.7 copy-start.4
  47.0 4.6 %collective-permute-start.6 = (bf16[2,4,1,256]{3,2,1,0:T(2,128)(2,1)}, bf16[2,4,1,256]{3,2,1,0:T(2,128)(2,1)}, u32[]{:S(2)}, u32[]{:S(2)}) collective-permute-start(bf16[2,4,1,256]{3,2,1,0:T(2,128)(2,1)} %get-tuple-element.64), channel_id=1, source_target_pairs={{0,14},{2,4},{4,2},{6,8},{8,6},{10,12},{12,10},{14,0},{1,15},{3,5}... | collective-permute-start | bytes 12296 | tf_op jit(solution)/shard_map/ppermute | solution.py:14
  47.9 3.7 %collective-permute-start.7 = (bf16[2,4,1,256]{3,2,1,0:T(2,128)(2,1)}, bf16[2,4,1,256]{3,2,1,0:T(2,128)(2,1)}, u32[]{:S(2)}, u32[]{:S(2)}) collective-permute-start(bf16[2,4,1,256]{3,2,1,0:T(2,128)(2,1)} %get-tuple-element.65), channel_id=1, source_target_pairs={{0,2},{2,0},{4,6},{6,4},{8,10},{10,8},{12,14},{14,12},{1,3},{3,1},... | collective-permute-start | bytes 12296 | tf_op jit(solution)/shard_map/ppermute | solution.py:13
  53.2 15.5 %all-to-all-start = ((bf16[16,2,4,8,256]{4,3,2,1,0:T(8,128)(2,1)}), bf16[16,2,4,8,256]{4,3,2,1,0:T(8,128)(2,1)}, u32[]{:S(2)}, u32[]{:S(2)}) async-start(bf16[16,2,4,8,256]{4,3,2,1,0:T(8,128)(2,1)} %broadcast_in_dim.19), calls=%async_computation | async-start | bytes 1048576 | tf_op jit(solution)/shard_map/all_to_all | solution.py:414
  59.1 0.7 copy-start.10
  60.4 15.7 %collective-permute-start.10 = (bf16[1,8,8,256]{3,1,0,2:T(8,128)(2,1)}, bf16[1,8,8,256]{3,1,0,2:T(8,128)(2,1)}, u32[]{:S(2)}, u32[]{:S(2)}) collective-permute-start(bf16[1,8,8,256]{3,1,0,2:T(8,128)(2,1)} %get-tuple-element.54), channel_id=1, source_target_pairs={{0,112},{16,32},{32,16},{48,64},{64,48},{80,96},{96,80},{112,0},{1... | collective-permute-start | bytes 98312 | tf_op jit(solution)/shard_map/ppermute | solution.py:14
  65.9 10.3 %collective-permute-start.11 = (bf16[1,8,8,256]{3,1,0,2:T(8,128)(2,1)}, bf16[1,8,8,256]{3,1,0,2:T(8,128)(2,1)}, u32[]{:S(2)}, u32[]{:S(2)}) collective-permute-start(bf16[1,8,8,256]{3,1,0,2:T(8,128)(2,1)} %get-tuple-element.55), channel_id=1, source_target_pairs={{0,16},{16,0},{32,48},{48,32},{64,80},{80,64},{96,112},{112,96},{1... | collective-permute-start | bytes 98312 | tf_op jit(solution)/shard_map/ppermute | solution.py:13
  68.7 0.7 copy-start.6
  71.8 0.8 copy-start.3
  72.6 15.1 %copy-start.11 = (bf16[4,8,8,256]{3,1,0,2:T(8,128)(2,1)S(1)}, bf16[4,8,8,256]{3,1,0,2:T(8,128)(2,1)}, u32[]{:S(2)}) copy-start(bf16[4,8,8,256]{3,1,0,2:T(8,128)(2,1)} %copy-done.10) | copy-start | bytes 393220
  72.6 13.0 %all-to-all-start.1 = ((bf16[8,8,6,4,128]{4,3,2,1,0:T(4,128)(2,1)}), bf16[8,8,6,4,128]{4,3,2,1,0:T(4,128)(2,1)S(1)}, u32[]{:S(2)}, u32[]{:S(2)}) async-start(bf16[8,8,6,4,128]{4,3,2,1,0:T(4,128)(2,1)} %copy-done.3), calls=%async_computation.1 | async-start | bytes 786432 | tf_op jit(solution)/shard_map/all_to_all | solution.py:416
  76.1 17.3 %copy-start.7 = (s32[5]{0:T(128)S(1)}, s32[5]{0:T(128)}, u32[]{:S(2)}) copy-start(s32[5]{0:T(128)} %copy-done.5) | copy-start | bytes 64
  78.1 9.3 %collective-permute-start.13 = (bf16[6,1,8,256]{3,1,0,2:T(2,128)(2,1)S(1)}, bf16[6,1,8,256]{3,1,0,2:T(2,128)(2,1)S(1)}, u32[]{:S(2)}, u32[]{:S(2)}) collective-permute-start(bf16[6,1,8,256]{3,1,0,2:T(2,128)(2,1)S(1)} %broadcast_select_fusion.17), channel_id=1, source_target_pairs={{0,2},{2,0},{4,6},{6,4},{8,10},{10,8},{12,14},{14,12},{1,3},{3,1},... | collective-permute-start | bytes 73736 | tf_op jit(solution)/shard_map/ppermute | solution.py:13
  78.2 9.3 %collective-permute-start.12 = (bf16[6,1,8,256]{3,1,0,2:T(2,128)(2,1)S(1)}, bf16[6,1,8,256]{3,1,0,2:T(2,128)(2,1)S(1)}, u32[]{:S(2)}, u32[]{:S(2)}) collective-permute-start(bf16[6,1,8,256]{3,1,0,2:T(2,128)(2,1)S(1)} %get-tuple-element.21), channel_id=1, source_target_pairs={{0,14},{2,4},{4,2},{6,8},{8,6},{10,12},{12,10},{14,0},{1,15},{3,5}... | collective-permute-start | bytes 73736 | tf_op jit(solution)/shard_map/ppermute | solution.py:14
  86.0 6.4 %collective-permute-start.8 = (bf16[8,8,6,2,128]{4,3,2,1,0:T(2,128)(2,1)S(1)}, bf16[8,8,6,2,128]{4,3,2,1,0:T(2,128)(2,1)S(1)}, u32[]{:S(2)}, u32[]{:S(2)}) collective-permute-start(bf16[8,8,6,2,128]{4,3,2,1,0:T(2,128)(2,1)S(1)} %get-tuple-element.36), channel_id=1, source_target_pairs={{0,14},{2,4},{4,2},{6,8},{8,6},{10,12},{12,10},{14,0},{1,15},{3,5}... | collective-permute-start | bytes 589832 | tf_op jit(solution)/shard_map/ppermute | solution.py:14
  86.1 6.3 %collective-permute-start.9 = (bf16[8,8,6,2,128]{4,3,2,1,0:T(2,128)(2,1)S(1)}, bf16[8,8,6,2,128]{4,3,2,1,0:T(2,128)(2,1)S(1)}, u32[]{:S(2)}, u32[]{:S(2)}) collective-permute-start(bf16[8,8,6,2,128]{4,3,2,1,0:T(2,128)(2,1)S(1)} %get-tuple-element.37), channel_id=1, source_target_pairs={{0,2},{2,0},{4,6},{6,4},{8,10},{10,8},{12,14},{14,12},{1,3},{3,1},... | collective-permute-start | bytes 589832 | tf_op jit(solution)/shard_map/ppermute | solution.py:13
  96.9 11.8 %all-to-all-start.2 = ((bf16[8,2,6,8,128]{4,3,2,1,0:T(8,128)(2,1)}), bf16[8,2,6,8,128]{4,3,2,1,0:T(8,128)(2,1)S(1)}, u32[]{:S(2)}, u32[]{:S(2)}) async-start(bf16[8,2,6,8,128]{4,3,2,1,0:T(8,128)(2,1)} %bottom_out.1), calls=%async_computation.2 | async-start | bytes 393216 | tf_op jit(solution)/shard_map/all_to_all | solution.py:419
  100.3 4.2 %collective-permute-start.14 = (bf16[6,10,256]{2,1,0:T(8,128)(2,1)S(1)}, bf16[6,10,256]{2,1,0:T(8,128)(2,1)S(1)}, u32[]{:S(2)}, u32[]{:S(2)}) collective-permute-start(bf16[6,10,256]{2,1,0:T(8,128)(2,1)S(1)} %fusion.6), channel_id=1, source_target_pairs={{0,1},{1,0},{2,3},{3,2},{4,5},{5,4},{6,7},{7,6},{8,9},{9,8},{10,11... | collective-permute-start | bytes 92168 | tf_op jit(solution)/shard_map/ppermute | solution.py:389
  108.7 4.0 %copy-start = (bf16[3,3,3,768,256]{4,3,2,1,0:T(8,128)(2,1)S(1)}, bf16[3,3,3,768,256]{4,3,2,1,0:T(8,128)(2,1)}, u32[]{:S(2)}) copy-start(bf16[3,3,3,768,256]{4,3,2,1,0:T(8,128)(2,1)} %param.11) | copy-start | bytes 31850500

commit v4 on v3

--- a/solution.py
+++ b/solution.py
@@ -7,9 +7,12 @@
 
 
 def swaps(low, high, axis, count):
-    even = lax.axis_index(axis) % 2 == 0
+    both = isinstance(axis, tuple)
+    even = lax.axis_index(axis[0] if both else axis) % 2 == 0
     inner = [(i, i ^ 1) for i in range(count)]
     outer = [(i, (((i + 1) ^ 1) - 1) % count) for i in range(count)]
+    if both:
+        inner, outer = [[(2 * i + n, 2 * j + 1 - n) for i, j in pairs for n in range(2)] for pairs in (inner, outer)]
     got_in = lax.ppermute(jnp.where(even, high, low), axis, inner)
     got_out = lax.ppermute(jnp.where(even, low, high), axis, outer)
     return got_in, got_out
@@ -41,7 +44,7 @@
     filters = weights.shape[-1]
     rows, extra = size_x * size_y * size_z, size_x * size_y
 
-    def body(place_ref, field_ref, edge_ref, weights_ref, out_ref, coarse_ref, rows_ref):
+    def body(place_ref, field_ref, edge_ref, weights_ref, out_ref, coarse_ref, rows_ref, coarse_rows_ref):
         first = place_ref[2] == 0
         edge_plane = edge_ref[...].astype(jnp.float32)
         blocks = []
@@ -67,7 +70,8 @@
                     pooled = jnp.maximum(
                         rows_ref[pl.ds(start, count, stride=size_z), :], rows_ref[pl.ds(start + 1, count, stride=size_z), :]
                     )
-                    coarse_ref[x, z, :, 128 * part : 128 * part + 128] = pooled.astype(coarse_ref.dtype)
+                    coarse_rows_ref[x, count * z : count * z + count, 128 * part : 128 * part + 128] = pooled
+        coarse_ref[...] = coarse_rows_ref[...].astype(coarse_ref.dtype)
 
     return pl.pallas_call(
         body,
@@ -75,9 +79,12 @@
         out_specs=[pl.BlockSpec(memory_space=pltpu.VMEM)] * 2,
         out_shape=[
             jax.ShapeDtypeStruct((size_x, size_y, size_z, filters), jnp.bfloat16),
-            jax.ShapeDtypeStruct((size_x // 2, size_z // 2, size_y // 2, filters), jnp.bfloat16),
+            jax.ShapeDtypeStruct((size_x // 2, size_z * size_y // 4, filters), jnp.bfloat16),
         ],
-        scratch_shapes=[pltpu.VMEM((rows // 4, 128), jnp.float32)],
+        scratch_shapes=[
+            pltpu.VMEM((rows // 4, 128), jnp.float32),
+            pltpu.VMEM((size_x // 2, size_z * size_y // 4, filters), jnp.float32),
+        ],
         compiler_params=pltpu.CompilerParams(vmem_limit_bytes=12 << 20),
         name="half_level",
     )(place, field, edge, weights)
@@ -215,9 +222,10 @@
 
 
 def bottom_in(place, field, weights):
-    count, own_x, own_z, _, channels = field.shape
+    count, own_x, lines, channels = field.shape
     devices = count // 2
-    size_x, all_z, size_z, size_y = devices * own_x, 2 * own_z, own_z + 2, own_z
+    own_z = size_y = 4
+    size_x, all_z, size_z = devices * own_x, 2 * own_z, own_z + 2
 
     def body(place_ref, field_ref, weights_ref, out_ref, pad_ref):
         zero = jnp.zeros((all_z + 2, 8, channels), jnp.float32)
@@ -228,8 +236,15 @@
             pad_ref[x + 1, all_z + 1] = zero[0]
         for i in range(devices):
             for half in range(2):
-                block = field_ref[2 * i + half].astype(jnp.float32)
-                pad_ref[1 + own_x * i : 1 + own_x * i + own_x, 1 + own_z * half : 1 + own_z * half + own_z] = block
+                for x in range(own_x):
+                    block = field_ref[2 * i + half, x].astype(jnp.float32)
+                    for z in range(own_z):
+                        to = (1 + own_x * i + x, 1 + own_z * half + z)
+                        pad_ref[*to, 0:1] = block[own_z * size_y + z : own_z * size_y + z + 1]
+                        pad_ref[*to, 1 : size_y + 1] = block[size_y * z : size_y * z + size_y]
+                        line = own_z * (size_y + 1) + z
+                        pad_ref[*to, size_y + 1 : size_y + 2] = block[line : line + 1]
+                        pad_ref[*to, size_y + 2 :] = zero[0, size_y + 2 :]
         start = 2 * place_ref[2]
         for first in range(0, size_x, 4):
             total = column_product(pad_ref, weights_ref, first, start, 4, size_z)
@@ -390,26 +405,28 @@
 
         x_in, x_out = swaps(volume[:3], volume[-3:], "gx", gx)
         w_pair, w_out = paired(w_full), beside(w_bottom_out)
-        x_in, x_out, w_pair, w_out = lax.optimization_barrier((x_in, x_out, w_pair, w_out))
+        x_in, x_out, w_pair, w_out, w_bottom_in = lax.optimization_barrier((x_in, x_out, w_pair, w_out, w_bottom_in))
         below, above = ordered(x_in, x_out, "gx")
         y_low = jnp.concatenate([below[:, :3], volume[:, :3], above[:, :3]], axis=0)
         y_high = jnp.concatenate([below[:, -3:], volume[:, -3:], above[:, -3:]], axis=0)
         y_in, y_out = swaps(y_low, y_high, "gy", gy)
-        low, high = ordered(y_in, y_out, "gy")
-
-        def plane(z):
-            middle = jnp.concatenate([below[:, :, z], volume[:, :, z], above[:, :, z]], axis=0)
-            return jnp.concatenate([low[:, :, z], middle, high[:, :, z]], axis=1)
-
-        edge = edge_of(plane(0), plane(-1))
+
+        def outer_plane(block):
+            return jnp.where(place_z == 0, block[:, :, -1], block[:, :, 0])
+
+        edge = jnp.concatenate([outer_plane(below), outer_plane(volume), outer_plane(above)], axis=0)
+        edge_in, edge_out = swaps(edge[:, :3], edge[:, -3:], ("gy", "gz"), gy)
+        edge = lax.ppermute(edge, "gz", swap)
+        edge_low, edge_high = ordered(edge_in, edge_out, "gy")
+        edge = jnp.concatenate([edge_low, edge, edge_high], axis=1)
         edge, w_in = lax.optimization_barrier((edge, beside(w_bottom_in)))
         pooled = encode(place, volume, x_in, x_out, y_in, y_out, edge, w_pair)
 
         edge = edge_of(pooled[:, :, 0], pooled[:, :, -1])
         skip, coarse = half_level(place, pooled, edge, w_half.reshape(9, 3, w_half.shape[3], w_half.shape[4]))
-        own_y = coarse.shape[2]
-
-        column = jnp.pad(extend(coarse, "gy", gy, 2, 1), ((0, 0), (0, 0), (0, 6 - own_y), (0, 0)))
+        lines = coarse.reshape(coarse.shape[0], 4, 4, coarse.shape[2])
+        below, above = halo(lines, "gy", gy, 2, 1)
+        column = jnp.concatenate([coarse, below[:, :, 0], above[:, :, 0]], axis=1)
         column = jnp.broadcast_to(column[None], (gx * gz,) + column.shape)
         column = lax.all_to_all(column, ("gx", "gz"), 0, 0)
         first = bottom_in(place, column, w_in)

time: 118 us -> 128 us (1.085)
  other arithmetic: 8.83 us -> 14 us
  local copies, waits for them, and re-layouts: 24.2 us -> 28.6 us
    ppermute x6 -> x7, starting transfers between devices: 18.1 us -> 14.3 us  [swaps(): got_out = lax.ppermute(jnp.where(even, low, high), axis, outer)]
    ppermute x6 -> x7, starting transfers between devices: 1.45 us -> 4.97 us  [swaps(): got_in = lax.ppermute(jnp.where(even, high, low), axis, inner)]
    unnamed x40 -> x39, local copies, waits for them, and re-layouts: 10.1 us -> 12 us
    select_n x6 -> x7, other arithmetic: 4.01 us -> 5.84 us  [swaps(): got_out = lax.ppermute(jnp.where(even, low, high), axis, outer)]
    pad x2, local copies, waits for them, and re-layouts: 2.03 us -> 3.73 us  [beside(): return jnp.pad(weights, ((0, 0), (0, 0), (0, 256 - 3 * filters)))]
    ppermute x3 -> x2, waiting for transfers between devices: 8.28 us -> 6.65 us  [edge_of(): lax.ppermute(jnp.where(place_z == 0, plane_high, plane_low), 'gz', swap)]
    concatenate x0 -> x3, other arithmetic: none -> 1.5 us  [the longest x1 0.86 us: local(): edge = jnp.concatenate([edge_low, edge, edge_high], axis=1)]
    ppermute x0 -> x1, starting transfers between devices: none -> 1.49 us  [local(): edge = lax.ppermute(edge, 'gz', swap)]
  transfers between devices with their start and end apart: 18 -> 20, of which waited for: 9 -> 8; matrix products, arithmetic and copies ran while one was open for 15% -> 20% of each run, Pallas kernels for 2% -> 2%
where the time goes in v4:
time: 128 us; the launch traced here: 127 us
  starting transfers between devices  34 us (27%)
  waiting for transfers between devices  32.1 us (25%)
  local copies, waits for them, and re-layouts  28.6 us (22%)
  Pallas kernels  18 us (14%)
  other arithmetic  14 us (11%)
    ppermute x7, starting transfers between devices, swaps(): got_out = lax.ppermute(jnp.where(even, low, high), axis, outer)  14.3 us
    ppermute x7, waiting for transfers between devices, swaps(): got_out = lax.ppermute(jnp.where(even, low, high), axis, outer)  13.4 us
    unnamed x39, local copies, waits for them, and re-layouts  12 us
    ppermute x2, waiting for transfers between devices, edge_of(): lax.ppermute(jnp.where(place_z == 0, plane_high, plane_low), 'gz', swap)  6.65 us
    pallas_call x1, Pallas kernels, encode(): pl.pallas_call(body, in_specs=[pl.BlockSpec(memory_space=pltpu.SMEM)] + [...  5.98 us
    select_n x7, other arithmetic, swaps(): got_out = lax.ppermute(jnp.where(even, low, high), axis, outer)  5.84 us
    all_to_all x1, waiting for transfers between devices, local(): first = lax.all_to_all(first, 'gx', 0, 0)  5.76 us
    all_to_all x1, starting transfers between devices, local(): column = lax.all_to_all(column, ('gx', 'gz'), 0, 0)  5.06 us
  transfers between devices with their start and end apart: 20, of which 8 were waited for; matrix products, arithmetic and copies ran while one was open for 20% of the time, Pallas kernels for 2%

profile of v4, /device:TPU:0, one launch (start us, length us, event | category | flops | bytes accessed | tf_op | source)
XLA Modules:
  0.0 127.1 jit_solution(8012006667500838948)
XLA Ops:
  0.0 1.0 fusion.10
  1.1 0.8 broadcast_select_fusion.8
  1.9 3.1 %collective-permute-start = (bf16[3,16,16,128]{3,1,0,2:T(8,128)(2,1)}, bf16[3,16,16,128]{3,1,0,2:T(8,128)(2,1)S(1)}, u32[]{:S(2)}, u32[]{:S(2)}) collective-permute-start(bf16[3,16,16,128]{3,1,0,2:T(8,128)(2,1)} %get-tuple-element.39), channel_id=1, source_target_pairs={{0,16},{16,0},{32,48},{48,32},{64,80},{80,64},{96,112},{112,96},{1... | collective-permute-start | bytes 589832 | tf_op jit(solution)/shard_map/ppermute | solution.py:16
  5.0 4.0 %collective-permute-start.1 = (bf16[3,16,16,128]{3,1,0,2:T(8,128)(2,1)}, bf16[3,16,16,128]{3,1,0,2:T(8,128)(2,1)}, u32[]{:S(2)}, u32[]{:S(2)}) collective-permute-start(bf16[3,16,16,128]{3,1,0,2:T(8,128)(2,1)} %get-tuple-element.38), channel_id=1, source_target_pairs={{0,112},{16,32},{32,16},{48,64},{64,48},{80,96},{96,80},{112,0},{1... | collective-permute-start | bytes 589832 | tf_op jit(solution)/shard_map/ppermute | solution.py:17
  9.0 1.8 %fusion.8 = (bf16[8,16,1,128]{3,2,1,0:T(2,128)(2,1)}, bf16[8,16,1,128]{3,2,1,0:T(2,128)(2,1)}) fusion(bf16[8,16,16,128]{3,2,1,0:T(8,128)(2,1)} %own_ref.1), kind=kLoop, calls=%fused_computation.56 | loop fusion | bytes 131072 | tf_op jit(solution)/shard_map/slice | solution.py:415
  10.8 1.6 %fusion.9 = (bf16[8,3,16,128]{3,2,1,0:T(8,128)(2,1)S(1)}, bf16[8,3,16,128]{3,2,1,0:T(8,128)(2,1)}) fusion(bf16[8,16,16,128]{3,2,1,0:T(8,128)(2,1)} %own_ref.1), kind=kLoop, calls=%fused_computation.57 | loop fusion | bytes 393216 | tf_op jit(solution)/shard_map/slice | solution.py:411
  12.4 1.7 %copy.27 = bf16[3,3,3,512,64]{3,4,1,2,0:T(8,128)(2,1)S(1)} copy(bf16[3,3,3,512,64]{3,4,2,1,0:T(8,128)(2,1)} %param.10) | data formatting | bytes 3538944 | tf_op args[4]
  14.0 2.4 %copy.28 = bf16[9,512,192]{2,1,0:T(8,128)(2,1)} copy(bf16[9,512,192]{1,2,0:T(8,128)(2,1)S(1)} %bitcast.28) | data formatting | bytes 3538944 | tf_op jit(solution)/shard_map/reshape | solution.py:391
  16.5 1.7 %fusion.2.weights_ref = bf16[4,3,3,128,256]{4,3,2,1,0:T(8,128)(2,1)} fusion(bf16[3,3,3,128,128]{4,3,2,1,0:T(8,128)(2,1)S(1)} %copy-done.14), kind=kLoop, calls=%fused_computation.4 | loop fusion | flops 9437184 | bytes 3244032 | tf_op jit(solution)/shard_map/concatenate | solution.py:191
  18.2 2.1 %pad.22.weights_ref = bf16[9,512,256]{2,1,0:T(8,128)(2,1)S(1)} pad(bf16[9,512,192]{2,1,0:T(8,128)(2,1)} %copy.28, bf16[]{:T(256)} %constant.60.clone.1), padding=0_0x0_0x0_64 | pad | bytes 4128770 | tf_op jit(solution)/shard_map/jit(_pad)/pad | solution.py:392
  20.5 1.0 broadcast_select_fusion.7
  22.3 1.5 %collective-permute-start.6 = (bf16[14,16,128]{2,1,0:T(8,128)(2,1)}, bf16[14,16,128]{2,1,0:T(8,128)(2,1)}, u32[]{:S(2)}, u32[]{:S(2)}) collective-permute-start(bf16[14,16,128]{2,1,0:T(8,128)(2,1)} %pad_maximum_fusion.5), channel_id=1, source_target_pairs={{0,1},{1,0},{2,3},{3,2},{4,5},{5,4},{6,7},{7,6},{8,9},{9,8},{10,11... | collective-permute-start | bytes 172040 | tf_op jit(solution)/shard_map/ppermute | solution.py:419
  23.8 1.4 %broadcast_select_fusion.23 = (bf16[14,3,128]{2,1,0:T(4,128)(2,1)}, bf16[14,3,128]{2,1,0:T(4,128)(2,1)}) fusion(pred[]{:T(512)S(6)} %eq.38, bf16[14,16,128]{2,1,0:T(8,128)(2,1)} %pad_maximum_fusion.5), kind=kLoop, calls=%fused_computation.46 | loop fusion | flops 10752 | bytes 43009 | tf_op jit(solution)/shard_map/jit(_where)/select_n | solution.py:17
  25.2 1.6 %collective-permute-start.4 = (bf16[14,3,128]{2,1,0:T(4,128)(2,1)}, bf16[14,3,128]{2,1,0:T(4,128)(2,1)}, u32[]{:S(2)}, u32[]{:S(2)}) collective-permute-start(bf16[14,3,128]{2,1,0:T(4,128)(2,1)} %get-tuple-element.54), channel_id=1, source_target_pairs={{0,15},{1,14},{2,5},{3,4},{4,3},{5,2},{6,9},{7,8},{8,7},{9,6},{10,... | collective-permute-start | bytes 32264 | tf_op jit(solution)/shard_map/ppermute | solution.py:17
  26.8 1.2 collective-permute-start.5
  28.0 0.8 broadcast_select_fusion.10
  29.5 1.7 %copy.38.x_out_ref = bf16[3,16,16,128]{3,2,1,0:T(8,128)(2,1)} copy(bf16[3,16,16,128]{3,1,0,2:T(8,128)(2,1)} %collective-permute-done.1) | data formatting | bytes 393216 | tf_op jit(solution)/shard_map/optimization_barrier | solution.py:408
  31.3 1.5 %copy.36 = bf16[9,256,192]{2,1,0:T(8,128)(2,1)} copy(bf16[9,256,192]{1,2,0:T(8,128)(2,1)S(1)} %bitcast.29) | data formatting | bytes 1769472 | tf_op jit(solution)/shard_map/reshape | solution.py:391
  32.8 1.6 %pad.23.weights_ref = bf16[9,256,256]{2,1,0:T(8,128)(2,1)S(1)} pad(bf16[9,256,192]{2,1,0:T(8,128)(2,1)} %copy.36, bf16[]{:T(256)} %constant.60.clone.1), padding=0_0x0_0x0_64 | pad | bytes 2064386 | tf_op jit(solution)/shard_map/jit(_pad)/pad | solution.py:392
  34.9 1.3 %collective-permute-start.3 = (bf16[14,3,16,128]{3,2,1,0:T(8,128)(2,1)}, bf16[14,3,16,128]{3,2,1,0:T(8,128)(2,1)S(1)}, u32[]{:S(2)}, u32[]{:S(2)}) collective-permute-start(bf16[14,3,16,128]{3,2,1,0:T(8,128)(2,1)} %get-tuple-element.40), channel_id=1, source_target_pairs={{0,14},{2,4},{4,2},{6,8},{8,6},{10,12},{12,10},{14,0},{1,15},{3,5}... | collective-permute-start | bytes 516104 | tf_op jit(solution)/shard_map/ppermute | solution.py:17
  36.3 0.7 broadcast_select_fusion.21
  37.0 0.9 pad_maximum_fusion.4.edge_ref
  37.9 3.3 %collective-permute-done.3.y_out_ref = bf16[14,3,16,128]{3,2,1,0:T(8,128)(2,1)S(1)} collective-permute-done((bf16[14,3,16,128]{3,2,1,0:T(8,128)(2,1)}, bf16[14,3,16,128]{3,2,1,0:T(8,128)(2,1)S(1)}, u32[]{:S(2)}, u32[]{:S(2)}) %collective-permute-start.3) | collective-permute-done | bytes 172064 | tf_op jit(solution)/shard_map/ppermute | solution.py:17
  41.2 1.0 copy-done.2
  42.2 0.9 copy-done.5
  43.2 0.9 copy-done.6
  44.1 6.0 %encode.1.field_ref = bf16[6,10,8,128]{3,2,1,0:T(8,128)(2,1)S(1)} custom-call(s32[5]{0:T(128)S(1)} %pad_add_fusion.place_ref, bf16[8,16,16,128]{3,2,1,0:T(8,128)(2,1)S(1)} %copy-done.2, bf16[3,16,16,128]{3,2,1,0:T(8,128)(2,1)S(1)} %copy-done.5, bf16[3,16,16,128]{3,2,1,0:T(8,128)(2,1)S(1)} %copy-done.6, ...), custom_call_target="tpu_custom_call" | custom-call | tf_op jit(solution)/shard_map/encode/pallas_call | solution.py:174
  50.8 3.3 %collective-permute-done.7.edge_ref = bf16[6,10,128]{2,1,0:T(8,128)(2,1)S(1)} collective-permute-done((bf16[6,10,128]{2,1,0:T(8,128)(2,1)S(1)}, bf16[6,10,128]{2,1,0:T(8,128)(2,1)S(1)}, u32[]{:S(2)}, u32[]{:S(2)}) %collective-permute-start.7) | collective-permute-done | bytes 15392 | tf_op jit(solution)/shard_map/ppermute | solution.py:404
  54.7 1.4 %half_level.1 = (bf16[4,8,8,256]{3,2,1,0:T(8,128)(2,1)S(1)}, bf16[2,16,256]{2,1,0:T(8,128)(2,1)S(1)}) custom-call(s32[5]{0:T(128)S(1)} %copy-done.9, bf16[6,10,8,128]{3,2,1,0:T(8,128)(2,1)S(1)} %encode.1.field_ref, bf16[6,10,128]{2,1,0:T(8,128)(2,1)S(1)} %collective-permute-done.7.edge_ref, bf16[9,3,128,256]{3,2,1,0:T(8,128)(2,1)S(1)} %bitcast.27), custom_call_target="tpu_custom_call" | custom-call | tf_op jit(solution)/shard_map/half_level/pallas_call | solution.py:76
  57.6 4.4 %collective-permute-done.8 = bf16[2,4,1,256]{3,1,0,2:T(4,128)(2,1)} collective-permute-done((bf16[2,4,1,256]{3,1,0,2:T(4,128)(2,1)}, bf16[2,4,1,256]{3,1,0,2:T(4,128)(2,1)}, u32[]{:S(2)}, u32[]{:S(2)}) %collective-permute-start.8) | collective-permute-done | bytes 4128 | tf_op jit(solution)/shard_map/ppermute | solution.py:17
  62.7 0.8 broadcast_in_dim.19
  63.5 5.1 %all-to-all-start = ((bf16[16,2,24,256]{3,2,1,0:T(8,128)(2,1)}), bf16[16,2,24,256]{3,2,1,0:T(8,128)(2,1)}, u32[]{:S(2)}, u32[]{:S(2)}) async-start(bf16[16,2,24,256]{3,2,1,0:T(8,128)(2,1)} %broadcast_in_dim.19), calls=%async_computation | async-start | bytes 786432 | tf_op jit(solution)/shard_map/all_to_all | solution.py:431
  68.5 0.9 copy.44
  70.8 5.5 %collective-permute-start.12 = (bf16[1,8,8,256]{3,1,0,2:T(8,128)(2,1)}, bf16[1,8,8,256]{3,1,0,2:T(8,128)(2,1)}, u32[]{:S(2)}, u32[]{:S(2)}) collective-permute-start(bf16[1,8,8,256]{3,1,0,2:T(8,128)(2,1)} %get-tuple-element.46), channel_id=1, source_target_pairs={{0,112},{16,32},{32,16},{48,64},{64,48},{80,96},{96,80},{112,0},{1... | collective-permute-start | bytes 98312 | tf_op jit(solution)/shard_map/ppermute | solution.py:17
  76.3 2.1 %all-to-all-done.field_ref = bf16[16,2,24,256]{3,2,1,0:T(8,128)(2,1)} async-done(((bf16[16,2,24,256]{3,2,1,0:T(8,128)(2,1)}), bf16[16,2,24,256]{3,2,1,0:T(8,128)(2,1)}, u32[]{:S(2)}, u32[]{:S(2)}) %all-to-all-start) | async-done | bytes 393248 | tf_op jit(solution)/shard_map/all_to_all | solution.py:431
  79.0 2.5 %bottom_in.1 = bf16[8,8,6,4,128]{4,3,2,1,0:T(4,128)(2,1)S(1)} custom-call(s32[5]{0:T(128)S(1)} %copy-done.10, bf16[16,2,24,256]{3,2,1,0:T(8,128)(2,1)} %all-to-all-done.field_ref, bf16[9,256,256]{2,1,0:T(8,128)(2,1)S(1)} %pad.23.weights_ref), custom_call_target="tpu_custom_call" | custom-call | tf_op jit(solution)/shard_map/bottom_in/pallas_call | solution.py:256
  82.2 3.6 %all-to-all-start.1 = ((bf16[8,8,6,4,128]{4,3,2,1,0:T(4,128)(2,1)}), bf16[8,8,6,4,128]{4,3,2,1,0:T(4,128)(2,1)S(1)}, u32[]{:S(2)}, u32[]{:S(2)}) async-start(bf16[8,8,6,4,128]{4,3,2,1,0:T(4,128)(2,1)} %copy-done.4), calls=%async_computation.1 | async-start | bytes 786432 | tf_op jit(solution)/shard_map/all_to_all | solution.py:433
  85.9 0.8 select_select_fusion.1
  86.7 1.1 broadcast_select_fusion.16
  87.9 1.6 %collective-permute-start.14 = (bf16[6,1,8,256]{3,1,0,2:T(2,128)(2,1)S(1)}, bf16[6,1,8,256]{3,1,0,2:T(2,128)(2,1)S(1)}, u32[]{:S(2)}, u32[]{:S(2)}) collective-permute-start(bf16[6,1,8,256]{3,1,0,2:T(2,128)(2,1)S(1)} %get-tuple-element.23), channel_id=1, source_target_pairs={{0,14},{2,4},{4,2},{6,8},{8,6},{10,12},{12,10},{14,0},{1,15},{3,5}... | collective-permute-start | bytes 73736 | tf_op jit(solution)/shard_map/ppermute | solution.py:17
  89.5 5.8 %all-to-all-done.1 = bf16[8,8,6,4,128]{4,3,2,1,0:T(4,128)(2,1)S(1)} async-done(((bf16[8,8,6,4,128]{4,3,2,1,0:T(4,128)(2,1)}), bf16[8,8,6,4,128]{4,3,2,1,0:T(4,128)(2,1)S(1)}, u32[]{:S(2)}, u32[]{:S(2)}) %all-to-all-start.1) | async-done | bytes 393248 | tf_op jit(solution)/shard_map/all_to_all | solution.py:433
  96.3 5.8 %collective-permute-done.10 = bf16[8,8,6,2,128]{4,3,2,1,0:T(2,128)(2,1)S(1)} collective-permute-done((bf16[8,8,6,2,128]{4,3,2,1,0:T(2,128)(2,1)S(1)}, bf16[8,8,6,2,128]{4,3,2,1,0:T(2,128)(2,1)S(1)}, u32[]{:S(2)}, u32[]{:S(2)}) %collective-permute-start.10) | collective-permute-done | bytes 196640 | tf_op jit(solution)/shard_map/ppermute | solution.py:17
  103.2 3.4 %bottom_out.1 = bf16[8,2,6,8,128]{4,3,2,1,0:T(8,128)(2,1)} custom-call(s32[5]{0:T(128)S(1)} %copy-done.11, bf16[8,8,6,8,128]{4,3,2,1,0:T(8,128)(2,1)S(1)} %pad_maximum_fusion.field_ref, bf16[9,512,256]{2,1,0:T(8,128)(2,1)S(1)} %pad.22.weights_ref), custom_call_target="tpu_custom_call" | custom-call | tf_op jit(solution)/shard_map/bottom_out/pallas_call | solution.py:299
  106.6 3.4 %all-to-all-start.2 = ((bf16[8,2,6,8,128]{4,3,2,1,0:T(8,128)(2,1)}), bf16[8,2,6,8,128]{4,3,2,1,0:T(8,128)(2,1)S(1)}, u32[]{:S(2)}, u32[]{:S(2)}) async-start(bf16[8,2,6,8,128]{4,3,2,1,0:T(8,128)(2,1)} %bottom_out.1), calls=%async_computation.2 | async-start | bytes 393216 | tf_op jit(solution)/shard_map/all_to_all | solution.py:436
  110.8 3.4 %collective-permute-done.16 = bf16[6,10,256]{2,1,0:T(8,128)(2,1)S(1)} collective-permute-done((bf16[6,10,256]{2,1,0:T(8,128)(2,1)S(1)}, bf16[6,10,256]{2,1,0:T(8,128)(2,1)S(1)}, u32[]{:S(2)}, u32[]{:S(2)}) %collective-permute-start.16) | collective-permute-done | bytes 30752 | tf_op jit(solution)/shard_map/ppermute | solution.py:404
  114.2 4.2 %all-to-all-done.2.bottom_ref = bf16[8,2,6,8,128]{4,3,2,1,0:T(8,128)(2,1)S(1)} async-done(((bf16[8,2,6,8,128]{4,3,2,1,0:T(8,128)(2,1)}), bf16[8,2,6,8,128]{4,3,2,1,0:T(8,128)(2,1)S(1)}, u32[]{:S(2)}, u32[]{:S(2)}) %all-to-all-start.2) | async-done | bytes 196640 | tf_op jit(solution)/shard_map/all_to_all | solution.py:436
  118.4 4.0 %copy-done = bf16[3,3,3,768,256]{4,3,2,1,0:T(8,128)(2,1)S(1)} copy-done((bf16[3,3,3,768,256]{4,3,2,1,0:T(8,128)(2,1)S(1)}, bf16[3,3,3,768,256]{4,3,2,1,0:T(8,128)(2,1)}, u32[]{:S(2)}) %copy-start) | copy-done | bytes 10616856
  122.4 4.7 %decode.1 = bf16[4,8,8,256]{3,2,1,0:T(8,128)(2,1)} custom-call(s32[5]{0:T(128)S(1)} %copy-done.11, bf16[8,2,6,8,128]{4,3,2,1,0:T(8,128)(2,1)S(1)} %all-to-all-done.2.bottom_ref, bf16[6,10,8,256]{3,2,1,0:T(8,128)(2,1)S(1)} %copy.47.skip_ref, bf16[6,16,256]{2,1,0:T(8,128)(2,1)S(1)} %pad.24.edge_ref, bf16[9,3,768,256]{3,2,1,0:T(8,128)(2,1)S(1)} %bitcast.26), custom_call_target="tpu_custom_call" | custom-call | tf_op jit(solution)/shard_map/decode/pallas_call | solution.py:373
  (84 shorter events, 11.5 us)
Async XLA Ops:
  1.9 18.6 %collective-permute-start = (bf16[3,16,16,128]{3,1,0,2:T(8,128)(2,1)}, bf16[3,16,16,128]{3,1,0,2:T(8,128)(2,1)S(1)}, u32[]{:S(2)}, u32[]{:S(2)}) collective-permute-start(bf16[3,16,16,128]{3,1,0,2:T(8,128)(2,1)} %get-tuple-element.39), channel_id=1, source_target_pairs={{0,16},{16,0},{32,48},{48,32},{64,80},{80,64},{96,112},{112,96},{1... | collective-permute-start | bytes 589832 | tf_op jit(solution)/shard_map/ppermute | solution.py:16
  5.0 15.5 %collective-permute-start.1 = (bf16[3,16,16,128]{3,1,0,2:T(8,128)(2,1)}, bf16[3,16,16,128]{3,1,0,2:T(8,128)(2,1)}, u32[]{:S(2)}, u32[]{:S(2)}) collective-permute-start(bf16[3,16,16,128]{3,1,0,2:T(8,128)(2,1)} %get-tuple-element.38), channel_id=1, source_target_pairs={{0,112},{16,32},{32,16},{48,64},{64,48},{80,96},{96,80},{112,0},{1... | collective-permute-start | bytes 589832 | tf_op jit(solution)/shard_map/ppermute | solution.py:17
  14.0 2.5 %copy-start.14 = (bf16[3,3,3,128,128]{4,3,2,1,0:T(8,128)(2,1)S(1)}, bf16[3,3,3,128,128]{4,3,2,1,0:T(8,128)(2,1)}, u32[]{:S(2)}) copy-start(bf16[3,3,3,128,128]{4,3,2,1,0:T(8,128)(2,1)} %param.7) | copy-start | bytes 2654212
  18.2 2.2 %copy-start.17 = (bf16[8,16,1,128]{3,2,1,0:T(2,128)(2,1)S(1)}, bf16[8,16,1,128]{3,2,1,0:T(2,128)(2,1)}, u32[]{:S(2)}) copy-start(bf16[8,16,1,128]{3,2,1,0:T(2,128)(2,1)} %get-tuple-element.26) | copy-start | bytes 98308
  18.2 2.2 %copy-start.18 = (bf16[8,16,1,128]{3,2,1,0:T(2,128)(2,1)S(1)}, bf16[8,16,1,128]{3,2,1,0:T(2,128)(2,1)}, u32[]{:S(2)}) copy-start(bf16[8,16,1,128]{3,2,1,0:T(2,128)(2,1)} %get-tuple-element.27) | copy-start | bytes 98308
  18.2 9.8 %copy-start.16 = (bf16[8,3,16,128]{3,2,1,0:T(8,128)(2,1)S(1)}, bf16[8,3,16,128]{3,2,1,0:T(8,128)(2,1)}, u32[]{:S(2)}) copy-start(bf16[8,3,16,128]{3,2,1,0:T(8,128)(2,1)} %get-tuple-element.29) | copy-start | bytes 294916
  20.3 10.8 %copy-start.15 = (bf16[3,3,3,256,64]{3,4,2,1,0:T(8,128)(2,1)S(1)}, bf16[3,3,3,256,64]{3,4,2,1,0:T(8,128)(2,1)}, u32[]{:S(2)}) copy-start(bf16[3,3,3,256,64]{3,4,2,1,0:T(8,128)(2,1)} %param.9) | copy-start | bytes 2654212
  20.4 20.7 %copy-start.8 = (s32[5]{0:T(128)}, s32[5]{0:T(128)S(1)}, u32[]{:S(2)}) copy-start(s32[5]{0:T(128)S(1)} %pad_add_fusion.place_ref) | copy-start | bytes 64
  22.3 14.8 %collective-permute-start.6 = (bf16[14,16,128]{2,1,0:T(8,128)(2,1)}, bf16[14,16,128]{2,1,0:T(8,128)(2,1)}, u32[]{:S(2)}, u32[]{:S(2)}) collective-permute-start(bf16[14,16,128]{2,1,0:T(8,128)(2,1)} %pad_maximum_fusion.5), channel_id=1, source_target_pairs={{0,1},{1,0},{2,3},{3,2},{4,5},{5,4},{6,7},{7,6},{8,9},{9,8},{10,11... | collective-permute-start | bytes 172040 | tf_op jit(solution)/shard_map/ppermute | solution.py:419
  25.2 11.1 %collective-permute-start.4 = (bf16[14,3,128]{2,1,0:T(4,128)(2,1)}, bf16[14,3,128]{2,1,0:T(4,128)(2,1)}, u32[]{:S(2)}, u32[]{:S(2)}) collective-permute-start(bf16[14,3,128]{2,1,0:T(4,128)(2,1)} %get-tuple-element.54), channel_id=1, source_target_pairs={{0,15},{1,14},{2,5},{3,4},{4,3},{5,2},{6,9},{7,8},{8,7},{9,6},{10,... | collective-permute-start | bytes 32264 | tf_op jit(solution)/shard_map/ppermute | solution.py:17
  26.8 9.5 %collective-permute-start.5 = (bf16[14,3,128]{2,1,0:T(4,128)(2,1)}, bf16[14,3,128]{2,1,0:T(4,128)(2,1)}, u32[]{:S(2)}, u32[]{:S(2)}) collective-permute-start(bf16[14,3,128]{2,1,0:T(4,128)(2,1)} %get-tuple-element.55), channel_id=1, source_target_pairs={{0,3},{1,2},{2,1},{3,0},{4,7},{5,6},{6,5},{7,4},{8,11},{9,10},{10,... | collective-permute-start | bytes 32264 | tf_op jit(solution)/shard_map/ppermute | solution.py:16
  32.8 8.4 %copy-start.1 = (bf16[4,3,3,128,256]{4,3,2,1,0:T(8,128)(2,1)S(1)}, bf16[4,3,3,128,256]{4,3,2,1,0:T(8,128)(2,1)}, u32[]{:S(2)}) copy-start(bf16[4,3,3,128,256]{4,3,2,1,0:T(8,128)(2,1)} %fusion.2.weights_ref) | copy-start | bytes 7077892
  34.4 3.5 %collective-permute-start.2 = (bf16[14,3,16,128]{3,2,1,0:T(8,128)(2,1)}, bf16[14,3,16,128]{3,2,1,0:T(8,128)(2,1)S(1)}, u32[]{:S(2)}, u32[]{:S(2)}) collective-permute-start(bf16[14,3,16,128]{3,2,1,0:T(8,128)(2,1)} %get-tuple-element.41), channel_id=1, source_target_pairs={{0,2},{2,0},{4,6},{6,4},{8,10},{10,8},{12,14},{14,12},{1,3},{3,1},... | collective-permute-start | bytes 516104 | tf_op jit(solution)/shard_map/ppermute | solution.py:16
  34.9 6.3 %collective-permute-start.3 = (bf16[14,3,16,128]{3,2,1,0:T(8,128)(2,1)}, bf16[14,3,16,128]{3,2,1,0:T(8,128)(2,1)S(1)}, u32[]{:S(2)}, u32[]{:S(2)}) collective-permute-start(bf16[14,3,16,128]{3,2,1,0:T(8,128)(2,1)} %get-tuple-element.40), channel_id=1, source_target_pairs={{0,14},{2,4},{4,2},{6,8},{8,6},{10,12},{12,10},{14,0},{1,15},{3,5}... | collective-permute-start | bytes 516104 | tf_op jit(solution)/shard_map/ppermute | solution.py:17
  41.2 1.0 copy-start.2
  42.2 0.9 copy-start.5
  43.2 0.9 copy-start.6
  44.1 10.0 %copy-start.3 = (bf16[3,3,3,128,256]{4,3,2,1,0:T(8,128)(2,1)S(1)}, bf16[3,3,3,128,256]{4,3,2,1,0:T(8,128)(2,1)}, u32[]{:S(2)}) copy-start(bf16[3,3,3,128,256]{4,3,2,1,0:T(8,128)(2,1)} %param.8) | copy-start | bytes 5308420
  50.1 3.9 %collective-permute-start.7 = (bf16[6,10,128]{2,1,0:T(8,128)(2,1)S(1)}, bf16[6,10,128]{2,1,0:T(8,128)(2,1)S(1)}, u32[]{:S(2)}, u32[]{:S(2)}) collective-permute-start(bf16[6,10,128]{2,1,0:T(8,128)(2,1)S(1)} %fusion.5), channel_id=1, source_target_pairs={{0,1},{1,0},{2,3},{3,2},{4,5},{5,4},{6,7},{7,6},{8,9},{9,8},{10,11... | collective-permute-start | bytes 46088 | tf_op jit(solution)/shard_map/ppermute | solution.py:404
  54.1 0.7 copy-start.9
  56.1 0.7 copy-start.7
  57.4 4.6 %collective-permute-start.8 = (bf16[2,4,1,256]{3,1,0,2:T(4,128)(2,1)}, bf16[2,4,1,256]{3,1,0,2:T(4,128)(2,1)}, u32[]{:S(2)}, u32[]{:S(2)}) collective-permute-start(bf16[2,4,1,256]{3,1,0,2:T(4,128)(2,1)} %get-tuple-element.62), channel_id=1, source_target_pairs={{0,14},{2,4},{4,2},{6,8},{8,6},{10,12},{12,10},{14,0},{1,15},{3,5}... | collective-permute-start | bytes 12296 | tf_op jit(solution)/shard_map/ppermute | solution.py:17
  57.6 4.4 %collective-permute-start.9 = (bf16[2,4,1,256]{3,1,0,2:T(4,128)(2,1)}, bf16[2,4,1,256]{3,1,0,2:T(4,128)(2,1)}, u32[]{:S(2)}, u32[]{:S(2)}) collective-permute-start(bf16[2,4,1,256]{3,1,0,2:T(4,128)(2,1)} %get-tuple-element.63), channel_id=1, source_target_pairs={{0,2},{2,0},{4,6},{6,4},{8,10},{10,8},{12,14},{14,12},{1,3},{3,1},... | collective-permute-start | bytes 12296 | tf_op jit(solution)/shard_map/ppermute | solution.py:16
  63.5 14.9 %all-to-all-start = ((bf16[16,2,24,256]{3,2,1,0:T(8,128)(2,1)}), bf16[16,2,24,256]{3,2,1,0:T(8,128)(2,1)}, u32[]{:S(2)}, u32[]{:S(2)}) async-start(bf16[16,2,24,256]{3,2,1,0:T(8,128)(2,1)} %broadcast_in_dim.19), calls=%async_computation | async-start | bytes 786432 | tf_op jit(solution)/shard_map/all_to_all | solution.py:431
  69.5 0.7 copy-start.12
  70.8 15.1 %collective-permute-start.12 = (bf16[1,8,8,256]{3,1,0,2:T(8,128)(2,1)}, bf16[1,8,8,256]{3,1,0,2:T(8,128)(2,1)}, u32[]{:S(2)}, u32[]{:S(2)}) collective-permute-start(bf16[1,8,8,256]{3,1,0,2:T(8,128)(2,1)} %get-tuple-element.46), channel_id=1, source_target_pairs={{0,112},{16,32},{32,16},{48,64},{64,48},{80,96},{96,80},{112,0},{1... | collective-permute-start | bytes 98312 | tf_op jit(solution)/shard_map/ppermute | solution.py:17
  76.3 9.6 %collective-permute-start.13 = (bf16[1,8,8,256]{3,1,0,2:T(8,128)(2,1)}, bf16[1,8,8,256]{3,1,0,2:T(8,128)(2,1)}, u32[]{:S(2)}, u32[]{:S(2)}) collective-permute-start(bf16[1,8,8,256]{3,1,0,2:T(8,128)(2,1)} %get-tuple-element.47), channel_id=1, source_target_pairs={{0,16},{16,0},{32,48},{48,32},{64,80},{80,64},{96,112},{112,96},{1... | collective-permute-start | bytes 98312 | tf_op jit(solution)/shard_map/ppermute | solution.py:16
  78.3 0.7 copy-start.10
  81.5 0.8 copy-start.4
  82.2 13.8 %copy-start.13 = (bf16[4,8,8,256]{3,1,0,2:T(8,128)(2,1)S(1)}, bf16[4,8,8,256]{3,1,0,2:T(8,128)(2,1)}, u32[]{:S(2)}) copy-start(bf16[4,8,8,256]{3,1,0,2:T(8,128)(2,1)} %copy-done.12) | copy-start | bytes 393220
  82.2 13.0 %all-to-all-start.1 = ((bf16[8,8,6,4,128]{4,3,2,1,0:T(4,128)(2,1)}), bf16[8,8,6,4,128]{4,3,2,1,0:T(4,128)(2,1)S(1)}, u32[]{:S(2)}, u32[]{:S(2)}) async-start(bf16[8,8,6,4,128]{4,3,2,1,0:T(4,128)(2,1)} %copy-done.4), calls=%async_computation.1 | async-start | bytes 786432 | tf_op jit(solution)/shard_map/all_to_all | solution.py:433
  85.8 17.3 %copy-start.11 = (s32[5]{0:T(128)S(1)}, s32[5]{0:T(128)}, u32[]{:S(2)}) copy-start(s32[5]{0:T(128)} %copy-done.8) | copy-start | bytes 64
  87.8 8.1 %collective-permute-start.15 = (bf16[6,1,8,256]{3,1,0,2:T(2,128)(2,1)S(1)}, bf16[6,1,8,256]{3,1,0,2:T(2,128)(2,1)S(1)}, u32[]{:S(2)}, u32[]{:S(2)}) collective-permute-start(bf16[6,1,8,256]{3,1,0,2:T(2,128)(2,1)S(1)} %broadcast_select_fusion.15), channel_id=1, source_target_pairs={{0,2},{2,0},{4,6},{6,4},{8,10},{10,8},{12,14},{14,12},{1,3},{3,1},... | collective-permute-start | bytes 73736 | tf_op jit(solution)/shard_map/ppermute | solution.py:16
  87.9 8.0 %collective-permute-start.14 = (bf16[6,1,8,256]{3,1,0,2:T(2,128)(2,1)S(1)}, bf16[6,1,8,256]{3,1,0,2:T(2,128)(2,1)S(1)}, u32[]{:S(2)}, u32[]{:S(2)}) collective-permute-start(bf16[6,1,8,256]{3,1,0,2:T(2,128)(2,1)S(1)} %get-tuple-element.23), channel_id=1, source_target_pairs={{0,14},{2,4},{4,2},{6,8},{8,6},{10,12},{12,10},{14,0},{1,15},{3,5}... | collective-permute-start | bytes 73736 | tf_op jit(solution)/shard_map/ppermute | solution.py:17
  95.7 6.4 %collective-permute-start.10 = (bf16[8,8,6,2,128]{4,3,2,1,0:T(2,128)(2,1)S(1)}, bf16[8,8,6,2,128]{4,3,2,1,0:T(2,128)(2,1)S(1)}, u32[]{:S(2)}, u32[]{:S(2)}) collective-permute-start(bf16[8,8,6,2,128]{4,3,2,1,0:T(2,128)(2,1)S(1)} %get-tuple-element.34), channel_id=1, source_target_pairs={{0,14},{2,4},{4,2},{6,8},{8,6},{10,12},{12,10},{14,0},{1,15},{3,5}... | collective-permute-start | bytes 589832 | tf_op jit(solution)/shard_map/ppermute | solution.py:17
  95.8 6.3 %collective-permute-start.11 = (bf16[8,8,6,2,128]{4,3,2,1,0:T(2,128)(2,1)S(1)}, bf16[8,8,6,2,128]{4,3,2,1,0:T(2,128)(2,1)S(1)}, u32[]{:S(2)}, u32[]{:S(2)}) collective-permute-start(bf16[8,8,6,2,128]{4,3,2,1,0:T(2,128)(2,1)S(1)} %get-tuple-element.35), channel_id=1, source_target_pairs={{0,2},{2,0},{4,6},{6,4},{8,10},{10,8},{12,14},{14,12},{1,3},{3,1},... | collective-permute-start | bytes 589832 | tf_op jit(solution)/shard_map/ppermute | solution.py:16
  106.6 11.8 %all-to-all-start.2 = ((bf16[8,2,6,8,128]{4,3,2,1,0:T(8,128)(2,1)}), bf16[8,2,6,8,128]{4,3,2,1,0:T(8,128)(2,1)S(1)}, u32[]{:S(2)}, u32[]{:S(2)}) async-start(bf16[8,2,6,8,128]{4,3,2,1,0:T(8,128)(2,1)} %bottom_out.1), calls=%async_computation.2 | async-start | bytes 393216 | tf_op jit(solution)/shard_map/all_to_all | solution.py:436
  110.0 4.2 %collective-permute-start.16 = (bf16[6,10,256]{2,1,0:T(8,128)(2,1)S(1)}, bf16[6,10,256]{2,1,0:T(8,128)(2,1)S(1)}, u32[]{:S(2)}, u32[]{:S(2)}) collective-permute-start(bf16[6,10,256]{2,1,0:T(8,128)(2,1)S(1)} %fusion.3), channel_id=1, source_target_pairs={{0,1},{1,0},{2,3},{3,2},{4,5},{5,4},{6,7},{7,6},{8,9},{9,8},{10,11... | collective-permute-start | bytes 92168 | tf_op jit(solution)/shard_map/ppermute | solution.py:404
  118.4 4.0 %copy-start = (bf16[3,3,3,768,256]{4,3,2,1,0:T(8,128)(2,1)S(1)}, bf16[3,3,3,768,256]{4,3,2,1,0:T(8,128)(2,1)}, u32[]{:S(2)}) copy-start(bf16[3,3,3,768,256]{4,3,2,1,0:T(8,128)(2,1)} %param.11) | copy-start | bytes 31850500

commit v5 on v4

--- a/solution.py
+++ b/solution.py
@@ -6,16 +6,15 @@
 from jax.sharding import PartitionSpec as P
 
 
-def swaps(low, high, axis, count):
-    both = isinstance(axis, tuple)
-    even = lax.axis_index(axis[0] if both else axis) % 2 == 0
+def send(inner_block, outer_block, axis, count):
     inner = [(i, i ^ 1) for i in range(count)]
     outer = [(i, (((i + 1) ^ 1) - 1) % count) for i in range(count)]
-    if both:
-        inner, outer = [[(2 * i + n, 2 * j + 1 - n) for i, j in pairs for n in range(2)] for pairs in (inner, outer)]
-    got_in = lax.ppermute(jnp.where(even, high, low), axis, inner)
-    got_out = lax.ppermute(jnp.where(even, low, high), axis, outer)
-    return got_in, got_out
+    return lax.ppermute(inner_block, axis, inner), lax.ppermute(outer_block, axis, outer)
+
+
+def swaps(low, high, axis, count):
+    even = lax.axis_index(axis) % 2 == 0
+    return send(jnp.where(even, high, low), jnp.where(even, low, high), axis, count)
 
 
 def ordered(got_in, got_out, axis):
@@ -186,9 +185,114 @@
     )(place, own, x_in, x_out, y_in, y_out, edge, weights)
 
 
-def paired(weights):
-    grow = [(0, 0)] * 4
-    return jnp.concatenate([jnp.pad(weights, [(0, 1)] + grow), jnp.pad(weights, [(1, 0)] + grow)], axis=4)
+def prepare(w_full, w_bottom_in, w_bottom_out):
+    channels, filters = w_full.shape[3:]
+
+    def body(full_ref, in_ref, out_ref, pair_ref, beside_in_ref, beside_out_ref):
+        zero = jnp.zeros((3, 3, channels, filters), jnp.bfloat16)
+        for plane in range(4):
+            pair_ref[plane, :, :, :, :filters] = full_ref[plane] if plane < 3 else zero
+            pair_ref[plane, :, :, :, filters:] = full_ref[plane - 1] if plane > 0 else zero
+        for ref, to in ((in_ref, beside_in_ref), (out_ref, beside_out_ref)):
+            depth = ref.shape[3]
+            gap = jnp.zeros((depth, 64), jnp.float32)
+            for dx in range(3):
+                for dz in range(3):
+                    first, second, third = [ref[dx, dy, dz].astype(jnp.float32) for dy in range(3)]
+                    to[3 * dx + dz, :, :128] = jnp.concatenate([first, second], axis=1).astype(jnp.bfloat16)
+                    to[3 * dx + dz, :, 128:] = jnp.concatenate([third, gap], axis=1).astype(jnp.bfloat16)
+
+    return pl.pallas_call(
+        body,
+        in_specs=[pl.BlockSpec(memory_space=pltpu.VMEM)] * 3,
+        out_specs=[pl.BlockSpec(memory_space=pltpu.VMEM)] * 3,
+        out_shape=[jax.ShapeDtypeStruct((4, 3, 3, channels, 2 * filters), jnp.bfloat16)]
+        + [jax.ShapeDtypeStruct((9, w.shape[3], 256), jnp.bfloat16) for w in (w_bottom_in, w_bottom_out)],
+        compiler_params=pltpu.CompilerParams(vmem_limit_bytes=8 << 20),
+        name="prepare",
+    )(w_full, w_bottom_in, w_bottom_out)
+
+
+def pack_y(place, own, x_in, x_out):
+    own_x, own_y, size_z, channels = own.shape
+    reach = x_in.shape[0]
+    full_x = own_x + 2 * reach
+
+    def body(place_ref, own_ref, x_in_ref, x_out_ref, inner_ref, outer_ref, plane_ref, rows_ref):
+        even_x, even_y, first = place_ref[0] % 2 == 0, place_ref[1] % 2 == 0, place_ref[2] == 0
+        below = jnp.where(even_x, x_out_ref[...], x_in_ref[...])
+        above = jnp.where(even_x, x_in_ref[...], x_out_ref[...])
+        for start, block in ((0, below), (reach, own_ref[...]), (reach + own_x, above)):
+            size = block.shape[0]
+            low, high = block[:, :reach], block[:, own_y - reach :]
+            inner_ref[start : start + size] = jnp.where(even_y, high, low)
+            outer_ref[start : start + size] = jnp.where(even_y, low, high)
+            block = block.astype(jnp.float32)
+            edge = jnp.where(first, block[:, :, size_z - 1 :], block[:, :, :1])
+            for x in range(size):
+                for y in range(own_y):
+                    rows_ref[start + x, y : y + 1] = edge[x, y]
+        plane_ref[...] = rows_ref[...].astype(plane_ref.dtype)
+
+    return pl.pallas_call(
+        body,
+        in_specs=[pl.BlockSpec(memory_space=pltpu.SMEM)] + [pl.BlockSpec(memory_space=pltpu.VMEM)] * 3,
+        out_specs=[pl.BlockSpec(memory_space=pltpu.VMEM)] * 3,
+        out_shape=[jax.ShapeDtypeStruct((full_x, reach, size_z, channels), jnp.bfloat16)] * 2
+        + [jax.ShapeDtypeStruct((full_x, own_y, channels), jnp.bfloat16)],
+        scratch_shapes=[pltpu.VMEM((full_x, own_y, channels), jnp.float32)],
+        compiler_params=pltpu.CompilerParams(vmem_limit_bytes=8 << 20),
+        name="pack_y",
+    )(place, own, x_in, x_out)
+
+
+def pack_z(place, plane, y_in, y_out):
+    full_x, own_y, channels = plane.shape
+    reach, size_z = y_in.shape[1:3]
+    full_y = own_y + 2 * reach
+
+    def body(place_ref, plane_ref, y_in_ref, y_out_ref, out_ref, rows_ref):
+        even_y, first = place_ref[1] % 2 == 0, place_ref[2] == 0
+        rows_ref[:, reach : reach + own_y] = plane_ref[...].astype(jnp.float32)
+        edges = []
+        for ref in (y_in_ref, y_out_ref):
+            block = ref[...].astype(jnp.float32)
+            edges.append(jnp.where(first, block[:, :, size_z - 1 :], block[:, :, :1]))
+        below, above = jnp.where(even_y, edges[1], edges[0]), jnp.where(even_y, edges[0], edges[1])
+        for x in range(full_x):
+            for y in range(reach):
+                rows_ref[x, y : y + 1] = below[x, y]
+                rows_ref[x, reach + own_y + y : reach + own_y + y + 1] = above[x, y]
+        out_ref[...] = rows_ref[...].astype(out_ref.dtype)
+
+    return pl.pallas_call(
+        body,
+        in_specs=[pl.BlockSpec(memory_space=pltpu.SMEM)] + [pl.BlockSpec(memory_space=pltpu.VMEM)] * 3,
+        out_specs=pl.BlockSpec(memory_space=pltpu.VMEM),
+        out_shape=jax.ShapeDtypeStruct((full_x, full_y, channels), jnp.bfloat16),
+        scratch_shapes=[pltpu.VMEM((full_x, full_y, channels), jnp.float32)],
+        compiler_params=pltpu.CompilerParams(vmem_limit_bytes=8 << 20),
+        name="pack_z",
+    )(place, plane, y_in, y_out)
+
+
+def fetch(weights, after):
+    def body(weights_ref, after_ref, out_ref, sems):
+        copies = [pltpu.make_async_copy(weights_ref.at[i], out_ref.at[i], sems.at[i]) for i in range(9)]
+        for copy in copies:
+            copy.start()
+        for copy in copies:
+            copy.wait()
+
+    return pl.pallas_call(
+        body,
+        in_specs=[pl.BlockSpec(memory_space=pltpu.HBM)] * 2,
+        out_specs=pl.BlockSpec(memory_space=pltpu.VMEM),
+        out_shape=jax.ShapeDtypeStruct(weights.shape, weights.dtype),
+        scratch_shapes=[pltpu.SemaphoreType.DMA((9,))],
+        compiler_params=pltpu.CompilerParams(vmem_limit_bytes=12 << 20),
+        name="fetch",
+    )(weights, after)
 
 
 def halves(pair_low, pair_high):
@@ -264,12 +368,14 @@
     )(place, field, weights)
 
 
-def bottom_out(place, field, weights):
+def bottom_out(place, field, y_in, y_out, weights):
     devices, pairs, size_z, _, _ = field.shape
     size_x, channels = 2 * pairs, 64 * devices
     own_x = size_x // devices
 
-    def body(place_ref, field_ref, weights_ref, out_ref, pad_ref, total_ref):
+    def body(place_ref, field_ref, y_in_ref, y_out_ref, weights_ref, out_ref, pad_ref, total_ref):
+        even_y = place_ref[1] % 2 == 0
+        low_y, high_y = place_ref[1] > 0, place_ref[1] < place_ref[4]
         zero = jnp.zeros((size_z + 2, 8, channels), jnp.float32)
         for ref in (pad_ref, total_ref):
             wide = ref.shape[-1]
@@ -280,10 +386,18 @@
                 ref[x + 1, size_z + 1] = zero[0, :, :wide]
         for k in range(devices // 2):
             for pair in range(pairs):
-                low, high = [field_ref[2 * k + i, pair].astype(jnp.float32) for i in range(2)]
-                even, odd = halves(low, high)
-                pad_ref[1 + 2 * pair, 1 : size_z + 1, :, 128 * k : 128 * k + 128] = even
-                pad_ref[2 + 2 * pair, 1 : size_z + 1, :, 128 * k : 128 * k + 128] = odd
+                y_first, y_last = [], []
+                for i in range(2):
+                    one = y_in_ref[2 * k + i, pair].astype(jnp.float32)
+                    other = y_out_ref[2 * k + i, pair].astype(jnp.float32)
+                    y_first.append(jnp.where(low_y, jnp.where(even_y, other, one), 0.0))
+                    y_last.append(jnp.where(high_y, jnp.where(even_y, one, other), 0.0))
+                own = [field_ref[2 * k + i, pair].astype(jnp.float32) for i in range(2)]
+                for line, blocks in ((0, y_first), (2, own), (6, y_last)):
+                    even, odd = halves(*blocks)
+                    lines = slice(line, line + even.shape[1])
+                    pad_ref[1 + 2 * pair, 1 : size_z + 1, lines, 128 * k : 128 * k + 128] = even
+                    pad_ref[2 + 2 * pair, 1 : size_z + 1, lines, 128 * k : 128 * k + 128] = odd
         for first in range(0, size_x, 4):
             total = column_product(pad_ref, weights_ref, first, 0, 4, size_z)
             total_ref[1 + first : 5 + first, 1 : size_z + 1] = total
@@ -298,7 +412,7 @@
 
     return pl.pallas_call(
         body,
-        in_specs=[pl.BlockSpec(memory_space=pltpu.SMEM)] + [pl.BlockSpec(memory_space=pltpu.VMEM)] * 2,
+        in_specs=[pl.BlockSpec(memory_space=pltpu.SMEM)] + [pl.BlockSpec(memory_space=pltpu.VMEM)] * 4,
         out_specs=pl.BlockSpec(memory_space=pltpu.VMEM),
         out_shape=jax.ShapeDtypeStruct((devices, own_x, size_z, 8, 128), jnp.bfloat16),
         scratch_shapes=[
@@ -307,7 +421,7 @@
         ],
         compiler_params=pltpu.CompilerParams(vmem_limit_bytes=16 << 20),
         name="bottom_out",
-    )(place, field, weights)
+    )(place, field, y_in, y_out, weights)
 
 
 def decode(place, bottom, skip, edge, weights):
@@ -317,7 +431,6 @@
     channels = 64 * devices + skip_channels
     filters = weights.shape[-1]
     rows, extra = size_x * size_y * size_z, size_x * size_y
-    weights = weights.reshape(9, 3, channels, filters)
 
     def body(place_ref, bottom_ref, skip_ref, edge_ref, weights_ref, out_ref, main_ref, side_ref, sums_ref):
         first = place_ref[2] == 0
@@ -386,12 +499,6 @@
     )(place, bottom, skip, edge, weights)
 
 
-def beside(weights):
-    channels, filters = weights.shape[3:]
-    weights = weights.transpose(0, 2, 3, 1, 4).reshape(9, channels, 3 * filters)
-    return jnp.pad(weights, ((0, 0), (0, 0), (0, 256 - 3 * filters)))
-
-
 def solution(mesh):
     gx, gy, gz = mesh.shape["gx"], mesh.shape["gy"], mesh.shape["gz"]
 
@@ -404,22 +511,11 @@
             return lax.ppermute(jnp.where(place_z == 0, plane_high, plane_low), "gz", swap)
 
         x_in, x_out = swaps(volume[:3], volume[-3:], "gx", gx)
-        w_pair, w_out = paired(w_full), beside(w_bottom_out)
-        x_in, x_out, w_pair, w_out, w_bottom_in = lax.optimization_barrier((x_in, x_out, w_pair, w_out, w_bottom_in))
-        below, above = ordered(x_in, x_out, "gx")
-        y_low = jnp.concatenate([below[:, :3], volume[:, :3], above[:, :3]], axis=0)
-        y_high = jnp.concatenate([below[:, -3:], volume[:, -3:], above[:, -3:]], axis=0)
-        y_in, y_out = swaps(y_low, y_high, "gy", gy)
-
-        def outer_plane(block):
-            return jnp.where(place_z == 0, block[:, :, -1], block[:, :, 0])
-
-        edge = jnp.concatenate([outer_plane(below), outer_plane(volume), outer_plane(above)], axis=0)
-        edge_in, edge_out = swaps(edge[:, :3], edge[:, -3:], ("gy", "gz"), gy)
-        edge = lax.ppermute(edge, "gz", swap)
-        edge_low, edge_high = ordered(edge_in, edge_out, "gy")
-        edge = jnp.concatenate([edge_low, edge, edge_high], axis=1)
-        edge, w_in = lax.optimization_barrier((edge, beside(w_bottom_in)))
+        weights = prepare(w_full, w_bottom_in, w_bottom_out)
+        (w_pair, w_in, w_out), x_in, x_out = lax.optimization_barrier((weights, x_in, x_out))
+        y_inner, y_outer, plane = pack_y(place, volume, x_in, x_out)
+        y_in, y_out = send(y_inner, y_outer, "gy", gy)
+        edge = lax.ppermute(pack_z(place, plane, y_in, y_out), "gz", swap)
         pooled = encode(place, volume, x_in, x_out, y_in, y_out, edge, w_pair)
 
         edge = edge_of(pooled[:, :, 0], pooled[:, :, -1])
@@ -431,8 +527,9 @@
         column = lax.all_to_all(column, ("gx", "gz"), 0, 0)
         first = bottom_in(place, column, w_in)
         first = lax.all_to_all(first, "gx", 0, 0)
-        first = extend(first, "gy", gy, 3, 2)
-        second = bottom_out(place, first, w_out)
+        y_in, y_out = swaps(first[:, :, :, :2], first[:, :, :, -2:], "gy", gy)
+        second = bottom_out(place, first, y_in, y_out, w_out)
+        w_up = fetch(w_up.reshape(9, 3, w_up.shape[3], w_up.shape[4]), second)
         second = lax.all_to_all(second, "gx", 0, 0)
 
         around = extend(skip, "gx", gx, 0, 1)

time: 128 us -> 127 us (level)
  other arithmetic: 14 us -> 2.95 us
  Pallas kernels: 18 us -> 25.3 us
  starting transfers between devices: 34 us -> 36.8 us
  waiting for transfers between devices: 32.1 us -> 30.6 us
    unnamed x39 -> x30, local copies, waits for them, and re-layouts: 12 us -> 28.6 us
    pallas_call x0 -> x4, Pallas kernels: none -> 5.67 us  [the longest x1 2.25 us: fetch(): pl.pallas_call(body, in_specs=[pl.BlockSpec(memory_space=pltpu.HBM)] * 2,...]
    select_n x12 -> x6, other arithmetic: 7.73 us -> 2.46 us  [the longest x5 2.38 us: swaps(): jnp.where(even, low, high)]
    slice x8 -> x0, local copies, waits for them, and re-layouts: 4.54 us -> none  [the longest x1 1.79 us: outer_plane(): return jnp.where(place_z == 0, block[:, :, -1], block[:, :, 0])]
    all_to_all x1, waiting for transfers between devices: 4.19 us -> 0.01 us  [local(): second = lax.all_to_all(second, 'gx', 0, 0)]
    reshape x2 -> x0, local copies, waits for them, and re-layouts: 3.96 us -> none  [beside(): weights = weights.transpose(0, 2, 3, 1, 4).reshape(9, channels, 3 * filters)]
    pad x2 -> x0, local copies, waits for them, and re-layouts: 3.73 us -> none  [beside(): return jnp.pad(weights, ((0, 0), (0, 0), (0, 256 - 3 * filters)))]
    concatenate x3 -> x0, other arithmetic: 3.22 us -> none  [the longest x1 1.74 us: paired(): jnp.concatenate([jnp.pad(weights, [(0, 1)] + grow), jnp.pad(weights, [(1,...]
  transfers between devices with their start and end apart: 20 -> 18, of which waited for: 8 -> 8; matrix products, arithmetic and copies ran while one was open for 20% -> 6% of each run, Pallas kernels for 2% -> 5%
where the time goes in v5:
time: 127 us; the launch traced here: 125 us
  starting transfers between devices  36.8 us (29%)
  waiting for transfers between devices  30.6 us (24%)
  local copies, waits for them, and re-layouts  29.6 us (23%)
  Pallas kernels  25.3 us (20%)
  other arithmetic  2.95 us (2%)
    unnamed x30, local copies, waits for them, and re-layouts  28.6 us
    ppermute x6, starting transfers between devices, send(): lax.ppermute(outer_block, axis, outer)  17.2 us
    ppermute x6, waiting for transfers between devices, send(): lax.ppermute(outer_block, axis, outer)  9.72 us
    all_to_all x1, waiting for transfers between devices, local(): first = lax.all_to_all(first, 'gx', 0, 0)  8.1 us
    pallas_call x1, Pallas kernels, encode(): pl.pallas_call(body, in_specs=[pl.BlockSpec(memory_space=pltpu.SMEM)] + [...  6.59 us
    ppermute x2, waiting for transfers between devices, edge_of(): lax.ppermute(jnp.where(place_z == 0, plane_high, plane_low), 'gz', swap)  5.79 us
    all_to_all x1, starting transfers between devices, local(): column = lax.all_to_all(column, ('gx', 'gz'), 0, 0)  5.31 us
    pallas_call x1, Pallas kernels, decode(): pl.pallas_call(body, in_specs=[pl.BlockSpec(memory_space=pltpu.SMEM)] + [...  4.76 us
  transfers between devices with their start and end apart: 18, of which 8 were waited for; matrix products, arithmetic and copies ran while one was open for 6% of the time, Pallas kernels for 5%

profile of v5, /device:TPU:0, one launch (start us, length us, event | category | flops | bytes accessed | tf_op | source)
XLA Modules:
  0.0 125.5 jit_solution(1747482787921528182)
XLA Ops:
  0.0 1.8 %broadcast_select_fusion.2 = (bf16[3,16,16,128]{3,2,1,0:T(8,128)(2,1)}, bf16[3,16,16,128]{3,2,1,0:T(8,128)(2,1)}) fusion(pred[]{:T(512)S(6)} %eq.25, bf16[8,16,16,128]{3,2,1,0:T(8,128)(2,1)} %own_ref.3), kind=kLoop, calls=%fused_computation.3 | loop fusion | flops 196608 | bytes 786433 | tf_op jit(solution)/shard_map/jit(_where)/select_n | solution.py:17
  1.8 3.1 %collective-permute-start = (bf16[3,16,16,128]{3,2,1,0:T(8,128)(2,1)}, bf16[3,16,16,128]{3,2,1,0:T(8,128)(2,1)}, u32[]{:S(2)}, u32[]{:S(2)}) collective-permute-start(bf16[3,16,16,128]{3,2,1,0:T(8,128)(2,1)} %get-tuple-element.35), channel_id=1, source_target_pairs={{0,16},{16,0},{32,48},{48,32},{64,80},{80,64},{96,112},{112,96},{1... | collective-permute-start | bytes 589832 | tf_op jit(solution)/shard_map/ppermute | solution.py:12
  4.9 4.0 %collective-permute-start.1 = (bf16[3,16,16,128]{3,2,1,0:T(8,128)(2,1)}, bf16[3,16,16,128]{3,2,1,0:T(8,128)(2,1)}, u32[]{:S(2)}, u32[]{:S(2)}) collective-permute-start(bf16[3,16,16,128]{3,2,1,0:T(8,128)(2,1)} %get-tuple-element.34), channel_id=1, source_target_pairs={{0,112},{16,32},{32,16},{48,64},{64,48},{80,96},{96,80},{112,0},{1... | collective-permute-start | bytes 589832 | tf_op jit(solution)/shard_map/ppermute | solution.py:12
  8.9 2.6 %copy.15.in_ref = bf16[3,3,3,256,64]{4,3,2,1,0:T(8,128)(2,1)} copy(bf16[3,3,3,256,64]{3,4,2,1,0:T(8,128)(2,1)} %param.9) | data formatting | bytes 1769472 | tf_op args[3]
  11.5 3.4 %copy.16.out_ref = bf16[3,3,3,512,64]{4,3,2,1,0:T(8,128)(2,1)S(1)} copy(bf16[3,3,3,512,64]{3,4,2,1,0:T(8,128)(2,1)} %param.10) | data formatting | bytes 3538944 | tf_op args[4]
  14.9 1.5 %copy-done.3 = bf16[3,3,3,256,64]{4,3,2,1,0:T(8,128)(2,1)S(1)} copy-done((bf16[3,3,3,256,64]{4,3,2,1,0:T(8,128)(2,1)S(1)}, bf16[3,3,3,256,64]{4,3,2,1,0:T(8,128)(2,1)}, u32[]{:S(2)}) %copy-start.3) | copy-done | bytes 884760
  16.3 1.2 copy-done.13
  17.5 1.4 %prepare.1 = (bf16[4,3,3,128,256]{4,3,2,1,0:T(8,128)(2,1)S(1)}, bf16[9,256,256]{2,1,0:T(8,128)(2,1)S(1)}, bf16[9,512,256]{2,1,0:T(8,128)(2,1)S(1)}) custom-call(bf16[3,3,3,128,128]{4,3,2,1,0:T(8,128)(2,1)S(1)} %copy-done.13, bf16[3,3,3,256,64]{4,3,2,1,0:T(8,128)(2,1)S(1)} %copy-done.3, bf16[3,3,3,512,64]{4,3,2,1,0:T(8,128)(2,1)S(1)} %copy.16.out_ref), custom_call_target="tpu_custom_call" | custom-call | tf_op jit(solution)/shard_map/prepare/pallas_call | solution.py:205
  18.9 1.4 %copy-done.6 = bf16[9,512,256]{2,1,0:T(8,128)(2,1)} copy-done((bf16[9,512,256]{2,1,0:T(8,128)(2,1)}, bf16[9,512,256]{2,1,0:T(8,128)(2,1)S(1)}, u32[]{:S(2)}) %copy-start.6) | copy-done | bytes 2359320
  20.3 1.4 %copy-done.8 = bf16[4,3,3,128,256]{4,3,2,1,0:T(8,128)(2,1)} copy-done((bf16[4,3,3,128,256]{4,3,2,1,0:T(8,128)(2,1)}, bf16[4,3,3,128,256]{4,3,2,1,0:T(8,128)(2,1)S(1)}, u32[]{:S(2)}) %copy-start.8) | copy-done | bytes 2359320
  21.8 1.0 copy-done.11
  22.9 1.4 %pack_y.1 = (bf16[14,3,16,128]{3,2,1,0:T(8,128)(2,1)S(1)}, bf16[14,3,16,128]{3,2,1,0:T(8,128)(2,1)S(1)}, bf16[14,16,128]{2,1,0:T(8,128)(2,1)S(1)}) custom-call(s32[5]{0:T(128)S(1)} %pad_add_fusion.place_ref, bf16[8,16,16,128]{3,2,1,0:T(8,128)(2,1)S(1)} %copy-done.4, bf16[3,16,16,128]{3,2,1,0:T(8,128)(2,1)} %collective-permute-done.x_in_ref, ...), custom_call_target="tpu_custom_call" | custom-call | tf_op jit(solution)/shard_map/pack_y/pallas_call | solution.py:237
  24.4 3.1 %collective-permute-start.3 = (bf16[14,3,16,128]{3,2,1,0:T(8,128)(2,1)S(1)}, bf16[14,3,16,128]{3,2,1,0:T(8,128)(2,1)S(1)}, u32[]{:S(2)}, u32[]{:S(2)}) collective-permute-start(bf16[14,3,16,128]{3,2,1,0:T(8,128)(2,1)S(1)} %get-tuple-element.24), channel_id=1, source_target_pairs={{0,14},{2,4},{4,2},{6,8},{8,6},{10,12},{12,10},{14,0},{1,15},{3,5}... | collective-permute-start | bytes 516104 | tf_op jit(solution)/shard_map/ppermute | solution.py:12
  27.5 3.1 %collective-permute-done.3.y_out_ref = bf16[14,3,16,128]{3,2,1,0:T(8,128)(2,1)S(1)} collective-permute-done((bf16[14,3,16,128]{3,2,1,0:T(8,128)(2,1)S(1)}, bf16[14,3,16,128]{3,2,1,0:T(8,128)(2,1)S(1)}, u32[]{:S(2)}, u32[]{:S(2)}) %collective-permute-start.3) | collective-permute-done | bytes 172064 | tf_op jit(solution)/shard_map/ppermute | solution.py:12
  30.6 0.6 pack_z.1
  31.2 1.6 %collective-permute-start.4 = (bf16[14,22,128]{2,1,0:T(8,128)(2,1)S(1)}, bf16[14,22,128]{2,1,0:T(8,128)(2,1)S(1)}, u32[]{:S(2)}, u32[]{:S(2)}) collective-permute-start(bf16[14,22,128]{2,1,0:T(8,128)(2,1)S(1)} %pack_z.1), channel_id=1, source_target_pairs={{0,1},{1,0},{2,3},{3,2},{4,5},{5,4},{6,7},{7,6},{8,9},{9,8},{10,11... | collective-permute-start | bytes 236552 | tf_op jit(solution)/shard_map/ppermute | solution.py:518
  32.8 3.0 %collective-permute-done.4.edge_ref = bf16[14,22,128]{2,1,0:T(8,128)(2,1)S(1)} collective-permute-done((bf16[14,22,128]{2,1,0:T(8,128)(2,1)S(1)}, bf16[14,22,128]{2,1,0:T(8,128)(2,1)S(1)}, u32[]{:S(2)}, u32[]{:S(2)}) %collective-permute-start.4) | collective-permute-done | bytes 78880 | tf_op jit(solution)/shard_map/ppermute | solution.py:518
  35.8 1.0 copy-done.5
  36.9 1.7 %copy-done.9 = bf16[4,3,3,128,256]{4,3,2,1,0:T(8,128)(2,1)S(1)} copy-done((bf16[4,3,3,128,256]{4,3,2,1,0:T(8,128)(2,1)S(1)}, bf16[4,3,3,128,256]{4,3,2,1,0:T(8,128)(2,1)}, u32[]{:S(2)}) %copy-start.9) | copy-done | bytes 2359320
  38.5 6.6 %encode.1.field_ref = bf16[6,10,8,128]{3,2,1,0:T(8,128)(2,1)S(1)} custom-call(s32[5]{0:T(128)S(1)} %pad_add_fusion.place_ref, bf16[8,16,16,128]{3,2,1,0:T(8,128)(2,1)S(1)} %copy-done.5, bf16[3,16,16,128]{3,2,1,0:T(8,128)(2,1)} %collective-permute-done.x_in_ref, bf16[3,16,16,128]{3,2,1,0:T(8,128)(2,1)} %collective-permute-done.1.x_out_ref, ...), custom_call_target="tpu_custom_call" | custom-call | tf_op jit(solution)/shard_map/encode/pallas_call | solution.py:173
  45.2 1.6 %collective-permute-start.5 = (bf16[6,10,128]{2,1,0:T(8,128)(2,1)S(1)}, bf16[6,10,128]{2,1,0:T(8,128)(2,1)S(1)}, u32[]{:S(2)}, u32[]{:S(2)}) collective-permute-start(bf16[6,10,128]{2,1,0:T(8,128)(2,1)S(1)} %fusion.1), channel_id=1, source_target_pairs={{0,1},{1,0},{2,3},{3,2},{4,5},{5,4},{6,7},{7,6},{8,9},{9,8},{10,11... | collective-permute-start | bytes 46088 | tf_op jit(solution)/shard_map/ppermute | solution.py:511
  46.8 2.3 %collective-permute-done.5.edge_ref = bf16[6,10,128]{2,1,0:T(8,128)(2,1)S(1)} collective-permute-done((bf16[6,10,128]{2,1,0:T(8,128)(2,1)S(1)}, bf16[6,10,128]{2,1,0:T(8,128)(2,1)S(1)}, u32[]{:S(2)}, u32[]{:S(2)}) %collective-permute-start.5) | collective-permute-done | bytes 15392 | tf_op jit(solution)/shard_map/ppermute | solution.py:511
  49.1 1.4 %half_level.1 = (bf16[4,8,8,256]{3,2,1,0:T(8,128)(2,1)S(1)}, bf16[2,16,256]{2,1,0:T(8,128)(2,1)S(1)}) custom-call(s32[5]{0:T(128)S(1)} %pad_add_fusion.place_ref, bf16[6,10,8,128]{3,2,1,0:T(8,128)(2,1)S(1)} %encode.1.field_ref, bf16[6,10,128]{2,1,0:T(8,128)(2,1)S(1)} %collective-permute-done.5.edge_ref, bf16[9,3,128,256]{3,2,1,0:T(8,128)(2,1)S(1)} %bitcast.15), custom_call_target="tpu_custom_call" | custom-call | tf_op jit(solution)/shard_map/half_level/pallas_call | solution.py:75
  50.5 1.0 collective-permute-start.6
  51.5 3.3 %collective-permute-done.6 = bf16[2,4,1,256]{3,1,0,2:T(4,128)(2,1)S(1)} collective-permute-done((bf16[2,4,1,256]{3,1,0,2:T(4,128)(2,1)S(1)}, bf16[2,4,1,256]{3,1,0,2:T(4,128)(2,1)S(1)}, u32[]{:S(2)}, u32[]{:S(2)}) %collective-permute-start.6) | collective-permute-done | bytes 4128 | tf_op jit(solution)/shard_map/ppermute | solution.py:12
  54.9 0.8 broadcast_in_dim.16
  55.7 5.3 %all-to-all-start = ((bf16[16,2,24,256]{3,2,1,0:T(8,128)(2,1)}), bf16[16,2,24,256]{3,2,1,0:T(8,128)(2,1)S(1)}, u32[]{:S(2)}, u32[]{:S(2)}) async-start(bf16[16,2,24,256]{3,2,1,0:T(8,128)(2,1)} %broadcast_in_dim.16), calls=%async_computation | async-start | bytes 786432 | tf_op jit(solution)/shard_map/all_to_all | solution.py:527
  61.0 5.6 %collective-permute-start.10 = (bf16[1,8,8,256]{3,1,0,2:T(8,128)(2,1)S(1)}, bf16[1,8,8,256]{3,1,0,2:T(8,128)(2,1)S(1)}, u32[]{:S(2)}, u32[]{:S(2)}) collective-permute-start(bf16[1,8,8,256]{3,1,0,2:T(8,128)(2,1)S(1)} %get-tuple-element.38), channel_id=1, source_target_pairs={{0,112},{16,32},{32,16},{48,64},{64,48},{80,96},{96,80},{112,0},{1... | collective-permute-start | bytes 98312 | tf_op jit(solution)/shard_map/ppermute | solution.py:12
  66.7 4.0 %all-to-all-done.field_ref = bf16[16,2,24,256]{3,2,1,0:T(8,128)(2,1)S(1)} async-done(((bf16[16,2,24,256]{3,2,1,0:T(8,128)(2,1)}), bf16[16,2,24,256]{3,2,1,0:T(8,128)(2,1)S(1)}, u32[]{:S(2)}, u32[]{:S(2)}) %all-to-all-start) | async-done | bytes 393248 | tf_op jit(solution)/shard_map/all_to_all | solution.py:527
  70.7 1.3 %copy-done.12 = bf16[9,256,256]{2,1,0:T(8,128)(2,1)S(1)} copy-done((bf16[9,256,256]{2,1,0:T(8,128)(2,1)S(1)}, bf16[9,256,256]{2,1,0:T(8,128)(2,1)}, u32[]{:S(2)}) %copy-start.12) | copy-done | bytes 1179672
  72.0 2.8 %bottom_in.1 = bf16[8,8,6,4,128]{4,3,2,1,0:T(4,128)(2,1)} custom-call(s32[5]{0:T(128)S(1)} %pad_add_fusion.place_ref, bf16[16,2,24,256]{3,2,1,0:T(8,128)(2,1)S(1)} %all-to-all-done.field_ref, bf16[9,256,256]{2,1,0:T(8,128)(2,1)S(1)} %copy-done.12), custom_call_target="tpu_custom_call" | custom-call | tf_op jit(solution)/shard_map/bottom_in/pallas_call | solution.py:360
  74.7 3.5 %all-to-all-start.1 = ((bf16[8,8,6,4,128]{4,3,2,1,0:T(4,128)(2,1)}), bf16[8,8,6,4,128]{4,3,2,1,0:T(4,128)(2,1)S(1)}, u32[]{:S(2)}, u32[]{:S(2)}) async-start(bf16[8,8,6,4,128]{4,3,2,1,0:T(4,128)(2,1)} %bottom_in.1), calls=%async_computation.1 | async-start | bytes 786432 | tf_op jit(solution)/shard_map/all_to_all | solution.py:529
  78.3 0.8 collective-permute-start.12
  79.2 0.3 collective-permute-start.13
  79.5 8.1 %all-to-all-done.1.field_ref = bf16[8,8,6,4,128]{4,3,2,1,0:T(4,128)(2,1)S(1)} async-done(((bf16[8,8,6,4,128]{4,3,2,1,0:T(4,128)(2,1)}), bf16[8,8,6,4,128]{4,3,2,1,0:T(4,128)(2,1)S(1)}, u32[]{:S(2)}, u32[]{:S(2)}) %all-to-all-start.1) | async-done | bytes 393248 | tf_op jit(solution)/shard_map/all_to_all | solution.py:529
  87.6 0.5 broadcast_select_fusion
  88.2 2.7 %collective-permute-start.9 = (bf16[8,8,6,2,128]{4,3,2,1,0:T(2,128)(2,1)S(1)}, bf16[8,8,6,2,128]{4,3,2,1,0:T(2,128)(2,1)S(1)}, u32[]{:S(2)}, u32[]{:S(2)}) collective-permute-start(bf16[8,8,6,2,128]{4,3,2,1,0:T(2,128)(2,1)S(1)} %get-tuple-element.36), channel_id=1, source_target_pairs={{0,14},{2,4},{4,2},{6,8},{8,6},{10,12},{12,10},{14,0},{1,15},{3,5}... | collective-permute-start | bytes 589832 | tf_op jit(solution)/shard_map/ppermute | solution.py:12
  91.0 0.2 pad_maximum_fusion
  91.2 3.3 %collective-permute-done.9.y_out_ref = bf16[8,8,6,2,128]{4,3,2,1,0:T(2,128)(2,1)S(1)} collective-permute-done((bf16[8,8,6,2,128]{4,3,2,1,0:T(2,128)(2,1)S(1)}, bf16[8,8,6,2,128]{4,3,2,1,0:T(2,128)(2,1)S(1)}, u32[]{:S(2)}, u32[]{:S(2)}) %collective-permute-start.9) | collective-permute-done | bytes 196640 | tf_op jit(solution)/shard_map/ppermute | solution.py:12
  94.6 4.1 %bottom_out.1.after_ref = bf16[8,2,6,8,128]{4,3,2,1,0:T(8,128)(2,1)} custom-call(s32[5]{0:T(128)S(1)} %pad_add_fusion.place_ref, bf16[8,8,6,4,128]{4,3,2,1,0:T(4,128)(2,1)S(1)} %all-to-all-done.1.field_ref, bf16[8,8,6,2,128]{4,3,2,1,0:T(2,128)(2,1)S(1)} %collective-permute-done.8.y_in_ref, bf16[8,8,6,2,128]{4,3,2,1,0:T(2,128)(2,1)S(1)} %collective-permute-done.9.y_out_ref, ...), custom_call_target="tpu_custom_call" | custom-call | tf_op jit(solution)/shard_map/bottom_out/pallas_call | solution.py:413
  98.7 3.4 %all-to-all-start.2 = ((bf16[8,2,6,8,128]{4,3,2,1,0:T(8,128)(2,1)}), bf16[8,2,6,8,128]{4,3,2,1,0:T(8,128)(2,1)S(1)}, u32[]{:S(2)}, u32[]{:S(2)}) async-start(bf16[8,2,6,8,128]{4,3,2,1,0:T(8,128)(2,1)} %bottom_out.1.after_ref), calls=%async_computation.2 | async-start | bytes 393216 | tf_op jit(solution)/shard_map/all_to_all | solution.py:533
  102.1 0.7 collective-permute-start.14
  102.9 3.4 %collective-permute-done.14 = bf16[6,10,256]{2,1,0:T(8,128)(2,1)S(1)} collective-permute-done((bf16[6,10,256]{2,1,0:T(8,128)(2,1)S(1)}, bf16[6,10,256]{2,1,0:T(8,128)(2,1)S(1)}, u32[]{:S(2)}, u32[]{:S(2)}) %collective-permute-start.14) | collective-permute-done | bytes 30752 | tf_op jit(solution)/shard_map/ppermute | solution.py:511
  106.4 4.0 %copy-done.2 = bf16[3,3,3,768,256]{4,3,2,1,0:T(8,128)(2,1)S(1)} copy-done((bf16[3,3,3,768,256]{4,3,2,1,0:T(8,128)(2,1)S(1)}, bf16[3,3,3,768,256]{4,3,2,1,0:T(8,128)(2,1)}, u32[]{:S(2)}) %copy-start.2) | copy-done | bytes 10616856
  110.4 2.2 %fetch.1.weights_ref = bf16[9,3,768,256]{3,2,1,0:T(8,128)(2,1)S(1)} custom-call(bf16[9,3,768,256]{3,2,1,0:T(8,128)(2,1)S(1)} %bitcast.14, bf16[8,2,6,8,128]{4,3,2,1,0:T(8,128)(2,1)} %bottom_out.1.after_ref), custom_call_target="tpu_custom_call" | custom-call | tf_op jit(solution)/shard_map/fetch/pallas_call | solution.py:287
  112.7 4.1 %copy-done = bf16[9,3,768,256]{3,2,1,0:T(8,128)(2,1)} copy-done((bf16[9,3,768,256]{3,2,1,0:T(8,128)(2,1)}, bf16[9,3,768,256]{3,2,1,0:T(8,128)(2,1)S(1)}, u32[]{:S(2)}) %copy-start) | copy-done | bytes 10616856
  116.7 4.0 %copy-done.1 = bf16[9,3,768,256]{3,2,1,0:T(8,128)(2,1)S(1)} copy-done((bf16[9,3,768,256]{3,2,1,0:T(8,128)(2,1)S(1)}, bf16[9,3,768,256]{3,2,1,0:T(8,128)(2,1)}, u32[]{:S(2)}) %copy-start.1) | copy-done | bytes 10616856
  120.7 4.8 %decode.1 = bf16[4,8,8,256]{3,2,1,0:T(8,128)(2,1)} custom-call(s32[5]{0:T(128)S(1)} %pad_add_fusion.place_ref, bf16[8,2,6,8,128]{4,3,2,1,0:T(8,128)(2,1)S(1)} %all-to-all-done.2.bottom_ref, bf16[6,10,8,256]{3,2,1,0:T(8,128)(2,1)S(1)} %copy.25.skip_ref, bf16[6,16,256]{2,1,0:T(8,128)(2,1)S(1)} %pad.4.edge_ref, bf16[9,3,768,256]{3,2,1,0:T(8,128)(2,1)S(1)} %copy-done.1), custom_call_target="tpu_custom_call" | custom-call | tf_op jit(solution)/shard_map/decode/pallas_call | solution.py:486
  (49 shorter events, 0.9 us)
Async XLA Ops:
  1.8 21.1 %collective-permute-start = (bf16[3,16,16,128]{3,2,1,0:T(8,128)(2,1)}, bf16[3,16,16,128]{3,2,1,0:T(8,128)(2,1)}, u32[]{:S(2)}, u32[]{:S(2)}) collective-permute-start(bf16[3,16,16,128]{3,2,1,0:T(8,128)(2,1)} %get-tuple-element.35), channel_id=1, source_target_pairs={{0,16},{16,0},{32,48},{48,32},{64,80},{80,64},{96,112},{112,96},{1... | collective-permute-start | bytes 589832 | tf_op jit(solution)/shard_map/ppermute | solution.py:12
  4.9 18.0 %collective-permute-start.1 = (bf16[3,16,16,128]{3,2,1,0:T(8,128)(2,1)}, bf16[3,16,16,128]{3,2,1,0:T(8,128)(2,1)}, u32[]{:S(2)}, u32[]{:S(2)}) collective-permute-start(bf16[3,16,16,128]{3,2,1,0:T(8,128)(2,1)} %get-tuple-element.34), channel_id=1, source_target_pairs={{0,112},{16,32},{32,16},{48,64},{64,48},{80,96},{96,80},{112,0},{1... | collective-permute-start | bytes 589832 | tf_op jit(solution)/shard_map/ppermute | solution.py:12
  14.8 1.5 %copy-start.3 = (bf16[3,3,3,256,64]{4,3,2,1,0:T(8,128)(2,1)S(1)}, bf16[3,3,3,256,64]{4,3,2,1,0:T(8,128)(2,1)}, u32[]{:S(2)}) copy-start(bf16[3,3,3,256,64]{4,3,2,1,0:T(8,128)(2,1)} %copy.15.in_ref) | copy-start | bytes 2654212
  16.3 1.2 copy-start.13
  17.5 5.4 %copy-start.4 = (bf16[8,16,16,128]{3,2,1,0:T(8,128)(2,1)S(1)}, bf16[8,16,16,128]{3,2,1,0:T(8,128)(2,1)}, u32[]{:S(2)}) copy-start(bf16[8,16,16,128]{3,2,1,0:T(8,128)(2,1)} %own_ref.3) | copy-start | bytes 1572868
  18.9 1.4 %copy-start.6 = (bf16[9,512,256]{2,1,0:T(8,128)(2,1)}, bf16[9,512,256]{2,1,0:T(8,128)(2,1)S(1)}, u32[]{:S(2)}) copy-start(bf16[9,512,256]{2,1,0:T(8,128)(2,1)S(1)} %get-tuple-element.29.weights_ref) | copy-start | bytes 7077892
  20.3 1.4 %copy-start.8 = (bf16[4,3,3,128,256]{4,3,2,1,0:T(8,128)(2,1)}, bf16[4,3,3,128,256]{4,3,2,1,0:T(8,128)(2,1)S(1)}, u32[]{:S(2)}) copy-start(bf16[4,3,3,128,256]{4,3,2,1,0:T(8,128)(2,1)S(1)} %get-tuple-element.26.weights_ref) | copy-start | bytes 7077892
  21.8 1.0 copy-start.11
  24.3 3.2 %collective-permute-start.2 = (bf16[14,3,16,128]{3,2,1,0:T(8,128)(2,1)S(1)}, bf16[14,3,16,128]{3,2,1,0:T(8,128)(2,1)S(1)}, u32[]{:S(2)}, u32[]{:S(2)}) collective-permute-start(bf16[14,3,16,128]{3,2,1,0:T(8,128)(2,1)S(1)} %get-tuple-element.23), channel_id=1, source_target_pairs={{0,2},{2,0},{4,6},{6,4},{8,10},{10,8},{12,14},{14,12},{1,3},{3,1},... | collective-permute-start | bytes 516104 | tf_op jit(solution)/shard_map/ppermute | solution.py:12
  24.4 6.2 %collective-permute-start.3 = (bf16[14,3,16,128]{3,2,1,0:T(8,128)(2,1)S(1)}, bf16[14,3,16,128]{3,2,1,0:T(8,128)(2,1)S(1)}, u32[]{:S(2)}, u32[]{:S(2)}) collective-permute-start(bf16[14,3,16,128]{3,2,1,0:T(8,128)(2,1)S(1)} %get-tuple-element.24), channel_id=1, source_target_pairs={{0,14},{2,4},{4,2},{6,8},{8,6},{10,12},{12,10},{14,0},{1,15},{3,5}... | collective-permute-start | bytes 516104 | tf_op jit(solution)/shard_map/ppermute | solution.py:12
  31.2 4.6 %collective-permute-start.4 = (bf16[14,22,128]{2,1,0:T(8,128)(2,1)S(1)}, bf16[14,22,128]{2,1,0:T(8,128)(2,1)S(1)}, u32[]{:S(2)}, u32[]{:S(2)}) collective-permute-start(bf16[14,22,128]{2,1,0:T(8,128)(2,1)S(1)} %pack_z.1), channel_id=1, source_target_pairs={{0,1},{1,0},{2,3},{3,2},{4,5},{5,4},{6,7},{7,6},{8,9},{9,8},{10,11... | collective-permute-start | bytes 236552 | tf_op jit(solution)/shard_map/ppermute | solution.py:518
  35.8 1.0 copy-start.5
  36.9 1.7 %copy-start.9 = (bf16[4,3,3,128,256]{4,3,2,1,0:T(8,128)(2,1)S(1)}, bf16[4,3,3,128,256]{4,3,2,1,0:T(8,128)(2,1)}, u32[]{:S(2)}) copy-start(bf16[4,3,3,128,256]{4,3,2,1,0:T(8,128)(2,1)} %copy-done.8) | copy-start | bytes 7077892
  38.5 10.6 %copy-start.10 = (bf16[3,3,3,128,256]{4,3,2,1,0:T(8,128)(2,1)S(1)}, bf16[3,3,3,128,256]{4,3,2,1,0:T(8,128)(2,1)}, u32[]{:S(2)}) copy-start(bf16[3,3,3,128,256]{4,3,2,1,0:T(8,128)(2,1)} %param.8) | copy-start | bytes 5308420
  45.2 3.9 %collective-permute-start.5 = (bf16[6,10,128]{2,1,0:T(8,128)(2,1)S(1)}, bf16[6,10,128]{2,1,0:T(8,128)(2,1)S(1)}, u32[]{:S(2)}, u32[]{:S(2)}) collective-permute-start(bf16[6,10,128]{2,1,0:T(8,128)(2,1)S(1)} %fusion.1), channel_id=1, source_target_pairs={{0,1},{1,0},{2,3},{3,2},{4,5},{5,4},{6,7},{7,6},{8,9},{9,8},{10,11... | collective-permute-start | bytes 46088 | tf_op jit(solution)/shard_map/ppermute | solution.py:511
  50.5 4.3 %collective-permute-start.6 = (bf16[2,4,1,256]{3,1,0,2:T(4,128)(2,1)S(1)}, bf16[2,4,1,256]{3,1,0,2:T(4,128)(2,1)S(1)}, u32[]{:S(2)}, u32[]{:S(2)}) collective-permute-start(bf16[2,4,1,256]{3,1,0,2:T(4,128)(2,1)S(1)} %get-tuple-element.50), channel_id=1, source_target_pairs={{0,14},{2,4},{4,2},{6,8},{8,6},{10,12},{12,10},{14,0},{1,15},{3,5}... | collective-permute-start | bytes 12296 | tf_op jit(solution)/shard_map/ppermute | solution.py:12
  51.5 3.3 %collective-permute-start.7 = (bf16[2,4,1,256]{3,1,0,2:T(4,128)(2,1)S(1)}, bf16[2,4,1,256]{3,1,0,2:T(4,128)(2,1)S(1)}, u32[]{:S(2)}, u32[]{:S(2)}) collective-permute-start(bf16[2,4,1,256]{3,1,0,2:T(4,128)(2,1)S(1)} %get-tuple-element.51), channel_id=1, source_target_pairs={{0,2},{2,0},{4,6},{6,4},{8,10},{10,8},{12,14},{14,12},{1,3},{3,1},... | collective-permute-start | bytes 12296 | tf_op jit(solution)/shard_map/ppermute | solution.py:12
  55.7 15.0 %all-to-all-start = ((bf16[16,2,24,256]{3,2,1,0:T(8,128)(2,1)}), bf16[16,2,24,256]{3,2,1,0:T(8,128)(2,1)S(1)}, u32[]{:S(2)}, u32[]{:S(2)}) async-start(bf16[16,2,24,256]{3,2,1,0:T(8,128)(2,1)} %broadcast_in_dim.16), calls=%async_computation | async-start | bytes 786432 | tf_op jit(solution)/shard_map/all_to_all | solution.py:527
  61.0 17.2 %collective-permute-start.10 = (bf16[1,8,8,256]{3,1,0,2:T(8,128)(2,1)S(1)}, bf16[1,8,8,256]{3,1,0,2:T(8,128)(2,1)S(1)}, u32[]{:S(2)}, u32[]{:S(2)}) collective-permute-start(bf16[1,8,8,256]{3,1,0,2:T(8,128)(2,1)S(1)} %get-tuple-element.38), channel_id=1, source_target_pairs={{0,112},{16,32},{32,16},{48,64},{64,48},{80,96},{96,80},{112,0},{1... | collective-permute-start | bytes 98312 | tf_op jit(solution)/shard_map/ppermute | solution.py:12
  66.6 11.5 %collective-permute-start.11 = (bf16[1,8,8,256]{3,1,0,2:T(8,128)(2,1)S(1)}, bf16[1,8,8,256]{3,1,0,2:T(8,128)(2,1)S(1)}, u32[]{:S(2)}, u32[]{:S(2)}) collective-permute-start(bf16[1,8,8,256]{3,1,0,2:T(8,128)(2,1)S(1)} %get-tuple-element.39), channel_id=1, source_target_pairs={{0,16},{16,0},{32,48},{48,32},{64,80},{80,64},{96,112},{112,96},{1... | collective-permute-start | bytes 98312 | tf_op jit(solution)/shard_map/ppermute | solution.py:12
  66.7 27.9 %copy-start.7 = (bf16[9,512,256]{2,1,0:T(8,128)(2,1)S(1)}, bf16[9,512,256]{2,1,0:T(8,128)(2,1)}, u32[]{:S(2)}) copy-start(bf16[9,512,256]{2,1,0:T(8,128)(2,1)} %copy-done.6) | copy-start | bytes 7077892
  70.7 1.3 %copy-start.12 = (bf16[9,256,256]{2,1,0:T(8,128)(2,1)S(1)}, bf16[9,256,256]{2,1,0:T(8,128)(2,1)}, u32[]{:S(2)}) copy-start(bf16[9,256,256]{2,1,0:T(8,128)(2,1)} %copy-done.11) | copy-start | bytes 3538948
  74.7 12.9 %all-to-all-start.1 = ((bf16[8,8,6,4,128]{4,3,2,1,0:T(4,128)(2,1)}), bf16[8,8,6,4,128]{4,3,2,1,0:T(4,128)(2,1)S(1)}, u32[]{:S(2)}, u32[]{:S(2)}) async-start(bf16[8,8,6,4,128]{4,3,2,1,0:T(4,128)(2,1)} %bottom_in.1), calls=%async_computation.1 | async-start | bytes 786432 | tf_op jit(solution)/shard_map/all_to_all | solution.py:529
  78.3 12.5 %collective-permute-start.12 = (bf16[6,1,8,256]{3,1,0,2:T(2,128)(2,1)S(1)}, bf16[6,1,8,256]{3,1,0,2:T(2,128)(2,1)S(1)}, u32[]{:S(2)}, u32[]{:S(2)}) collective-permute-start(bf16[6,1,8,256]{3,1,0,2:T(2,128)(2,1)S(1)} %get-tuple-element.31), channel_id=1, source_target_pairs={{0,14},{2,4},{4,2},{6,8},{8,6},{10,12},{12,10},{14,0},{1,15},{3,5}... | collective-permute-start | bytes 73736 | tf_op jit(solution)/shard_map/ppermute | solution.py:12
  79.2 11.7 %collective-permute-start.13 = (bf16[6,1,8,256]{3,1,0,2:T(2,128)(2,1)S(1)}, bf16[6,1,8,256]{3,1,0,2:T(2,128)(2,1)S(1)}, u32[]{:S(2)}, u32[]{:S(2)}) collective-permute-start(bf16[6,1,8,256]{3,1,0,2:T(2,128)(2,1)S(1)} %broadcast_select_fusion.7), channel_id=1, source_target_pairs={{0,2},{2,0},{4,6},{6,4},{8,10},{10,8},{12,14},{14,12},{1,3},{3,1},... | collective-permute-start | bytes 73736 | tf_op jit(solution)/shard_map/ppermute | solution.py:12
  88.1 3.2 %collective-permute-start.8 = (bf16[8,8,6,2,128]{4,3,2,1,0:T(2,128)(2,1)S(1)}, bf16[8,8,6,2,128]{4,3,2,1,0:T(2,128)(2,1)S(1)}, u32[]{:S(2)}, u32[]{:S(2)}) collective-permute-start(bf16[8,8,6,2,128]{4,3,2,1,0:T(2,128)(2,1)S(1)} %get-tuple-element.37), channel_id=1, source_target_pairs={{0,2},{2,0},{4,6},{6,4},{8,10},{10,8},{12,14},{14,12},{1,3},{3,1},... | collective-permute-start | bytes 589832 | tf_op jit(solution)/shard_map/ppermute | solution.py:12
  88.2 6.4 %collective-permute-start.9 = (bf16[8,8,6,2,128]{4,3,2,1,0:T(2,128)(2,1)S(1)}, bf16[8,8,6,2,128]{4,3,2,1,0:T(2,128)(2,1)S(1)}, u32[]{:S(2)}, u32[]{:S(2)}) collective-permute-start(bf16[8,8,6,2,128]{4,3,2,1,0:T(2,128)(2,1)S(1)} %get-tuple-element.36), channel_id=1, source_target_pairs={{0,14},{2,4},{4,2},{6,8},{8,6},{10,12},{12,10},{14,0},{1,15},{3,5}... | collective-permute-start | bytes 589832 | tf_op jit(solution)/shard_map/ppermute | solution.py:12
  98.7 18.0 %all-to-all-start.2 = ((bf16[8,2,6,8,128]{4,3,2,1,0:T(8,128)(2,1)}), bf16[8,2,6,8,128]{4,3,2,1,0:T(8,128)(2,1)S(1)}, u32[]{:S(2)}, u32[]{:S(2)}) async-start(bf16[8,2,6,8,128]{4,3,2,1,0:T(8,128)(2,1)} %bottom_out.1.after_ref), calls=%async_computation.2 | async-start | bytes 393216 | tf_op jit(solution)/shard_map/all_to_all | solution.py:533
  102.1 4.3 %collective-permute-start.14 = (bf16[6,10,256]{2,1,0:T(8,128)(2,1)S(1)}, bf16[6,10,256]{2,1,0:T(8,128)(2,1)S(1)}, u32[]{:S(2)}, u32[]{:S(2)}) collective-permute-start(bf16[6,10,256]{2,1,0:T(8,128)(2,1)S(1)} %fusion), channel_id=1, source_target_pairs={{0,1},{1,0},{2,3},{3,2},{4,5},{5,4},{6,7},{7,6},{8,9},{9,8},{10,11... | collective-permute-start | bytes 92168 | tf_op jit(solution)/shard_map/ppermute | solution.py:511
  106.4 4.0 %copy-start.2 = (bf16[3,3,3,768,256]{4,3,2,1,0:T(8,128)(2,1)S(1)}, bf16[3,3,3,768,256]{4,3,2,1,0:T(8,128)(2,1)}, u32[]{:S(2)}) copy-start(bf16[3,3,3,768,256]{4,3,2,1,0:T(8,128)(2,1)} %param.11) | copy-start | bytes 31850500
  112.7 4.1 %copy-start = (bf16[9,3,768,256]{3,2,1,0:T(8,128)(2,1)}, bf16[9,3,768,256]{3,2,1,0:T(8,128)(2,1)S(1)}, u32[]{:S(2)}) copy-start(bf16[9,3,768,256]{3,2,1,0:T(8,128)(2,1)S(1)} %fetch.1.weights_ref) | copy-start | bytes 31850500
  116.7 4.0 %copy-start.1 = (bf16[9,3,768,256]{3,2,1,0:T(8,128)(2,1)S(1)}, bf16[9,3,768,256]{3,2,1,0:T(8,128)(2,1)}, u32[]{:S(2)}) copy-start(bf16[9,3,768,256]{3,2,1,0:T(8,128)(2,1)} %copy-done) | copy-start | bytes 31850500

commit v6 on v5

--- a/solution.py
+++ b/solution.py
@@ -110,8 +110,25 @@
     pool_y, pool_z = size_y // 2, size_z // 2
 
     def body(
-        place_ref, own_ref, x_in_ref, x_out_ref, y_in_ref, y_out_ref, edge_ref, weights_ref, out_ref, field_ref, side_ref, rows_ref
+        place_ref,
+        own_hbm,
+        x_in_ref,
+        x_out_ref,
+        y_in_ref,
+        y_out_ref,
+        edge_ref,
+        weights_hbm,
+        out_ref,
+        field_ref,
+        side_ref,
+        rows_ref,
+        weights_ref,
+        sems,
     ):
+        inner = field_ref.at[reach : reach + own_x, reach : reach + own_y]
+        copies = [pltpu.make_async_copy(own_hbm, inner, sems.at[0]), pltpu.make_async_copy(weights_hbm, weights_ref, sems.at[1])]
+        for copy in copies:
+            copy.start()
         even_x, even_y = place_ref[0] % 2 == 0, place_ref[1] % 2 == 0
         low_x, high_x = place_ref[0] > 0, place_ref[0] < place_ref[3]
         low_y, high_y = place_ref[1] > 0, place_ref[1] < place_ref[4]
@@ -120,7 +137,6 @@
         below, above = jnp.where(even_x, x_out_ref[...], x_in_ref[...]), jnp.where(even_x, x_in_ref[...], x_out_ref[...])
         field_ref[:reach, inner_y] = jnp.where(low_x, below, nil)
         field_ref[reach + own_x :, inner_y] = jnp.where(high_x, above, nil)
-        field_ref[reach : reach + own_x, inner_y] = own_ref[...]
         for x in range(full_x):
             here_low, here_high = low_y, high_y
             if x < reach:
@@ -142,6 +158,8 @@
                 side_ref[dy, x, size_y:] = jnp.zeros((extra - size_y, channels), jnp.float32)
 
         first = place_ref[2] == 0
+        for copy in copies:
+            copy.wait()
         line = lax.broadcasted_iota(jnp.int32, (pool_y, pool_z, filters), 0)
         inside_y = ((line > 0) | low_y) & ((line < pool_y - 1) | high_y)
         for pair in range(size_x // 2):
@@ -172,45 +190,30 @@
 
     return pl.pallas_call(
         body,
-        in_specs=[pl.BlockSpec(memory_space=pltpu.SMEM)] + [pl.BlockSpec(memory_space=pltpu.VMEM)] * 7,
+        in_specs=[pl.BlockSpec(memory_space=pltpu.SMEM), pl.BlockSpec(memory_space=pltpu.HBM)]
+        + [pl.BlockSpec(memory_space=pltpu.VMEM)] * 5
+        + [pl.BlockSpec(memory_space=pltpu.HBM)],
         out_specs=pl.BlockSpec(memory_space=pltpu.VMEM),
         out_shape=jax.ShapeDtypeStruct((size_x // 2, pool_y, pool_z, filters), jnp.bfloat16),
         scratch_shapes=[
             pltpu.VMEM((full_x, full_y, size_z, channels), jnp.bfloat16),
             pltpu.VMEM((3, full_x, extra, channels), jnp.float32),
             pltpu.VMEM((pool_y * size_z, filters), jnp.float32),
+            pltpu.VMEM(weights.shape, weights.dtype),
+            pltpu.SemaphoreType.DMA((2,)),
         ],
-        compiler_params=pltpu.CompilerParams(vmem_limit_bytes=16 << 20),
+        compiler_params=pltpu.CompilerParams(vmem_limit_bytes=20 << 20),
         name="encode",
-    )(place, own, x_in, x_out, y_in, y_out, edge, weights)
-
-
-def prepare(w_full, w_bottom_in, w_bottom_out):
-    channels, filters = w_full.shape[3:]
-
-    def body(full_ref, in_ref, out_ref, pair_ref, beside_in_ref, beside_out_ref):
-        zero = jnp.zeros((3, 3, channels, filters), jnp.bfloat16)
-        for plane in range(4):
-            pair_ref[plane, :, :, :, :filters] = full_ref[plane] if plane < 3 else zero
-            pair_ref[plane, :, :, :, filters:] = full_ref[plane - 1] if plane > 0 else zero
-        for ref, to in ((in_ref, beside_in_ref), (out_ref, beside_out_ref)):
-            depth = ref.shape[3]
-            gap = jnp.zeros((depth, 64), jnp.float32)
-            for dx in range(3):
-                for dz in range(3):
-                    first, second, third = [ref[dx, dy, dz].astype(jnp.float32) for dy in range(3)]
-                    to[3 * dx + dz, :, :128] = jnp.concatenate([first, second], axis=1).astype(jnp.bfloat16)
-                    to[3 * dx + dz, :, 128:] = jnp.concatenate([third, gap], axis=1).astype(jnp.bfloat16)
-
-    return pl.pallas_call(
-        body,
-        in_specs=[pl.BlockSpec(memory_space=pltpu.VMEM)] * 3,
-        out_specs=[pl.BlockSpec(memory_space=pltpu.VMEM)] * 3,
-        out_shape=[jax.ShapeDtypeStruct((4, 3, 3, channels, 2 * filters), jnp.bfloat16)]
-        + [jax.ShapeDtypeStruct((9, w.shape[3], 256), jnp.bfloat16) for w in (w_bottom_in, w_bottom_out)],
-        compiler_params=pltpu.CompilerParams(vmem_limit_bytes=8 << 20),
-        name="prepare",
-    )(w_full, w_bottom_in, w_bottom_out)
+    )(place, far(own), x_in, x_out, y_in, y_out, edge, far(weights))
+
+
+def paired(weights):
+    grow = [(0, 0)] * 4
+    return jnp.concatenate([jnp.pad(weights, [(0, 1)] + grow), jnp.pad(weights, [(1, 0)] + grow)], axis=4)
+
+
+def far(array):
+    return pltpu.with_memory_space_constraint(array, pltpu.HBM)
 
 
 def pack_y(place, own, x_in, x_out):
@@ -276,25 +279,6 @@
     )(place, plane, y_in, y_out)
 
 
-def fetch(weights, after):
-    def body(weights_ref, after_ref, out_ref, sems):
-        copies = [pltpu.make_async_copy(weights_ref.at[i], out_ref.at[i], sems.at[i]) for i in range(9)]
-        for copy in copies:
-            copy.start()
-        for copy in copies:
-            copy.wait()
-
-    return pl.pallas_call(
-        body,
-        in_specs=[pl.BlockSpec(memory_space=pltpu.HBM)] * 2,
-        out_specs=pl.BlockSpec(memory_space=pltpu.VMEM),
-        out_shape=jax.ShapeDtypeStruct(weights.shape, weights.dtype),
-        scratch_shapes=[pltpu.SemaphoreType.DMA((9,))],
-        compiler_params=pltpu.CompilerParams(vmem_limit_bytes=12 << 20),
-        name="fetch",
-    )(weights, after)
-
-
 def halves(pair_low, pair_high):
     lane = lax.broadcasted_iota(jnp.int32, pair_low.shape, pair_low.ndim - 1)
     axis = pair_low.ndim - 1
@@ -306,6 +290,20 @@
 def side_by_side(even, odd):
     lane = lax.broadcasted_iota(jnp.int32, even.shape, even.ndim - 1)
     return jnp.where(lane < 64, even, pltpu.roll(odd, 64, even.ndim - 1))
+
+
+def column_weights(weights_hbm, weights_ref, sems):
+    filters, channels = weights_hbm.shape[3:]
+    weights_ref[3 * filters :] = jnp.zeros((weights_ref.shape[0] - 3 * filters, 9 * channels), weights_ref.dtype)
+    copies = []
+    for dx in range(3):
+        for dy in range(3):
+            for dz in range(3):
+                lanes = pl.ds((3 * dx + dz) * channels, channels)
+                to = weights_ref.at[pl.ds(filters * dy, filters), lanes]
+                copies.append(pltpu.make_async_copy(weights_hbm.at[dx, dy, dz], to, sems.at[9 * dx + 3 * dy + dz]))
+                copies[-1].start()
+    return copies
 
 
 def column_product(pad_ref, weights_ref, first, start, planes, size_z):
@@ -317,7 +315,7 @@
             block = pad_ref[first + dx : first + dx + planes, pl.ds(start + dz, size_z)]
             blocks.append(block.reshape(rows, channels).astype(jnp.bfloat16))
     block = jnp.concatenate(blocks, axis=1)
-    total = jnp.dot(block, weights_ref[...].reshape(9 * channels, 256), preferred_element_type=jnp.float32)
+    total = lax.dot_general(block, weights_ref[...], (((1,), (1,)), ((), ())), preferred_element_type=jnp.float32)
     low = total[:, :128].reshape(planes * size_z, 8, 128)
     mid = pltpu.roll(total[:, :128], 64, 1).reshape(planes * size_z, 8, 128)
     high = total[:, 128:].reshape(planes * size_z, 8, 128)
@@ -331,7 +329,8 @@
     own_z = size_y = 4
     size_x, all_z, size_z = devices * own_x, 2 * own_z, own_z + 2
 
-    def body(place_ref, field_ref, weights_ref, out_ref, pad_ref):
+    def body(place_ref, field_ref, weights_hbm, out_ref, pad_ref, weights_ref, sems):
+        copies = column_weights(weights_hbm, weights_ref, sems)
         zero = jnp.zeros((all_z + 2, 8, channels), jnp.float32)
         pad_ref[0] = zero
         pad_ref[size_x + 1] = zero
@@ -350,6 +349,8 @@
                         pad_ref[*to, size_y + 1 : size_y + 2] = block[line : line + 1]
                         pad_ref[*to, size_y + 2 :] = zero[0, size_y + 2 :]
         start = 2 * place_ref[2]
+        for copy in copies:
+            copy.wait()
         for first in range(0, size_x, 4):
             total = column_product(pad_ref, weights_ref, first, start, 4, size_z)
             for pair in range(2):
@@ -359,13 +360,17 @@
 
     return pl.pallas_call(
         body,
-        in_specs=[pl.BlockSpec(memory_space=pltpu.SMEM)] + [pl.BlockSpec(memory_space=pltpu.VMEM)] * 2,
+        in_specs=[pl.BlockSpec(memory_space=space) for space in (pltpu.SMEM, pltpu.VMEM, pltpu.HBM)],
         out_specs=pl.BlockSpec(memory_space=pltpu.VMEM),
         out_shape=jax.ShapeDtypeStruct((devices, size_x // 2, size_z, size_y, 128), jnp.bfloat16),
-        scratch_shapes=[pltpu.VMEM((size_x + 2, all_z + 2, 8, channels), jnp.float32)],
+        scratch_shapes=[
+            pltpu.VMEM((size_x + 2, all_z + 2, 8, channels), jnp.float32),
+            pltpu.VMEM((256, 9 * channels), jnp.bfloat16),
+            pltpu.SemaphoreType.DMA((27,)),
+        ],
         compiler_params=pltpu.CompilerParams(vmem_limit_bytes=12 << 20),
         name="bottom_in",
-    )(place, field, weights)
+    )(place, field, far(weights))
 
 
 def bottom_out(place, field, y_in, y_out, weights):
@@ -373,7 +378,8 @@
     size_x, channels = 2 * pairs, 64 * devices
     own_x = size_x // devices
 
-    def body(place_ref, field_ref, y_in_ref, y_out_ref, weights_ref, out_ref, pad_ref, total_ref):
+    def body(place_ref, field_ref, y_in_ref, y_out_ref, weights_hbm, out_ref, pad_ref, total_ref, weights_ref, sems):
+        copies = column_weights(weights_hbm, weights_ref, sems)
         even_y = place_ref[1] % 2 == 0
         low_y, high_y = place_ref[1] > 0, place_ref[1] < place_ref[4]
         zero = jnp.zeros((size_z + 2, 8, channels), jnp.float32)
@@ -398,6 +404,8 @@
                     lines = slice(line, line + even.shape[1])
                     pad_ref[1 + 2 * pair, 1 : size_z + 1, lines, 128 * k : 128 * k + 128] = even
                     pad_ref[2 + 2 * pair, 1 : size_z + 1, lines, 128 * k : 128 * k + 128] = odd
+        for copy in copies:
+            copy.wait()
         for first in range(0, size_x, 4):
             total = column_product(pad_ref, weights_ref, first, 0, 4, size_z)
             total_ref[1 + first : 5 + first, 1 : size_z + 1] = total
@@ -412,16 +420,20 @@
 
     return pl.pallas_call(
         body,
-        in_specs=[pl.BlockSpec(memory_space=pltpu.SMEM)] + [pl.BlockSpec(memory_space=pltpu.VMEM)] * 4,
+        in_specs=[pl.BlockSpec(memory_space=pltpu.SMEM)]
+        + [pl.BlockSpec(memory_space=pltpu.VMEM)] * 3
+        + [pl.BlockSpec(memory_space=pltpu.HBM)],
         out_specs=pl.BlockSpec(memory_space=pltpu.VMEM),
         out_shape=jax.ShapeDtypeStruct((devices, own_x, size_z, 8, 128), jnp.bfloat16),
         scratch_shapes=[
             pltpu.VMEM((size_x + 2, size_z + 2, 8, channels), jnp.float32),
             pltpu.VMEM((size_x + 2, size_z + 2, 8, 128), jnp.float32),
+            pltpu.VMEM((256, 9 * channels), jnp.bfloat16),
+            pltpu.SemaphoreType.DMA((27,)),
         ],
-        compiler_params=pltpu.CompilerParams(vmem_limit_bytes=16 << 20),
+        compiler_params=pltpu.CompilerParams(vmem_limit_bytes=20 << 20),
         name="bottom_out",
-    )(place, field, y_in, y_out, weights)
+    )(place, field, y_in, y_out, far(weights))
 
 
 def decode(place, bottom, skip, edge, weights):
@@ -432,7 +444,10 @@
     filters = weights.shape[-1]
     rows, extra = size_x * size_y * size_z, size_x * size_y
 
-    def body(place_ref, bottom_ref, skip_ref, edge_ref, weights_ref, out_ref, main_ref, side_ref, sums_ref):
+    def body(place_ref, bottom_ref, skip_ref, edge_ref, weights_hbm, out_ref, main_ref, side_ref, sums_ref, weights_ref, sems):
+        copies = [pltpu.make_async_copy(weights_hbm.at[step], weights_ref.at[step], sems.at[step]) for step in range(9)]
+        for copy in copies:
+            copy.start()
         first = place_ref[2] == 0
         planes = [[] for _ in range(2 * pairs)]
         for k in range(devices // 2):
@@ -472,6 +487,7 @@
                 main = main_ref[dy, dx : dx + size_x].reshape(rows, channels)
                 side = side_ref[dy, dx : dx + size_x].reshape(extra, channels).astype(jnp.bfloat16)
                 blocks.append(jnp.concatenate([main, side], axis=0))
+                copies[3 * dx + dy].wait()
             block = jnp.concatenate(blocks, axis=1)
             for tap in range(3):
                 kernel = weights_ref[3 * dx : 3 * dx + 3, tap].reshape(3 * channels, filters)
@@ -486,17 +502,20 @@
     return pl.pallas_call(
         body,
         in_specs=[pl.BlockSpec(memory_space=pltpu.SMEM)]
-        + [pl.BlockSpec(memory_space=pltpu.VMEM)] * 4,
+        + [pl.BlockSpec(memory_space=pltpu.VMEM)] * 3
+        + [pl.BlockSpec(memory_space=pltpu.HBM)],
         out_specs=pl.BlockSpec(memory_space=pltpu.VMEM),
         out_shape=jax.ShapeDtypeStruct((size_x, size_y, size_z, filters), jnp.bfloat16),
         scratch_shapes=[
             pltpu.VMEM((3, full_x, size_y * size_z, channels), jnp.bfloat16),
             pltpu.VMEM((3, full_x, size_y, channels), jnp.float32),
             pltpu.VMEM((3, rows + extra, filters), jnp.float32),
+            pltpu.VMEM(weights.shape, weights.dtype),
+            pltpu.SemaphoreType.DMA((9,)),
         ],
-        compiler_params=pltpu.CompilerParams(vmem_limit_bytes=16 << 20),
+        compiler_params=pltpu.CompilerParams(vmem_limit_bytes=26 << 20),
         name="decode",
-    )(place, bottom, skip, edge, weights)
+    )(place, bottom, skip, edge, far(weights))
 
 
 def solution(mesh):
@@ -511,8 +530,7 @@
             return lax.ppermute(jnp.where(place_z == 0, plane_high, plane_low), "gz", swap)
 
         x_in, x_out = swaps(volume[:3], volume[-3:], "gx", gx)
-        weights = prepare(w_full, w_bottom_in, w_bottom_out)
-        (w_pair, w_in, w_out), x_in, x_out = lax.optimization_barrier((weights, x_in, x_out))
+        w_pair, x_in, x_out = lax.optimization_barrier((paired(w_full), x_in, x_out))
         y_inner, y_outer, plane = pack_y(place, volume, x_in, x_out)
         y_in, y_out = send(y_inner, y_outer, "gy", gy)
         edge = lax.ppermute(pack_z(place, plane, y_in, y_out), "gz", swap)
@@ -525,18 +543,17 @@
         column = jnp.concatenate([coarse, below[:, :, 0], above[:, :, 0]], axis=1)
         column = jnp.broadcast_to(column[None], (gx * gz,) + column.shape)
         column = lax.all_to_all(column, ("gx", "gz"), 0, 0)
-        first = bottom_in(place, column, w_in)
+        first = bottom_in(place, column, w_bottom_in.transpose(0, 1, 2, 4, 3))
         first = lax.all_to_all(first, "gx", 0, 0)
         y_in, y_out = swaps(first[:, :, :, :2], first[:, :, :, -2:], "gy", gy)
-        second = bottom_out(place, first, y_in, y_out, w_out)
-        w_up = fetch(w_up.reshape(9, 3, w_up.shape[3], w_up.shape[4]), second)
+        second = bottom_out(place, first, y_in, y_out, w_bottom_out.transpose(0, 1, 2, 4, 3))
         second = lax.all_to_all(second, "gx", 0, 0)
 
         around = extend(skip, "gx", gx, 0, 1)
         around = extend(around, "gy", gy, 1, 1)
         side = edge_of(around[:, :, 0], around[:, :, -1])
         side = jnp.pad(side, ((0, 0), (0, -side.shape[1] % 16), (0, 0)))
-        return decode(place, second, around, side, w_up)
+        return decode(place, second, around, side, w_up.reshape(9, 3, w_up.shape[3], w_up.shape[4]))
 
     space = P("gx", "gy", "gz", None)
     filters = P(None, None, None, None, "gx")

time: 127 us -> 116 us (0.913)
  local copies, waits for them, and re-layouts: 29.6 us -> 1.02 us
  waiting for transfers between devices: 30.6 us -> 38.6 us
  Pallas kernels: 25.3 us -> 30.7 us
  other arithmetic: 2.95 us -> 5.57 us
  starting transfers between devices: 36.8 us -> 38.5 us
    unnamed x30 -> x4, local copies, waits for them, and re-layouts: 28.6 us -> 0.01 us
    ppermute x6, waiting for transfers between devices: 9.72 us -> 15.3 us  [send(): lax.ppermute(outer_block, axis, outer)]
    all_to_all x1, waiting for transfers between devices: 0.01 us -> 4.19 us  [local(): second = lax.all_to_all(second, 'gx', 0, 0)]
    pallas_call x1, Pallas kernels: 4.76 us -> 8.19 us  [decode(): pl.pallas_call(body, in_specs=[pl.BlockSpec(memory_space=pltpu.SMEM)] + [...]
    pallas_call x1, Pallas kernels: 4.12 us -> 7.48 us  [bottom_out(): pl.pallas_call(body, in_specs=[pl.BlockSpec(memory_space=pltpu.SMEM)] + [...]
    concatenate x0 -> x1, other arithmetic: none -> 3.32 us  [paired(): jnp.concatenate([jnp.pad(weights, [(0, 1)] + grow), jnp.pad(weights, [(1,...]
    ppermute x6, starting transfers between devices: 17.2 us -> 19.1 us  [send(): lax.ppermute(outer_block, axis, outer)]
    all_to_all x1, waiting for transfers between devices: 8.1 us -> 6.42 us  [local(): first = lax.all_to_all(first, 'gx', 0, 0)]
  transfers between devices with their start and end apart: 18 -> 18, of which waited for: 8 -> 10; matrix products, arithmetic and copies ran while one was open for 6% -> 4% of each run, Pallas kernels for 5% -> 4%
where the time goes in v6:
time: 116 us; the launch traced here: 115 us
  waiting for transfers between devices  38.6 us (33%)
  starting transfers between devices  38.5 us (33%)
  Pallas kernels  30.7 us (26%)
  other arithmetic  5.57 us (5%)
    ppermute x6, starting transfers between devices, send(): lax.ppermute(outer_block, axis, outer)  19.1 us
    ppermute x6, waiting for transfers between devices, send(): lax.ppermute(outer_block, axis, outer)  15.3 us
    pallas_call x1, Pallas kernels, decode(): pl.pallas_call(body, in_specs=[pl.BlockSpec(memory_space=pltpu.SMEM)] + [...  8.19 us
    pallas_call x1, Pallas kernels, encode(): pl.pallas_call(body, in_specs=[pl.BlockSpec(memory_space=pltpu.SMEM), pl....  7.68 us
    pallas_call x1, Pallas kernels, bottom_out(): pl.pallas_call(body, in_specs=[pl.BlockSpec(memory_space=pltpu.SMEM)] + [...  7.48 us
    all_to_all x1, waiting for transfers between devices, local(): first = lax.all_to_all(first, 'gx', 0, 0)  6.42 us
    ppermute x2, waiting for transfers between devices, edge_of(): lax.ppermute(jnp.where(place_z == 0, plane_high, plane_low), 'gz', swap)  5.68 us
    all_to_all x1, starting transfers between devices, local(): column = lax.all_to_all(column, ('gx', 'gz'), 0, 0)  5.31 us
  transfers between devices with their start and end apart: 18, of which 10 were waited for; matrix products, arithmetic and copies ran while one was open for 4% of the time, Pallas kernels for 4%

profile of v6, /device:TPU:0, one launch (start us, length us, event | category | flops | bytes accessed | tf_op | source)
XLA Modules:
  0.0 114.9 jit_solution(4590998733817260550)
XLA Ops:
  0.0 1.1 broadcast_select_fusion.2
  1.1 3.2 %collective-permute-start = (bf16[3,16,16,128]{3,2,1,0:T(8,128)(2,1)S(1)}, bf16[3,16,16,128]{3,2,1,0:T(8,128)(2,1)S(1)}, u32[]{:S(2)}, u32[]{:S(2)}) collective-permute-start(bf16[3,16,16,128]{3,2,1,0:T(8,128)(2,1)S(1)} %get-tuple-element.25), channel_id=1, source_target_pairs={{0,16},{16,0},{32,48},{48,32},{64,80},{80,64},{96,112},{112,96},{1... | collective-permute-start | bytes 589832 | tf_op jit(solution)/shard_map/ppermute | solution.py:12
  4.3 4.0 %collective-permute-start.1 = (bf16[3,16,16,128]{3,2,1,0:T(8,128)(2,1)S(1)}, bf16[3,16,16,128]{3,2,1,0:T(8,128)(2,1)S(1)}, u32[]{:S(2)}, u32[]{:S(2)}) collective-permute-start(bf16[3,16,16,128]{3,2,1,0:T(8,128)(2,1)S(1)} %get-tuple-element.24), channel_id=1, source_target_pairs={{0,112},{16,32},{32,16},{48,64},{64,48},{80,96},{96,80},{112,0},{1... | collective-permute-start | bytes 589832 | tf_op jit(solution)/shard_map/ppermute | solution.py:12
  8.3 0.1 pad_add_fusion.place_ref
  8.4 3.3 %fusion.2.weights_hbm = bf16[4,3,3,128,256]{4,3,2,1,0:T(8,128)(2,1)} fusion(bf16[3,3,3,128,128]{4,3,2,1,0:T(8,128)(2,1)} %param.7), kind=kLoop, calls=%fused_computation.4 | loop fusion | flops 9437184 | bytes 3244032 | tf_op jit(solution)/shard_map/concatenate | solution.py:212
  11.7 5.4 %collective-permute-done.1.x_out_ref = bf16[3,16,16,128]{3,2,1,0:T(8,128)(2,1)S(1)} collective-permute-done((bf16[3,16,16,128]{3,2,1,0:T(8,128)(2,1)S(1)}, bf16[3,16,16,128]{3,2,1,0:T(8,128)(2,1)S(1)}, u32[]{:S(2)}, u32[]{:S(2)}) %collective-permute-start.1) | collective-permute-done | bytes 196640 | tf_op jit(solution)/shard_map/ppermute | solution.py:12
  17.1 0.9 pack_y.1
  18.0 0.0 copy-start.1
  18.0 0.1 collective-permute-start.2
  18.1 3.1 %collective-permute-start.3 = (bf16[14,3,16,128]{3,2,1,0:T(8,128)(2,1)S(1)}, bf16[14,3,16,128]{3,2,1,0:T(8,128)(2,1)S(1)}, u32[]{:S(2)}, u32[]{:S(2)}) collective-permute-start(bf16[14,3,16,128]{3,2,1,0:T(8,128)(2,1)S(1)} %get-tuple-element.16), channel_id=1, source_target_pairs={{0,14},{2,4},{4,2},{6,8},{8,6},{10,12},{12,10},{14,0},{1,15},{3,5}... | collective-permute-start | bytes 516104 | tf_op jit(solution)/shard_map/ppermute | solution.py:12
  21.2 0.0 collective-permute-done.2.y_in_ref
  21.2 3.1 %collective-permute-done.3.y_out_ref = bf16[14,3,16,128]{3,2,1,0:T(8,128)(2,1)S(1)} collective-permute-done((bf16[14,3,16,128]{3,2,1,0:T(8,128)(2,1)S(1)}, bf16[14,3,16,128]{3,2,1,0:T(8,128)(2,1)S(1)}, u32[]{:S(2)}, u32[]{:S(2)}) %collective-permute-start.3) | collective-permute-done | bytes 172064 | tf_op jit(solution)/shard_map/ppermute | solution.py:12
  24.3 0.6 pack_z.1
  25.0 1.6 %collective-permute-start.4 = (bf16[14,22,128]{2,1,0:T(8,128)(2,1)S(1)}, bf16[14,22,128]{2,1,0:T(8,128)(2,1)S(1)}, u32[]{:S(2)}, u32[]{:S(2)}) collective-permute-start(bf16[14,22,128]{2,1,0:T(8,128)(2,1)S(1)} %pack_z.1), channel_id=1, source_target_pairs={{0,1},{1,0},{2,3},{3,2},{4,5},{5,4},{6,7},{7,6},{8,9},{9,8},{10,11... | collective-permute-start | bytes 236552 | tf_op jit(solution)/shard_map/ppermute | solution.py:536
  26.5 3.0 %collective-permute-done.4.edge_ref = bf16[14,22,128]{2,1,0:T(8,128)(2,1)S(1)} collective-permute-done((bf16[14,22,128]{2,1,0:T(8,128)(2,1)S(1)}, bf16[14,22,128]{2,1,0:T(8,128)(2,1)S(1)}, u32[]{:S(2)}, u32[]{:S(2)}) %collective-permute-start.4) | collective-permute-done | bytes 78880 | tf_op jit(solution)/shard_map/ppermute | solution.py:536
  29.5 7.7 %encode.1.field_ref = bf16[6,10,8,128]{3,2,1,0:T(8,128)(2,1)S(1)} custom-call(s32[5]{0:T(128)S(1)} %pad_add_fusion.place_ref, bf16[8,16,16,128]{3,2,1,0:T(8,128)(2,1)} %own_hbm.1, bf16[3,16,16,128]{3,2,1,0:T(8,128)(2,1)S(1)} %collective-permute-done.x_in_ref, bf16[3,16,16,128]{3,2,1,0:T(8,128)(2,1)S(1)} %collective-permute-done.1.x_out_ref, ...), custom_call_target="tpu_custom_call" | custom-call | tf_op jit(solution)/shard_map/encode/pallas_call | solution.py:191
  37.3 1.6 %collective-permute-start.5 = (bf16[6,10,128]{2,1,0:T(8,128)(2,1)S(1)}, bf16[6,10,128]{2,1,0:T(8,128)(2,1)S(1)}, u32[]{:S(2)}, u32[]{:S(2)}) collective-permute-start(bf16[6,10,128]{2,1,0:T(8,128)(2,1)S(1)} %fusion.4), channel_id=1, source_target_pairs={{0,1},{1,0},{2,3},{3,2},{4,5},{5,4},{6,7},{7,6},{8,9},{9,8},{10,11... | collective-permute-start | bytes 46088 | tf_op jit(solution)/shard_map/ppermute | solution.py:530
  38.9 2.3 %collective-permute-done.5.edge_ref = bf16[6,10,128]{2,1,0:T(8,128)(2,1)S(1)} collective-permute-done((bf16[6,10,128]{2,1,0:T(8,128)(2,1)S(1)}, bf16[6,10,128]{2,1,0:T(8,128)(2,1)S(1)}, u32[]{:S(2)}, u32[]{:S(2)}) %collective-permute-start.5) | collective-permute-done | bytes 15392 | tf_op jit(solution)/shard_map/ppermute | solution.py:530
  41.2 1.4 %half_level.1 = (bf16[4,8,8,256]{3,2,1,0:T(8,128)(2,1)S(1)}, bf16[2,16,256]{2,1,0:T(8,128)(2,1)S(1)}) custom-call(s32[5]{0:T(128)S(1)} %pad_add_fusion.place_ref, bf16[6,10,8,128]{3,2,1,0:T(8,128)(2,1)S(1)} %encode.1.field_ref, bf16[6,10,128]{2,1,0:T(8,128)(2,1)S(1)} %collective-permute-done.5.edge_ref, bf16[9,3,128,256]{3,2,1,0:T(8,128)(2,1)S(1)} %bitcast.16), custom_call_target="tpu_custom_call" | custom-call | tf_op jit(solution)/shard_map/half_level/pallas_call | solution.py:75
  42.6 1.0 collective-permute-start.6
  43.7 3.3 %collective-permute-done.6 = bf16[2,4,1,256]{3,1,0,2:T(4,128)(2,1)S(1)} collective-permute-done((bf16[2,4,1,256]{3,1,0,2:T(4,128)(2,1)S(1)}, bf16[2,4,1,256]{3,1,0,2:T(4,128)(2,1)S(1)}, u32[]{:S(2)}, u32[]{:S(2)}) %collective-permute-start.6) | collective-permute-done | bytes 4128 | tf_op jit(solution)/shard_map/ppermute | solution.py:12
  47.0 0.0 collective-permute-done.7
  47.0 0.8 broadcast_in_dim.16
  47.8 5.3 %all-to-all-start = ((bf16[16,2,24,256]{3,2,1,0:T(8,128)(2,1)}), bf16[16,2,24,256]{3,2,1,0:T(8,128)(2,1)S(1)}, u32[]{:S(2)}, u32[]{:S(2)}) async-start(bf16[16,2,24,256]{3,2,1,0:T(8,128)(2,1)} %broadcast_in_dim.16), calls=%async_computation | async-start | bytes 786432 | tf_op jit(solution)/shard_map/all_to_all | solution.py:545
  53.1 5.6 %collective-permute-start.10 = (bf16[1,8,8,256]{3,1,0,2:T(8,128)(2,1)S(1)}, bf16[1,8,8,256]{3,1,0,2:T(8,128)(2,1)S(1)}, u32[]{:S(2)}, u32[]{:S(2)}) collective-permute-start(bf16[1,8,8,256]{3,1,0,2:T(8,128)(2,1)S(1)} %get-tuple-element.28), channel_id=1, source_target_pairs={{0,112},{16,32},{32,16},{48,64},{64,48},{80,96},{96,80},{112,0},{1... | collective-permute-start | bytes 98312 | tf_op jit(solution)/shard_map/ppermute | solution.py:12
  58.7 0.0 collective-permute-start.11
  58.8 4.0 %all-to-all-done.field_ref = bf16[16,2,24,256]{3,2,1,0:T(8,128)(2,1)S(1)} async-done(((bf16[16,2,24,256]{3,2,1,0:T(8,128)(2,1)}), bf16[16,2,24,256]{3,2,1,0:T(8,128)(2,1)S(1)}, u32[]{:S(2)}, u32[]{:S(2)}) %all-to-all-start) | async-done | bytes 393248 | tf_op jit(solution)/shard_map/all_to_all | solution.py:545
  62.8 4.5 %bottom_in.1 = bf16[8,8,6,4,128]{4,3,2,1,0:T(4,128)(2,1)} custom-call(s32[5]{0:T(128)S(1)} %pad_add_fusion.place_ref, bf16[16,2,24,256]{3,2,1,0:T(8,128)(2,1)S(1)} %all-to-all-done.field_ref, bf16[3,3,3,64,256]{4,3,2,1,0:T(8,128)(2,1)} %bitcast.19), custom_call_target="tpu_custom_call" | custom-call | tf_op jit(solution)/shard_map/bottom_in/pallas_call | solution.py:361
  67.3 3.5 %all-to-all-start.1 = ((bf16[8,8,6,4,128]{4,3,2,1,0:T(4,128)(2,1)}), bf16[8,8,6,4,128]{4,3,2,1,0:T(4,128)(2,1)S(1)}, u32[]{:S(2)}, u32[]{:S(2)}) async-start(bf16[8,8,6,4,128]{4,3,2,1,0:T(4,128)(2,1)} %bottom_in.1), calls=%async_computation.1 | async-start | bytes 786432 | tf_op jit(solution)/shard_map/all_to_all | solution.py:547
  70.7 0.0 collective-permute-done.10
  70.8 0.1 broadcast_select_fusion.8
  70.9 0.1 broadcast_select_fusion.7
  71.0 0.1 collective-permute-start.13
  71.1 2.7 %collective-permute-start.12 = (bf16[6,1,8,256]{3,1,0,2:T(2,128)(2,1)S(1)}, bf16[6,1,8,256]{3,1,0,2:T(2,128)(2,1)S(1)}, u32[]{:S(2)}, u32[]{:S(2)}) collective-permute-start(bf16[6,1,8,256]{3,1,0,2:T(2,128)(2,1)S(1)} %get-tuple-element.21), channel_id=1, source_target_pairs={{0,14},{2,4},{4,2},{6,8},{8,6},{10,12},{12,10},{14,0},{1,15},{3,5}... | collective-permute-start | bytes 73736 | tf_op jit(solution)/shard_map/ppermute | solution.py:12
  73.8 6.4 %all-to-all-done.1.field_ref = bf16[8,8,6,4,128]{4,3,2,1,0:T(4,128)(2,1)S(1)} async-done(((bf16[8,8,6,4,128]{4,3,2,1,0:T(4,128)(2,1)}), bf16[8,8,6,4,128]{4,3,2,1,0:T(4,128)(2,1)S(1)}, u32[]{:S(2)}, u32[]{:S(2)}) %all-to-all-start.1) | async-done | bytes 393248 | tf_op jit(solution)/shard_map/all_to_all | solution.py:547
  80.2 0.5 broadcast_select_fusion
  80.6 0.1 collective-permute-start.8
  80.7 2.7 %collective-permute-start.9 = (bf16[8,8,6,2,128]{4,3,2,1,0:T(2,128)(2,1)S(1)}, bf16[8,8,6,2,128]{4,3,2,1,0:T(2,128)(2,1)S(1)}, u32[]{:S(2)}, u32[]{:S(2)}) collective-permute-start(bf16[8,8,6,2,128]{4,3,2,1,0:T(2,128)(2,1)S(1)} %get-tuple-element.26), channel_id=1, source_target_pairs={{0,14},{2,4},{4,2},{6,8},{8,6},{10,12},{12,10},{14,0},{1,15},{3,5}... | collective-permute-start | bytes 589832 | tf_op jit(solution)/shard_map/ppermute | solution.py:12
  83.4 0.1 broadcast_select_fusion.9
  83.5 0.2 pad_maximum_fusion
  83.8 3.5 %collective-permute-done.9.y_out_ref = bf16[8,8,6,2,128]{4,3,2,1,0:T(2,128)(2,1)S(1)} collective-permute-done((bf16[8,8,6,2,128]{4,3,2,1,0:T(2,128)(2,1)S(1)}, bf16[8,8,6,2,128]{4,3,2,1,0:T(2,128)(2,1)S(1)}, u32[]{:S(2)}, u32[]{:S(2)}) %collective-permute-start.9) | collective-permute-done | bytes 196640 | tf_op jit(solution)/shard_map/ppermute | solution.py:12
  87.3 7.5 %bottom_out.1 = bf16[8,2,6,8,128]{4,3,2,1,0:T(8,128)(2,1)} custom-call(s32[5]{0:T(128)S(1)} %pad_add_fusion.place_ref, bf16[8,8,6,4,128]{4,3,2,1,0:T(4,128)(2,1)S(1)} %all-to-all-done.1.field_ref, bf16[8,8,6,2,128]{4,3,2,1,0:T(2,128)(2,1)S(1)} %collective-permute-done.8.y_in_ref, bf16[8,8,6,2,128]{4,3,2,1,0:T(2,128)(2,1)S(1)} %collective-permute-done.9.y_out_ref, ...), custom_call_target="tpu_custom_call" | custom-call | tf_op jit(solution)/shard_map/bottom_out/pallas_call | solution.py:421
  94.8 3.4 %all-to-all-start.2 = ((bf16[8,2,6,8,128]{4,3,2,1,0:T(8,128)(2,1)}), bf16[8,2,6,8,128]{4,3,2,1,0:T(8,128)(2,1)S(1)}, u32[]{:S(2)}, u32[]{:S(2)}) async-start(bf16[8,2,6,8,128]{4,3,2,1,0:T(8,128)(2,1)} %bottom_out.1), calls=%async_computation.2 | async-start | bytes 393216 | tf_op jit(solution)/shard_map/all_to_all | solution.py:550
  98.2 0.7 collective-permute-start.14
  98.9 0.1 copy.21.skip_ref
  99.0 3.3 %collective-permute-done.14 = bf16[6,10,256]{2,1,0:T(8,128)(2,1)S(1)} collective-permute-done((bf16[6,10,256]{2,1,0:T(8,128)(2,1)S(1)}, bf16[6,10,256]{2,1,0:T(8,128)(2,1)S(1)}, u32[]{:S(2)}, u32[]{:S(2)}) %collective-permute-start.14) | collective-permute-done | bytes 30752 | tf_op jit(solution)/shard_map/ppermute | solution.py:530
  102.4 4.2 %all-to-all-done.2.bottom_ref = bf16[8,2,6,8,128]{4,3,2,1,0:T(8,128)(2,1)S(1)} async-done(((bf16[8,2,6,8,128]{4,3,2,1,0:T(8,128)(2,1)}), bf16[8,2,6,8,128]{4,3,2,1,0:T(8,128)(2,1)S(1)}, u32[]{:S(2)}, u32[]{:S(2)}) %all-to-all-start.2) | async-done | bytes 196640 | tf_op jit(solution)/shard_map/all_to_all | solution.py:550
  106.6 8.2 %decode.1 = bf16[4,8,8,256]{3,2,1,0:T(8,128)(2,1)} custom-call(s32[5]{0:T(128)S(1)} %pad_add_fusion.place_ref, bf16[8,2,6,8,128]{4,3,2,1,0:T(8,128)(2,1)S(1)} %all-to-all-done.2.bottom_ref, bf16[6,10,8,256]{3,2,1,0:T(8,128)(2,1)S(1)} %copy.21.skip_ref, bf16[6,16,256]{2,1,0:T(8,128)(2,1)S(1)} %pad.14.edge_ref, bf16[9,3,768,256]{3,2,1,0:T(8,128)(2,1)} %bitcast.17), custom_call_target="tpu_custom_call" | custom-call | tf_op jit(solution)/shard_map/decode/pallas_call | solution.py:502
  (22 shorter events, 0.2 us)
Async XLA Ops:
  0.0 17.1 %copy-start = (bf16[8,16,16,128]{3,2,1,0:T(8,128)(2,1)S(1)}, bf16[8,16,16,128]{3,2,1,0:T(8,128)(2,1)}, u32[]{:S(2)}) copy-start(bf16[8,16,16,128]{3,2,1,0:T(8,128)(2,1)} %own_hbm.1) | copy-start | bytes 1572868
  1.1 10.6 %collective-permute-start = (bf16[3,16,16,128]{3,2,1,0:T(8,128)(2,1)S(1)}, bf16[3,16,16,128]{3,2,1,0:T(8,128)(2,1)S(1)}, u32[]{:S(2)}, u32[]{:S(2)}) collective-permute-start(bf16[3,16,16,128]{3,2,1,0:T(8,128)(2,1)S(1)} %get-tuple-element.25), channel_id=1, source_target_pairs={{0,16},{16,0},{32,48},{48,32},{64,80},{80,64},{96,112},{112,96},{1... | collective-permute-start | bytes 589832 | tf_op jit(solution)/shard_map/ppermute | solution.py:12
  4.3 12.8 %collective-permute-start.1 = (bf16[3,16,16,128]{3,2,1,0:T(8,128)(2,1)S(1)}, bf16[3,16,16,128]{3,2,1,0:T(8,128)(2,1)S(1)}, u32[]{:S(2)}, u32[]{:S(2)}) collective-permute-start(bf16[3,16,16,128]{3,2,1,0:T(8,128)(2,1)S(1)} %get-tuple-element.24), channel_id=1, source_target_pairs={{0,112},{16,32},{32,16},{48,64},{64,48},{80,96},{96,80},{112,0},{1... | collective-permute-start | bytes 589832 | tf_op jit(solution)/shard_map/ppermute | solution.py:12
  18.0 23.2 %copy-start.1 = (bf16[3,3,3,128,256]{4,3,2,1,0:T(8,128)(2,1)S(1)}, bf16[3,3,3,128,256]{4,3,2,1,0:T(8,128)(2,1)}, u32[]{:S(2)}) copy-start(bf16[3,3,3,128,256]{4,3,2,1,0:T(8,128)(2,1)} %param.8) | copy-start | bytes 5308420
  18.0 3.2 %collective-permute-start.2 = (bf16[14,3,16,128]{3,2,1,0:T(8,128)(2,1)S(1)}, bf16[14,3,16,128]{3,2,1,0:T(8,128)(2,1)S(1)}, u32[]{:S(2)}, u32[]{:S(2)}) collective-permute-start(bf16[14,3,16,128]{3,2,1,0:T(8,128)(2,1)S(1)} %get-tuple-element.15), channel_id=1, source_target_pairs={{0,2},{2,0},{4,6},{6,4},{8,10},{10,8},{12,14},{14,12},{1,3},{3,1},... | collective-permute-start | bytes 516104 | tf_op jit(solution)/shard_map/ppermute | solution.py:12
  18.1 6.2 %collective-permute-start.3 = (bf16[14,3,16,128]{3,2,1,0:T(8,128)(2,1)S(1)}, bf16[14,3,16,128]{3,2,1,0:T(8,128)(2,1)S(1)}, u32[]{:S(2)}, u32[]{:S(2)}) collective-permute-start(bf16[14,3,16,128]{3,2,1,0:T(8,128)(2,1)S(1)} %get-tuple-element.16), channel_id=1, source_target_pairs={{0,14},{2,4},{4,2},{6,8},{8,6},{10,12},{12,10},{14,0},{1,15},{3,5}... | collective-permute-start | bytes 516104 | tf_op jit(solution)/shard_map/ppermute | solution.py:12
  25.0 4.6 %collective-permute-start.4 = (bf16[14,22,128]{2,1,0:T(8,128)(2,1)S(1)}, bf16[14,22,128]{2,1,0:T(8,128)(2,1)S(1)}, u32[]{:S(2)}, u32[]{:S(2)}) collective-permute-start(bf16[14,22,128]{2,1,0:T(8,128)(2,1)S(1)} %pack_z.1), channel_id=1, source_target_pairs={{0,1},{1,0},{2,3},{3,2},{4,5},{5,4},{6,7},{7,6},{8,9},{9,8},{10,11... | collective-permute-start | bytes 236552 | tf_op jit(solution)/shard_map/ppermute | solution.py:536
  37.3 3.9 %collective-permute-start.5 = (bf16[6,10,128]{2,1,0:T(8,128)(2,1)S(1)}, bf16[6,10,128]{2,1,0:T(8,128)(2,1)S(1)}, u32[]{:S(2)}, u32[]{:S(2)}) collective-permute-start(bf16[6,10,128]{2,1,0:T(8,128)(2,1)S(1)} %fusion.4), channel_id=1, source_target_pairs={{0,1},{1,0},{2,3},{3,2},{4,5},{5,4},{6,7},{7,6},{8,9},{9,8},{10,11... | collective-permute-start | bytes 46088 | tf_op jit(solution)/shard_map/ppermute | solution.py:530
  42.6 4.3 %collective-permute-start.6 = (bf16[2,4,1,256]{3,1,0,2:T(4,128)(2,1)S(1)}, bf16[2,4,1,256]{3,1,0,2:T(4,128)(2,1)S(1)}, u32[]{:S(2)}, u32[]{:S(2)}) collective-permute-start(bf16[2,4,1,256]{3,1,0,2:T(4,128)(2,1)S(1)} %get-tuple-element.40), channel_id=1, source_target_pairs={{0,14},{2,4},{4,2},{6,8},{8,6},{10,12},{12,10},{14,0},{1,15},{3,5}... | collective-permute-start | bytes 12296 | tf_op jit(solution)/shard_map/ppermute | solution.py:12
  43.6 3.3 %collective-permute-start.7 = (bf16[2,4,1,256]{3,1,0,2:T(4,128)(2,1)S(1)}, bf16[2,4,1,256]{3,1,0,2:T(4,128)(2,1)S(1)}, u32[]{:S(2)}, u32[]{:S(2)}) collective-permute-start(bf16[2,4,1,256]{3,1,0,2:T(4,128)(2,1)S(1)} %get-tuple-element.41), channel_id=1, source_target_pairs={{0,2},{2,0},{4,6},{6,4},{8,10},{10,8},{12,14},{14,12},{1,3},{3,1},... | collective-permute-start | bytes 12296 | tf_op jit(solution)/shard_map/ppermute | solution.py:12
  47.8 15.0 %all-to-all-start = ((bf16[16,2,24,256]{3,2,1,0:T(8,128)(2,1)}), bf16[16,2,24,256]{3,2,1,0:T(8,128)(2,1)S(1)}, u32[]{:S(2)}, u32[]{:S(2)}) async-start(bf16[16,2,24,256]{3,2,1,0:T(8,128)(2,1)} %broadcast_in_dim.16), calls=%async_computation | async-start | bytes 786432 | tf_op jit(solution)/shard_map/all_to_all | solution.py:545
  53.1 17.6 %collective-permute-start.10 = (bf16[1,8,8,256]{3,1,0,2:T(8,128)(2,1)S(1)}, bf16[1,8,8,256]{3,1,0,2:T(8,128)(2,1)S(1)}, u32[]{:S(2)}, u32[]{:S(2)}) collective-permute-start(bf16[1,8,8,256]{3,1,0,2:T(8,128)(2,1)S(1)} %get-tuple-element.28), channel_id=1, source_target_pairs={{0,112},{16,32},{32,16},{48,64},{64,48},{80,96},{96,80},{112,0},{1... | collective-permute-start | bytes 98312 | tf_op jit(solution)/shard_map/ppermute | solution.py:12
  58.7 12.0 %collective-permute-start.11 = (bf16[1,8,8,256]{3,1,0,2:T(8,128)(2,1)S(1)}, bf16[1,8,8,256]{3,1,0,2:T(8,128)(2,1)S(1)}, u32[]{:S(2)}, u32[]{:S(2)}) collective-permute-start(bf16[1,8,8,256]{3,1,0,2:T(8,128)(2,1)S(1)} %get-tuple-element.29), channel_id=1, source_target_pairs={{0,16},{16,0},{32,48},{48,32},{64,80},{80,64},{96,112},{112,96},{1... | collective-permute-start | bytes 98312 | tf_op jit(solution)/shard_map/ppermute | solution.py:12
  67.3 12.9 %all-to-all-start.1 = ((bf16[8,8,6,4,128]{4,3,2,1,0:T(4,128)(2,1)}), bf16[8,8,6,4,128]{4,3,2,1,0:T(4,128)(2,1)S(1)}, u32[]{:S(2)}, u32[]{:S(2)}) async-start(bf16[8,8,6,4,128]{4,3,2,1,0:T(4,128)(2,1)} %bottom_in.1), calls=%async_computation.1 | async-start | bytes 786432 | tf_op jit(solution)/shard_map/all_to_all | solution.py:547
  71.0 12.4 %collective-permute-start.13 = (bf16[6,1,8,256]{3,1,0,2:T(2,128)(2,1)S(1)}, bf16[6,1,8,256]{3,1,0,2:T(2,128)(2,1)S(1)}, u32[]{:S(2)}, u32[]{:S(2)}) collective-permute-start(bf16[6,1,8,256]{3,1,0,2:T(2,128)(2,1)S(1)} %broadcast_select_fusion.7), channel_id=1, source_target_pairs={{0,2},{2,0},{4,6},{6,4},{8,10},{10,8},{12,14},{14,12},{1,3},{3,1},... | collective-permute-start | bytes 73736 | tf_op jit(solution)/shard_map/ppermute | solution.py:12
  71.1 12.3 %collective-permute-start.12 = (bf16[6,1,8,256]{3,1,0,2:T(2,128)(2,1)S(1)}, bf16[6,1,8,256]{3,1,0,2:T(2,128)(2,1)S(1)}, u32[]{:S(2)}, u32[]{:S(2)}) collective-permute-start(bf16[6,1,8,256]{3,1,0,2:T(2,128)(2,1)S(1)} %get-tuple-element.21), channel_id=1, source_target_pairs={{0,14},{2,4},{4,2},{6,8},{8,6},{10,12},{12,10},{14,0},{1,15},{3,5}... | collective-permute-start | bytes 73736 | tf_op jit(solution)/shard_map/ppermute | solution.py:12
  80.6 3.1 %collective-permute-start.8 = (bf16[8,8,6,2,128]{4,3,2,1,0:T(2,128)(2,1)S(1)}, bf16[8,8,6,2,128]{4,3,2,1,0:T(2,128)(2,1)S(1)}, u32[]{:S(2)}, u32[]{:S(2)}) collective-permute-start(bf16[8,8,6,2,128]{4,3,2,1,0:T(2,128)(2,1)S(1)} %get-tuple-element.27), channel_id=1, source_target_pairs={{0,2},{2,0},{4,6},{6,4},{8,10},{10,8},{12,14},{14,12},{1,3},{3,1},... | collective-permute-start | bytes 589832 | tf_op jit(solution)/shard_map/ppermute | solution.py:12
  80.7 6.6 %collective-permute-start.9 = (bf16[8,8,6,2,128]{4,3,2,1,0:T(2,128)(2,1)S(1)}, bf16[8,8,6,2,128]{4,3,2,1,0:T(2,128)(2,1)S(1)}, u32[]{:S(2)}, u32[]{:S(2)}) collective-permute-start(bf16[8,8,6,2,128]{4,3,2,1,0:T(2,128)(2,1)S(1)} %get-tuple-element.26), channel_id=1, source_target_pairs={{0,14},{2,4},{4,2},{6,8},{8,6},{10,12},{12,10},{14,0},{1,15},{3,5}... | collective-permute-start | bytes 589832 | tf_op jit(solution)/shard_map/ppermute | solution.py:12
  94.8 11.8 %all-to-all-start.2 = ((bf16[8,2,6,8,128]{4,3,2,1,0:T(8,128)(2,1)}), bf16[8,2,6,8,128]{4,3,2,1,0:T(8,128)(2,1)S(1)}, u32[]{:S(2)}, u32[]{:S(2)}) async-start(bf16[8,2,6,8,128]{4,3,2,1,0:T(8,128)(2,1)} %bottom_out.1), calls=%async_computation.2 | async-start | bytes 393216 | tf_op jit(solution)/shard_map/all_to_all | solution.py:550
  98.2 4.2 %collective-permute-start.14 = (bf16[6,10,256]{2,1,0:T(8,128)(2,1)S(1)}, bf16[6,10,256]{2,1,0:T(8,128)(2,1)S(1)}, u32[]{:S(2)}, u32[]{:S(2)}) collective-permute-start(bf16[6,10,256]{2,1,0:T(8,128)(2,1)S(1)} %fusion.3), channel_id=1, source_target_pairs={{0,1},{1,0},{2,3},{3,2},{4,5},{5,4},{6,7},{7,6},{8,9},{9,8},{10,11... | collective-permute-start | bytes 92168 | tf_op jit(solution)/shard_map/ppermute | solution.py:530

commit v7 on v6

--- a/solution.py
+++ b/solution.py
@@ -126,7 +126,9 @@
         sems,
     ):
         inner = field_ref.at[reach : reach + own_x, reach : reach + own_y]
-        copies = [pltpu.make_async_copy(own_hbm, inner, sems.at[0]), pltpu.make_async_copy(weights_hbm, weights_ref, sems.at[1])]
+        copies = [pltpu.make_async_copy(own_hbm, inner, sems.at[0])]
+        for tap in range(3):
+            copies.append(pltpu.make_async_copy(weights_hbm.at[:, :, tap], weights_ref.at[tap], sems.at[1 + tap]))
         for copy in copies:
             copy.start()
         even_x, even_y = place_ref[0] % 2 == 0, place_ref[1] % 2 == 0
@@ -158,8 +160,7 @@
                 side_ref[dy, x, size_y:] = jnp.zeros((extra - size_y, channels), jnp.float32)
 
         first = place_ref[2] == 0
-        for copy in copies:
-            copy.wait()
+        copies[0].wait()
         line = lax.broadcasted_iota(jnp.int32, (pool_y, pool_z, filters), 0)
         inside_y = ((line > 0) | low_y) & ((line < pool_y - 1) | high_y)
         for pair in range(size_x // 2):
@@ -172,7 +173,9 @@
             block = jnp.concatenate(blocks, axis=1)
             sums = []
             for tap in range(3):
-                kernel = weights_ref[:, :, tap].reshape(12 * channels, 2 * filters)
+                if pair == 0:
+                    copies[1 + tap].wait()
+                kernel = weights_ref[tap].reshape(12 * channels, 2 * filters)
                 sums.append(jnp.dot(block, kernel, preferred_element_type=jnp.float32))
             total = jnp.maximum(join_taps(first, sums, size_y, size_z), 0.0)
             total = jnp.maximum(total[..., :filters], total[..., filters:])
@@ -199,21 +202,69 @@
             pltpu.VMEM((full_x, full_y, size_z, channels), jnp.bfloat16),
             pltpu.VMEM((3, full_x, extra, channels), jnp.float32),
             pltpu.VMEM((pool_y * size_z, filters), jnp.float32),
-            pltpu.VMEM(weights.shape, weights.dtype),
-            pltpu.SemaphoreType.DMA((2,)),
+            pltpu.VMEM((3, 4, 3, channels, 2 * filters), weights.dtype),
+            pltpu.SemaphoreType.DMA((4,)),
         ],
         compiler_params=pltpu.CompilerParams(vmem_limit_bytes=20 << 20),
         name="encode",
     )(place, far(own), x_in, x_out, y_in, y_out, edge, far(weights))
 
 
-def paired(weights):
-    grow = [(0, 0)] * 4
-    return jnp.concatenate([jnp.pad(weights, [(0, 1)] + grow), jnp.pad(weights, [(1, 0)] + grow)], axis=4)
-
-
 def far(array):
     return pltpu.with_memory_space_constraint(array, pltpu.HBM)
+
+
+def prepare(w_full, w_in, w_out):
+    channels, filters = w_full.shape[3:]
+    depths = [w.shape[4] for w in (w_in, w_out)]
+
+    def body(
+        full_hbm, in_hbm, out_hbm, pair_hbm, to_in_hbm, to_out_hbm, full_ref, pair_ref, in_ref, out_ref, to_in_ref, to_out_ref, sems
+    ):
+        first = pltpu.make_async_copy(full_hbm, full_ref, sems.at[0])
+        first.start()
+        jobs = []
+        for order, (hbm, ref) in enumerate(((in_hbm, in_ref), (out_hbm, out_ref))):
+            copies = []
+            for step in range(9):
+                for dy in range(3):
+                    to = ref.at[step, pl.ds(64 * dy, 64)]
+                    sem = sems.at[1 + 27 * order + 3 * step + dy]
+                    copies.append(pltpu.make_async_copy(hbm.at[step // 3, dy, step % 3], to, sem))
+                    copies[-1].start()
+            jobs.append(copies)
+        first.wait()
+        zero = jnp.zeros((3, 3, channels, filters), jnp.bfloat16)
+        results = []
+        for plane in range(4):
+            pair_ref[plane, :, :, :, :filters] = full_ref[plane] if plane < 3 else zero
+            pair_ref[plane, :, :, :, filters:] = full_ref[plane - 1] if plane > 0 else zero
+            results.append(pltpu.make_async_copy(pair_ref.at[plane], pair_hbm.at[plane], sems.at[55 + plane]))
+            results[-1].start()
+        for order, (ref, to_ref, to_hbm) in enumerate(((in_ref, to_in_ref, to_in_hbm), (out_ref, to_out_ref, to_out_hbm))):
+            for step in range(9):
+                ref[step, 192:] = jnp.zeros((64, depths[order]), jnp.bfloat16)
+                for copy in jobs[order][3 * step : 3 * step + 3]:
+                    copy.wait()
+                to_ref[step] = ref[step].T
+                results.append(pltpu.make_async_copy(to_ref.at[step], to_hbm.at[step], sems.at[59 + 9 * order + step]))
+                results[-1].start()
+        for copy in results:
+            copy.wait()
+
+    shapes = [(4, 3, 3, channels, 2 * filters)] + [(9, depth, 256) for depth in depths]
+    return pl.pallas_call(
+        body,
+        in_specs=[pl.BlockSpec(memory_space=pltpu.HBM)] * 3,
+        out_specs=[pl.BlockSpec(memory_space=pltpu.HBM)] * 3,
+        out_shape=[pltpu.HBM(shape, jnp.bfloat16) for shape in shapes],
+        scratch_shapes=[pltpu.VMEM(w_full.shape, jnp.bfloat16), pltpu.VMEM(shapes[0], jnp.bfloat16)]
+        + [pltpu.VMEM((9, 256, depth), jnp.bfloat16) for depth in depths]
+        + [pltpu.VMEM((9, depth, 256), jnp.bfloat16) for depth in depths]
+        + [pltpu.SemaphoreType.DMA((77,))],
+        compiler_params=pltpu.CompilerParams(vmem_limit_bytes=20 << 20),
+        name="prepare",
+    )(far(w_full), far(w_in), far(w_out))
 
 
 def pack_y(place, own, x_in, x_out):
@@ -292,20 +343,6 @@
     return jnp.where(lane < 64, even, pltpu.roll(odd, 64, even.ndim - 1))
 
 
-def column_weights(weights_hbm, weights_ref, sems):
-    filters, channels = weights_hbm.shape[3:]
-    weights_ref[3 * filters :] = jnp.zeros((weights_ref.shape[0] - 3 * filters, 9 * channels), weights_ref.dtype)
-    copies = []
-    for dx in range(3):
-        for dy in range(3):
-            for dz in range(3):
-                lanes = pl.ds((3 * dx + dz) * channels, channels)
-                to = weights_ref.at[pl.ds(filters * dy, filters), lanes]
-                copies.append(pltpu.make_async_copy(weights_hbm.at[dx, dy, dz], to, sems.at[9 * dx + 3 * dy + dz]))
-                copies[-1].start()
-    return copies
-
-
 def column_product(pad_ref, weights_ref, first, start, planes, size_z):
     channels = pad_ref.shape[-1]
     rows = planes * size_z * 8
@@ -315,7 +352,7 @@
             block = pad_ref[first + dx : first + dx + planes, pl.ds(start + dz, size_z)]
             blocks.append(block.reshape(rows, channels).astype(jnp.bfloat16))
     block = jnp.concatenate(blocks, axis=1)
-    total = lax.dot_general(block, weights_ref[...], (((1,), (1,)), ((), ())), preferred_element_type=jnp.float32)
+    total = jnp.dot(block, weights_ref[...].reshape(9 * channels, 256), preferred_element_type=jnp.float32)
     low = total[:, :128].reshape(planes * size_z, 8, 128)
     mid = pltpu.roll(total[:, :128], 64, 1).reshape(planes * size_z, 8, 128)
     high = total[:, 128:].reshape(planes * size_z, 8, 128)
@@ -329,8 +366,9 @@
     own_z = size_y = 4
     size_x, all_z, size_z = devices * own_x, 2 * own_z, own_z + 2
 
-    def body(place_ref, field_ref, weights_hbm, out_ref, pad_ref, weights_ref, sems):
-        copies = column_weights(weights_hbm, weights_ref, sems)
+    def body(place_ref, field_ref, weights_hbm, out_ref, pad_ref, weights_ref, sem):
+        copy = pltpu.make_async_copy(weights_hbm, weights_ref, sem)
+        copy.start()
         zero = jnp.zeros((all_z + 2, 8, channels), jnp.float32)
         pad_ref[0] = zero
         pad_ref[size_x + 1] = zero
@@ -349,8 +387,7 @@
                         pad_ref[*to, size_y + 1 : size_y + 2] = block[line : line + 1]
                         pad_ref[*to, size_y + 2 :] = zero[0, size_y + 2 :]
         start = 2 * place_ref[2]
-        for copy in copies:
-            copy.wait()
+        copy.wait()
         for first in range(0, size_x, 4):
             total = column_product(pad_ref, weights_ref, first, start, 4, size_z)
             for pair in range(2):
@@ -365,8 +402,8 @@
         out_shape=jax.ShapeDtypeStruct((devices, size_x // 2, size_z, size_y, 128), jnp.bfloat16),
         scratch_shapes=[
             pltpu.VMEM((size_x + 2, all_z + 2, 8, channels), jnp.float32),
-            pltpu.VMEM((256, 9 * channels), jnp.bfloat16),
-            pltpu.SemaphoreType.DMA((27,)),
+            pltpu.VMEM(weights.shape, weights.dtype),
+            pltpu.SemaphoreType.DMA(()),
         ],
         compiler_params=pltpu.CompilerParams(vmem_limit_bytes=12 << 20),
         name="bottom_in",
@@ -378,8 +415,9 @@
     size_x, channels = 2 * pairs, 64 * devices
     own_x = size_x // devices
 
-    def body(place_ref, field_ref, y_in_ref, y_out_ref, weights_hbm, out_ref, pad_ref, total_ref, weights_ref, sems):
-        copies = column_weights(weights_hbm, weights_ref, sems)
+    def body(place_ref, field_ref, y_in_ref, y_out_ref, weights_hbm, out_ref, pad_ref, total_ref, weights_ref, sem):
+        copy = pltpu.make_async_copy(weights_hbm, weights_ref, sem)
+        copy.start()
         even_y = place_ref[1] % 2 == 0
         low_y, high_y = place_ref[1] > 0, place_ref[1] < place_ref[4]
         zero = jnp.zeros((size_z + 2, 8, channels), jnp.float32)
@@ -404,8 +442,7 @@
                     lines = slice(line, line + even.shape[1])
                     pad_ref[1 + 2 * pair, 1 : size_z + 1, lines, 128 * k : 128 * k + 128] = even
                     pad_ref[2 + 2 * pair, 1 : size_z + 1, lines, 128 * k : 128 * k + 128] = odd
-        for copy in copies:
-            copy.wait()
+        copy.wait()
         for first in range(0, size_x, 4):
             total = column_product(pad_ref, weights_ref, first, 0, 4, size_z)
             total_ref[1 + first : 5 + first, 1 : size_z + 1] = total
@@ -428,24 +465,81 @@
         scratch_shapes=[
             pltpu.VMEM((size_x + 2, size_z + 2, 8, channels), jnp.float32),
             pltpu.VMEM((size_x + 2, size_z + 2, 8, 128), jnp.float32),
-            pltpu.VMEM((256, 9 * channels), jnp.bfloat16),
-            pltpu.SemaphoreType.DMA((27,)),
+            pltpu.VMEM(weights.shape, weights.dtype),
+            pltpu.SemaphoreType.DMA(()),
         ],
         compiler_params=pltpu.CompilerParams(vmem_limit_bytes=20 << 20),
         name="bottom_out",
     )(place, field, y_in, y_out, far(weights))
 
 
-def decode(place, bottom, skip, edge, weights):
+def decode_skip(place, skip, edge, weights):
+    full_x, full_y, size_z, channels = skip.shape
+    size_x, size_y = full_x - 2, full_y - 2
+    filters = weights.shape[-1]
+    deep = weights.shape[2] - channels
+    rows, extra = size_x * size_y * size_z, size_x * size_y
+
+    def body(skip_ref, edge_ref, weights_hbm, out_ref, *refs):
+        rest_refs, (weights_ref, sems) = refs[:3], refs[3:]
+        copies = [
+            pltpu.make_async_copy(weights_hbm.at[step, :, pl.ds(deep, channels)], weights_ref.at[step], sems.at[step])
+            for step in range(9)
+        ]
+        rest = [
+            pltpu.make_async_copy(weights_hbm.at[step, :, pl.ds(0, deep)], rest_refs[step], sems.at[9 + step])
+            for step in range(3)
+        ]
+        for copy in copies + rest:
+            copy.start()
+        edge_plane = edge_ref[...].astype(jnp.float32)
+        blocks = []
+        for dx in range(3):
+            for dy in range(3):
+                main = skip_ref[dx : dx + size_x, dy : dy + size_y].astype(jnp.float32).reshape(rows, channels)
+                side = edge_plane[dx : dx + size_x, dy : dy + size_y].reshape(extra, channels)
+                blocks.append(jnp.concatenate([main, side], axis=0).astype(jnp.bfloat16))
+        for copy in copies:
+            copy.wait()
+        block = jnp.concatenate(blocks, axis=1)
+        for tap in range(3):
+            kernel = weights_ref[:, tap].reshape(9 * channels, filters)
+            out_ref[tap] = jnp.dot(block, kernel, preferred_element_type=jnp.float32)
+        for copy in rest:
+            copy.wait()
+
+    return pl.pallas_call(
+        body,
+        in_specs=[pl.BlockSpec(memory_space=pltpu.VMEM)] * 2 + [pl.BlockSpec(memory_space=pltpu.HBM)],
+        out_specs=[pl.BlockSpec(memory_space=pltpu.VMEM)] * 4,
+        out_shape=[
+            pltpu.VMEM((3, rows + extra, filters), jnp.float32),
+        ]
+        + [pltpu.VMEM((3, deep, filters), jnp.bfloat16)] * 3,
+        scratch_shapes=[pltpu.VMEM((9, 3, channels, filters), jnp.bfloat16), pltpu.SemaphoreType.DMA((12,))],
+        compiler_params=pltpu.CompilerParams(vmem_limit_bytes=14 << 20),
+        name="decode_skip",
+    )(skip, edge, far(weights))
+
+
+def near(array):
+    return pltpu.with_memory_space_constraint(array, pltpu.VMEM)
+
+
+def decode(place, bottom, skip_sums, first_weights, weights, shape):
     devices, pairs, coarse_z, _, _ = bottom.shape
-    full_x, full_y, size_z, skip_channels = skip.shape
-    size_x, size_y = full_x - 2, full_y - 2
-    channels = 64 * devices + skip_channels
+    size_x, size_y, size_z = shape
+    full_x, full_y = size_x + 2, size_y + 2
+    channels = 64 * devices
     filters = weights.shape[-1]
     rows, extra = size_x * size_y * size_z, size_x * size_y
 
-    def body(place_ref, bottom_ref, skip_ref, edge_ref, weights_hbm, out_ref, main_ref, side_ref, sums_ref, weights_ref, sems):
-        copies = [pltpu.make_async_copy(weights_hbm.at[step], weights_ref.at[step], sems.at[step]) for step in range(9)]
+    def body(place_ref, bottom_ref, skip_ref, *refs):
+        near_refs, (weights_hbm, out_ref, main_ref, side_ref, sums_ref, weights_ref, sems) = refs[:3], refs[3:]
+        copies = [
+            pltpu.make_async_copy(weights_hbm.at[3 + step, :, pl.ds(0, channels)], weights_ref.at[step], sems.at[step])
+            for step in range(6)
+        ]
         for copy in copies:
             copy.start()
         first = place_ref[2] == 0
@@ -476,33 +570,32 @@
             for x in range(full_x):
                 if (x + 1) // 2 != plane:
                     continue
-                joined = jnp.concatenate([fine, skip_ref[x].astype(jnp.float32).reshape(full_y * size_z, skip_channels)], axis=1)
-                joined_edge = jnp.concatenate([fine_edge, edge_ref[x].astype(jnp.float32)], axis=1)
                 for dy in range(3):
-                    main_ref[dy, x] = joined[8 * dy : 8 * dy + size_y * size_z].astype(jnp.bfloat16)
-                    side_ref[dy, x] = joined_edge[dy : dy + size_y]
+                    main_ref[dy, x] = fine[8 * dy : 8 * dy + size_y * size_z].astype(jnp.bfloat16)
+                    side_ref[dy, x] = fine_edge[dy : dy + size_y]
         for dx in range(3):
             blocks = []
             for dy in range(3):
                 main = main_ref[dy, dx : dx + size_x].reshape(rows, channels)
                 side = side_ref[dy, dx : dx + size_x].reshape(extra, channels).astype(jnp.bfloat16)
                 blocks.append(jnp.concatenate([main, side], axis=0))
-                copies[3 * dx + dy].wait()
+                if dx:
+                    copies[3 * dx + dy - 3].wait()
             block = jnp.concatenate(blocks, axis=1)
             for tap in range(3):
-                kernel = weights_ref[3 * dx : 3 * dx + 3, tap].reshape(3 * channels, filters)
-                product = jnp.dot(block, kernel, preferred_element_type=jnp.float32)
                 if dx == 0:
-                    sums_ref[tap] = product
+                    kernel = jnp.concatenate([ref[tap] for ref in near_refs], axis=0)
+                    sums_ref[tap] = skip_ref[tap] + jnp.dot(block, kernel, preferred_element_type=jnp.float32)
                 else:
-                    sums_ref[tap] += product
+                    kernel = weights_ref[3 * dx - 3 : 3 * dx, tap].reshape(3 * channels, filters)
+                    sums_ref[tap] += jnp.dot(block, kernel, preferred_element_type=jnp.float32)
         total = join_taps(first, [sums_ref[tap] for tap in range(3)], extra, size_z)
         out_ref[...] = total.reshape(size_x, size_y, size_z, filters).astype(out_ref.dtype)
 
     return pl.pallas_call(
         body,
         in_specs=[pl.BlockSpec(memory_space=pltpu.SMEM)]
-        + [pl.BlockSpec(memory_space=pltpu.VMEM)] * 3
+        + [pl.BlockSpec(memory_space=pltpu.VMEM)] * 5
         + [pl.BlockSpec(memory_space=pltpu.HBM)],
         out_specs=pl.BlockSpec(memory_space=pltpu.VMEM),
         out_shape=jax.ShapeDtypeStruct((size_x, size_y, size_z, filters), jnp.bfloat16),
@@ -510,12 +603,12 @@
             pltpu.VMEM((3, full_x, size_y * size_z, channels), jnp.bfloat16),
             pltpu.VMEM((3, full_x, size_y, channels), jnp.float32),
             pltpu.VMEM((3, rows + extra, filters), jnp.float32),
-            pltpu.VMEM(weights.shape, weights.dtype),
-            pltpu.SemaphoreType.DMA((9,)),
+            pltpu.VMEM((6, 3, channels, filters), jnp.bfloat16),
+            pltpu.SemaphoreType.DMA((6,)),
         ],
-        compiler_params=pltpu.CompilerParams(vmem_limit_bytes=26 << 20),
+        compiler_params=pltpu.CompilerParams(vmem_limit_bytes=20 << 20),
         name="decode",
-    )(place, bottom, skip, edge, far(weights))
+    )(place, bottom, near(skip_sums), *map(near, first_weights), far(weights))
 
 
 def solution(mesh):
@@ -530,7 +623,8 @@
             return lax.ppermute(jnp.where(place_z == 0, plane_high, plane_low), "gz", swap)
 
         x_in, x_out = swaps(volume[:3], volume[-3:], "gx", gx)
-        w_pair, x_in, x_out = lax.optimization_barrier((paired(w_full), x_in, x_out))
+        turned = [w.transpose(0, 1, 2, 4, 3) for w in (w_bottom_in, w_bottom_out)]
+        (w_pair, w_in, w_out), x_in, x_out = lax.optimization_barrier((prepare(w_full, *turned), x_in, x_out))
         y_inner, y_outer, plane = pack_y(place, volume, x_in, x_out)
         y_in, y_out = send(y_inner, y_outer, "gy", gy)
         edge = lax.ppermute(pack_z(place, plane, y_in, y_out), "gz", swap)
@@ -543,17 +637,18 @@
         column = jnp.concatenate([coarse, below[:, :, 0], above[:, :, 0]], axis=1)
         column = jnp.broadcast_to(column[None], (gx * gz,) + column.shape)
         column = lax.all_to_all(column, ("gx", "gz"), 0, 0)
-        first = bottom_in(place, column, w_bottom_in.transpose(0, 1, 2, 4, 3))
+        first = bottom_in(place, column, w_in)
         first = lax.all_to_all(first, "gx", 0, 0)
         y_in, y_out = swaps(first[:, :, :, :2], first[:, :, :, -2:], "gy", gy)
-        second = bottom_out(place, first, y_in, y_out, w_bottom_out.transpose(0, 1, 2, 4, 3))
-        second = lax.all_to_all(second, "gx", 0, 0)
-
         around = extend(skip, "gx", gx, 0, 1)
         around = extend(around, "gy", gy, 1, 1)
         side = edge_of(around[:, :, 0], around[:, :, -1])
-        side = jnp.pad(side, ((0, 0), (0, -side.shape[1] % 16), (0, 0)))
-        return decode(place, second, around, side, w_up.reshape(9, 3, w_up.shape[3], w_up.shape[4]))
+        y_in, y_out, around, side = lax.optimization_barrier((y_in, y_out, around, side))
+        second = bottom_out(place, first, y_in, y_out, w_out)
+        second = lax.all_to_all(second, "gx", 0, 0)
+        w_up = w_up.reshape(9, 3, w_up.shape[3], w_up.shape[4])
+        skip_sums, *w_near = decode_skip(place, around, side, w_up)
+        return decode(place, second, skip_sums, w_near, w_up, skip.shape[:3])
 
     space = P("gx", "gy", "gz", None)
     filters = P(None, None, None, None, "gx")

time: 116 us -> 112 us (0.966)
  Pallas kernels: 30.7 us -> 35.2 us
  starting transfers between devices: 38.5 us -> 34.2 us
  other arithmetic: 5.57 us -> 2.25 us
    pallas_call x0 -> x2, Pallas kernels: none -> 8.14 us  [the longest x1 4.88 us: prepare(): pl.pallas_call(body, in_specs=[pl.BlockSpec(memory_space=pltpu.HBM)] * 3,...]
    ppermute x6, waiting for transfers between devices: 15.3 us -> 8.66 us  [send(): lax.ppermute(outer_block, axis, outer)]
    ppermute x6, starting transfers between devices: 19.1 us -> 14.4 us  [send(): lax.ppermute(outer_block, axis, outer)]
    all_to_all x1, waiting for transfers between devices: 4.02 us -> 7.35 us  [local(): column = lax.all_to_all(column, ('gx', 'gz'), 0, 0)]
    concatenate x1 -> x0, other arithmetic: 3.32 us -> none  [paired(): jnp.concatenate([jnp.pad(weights, [(0, 1)] + grow), jnp.pad(weights, [(1,...]
    all_to_all x1, waiting for transfers between devices: 6.42 us -> 9.04 us  [local(): first = lax.all_to_all(first, 'gx', 0, 0)]
    pallas_call x1, Pallas kernels: 8.19 us -> 6.06 us  [decode(): pl.pallas_call(body, in_specs=[pl.BlockSpec(memory_space=pltpu.SMEM)] + [...]
    pallas_call x1, Pallas kernels: 7.48 us -> 6.19 us  [bottom_out(): pl.pallas_call(body, in_specs=[pl.BlockSpec(memory_space=pltpu.SMEM)] + [...]
  transfers between devices with their start and end apart: 18 -> 18, of which waited for: 10 -> 10; matrix products, arithmetic and copies ran while one was open for 4% -> 1% of each run, Pallas kernels for 4% -> 11%
where the time goes in v7:
time: 112 us
  waiting for transfers between devices  38.9 us (35%)
  Pallas kernels  35.2 us (31%)
  starting transfers between devices  34.2 us (31%)
  other arithmetic  2.25 us (2%)
    ppermute x6, starting transfers between devices, send(): lax.ppermute(outer_block, axis, outer)  14.4 us
    all_to_all x1, waiting for transfers between devices, local(): first = lax.all_to_all(first, 'gx', 0, 0)  9.04 us
    ppermute x6, waiting for transfers between devices, send(): lax.ppermute(outer_block, axis, outer)  8.66 us
    pallas_call x1, Pallas kernels, encode(): pl.pallas_call(body, in_specs=[pl.BlockSpec(memory_space=pltpu.SMEM), pl....  8.03 us
    all_to_all x1, waiting for transfers between devices, local(): column = lax.all_to_all(column, ('gx', 'gz'), 0, 0)  7.35 us
    pallas_call x1, Pallas kernels, bottom_out(): pl.pallas_call(body, in_specs=[pl.BlockSpec(memory_space=pltpu.SMEM)] + [...  6.19 us
    pallas_call x1, Pallas kernels, decode(): pl.pallas_call(body, in_specs=[pl.BlockSpec(memory_space=pltpu.SMEM)] + [...  6.06 us
    ppermute x2, waiting for transfers between devices, edge_of(): lax.ppermute(jnp.where(place_z == 0, plane_high, plane_low), 'gz', swap)  5.82 us
  transfers between devices with their start and end apart: 18, of which 10 were waited for; matrix products, arithmetic and copies ran while one was open for 1% of the time, Pallas kernels for 11%

profile of v7, /device:TPU:0, one launch (start us, length us, event | category | flops | bytes accessed | tf_op | source)
XLA Modules:
  0.0 111.9 jit_solution(13228030828422411852)
XLA Ops:
  0.0 1.1 broadcast_select_fusion.2
  1.1 3.2 %collective-permute-start = (bf16[3,16,16,128]{3,2,1,0:T(8,128)(2,1)S(1)}, bf16[3,16,16,128]{3,2,1,0:T(8,128)(2,1)S(1)}, u32[]{:S(2)}, u32[]{:S(2)}) collective-permute-start(bf16[3,16,16,128]{3,2,1,0:T(8,128)(2,1)S(1)} %get-tuple-element.51), channel_id=1, source_target_pairs={{0,16},{16,0},{32,48},{48,32},{64,80},{80,64},{96,112},{112,96},{1... | collective-permute-start | bytes 589832 | tf_op jit(solution)/shard_map/ppermute | solution.py:12
  4.3 4.0 %collective-permute-start.1 = (bf16[3,16,16,128]{3,2,1,0:T(8,128)(2,1)S(1)}, bf16[3,16,16,128]{3,2,1,0:T(8,128)(2,1)S(1)}, u32[]{:S(2)}, u32[]{:S(2)}) collective-permute-start(bf16[3,16,16,128]{3,2,1,0:T(8,128)(2,1)S(1)} %get-tuple-element.50), channel_id=1, source_target_pairs={{0,112},{16,32},{32,16},{48,64},{64,48},{80,96},{96,80},{112,0},{1... | collective-permute-start | bytes 589832 | tf_op jit(solution)/shard_map/ppermute | solution.py:12
  8.3 4.9 %prepare.1 = (bf16[4,3,3,128,256]{4,3,2,1,0:T(8,128)(2,1)}, bf16[9,256,256]{2,1,0:T(8,128)(2,1)}, bf16[9,512,256]{2,1,0:T(8,128)(2,1)}) custom-call(bf16[3,3,3,128,128]{4,3,2,1,0:T(8,128)(2,1)} %full_hbm.1, bf16[3,3,3,64,256]{4,3,2,1,0:T(8,128)(2,1)} %bitcast.20, bf16[3,3,3,64,512]{4,3,2,1,0:T(8,128)(2,1)} %bitcast.19), custom_call_target="tpu_custom_call" | custom-call | tf_op jit(solution)/shard_map/prepare/pallas_call | solution.py:256
  13.2 0.1 pad_add_fusion.place_ref
  13.3 0.0 collective-permute-done.x_in_ref
  13.3 3.8 %collective-permute-done.1.x_out_ref = bf16[3,16,16,128]{3,2,1,0:T(8,128)(2,1)S(1)} collective-permute-done((bf16[3,16,16,128]{3,2,1,0:T(8,128)(2,1)S(1)}, bf16[3,16,16,128]{3,2,1,0:T(8,128)(2,1)S(1)}, u32[]{:S(2)}, u32[]{:S(2)}) %collective-permute-start.1) | collective-permute-done | bytes 196640 | tf_op jit(solution)/shard_map/ppermute | solution.py:12
  17.1 0.9 pack_y.1
  18.0 0.0 copy-start.1
  18.0 0.1 collective-permute-start.2
  18.1 3.1 %collective-permute-start.3 = (bf16[14,3,16,128]{3,2,1,0:T(8,128)(2,1)S(1)}, bf16[14,3,16,128]{3,2,1,0:T(8,128)(2,1)S(1)}, u32[]{:S(2)}, u32[]{:S(2)}) collective-permute-start(bf16[14,3,16,128]{3,2,1,0:T(8,128)(2,1)S(1)} %get-tuple-element.32), channel_id=1, source_target_pairs={{0,14},{2,4},{4,2},{6,8},{8,6},{10,12},{12,10},{14,0},{1,15},{3,5}... | collective-permute-start | bytes 516104 | tf_op jit(solution)/shard_map/ppermute | solution.py:12
  21.2 3.1 %collective-permute-done.3.y_out_ref = bf16[14,3,16,128]{3,2,1,0:T(8,128)(2,1)S(1)} collective-permute-done((bf16[14,3,16,128]{3,2,1,0:T(8,128)(2,1)S(1)}, bf16[14,3,16,128]{3,2,1,0:T(8,128)(2,1)S(1)}, u32[]{:S(2)}, u32[]{:S(2)}) %collective-permute-start.3) | collective-permute-done | bytes 172064 | tf_op jit(solution)/shard_map/ppermute | solution.py:12
  24.3 0.6 pack_z.1
  25.0 1.6 %collective-permute-start.4 = (bf16[14,22,128]{2,1,0:T(8,128)(2,1)S(1)}, bf16[14,22,128]{2,1,0:T(8,128)(2,1)S(1)}, u32[]{:S(2)}, u32[]{:S(2)}) collective-permute-start(bf16[14,22,128]{2,1,0:T(8,128)(2,1)S(1)} %pack_z.1), channel_id=1, source_target_pairs={{0,1},{1,0},{2,3},{3,2},{4,5},{5,4},{6,7},{7,6},{8,9},{9,8},{10,11... | collective-permute-start | bytes 236552 | tf_op jit(solution)/shard_map/ppermute | solution.py:630
  26.5 3.0 %collective-permute-done.4.edge_ref = bf16[14,22,128]{2,1,0:T(8,128)(2,1)S(1)} collective-permute-done((bf16[14,22,128]{2,1,0:T(8,128)(2,1)S(1)}, bf16[14,22,128]{2,1,0:T(8,128)(2,1)S(1)}, u32[]{:S(2)}, u32[]{:S(2)}) %collective-permute-start.4) | collective-permute-done | bytes 78880 | tf_op jit(solution)/shard_map/ppermute | solution.py:630
  29.5 8.0 %encode.1.field_ref = bf16[6,10,8,128]{3,2,1,0:T(8,128)(2,1)S(1)} custom-call(s32[5]{0:T(128)S(1)} %pad_add_fusion.place_ref, bf16[8,16,16,128]{3,2,1,0:T(8,128)(2,1)} %own_hbm.1, bf16[3,16,16,128]{3,2,1,0:T(8,128)(2,1)S(1)} %collective-permute-done.x_in_ref, bf16[3,16,16,128]{3,2,1,0:T(8,128)(2,1)S(1)} %collective-permute-done.1.x_out_ref, ...), custom_call_target="tpu_custom_call" | custom-call | tf_op jit(solution)/shard_map/encode/pallas_call | solution.py:194
  37.6 1.6 %collective-permute-start.5 = (bf16[6,10,128]{2,1,0:T(8,128)(2,1)S(1)}, bf16[6,10,128]{2,1,0:T(8,128)(2,1)S(1)}, u32[]{:S(2)}, u32[]{:S(2)}) collective-permute-start(bf16[6,10,128]{2,1,0:T(8,128)(2,1)S(1)} %fusion.1), channel_id=1, source_target_pairs={{0,1},{1,0},{2,3},{3,2},{4,5},{5,4},{6,7},{7,6},{8,9},{9,8},{10,11... | collective-permute-start | bytes 46088 | tf_op jit(solution)/shard_map/ppermute | solution.py:623
  39.2 2.3 %collective-permute-done.5.edge_ref = bf16[6,10,128]{2,1,0:T(8,128)(2,1)S(1)} collective-permute-done((bf16[6,10,128]{2,1,0:T(8,128)(2,1)S(1)}, bf16[6,10,128]{2,1,0:T(8,128)(2,1)S(1)}, u32[]{:S(2)}, u32[]{:S(2)}) %collective-permute-start.5) | collective-permute-done | bytes 15392 | tf_op jit(solution)/shard_map/ppermute | solution.py:623
  41.5 1.4 %half_level.1 = (bf16[4,8,8,256]{3,2,1,0:T(8,128)(2,1)S(1)}, bf16[2,16,256]{2,1,0:T(8,128)(2,1)S(1)}) custom-call(s32[5]{0:T(128)S(1)} %pad_add_fusion.place_ref, bf16[6,10,8,128]{3,2,1,0:T(8,128)(2,1)S(1)} %encode.1.field_ref, bf16[6,10,128]{2,1,0:T(8,128)(2,1)S(1)} %collective-permute-done.5.edge_ref, bf16[9,3,128,256]{3,2,1,0:T(8,128)(2,1)S(1)} %bitcast.16), custom_call_target="tpu_custom_call" | custom-call | tf_op jit(solution)/shard_map/half_level/pallas_call | solution.py:75
  43.0 1.0 collective-permute-start.6
  44.0 1.7 %collective-permute-start.10 = (bf16[1,8,8,256]{3,1,0,2:T(8,128)(2,1)S(1)}, bf16[1,8,8,256]{3,1,0,2:T(8,128)(2,1)S(1)}, u32[]{:S(2)}, u32[]{:S(2)}) collective-permute-start(bf16[1,8,8,256]{3,1,0,2:T(8,128)(2,1)S(1)} %get-tuple-element.54), channel_id=1, source_target_pairs={{0,112},{16,32},{32,16},{48,64},{64,48},{80,96},{96,80},{112,0},{1... | collective-permute-start | bytes 98312 | tf_op jit(solution)/shard_map/ppermute | solution.py:12
  45.8 1.6 %collective-permute-done.6 = bf16[2,4,1,256]{3,1,0,2:T(4,128)(2,1)S(1)} collective-permute-done((bf16[2,4,1,256]{3,1,0,2:T(4,128)(2,1)S(1)}, bf16[2,4,1,256]{3,1,0,2:T(4,128)(2,1)S(1)}, u32[]{:S(2)}, u32[]{:S(2)}) %collective-permute-start.6) | collective-permute-done | bytes 4128 | tf_op jit(solution)/shard_map/ppermute | solution.py:12
  47.3 0.0 collective-permute-done.7
  47.4 0.8 broadcast_in_dim.16
  48.2 5.6 %all-to-all-start = ((bf16[16,2,24,256]{3,2,1,0:T(8,128)(2,1)}), bf16[16,2,24,256]{3,2,1,0:T(8,128)(2,1)S(1)}, u32[]{:S(2)}, u32[]{:S(2)}) async-start(bf16[16,2,24,256]{3,2,1,0:T(8,128)(2,1)} %broadcast_in_dim.16), calls=%async_computation | async-start | bytes 786432 | tf_op jit(solution)/shard_map/all_to_all | solution.py:639
  53.8 0.0 collective-permute-done.10
  53.8 0.1 broadcast_select_fusion.8
  53.9 0.1 broadcast_select_fusion.7
  54.0 0.1 collective-permute-start.13
  54.1 2.5 %collective-permute-start.12 = (bf16[6,1,8,256]{3,1,0,2:T(2,128)(2,1)S(1)}, bf16[6,1,8,256]{3,1,0,2:T(2,128)(2,1)S(1)}, u32[]{:S(2)}, u32[]{:S(2)}) collective-permute-start(bf16[6,1,8,256]{3,1,0,2:T(2,128)(2,1)S(1)} %get-tuple-element.47), channel_id=1, source_target_pairs={{0,14},{2,4},{4,2},{6,8},{8,6},{10,12},{12,10},{14,0},{1,15},{3,5}... | collective-permute-start | bytes 73736 | tf_op jit(solution)/shard_map/ppermute | solution.py:12
  56.6 7.4 %all-to-all-done.field_ref = bf16[16,2,24,256]{3,2,1,0:T(8,128)(2,1)S(1)} async-done(((bf16[16,2,24,256]{3,2,1,0:T(8,128)(2,1)}), bf16[16,2,24,256]{3,2,1,0:T(8,128)(2,1)S(1)}, u32[]{:S(2)}, u32[]{:S(2)}) %all-to-all-start) | async-done | bytes 393248 | tf_op jit(solution)/shard_map/all_to_all | solution.py:639
  64.0 3.9 %bottom_in.1 = bf16[8,8,6,4,128]{4,3,2,1,0:T(4,128)(2,1)} custom-call(s32[5]{0:T(128)S(1)} %pad_add_fusion.place_ref, bf16[16,2,24,256]{3,2,1,0:T(8,128)(2,1)S(1)} %all-to-all-done.field_ref, bf16[9,256,256]{2,1,0:T(8,128)(2,1)} %get-tuple-element.36.weights_hbm), custom_call_target="tpu_custom_call" | custom-call | tf_op jit(solution)/shard_map/bottom_in/pallas_call | solution.py:398
  67.9 3.5 %all-to-all-start.1 = ((bf16[8,8,6,4,128]{4,3,2,1,0:T(4,128)(2,1)}), bf16[8,8,6,4,128]{4,3,2,1,0:T(4,128)(2,1)S(1)}, u32[]{:S(2)}, u32[]{:S(2)}) async-start(bf16[8,8,6,4,128]{4,3,2,1,0:T(4,128)(2,1)} %bottom_in.1), calls=%async_computation.1 | async-start | bytes 786432 | tf_op jit(solution)/shard_map/all_to_all | solution.py:641
  71.4 0.1 broadcast_select_fusion.9
  71.5 0.2 pad_maximum_fusion
  71.7 9.0 %all-to-all-done.1.field_ref = bf16[8,8,6,4,128]{4,3,2,1,0:T(4,128)(2,1)S(1)} async-done(((bf16[8,8,6,4,128]{4,3,2,1,0:T(4,128)(2,1)}), bf16[8,8,6,4,128]{4,3,2,1,0:T(4,128)(2,1)S(1)}, u32[]{:S(2)}, u32[]{:S(2)}) %all-to-all-start.1) | async-done | bytes 393248 | tf_op jit(solution)/shard_map/all_to_all | solution.py:641
  80.8 0.5 broadcast_select_fusion
  81.2 0.1 collective-permute-start.8
  81.3 2.0 %collective-permute-start.9 = (bf16[8,8,6,2,128]{4,3,2,1,0:T(2,128)(2,1)S(1)}, bf16[8,8,6,2,128]{4,3,2,1,0:T(2,128)(2,1)S(1)}, u32[]{:S(2)}, u32[]{:S(2)}) collective-permute-start(bf16[8,8,6,2,128]{4,3,2,1,0:T(2,128)(2,1)S(1)} %get-tuple-element.52), channel_id=1, source_target_pairs={{0,14},{2,4},{4,2},{6,8},{8,6},{10,12},{12,10},{14,0},{1,15},{3,5}... | collective-permute-start | bytes 589832 | tf_op jit(solution)/shard_map/ppermute | solution.py:12
  83.4 0.7 collective-permute-start.14
  84.0 3.5 %collective-permute-done.14.edge_ref = bf16[6,10,256]{2,1,0:T(8,128)(2,1)S(1)} collective-permute-done((bf16[6,10,256]{2,1,0:T(8,128)(2,1)S(1)}, bf16[6,10,256]{2,1,0:T(8,128)(2,1)S(1)}, u32[]{:S(2)}, u32[]{:S(2)}) %collective-permute-start.14) | collective-permute-done | bytes 30752 | tf_op jit(solution)/shard_map/ppermute | solution.py:623
  87.5 0.2 collective-permute-done.9.y_out_ref
  87.7 6.2 %bottom_out.1 = bf16[8,2,6,8,128]{4,3,2,1,0:T(8,128)(2,1)} custom-call(s32[5]{0:T(128)S(1)} %pad_add_fusion.place_ref, bf16[8,8,6,4,128]{4,3,2,1,0:T(4,128)(2,1)S(1)} %all-to-all-done.1.field_ref, bf16[8,8,6,2,128]{4,3,2,1,0:T(2,128)(2,1)S(1)} %collective-permute-done.8.y_in_ref, bf16[8,8,6,2,128]{4,3,2,1,0:T(2,128)(2,1)S(1)} %collective-permute-done.9.y_out_ref, ...), custom_call_target="tpu_custom_call" | custom-call | tf_op jit(solution)/shard_map/bottom_out/pallas_call | solution.py:458
  93.9 3.4 %all-to-all-start.2 = ((bf16[8,2,6,8,128]{4,3,2,1,0:T(8,128)(2,1)}), bf16[8,2,6,8,128]{4,3,2,1,0:T(8,128)(2,1)S(1)}, u32[]{:S(2)}, u32[]{:S(2)}) async-start(bf16[8,2,6,8,128]{4,3,2,1,0:T(8,128)(2,1)} %bottom_out.1), calls=%async_computation.2 | async-start | bytes 393216 | tf_op jit(solution)/shard_map/all_to_all | solution.py:648
  97.3 0.1 copy.21.skip_ref
  97.5 3.3 %decode_skip.1 = (f32[3,288,256]{2,1,0:T(8,128)S(1)}, bf16[3,512,256]{2,1,0:T(8,128)(2,1)S(1)}, bf16[3,512,256]{2,1,0:T(8,128)(2,1)S(1)}, bf16[3,512,256]{2,1,0:T(8,128)(2,1)S(1)}) custom-call(bf16[6,10,8,256]{3,2,1,0:T(8,128)(2,1)S(1)} %copy.21.skip_ref, bf16[6,10,256]{2,1,0:T(8,128)(2,1)S(1)} %collective-permute-done.14.edge_ref, ...), custom_call_target="tpu_custom_call" | custom-call | tf_op jit(solution)/shard_map/decode_skip/pallas_call | solution.py:511
  100.7 5.0 %all-to-all-done.2.bottom_ref = bf16[8,2,6,8,128]{4,3,2,1,0:T(8,128)(2,1)S(1)} async-done(((bf16[8,2,6,8,128]{4,3,2,1,0:T(8,128)(2,1)}), bf16[8,2,6,8,128]{4,3,2,1,0:T(8,128)(2,1)S(1)}, u32[]{:S(2)}, u32[]{:S(2)}) %all-to-all-start.2) | async-done | bytes 196640 | tf_op jit(solution)/shard_map/all_to_all | solution.py:648
  105.7 6.1 %decode.1 = bf16[4,8,8,256]{3,2,1,0:T(8,128)(2,1)} custom-call(s32[5]{0:T(128)S(1)} %pad_add_fusion.place_ref, bf16[8,2,6,8,128]{4,3,2,1,0:T(8,128)(2,1)S(1)} %all-to-all-done.2.bottom_ref, f32[3,288,256]{2,1,0:T(8,128)S(1)} %get-tuple-element.43.skip_ref, bf16[3,512,256]{2,1,0:T(8,128)(2,1)S(1)} %get-tuple-element.44.refs_0_, ...), custom_call_target="tpu_custom_call" | custom-call | tf_op jit(solution)/shard_map/decode/pallas_call | solution.py:595
  (22 shorter events, 0.2 us)
Async XLA Ops:
  0.0 17.1 %copy-start = (bf16[8,16,16,128]{3,2,1,0:T(8,128)(2,1)S(1)}, bf16[8,16,16,128]{3,2,1,0:T(8,128)(2,1)}, u32[]{:S(2)}) copy-start(bf16[8,16,16,128]{3,2,1,0:T(8,128)(2,1)} %own_hbm.1) | copy-start | bytes 1572868
  1.1 12.2 %collective-permute-start = (bf16[3,16,16,128]{3,2,1,0:T(8,128)(2,1)S(1)}, bf16[3,16,16,128]{3,2,1,0:T(8,128)(2,1)S(1)}, u32[]{:S(2)}, u32[]{:S(2)}) collective-permute-start(bf16[3,16,16,128]{3,2,1,0:T(8,128)(2,1)S(1)} %get-tuple-element.51), channel_id=1, source_target_pairs={{0,16},{16,0},{32,48},{48,32},{64,80},{80,64},{96,112},{112,96},{1... | collective-permute-start | bytes 589832 | tf_op jit(solution)/shard_map/ppermute | solution.py:12
  4.3 12.8 %collective-permute-start.1 = (bf16[3,16,16,128]{3,2,1,0:T(8,128)(2,1)S(1)}, bf16[3,16,16,128]{3,2,1,0:T(8,128)(2,1)S(1)}, u32[]{:S(2)}, u32[]{:S(2)}) collective-permute-start(bf16[3,16,16,128]{3,2,1,0:T(8,128)(2,1)S(1)} %get-tuple-element.50), channel_id=1, source_target_pairs={{0,112},{16,32},{32,16},{48,64},{64,48},{80,96},{96,80},{112,0},{1... | collective-permute-start | bytes 589832 | tf_op jit(solution)/shard_map/ppermute | solution.py:12
  18.0 23.5 %copy-start.1 = (bf16[3,3,3,128,256]{4,3,2,1,0:T(8,128)(2,1)S(1)}, bf16[3,3,3,128,256]{4,3,2,1,0:T(8,128)(2,1)}, u32[]{:S(2)}) copy-start(bf16[3,3,3,128,256]{4,3,2,1,0:T(8,128)(2,1)} %param.8) | copy-start | bytes 5308420
  18.0 3.2 %collective-permute-start.2 = (bf16[14,3,16,128]{3,2,1,0:T(8,128)(2,1)S(1)}, bf16[14,3,16,128]{3,2,1,0:T(8,128)(2,1)S(1)}, u32[]{:S(2)}, u32[]{:S(2)}) collective-permute-start(bf16[14,3,16,128]{3,2,1,0:T(8,128)(2,1)S(1)} %get-tuple-element.31), channel_id=1, source_target_pairs={{0,2},{2,0},{4,6},{6,4},{8,10},{10,8},{12,14},{14,12},{1,3},{3,1},... | collective-permute-start | bytes 516104 | tf_op jit(solution)/shard_map/ppermute | solution.py:12
  18.1 6.2 %collective-permute-start.3 = (bf16[14,3,16,128]{3,2,1,0:T(8,128)(2,1)S(1)}, bf16[14,3,16,128]{3,2,1,0:T(8,128)(2,1)S(1)}, u32[]{:S(2)}, u32[]{:S(2)}) collective-permute-start(bf16[14,3,16,128]{3,2,1,0:T(8,128)(2,1)S(1)} %get-tuple-element.32), channel_id=1, source_target_pairs={{0,14},{2,4},{4,2},{6,8},{8,6},{10,12},{12,10},{14,0},{1,15},{3,5}... | collective-permute-start | bytes 516104 | tf_op jit(solution)/shard_map/ppermute | solution.py:12
  25.0 4.6 %collective-permute-start.4 = (bf16[14,22,128]{2,1,0:T(8,128)(2,1)S(1)}, bf16[14,22,128]{2,1,0:T(8,128)(2,1)S(1)}, u32[]{:S(2)}, u32[]{:S(2)}) collective-permute-start(bf16[14,22,128]{2,1,0:T(8,128)(2,1)S(1)} %pack_z.1), channel_id=1, source_target_pairs={{0,1},{1,0},{2,3},{3,2},{4,5},{5,4},{6,7},{7,6},{8,9},{9,8},{10,11... | collective-permute-start | bytes 236552 | tf_op jit(solution)/shard_map/ppermute | solution.py:630
  37.6 3.9 %collective-permute-start.5 = (bf16[6,10,128]{2,1,0:T(8,128)(2,1)S(1)}, bf16[6,10,128]{2,1,0:T(8,128)(2,1)S(1)}, u32[]{:S(2)}, u32[]{:S(2)}) collective-permute-start(bf16[6,10,128]{2,1,0:T(8,128)(2,1)S(1)} %fusion.1), channel_id=1, source_target_pairs={{0,1},{1,0},{2,3},{3,2},{4,5},{5,4},{6,7},{7,6},{8,9},{9,8},{10,11... | collective-permute-start | bytes 46088 | tf_op jit(solution)/shard_map/ppermute | solution.py:623
  43.0 4.3 %collective-permute-start.6 = (bf16[2,4,1,256]{3,1,0,2:T(4,128)(2,1)S(1)}, bf16[2,4,1,256]{3,1,0,2:T(4,128)(2,1)S(1)}, u32[]{:S(2)}, u32[]{:S(2)}) collective-permute-start(bf16[2,4,1,256]{3,1,0,2:T(4,128)(2,1)S(1)} %get-tuple-element.66), channel_id=1, source_target_pairs={{0,14},{2,4},{4,2},{6,8},{8,6},{10,12},{12,10},{14,0},{1,15},{3,5}... | collective-permute-start | bytes 12296 | tf_op jit(solution)/shard_map/ppermute | solution.py:12
  44.0 3.3 %collective-permute-start.7 = (bf16[2,4,1,256]{3,1,0,2:T(4,128)(2,1)S(1)}, bf16[2,4,1,256]{3,1,0,2:T(4,128)(2,1)S(1)}, u32[]{:S(2)}, u32[]{:S(2)}) collective-permute-start(bf16[2,4,1,256]{3,1,0,2:T(4,128)(2,1)S(1)} %get-tuple-element.67), channel_id=1, source_target_pairs={{0,2},{2,0},{4,6},{6,4},{8,10},{10,8},{12,14},{14,12},{1,3},{3,1},... | collective-permute-start | bytes 12296 | tf_op jit(solution)/shard_map/ppermute | solution.py:12
  44.0 9.8 %collective-permute-start.10 = (bf16[1,8,8,256]{3,1,0,2:T(8,128)(2,1)S(1)}, bf16[1,8,8,256]{3,1,0,2:T(8,128)(2,1)S(1)}, u32[]{:S(2)}, u32[]{:S(2)}) collective-permute-start(bf16[1,8,8,256]{3,1,0,2:T(8,128)(2,1)S(1)} %get-tuple-element.54), channel_id=1, source_target_pairs={{0,112},{16,32},{32,16},{48,64},{64,48},{80,96},{96,80},{112,0},{1... | collective-permute-start | bytes 98312 | tf_op jit(solution)/shard_map/ppermute | solution.py:12
  45.8 8.0 %collective-permute-start.11 = (bf16[1,8,8,256]{3,1,0,2:T(8,128)(2,1)S(1)}, bf16[1,8,8,256]{3,1,0,2:T(8,128)(2,1)S(1)}, u32[]{:S(2)}, u32[]{:S(2)}) collective-permute-start(bf16[1,8,8,256]{3,1,0,2:T(8,128)(2,1)S(1)} %get-tuple-element.55), channel_id=1, source_target_pairs={{0,16},{16,0},{32,48},{48,32},{64,80},{80,64},{96,112},{112,96},{1... | collective-permute-start | bytes 98312 | tf_op jit(solution)/shard_map/ppermute | solution.py:12
  48.2 15.8 %all-to-all-start = ((bf16[16,2,24,256]{3,2,1,0:T(8,128)(2,1)}), bf16[16,2,24,256]{3,2,1,0:T(8,128)(2,1)S(1)}, u32[]{:S(2)}, u32[]{:S(2)}) async-start(bf16[16,2,24,256]{3,2,1,0:T(8,128)(2,1)} %broadcast_in_dim.16), calls=%async_computation | async-start | bytes 786432 | tf_op jit(solution)/shard_map/all_to_all | solution.py:639
  54.0 17.3 %collective-permute-start.13 = (bf16[6,1,8,256]{3,1,0,2:T(2,128)(2,1)S(1)}, bf16[6,1,8,256]{3,1,0,2:T(2,128)(2,1)S(1)}, u32[]{:S(2)}, u32[]{:S(2)}) collective-permute-start(bf16[6,1,8,256]{3,1,0,2:T(2,128)(2,1)S(1)} %broadcast_select_fusion.7), channel_id=1, source_target_pairs={{0,2},{2,0},{4,6},{6,4},{8,10},{10,8},{12,14},{14,12},{1,3},{3,1},... | collective-permute-start | bytes 73736 | tf_op jit(solution)/shard_map/ppermute | solution.py:12
  54.1 17.2 %collective-permute-start.12 = (bf16[6,1,8,256]{3,1,0,2:T(2,128)(2,1)S(1)}, bf16[6,1,8,256]{3,1,0,2:T(2,128)(2,1)S(1)}, u32[]{:S(2)}, u32[]{:S(2)}) collective-permute-start(bf16[6,1,8,256]{3,1,0,2:T(2,128)(2,1)S(1)} %get-tuple-element.47), channel_id=1, source_target_pairs={{0,14},{2,4},{4,2},{6,8},{8,6},{10,12},{12,10},{14,0},{1,15},{3,5}... | collective-permute-start | bytes 73736 | tf_op jit(solution)/shard_map/ppermute | solution.py:12
  67.9 12.9 %all-to-all-start.1 = ((bf16[8,8,6,4,128]{4,3,2,1,0:T(4,128)(2,1)}), bf16[8,8,6,4,128]{4,3,2,1,0:T(4,128)(2,1)S(1)}, u32[]{:S(2)}, u32[]{:S(2)}) async-start(bf16[8,8,6,4,128]{4,3,2,1,0:T(4,128)(2,1)} %bottom_in.1), calls=%async_computation.1 | async-start | bytes 786432 | tf_op jit(solution)/shard_map/all_to_all | solution.py:641
  81.2 6.3 %collective-permute-start.8 = (bf16[8,8,6,2,128]{4,3,2,1,0:T(2,128)(2,1)S(1)}, bf16[8,8,6,2,128]{4,3,2,1,0:T(2,128)(2,1)S(1)}, u32[]{:S(2)}, u32[]{:S(2)}) collective-permute-start(bf16[8,8,6,2,128]{4,3,2,1,0:T(2,128)(2,1)S(1)} %get-tuple-element.53), channel_id=1, source_target_pairs={{0,2},{2,0},{4,6},{6,4},{8,10},{10,8},{12,14},{14,12},{1,3},{3,1},... | collective-permute-start | bytes 589832 | tf_op jit(solution)/shard_map/ppermute | solution.py:12
  81.3 6.4 %collective-permute-start.9 = (bf16[8,8,6,2,128]{4,3,2,1,0:T(2,128)(2,1)S(1)}, bf16[8,8,6,2,128]{4,3,2,1,0:T(2,128)(2,1)S(1)}, u32[]{:S(2)}, u32[]{:S(2)}) collective-permute-start(bf16[8,8,6,2,128]{4,3,2,1,0:T(2,128)(2,1)S(1)} %get-tuple-element.52), channel_id=1, source_target_pairs={{0,14},{2,4},{4,2},{6,8},{8,6},{10,12},{12,10},{14,0},{1,15},{3,5}... | collective-permute-start | bytes 589832 | tf_op jit(solution)/shard_map/ppermute | solution.py:12
  83.4 4.2 %collective-permute-start.14 = (bf16[6,10,256]{2,1,0:T(8,128)(2,1)S(1)}, bf16[6,10,256]{2,1,0:T(8,128)(2,1)S(1)}, u32[]{:S(2)}, u32[]{:S(2)}) collective-permute-start(bf16[6,10,256]{2,1,0:T(8,128)(2,1)S(1)} %fusion), channel_id=1, source_target_pairs={{0,1},{1,0},{2,3},{3,2},{4,5},{5,4},{6,7},{7,6},{8,9},{9,8},{10,11... | collective-permute-start | bytes 92168 | tf_op jit(solution)/shard_map/ppermute | solution.py:623
  93.9 11.8 %all-to-all-start.2 = ((bf16[8,2,6,8,128]{4,3,2,1,0:T(8,128)(2,1)}), bf16[8,2,6,8,128]{4,3,2,1,0:T(8,128)(2,1)S(1)}, u32[]{:S(2)}, u32[]{:S(2)}) async-start(bf16[8,2,6,8,128]{4,3,2,1,0:T(8,128)(2,1)} %bottom_out.1), calls=%async_computation.2 | async-start | bytes 393216 | tf_op jit(solution)/shard_map/all_to_all | solution.py:648

commit v8 on v7

--- a/solution.py
+++ b/solution.py
@@ -100,35 +100,18 @@
     return down + mid + up
 
 
-def encode(place, own, x_in, x_out, y_in, y_out, edge, weights):
+def assemble(place, own, x_in, x_out, y_in, y_out, weights):
     own_x, own_y, size_z, channels = own.shape
     reach = x_in.shape[0]
     full_x, full_y = own_x + 2 * reach, own_y + 2 * reach
-    size_x, size_y = full_x - 2, full_y - 2
-    filters = weights.shape[-1] // 2
-    rows, extra = size_y * size_z, size_y + (-size_y % 16)
-    pool_y, pool_z = size_y // 2, size_z // 2
 
     def body(
-        place_ref,
-        own_hbm,
-        x_in_ref,
-        x_out_ref,
-        y_in_ref,
-        y_out_ref,
-        edge_ref,
-        weights_hbm,
-        out_ref,
-        field_ref,
-        side_ref,
-        rows_ref,
-        weights_ref,
-        sems,
+        place_ref, own_hbm, x_in_ref, x_out_ref, y_in_ref, y_out_ref, weights_hbm, field_ref, weights_ref, sems
     ):
         inner = field_ref.at[reach : reach + own_x, reach : reach + own_y]
         copies = [pltpu.make_async_copy(own_hbm, inner, sems.at[0])]
-        for tap in range(3):
-            copies.append(pltpu.make_async_copy(weights_hbm.at[:, :, tap], weights_ref.at[tap], sems.at[1 + tap]))
+        for plane in range(4):
+            copies.append(pltpu.make_async_copy(weights_hbm.at[plane], weights_ref.at[plane], sems.at[1 + plane]))
         for copy in copies:
             copy.start()
         even_x, even_y = place_ref[0] % 2 == 0, place_ref[1] % 2 == 0
@@ -148,6 +131,38 @@
             below, above = jnp.where(even_y, y_out_ref[x], y_in_ref[x]), jnp.where(even_y, y_in_ref[x], y_out_ref[x])
             field_ref[x, :reach] = jnp.where(here_low, below, nil)
             field_ref[x, reach + own_y :] = jnp.where(here_high, above, nil)
+        for copy in copies:
+            copy.wait()
+
+    return pl.pallas_call(
+        body,
+        in_specs=[pl.BlockSpec(memory_space=pltpu.SMEM), pl.BlockSpec(memory_space=pltpu.HBM)]
+        + [pl.BlockSpec(memory_space=pltpu.VMEM)] * 4
+        + [pl.BlockSpec(memory_space=pltpu.HBM)],
+        out_specs=[pl.BlockSpec(memory_space=pltpu.VMEM)] * 2,
+        out_shape=[
+            pltpu.VMEM((full_x, full_y, size_z, channels), jnp.bfloat16),
+            pltpu.VMEM(weights.shape, weights.dtype),
+        ],
+        scratch_shapes=[pltpu.SemaphoreType.DMA((5,))],
+        compiler_params=pltpu.CompilerParams(vmem_limit_bytes=4 << 20),
+        name="assemble",
+    )(place, far(own), x_in, x_out, y_in, y_out, far(weights))
+
+
+def encode(place, field, edge, weights):
+    full_x, full_y, size_z, channels = field.shape
+    reach = 3
+    size_x, size_y = full_x - 2, full_y - 2
+    own_x, own_y = full_x - 2 * reach, full_y - 2 * reach
+    filters = weights.shape[-1] // 2
+    rows, extra = size_y * size_z, size_y + (-size_y % 16)
+    pool_y, pool_z = size_y // 2, size_z // 2
+
+    def body(place_ref, field_ref, edge_ref, weights_ref, out_ref, side_ref, rows_ref):
+        low_x, high_x = place_ref[0] > 0, place_ref[0] < place_ref[3]
+        low_y, high_y = place_ref[1] > 0, place_ref[1] < place_ref[4]
+        for x in range(full_x):
             line = lax.broadcasted_iota(jnp.int32, (full_y, channels), 0)
             inside = ((line >= reach) | low_y) & ((line < reach + own_y) | high_y)
             if x < reach:
@@ -160,7 +175,6 @@
                 side_ref[dy, x, size_y:] = jnp.zeros((extra - size_y, channels), jnp.float32)
 
         first = place_ref[2] == 0
-        copies[0].wait()
         line = lax.broadcasted_iota(jnp.int32, (pool_y, pool_z, filters), 0)
         inside_y = ((line > 0) | low_y) & ((line < pool_y - 1) | high_y)
         for pair in range(size_x // 2):
@@ -173,9 +187,7 @@
             block = jnp.concatenate(blocks, axis=1)
             sums = []
             for tap in range(3):
-                if pair == 0:
-                    copies[1 + tap].wait()
-                kernel = weights_ref[tap].reshape(12 * channels, 2 * filters)
+                kernel = weights_ref[:, :, tap].reshape(12 * channels, 2 * filters)
                 sums.append(jnp.dot(block, kernel, preferred_element_type=jnp.float32))
             total = jnp.maximum(join_taps(first, sums, size_y, size_z), 0.0)
             total = jnp.maximum(total[..., :filters], total[..., filters:])
@@ -193,21 +205,39 @@
 
     return pl.pallas_call(
         body,
-        in_specs=[pl.BlockSpec(memory_space=pltpu.SMEM), pl.BlockSpec(memory_space=pltpu.HBM)]
-        + [pl.BlockSpec(memory_space=pltpu.VMEM)] * 5
-        + [pl.BlockSpec(memory_space=pltpu.HBM)],
+        in_specs=[pl.BlockSpec(memory_space=pltpu.SMEM)] + [pl.BlockSpec(memory_space=pltpu.VMEM)] * 3,
         out_specs=pl.BlockSpec(memory_space=pltpu.VMEM),
         out_shape=jax.ShapeDtypeStruct((size_x // 2, pool_y, pool_z, filters), jnp.bfloat16),
         scratch_shapes=[
-            pltpu.VMEM((full_x, full_y, size_z, channels), jnp.bfloat16),
             pltpu.VMEM((3, full_x, extra, channels), jnp.float32),
             pltpu.VMEM((pool_y * size_z, filters), jnp.float32),
-            pltpu.VMEM((3, 4, 3, channels, 2 * filters), weights.dtype),
-            pltpu.SemaphoreType.DMA((4,)),
         ],
-        compiler_params=pltpu.CompilerParams(vmem_limit_bytes=20 << 20),
+        compiler_params=pltpu.CompilerParams(vmem_limit_bytes=14 << 20),
         name="encode",
-    )(place, far(own), x_in, x_out, y_in, y_out, edge, far(weights))
+    )(place, near(field), edge, near(weights))
+
+
+def near(array):
+    return pltpu.with_memory_space_constraint(array, pltpu.VMEM)
+
+
+def bring(weights, after):
+    def body(weights_hbm, after_ref, out_ref, sems):
+        copies = [pltpu.make_async_copy(weights_hbm.at[step], out_ref.at[step], sems.at[step]) for step in range(9)]
+        for copy in copies:
+            copy.start()
+        for copy in copies:
+            copy.wait()
+
+    return pl.pallas_call(
+        body,
+        in_specs=[pl.BlockSpec(memory_space=pltpu.HBM), pl.BlockSpec(memory_space=pl.ANY)],
+        out_specs=pl.BlockSpec(memory_space=pltpu.VMEM),
+        out_shape=pltpu.VMEM(weights.shape, weights.dtype),
+        scratch_shapes=[pltpu.SemaphoreType.DMA((9,))],
+        compiler_params=pltpu.CompilerParams(vmem_limit_bytes=4 << 20),
+        name="bring",
+    )(far(weights), after)
 
 
 def far(array):
@@ -366,9 +396,7 @@
     own_z = size_y = 4
     size_x, all_z, size_z = devices * own_x, 2 * own_z, own_z + 2
 
-    def body(place_ref, field_ref, weights_hbm, out_ref, pad_ref, weights_ref, sem):
-        copy = pltpu.make_async_copy(weights_hbm, weights_ref, sem)
-        copy.start()
+    def body(place_ref, field_ref, weights_ref, out_ref, pad_ref):
         zero = jnp.zeros((all_z + 2, 8, channels), jnp.float32)
         pad_ref[0] = zero
         pad_ref[size_x + 1] = zero
@@ -387,7 +415,6 @@
                         pad_ref[*to, size_y + 1 : size_y + 2] = block[line : line + 1]
                         pad_ref[*to, size_y + 2 :] = zero[0, size_y + 2 :]
         start = 2 * place_ref[2]
-        copy.wait()
         for first in range(0, size_x, 4):
             total = column_product(pad_ref, weights_ref, first, start, 4, size_z)
             for pair in range(2):
@@ -397,17 +424,15 @@
 
     return pl.pallas_call(
         body,
-        in_specs=[pl.BlockSpec(memory_space=space) for space in (pltpu.SMEM, pltpu.VMEM, pltpu.HBM)],
+        in_specs=[pl.BlockSpec(memory_space=space) for space in (pltpu.SMEM, pltpu.VMEM, pltpu.VMEM)],
         out_specs=pl.BlockSpec(memory_space=pltpu.VMEM),
         out_shape=jax.ShapeDtypeStruct((devices, size_x // 2, size_z, size_y, 128), jnp.bfloat16),
         scratch_shapes=[
             pltpu.VMEM((size_x + 2, all_z + 2, 8, channels), jnp.float32),
-            pltpu.VMEM(weights.shape, weights.dtype),
-            pltpu.SemaphoreType.DMA(()),
         ],
         compiler_params=pltpu.CompilerParams(vmem_limit_bytes=12 << 20),
         name="bottom_in",
-    )(place, field, far(weights))
+    )(place, field, near(weights))
 
 
 def bottom_out(place, field, y_in, y_out, weights):
@@ -415,9 +440,7 @@
     size_x, channels = 2 * pairs, 64 * devices
     own_x = size_x // devices
 
-    def body(place_ref, field_ref, y_in_ref, y_out_ref, weights_hbm, out_ref, pad_ref, total_ref, weights_ref, sem):
-        copy = pltpu.make_async_copy(weights_hbm, weights_ref, sem)
-        copy.start()
+    def body(place_ref, field_ref, y_in_ref, y_out_ref, weights_ref, out_ref, pad_ref, total_ref):
         even_y = place_ref[1] % 2 == 0
         low_y, high_y = place_ref[1] > 0, place_ref[1] < place_ref[4]
         zero = jnp.zeros((size_z + 2, 8, channels), jnp.float32)
@@ -442,7 +465,6 @@
                     lines = slice(line, line + even.shape[1])
                     pad_ref[1 + 2 * pair, 1 : size_z + 1, lines, 128 * k : 128 * k + 128] = even
                     pad_ref[2 + 2 * pair, 1 : size_z + 1, lines, 128 * k : 128 * k + 128] = odd
-        copy.wait()
         for first in range(0, size_x, 4):
             total = column_product(pad_ref, weights_ref, first, 0, 4, size_z)
             total_ref[1 + first : 5 + first, 1 : size_z + 1] = total
@@ -458,19 +480,16 @@
     return pl.pallas_call(
         body,
         in_specs=[pl.BlockSpec(memory_space=pltpu.SMEM)]
-        + [pl.BlockSpec(memory_space=pltpu.VMEM)] * 3
-        + [pl.BlockSpec(memory_space=pltpu.HBM)],
+        + [pl.BlockSpec(memory_space=pltpu.VMEM)] * 4,
         out_specs=pl.BlockSpec(memory_space=pltpu.VMEM),
         out_shape=jax.ShapeDtypeStruct((devices, own_x, size_z, 8, 128), jnp.bfloat16),
         scratch_shapes=[
             pltpu.VMEM((size_x + 2, size_z + 2, 8, channels), jnp.float32),
             pltpu.VMEM((size_x + 2, size_z + 2, 8, 128), jnp.float32),
-            pltpu.VMEM(weights.shape, weights.dtype),
-            pltpu.SemaphoreType.DMA(()),
         ],
-        compiler_params=pltpu.CompilerParams(vmem_limit_bytes=20 << 20),
+        compiler_params=pltpu.CompilerParams(vmem_limit_bytes=16 << 20),
         name="bottom_out",
-    )(place, field, y_in, y_out, far(weights))
+    )(place, field, y_in, y_out, near(weights))
 
 
 def decode_skip(place, skip, edge, weights):
@@ -520,10 +539,6 @@
         compiler_params=pltpu.CompilerParams(vmem_limit_bytes=14 << 20),
         name="decode_skip",
     )(skip, edge, far(weights))
-
-
-def near(array):
-    return pltpu.with_memory_space_constraint(array, pltpu.VMEM)
 
 
 def decode(place, bottom, skip_sums, first_weights, weights, shape):
@@ -628,7 +643,8 @@
         y_inner, y_outer, plane = pack_y(place, volume, x_in, x_out)
         y_in, y_out = send(y_inner, y_outer, "gy", gy)
         edge = lax.ppermute(pack_z(place, plane, y_in, y_out), "gz", swap)
-        pooled = encode(place, volume, x_in, x_out, y_in, y_out, edge, w_pair)
+        field, w_pair = assemble(place, volume, x_in, x_out, y_in, y_out, w_pair)
+        pooled = encode(place, field, edge, w_pair)
 
         edge = edge_of(pooled[:, :, 0], pooled[:, :, -1])
         skip, coarse = half_level(place, pooled, edge, w_half.reshape(9, 3, w_half.shape[3], w_half.shape[4]))
@@ -636,9 +652,11 @@
         below, above = halo(lines, "gy", gy, 2, 1)
         column = jnp.concatenate([coarse, below[:, :, 0], above[:, :, 0]], axis=1)
         column = jnp.broadcast_to(column[None], (gx * gz,) + column.shape)
+        w_in = bring(w_in, column)
         column = lax.all_to_all(column, ("gx", "gz"), 0, 0)
         first = bottom_in(place, column, w_in)
         first = lax.all_to_all(first, "gx", 0, 0)
+        w_out = bring(w_out, first)
         y_in, y_out = swaps(first[:, :, :, :2], first[:, :, :, -2:], "gy", gy)
         around = extend(skip, "gx", gx, 0, 1)
         around = extend(around, "gy", gy, 1, 1)

time: 112 us -> 107 us (0.955)
  waiting for transfers between devices: 38.9 us -> 34.1 us
    pallas_call x1 -> x4, Pallas kernels: 8.03 us -> 11.3 us  [the longest x1 5.91 us: encode(): pl.pallas_call(body, in_specs=[pl.BlockSpec(memory_space=pltpu.SMEM)] + [...]
    ppermute x1, waiting for transfers between devices: 2.99 us -> 0.63 us  [local(): edge = lax.ppermute(pack_z(place, plane, y_in, y_out), 'gz', swap)]
    pallas_call x1, Pallas kernels: 6.19 us -> 4.12 us  [bottom_out(): pl.pallas_call(body, in_specs=[pl.BlockSpec(memory_space=pltpu.SMEM)] + [...]
    ppermute x2, waiting for transfers between devices: 5.82 us -> 4.15 us  [edge_of(): lax.ppermute(jnp.where(place_z == 0, plane_high, plane_low), 'gz', swap)]
    ppermute x6, starting transfers between devices: 14.4 us -> 13.2 us  [send(): lax.ppermute(outer_block, axis, outer)]
  transfers between devices with their start and end apart: 18 -> 18, of which waited for: 10 -> 10; matrix products, arithmetic and copies ran while one was open for 1% -> 2% of each run, Pallas kernels for 11% -> 15%
where the time goes in v8:
time: 107 us
  Pallas kernels  35.3 us (33%)
  waiting for transfers between devices  34.1 us (32%)
  starting transfers between devices  33.5 us (31%)
  other arithmetic  2.25 us (2%)
    ppermute x6, starting transfers between devices, send(): lax.ppermute(outer_block, axis, outer)  13.2 us
    all_to_all x1, waiting for transfers between devices, local(): first = lax.all_to_all(first, 'gx', 0, 0)  9.04 us
    ppermute x6, waiting for transfers between devices, send(): lax.ppermute(outer_block, axis, outer)  8.56 us
    all_to_all x1, waiting for transfers between devices, local(): column = lax.all_to_all(column, ('gx', 'gz'), 0, 0)  6.69 us
    pallas_call x1, Pallas kernels, decode(): pl.pallas_call(body, in_specs=[pl.BlockSpec(memory_space=pltpu.SMEM)] + [...  6.06 us
    pallas_call x1, Pallas kernels, encode(): pl.pallas_call(body, in_specs=[pl.BlockSpec(memory_space=pltpu.SMEM)] + [...  5.91 us
    all_to_all x1, starting transfers between devices, local(): column = lax.all_to_all(column, ('gx', 'gz'), 0, 0)  5.66 us
    all_to_all x1, waiting for transfers between devices, local(): second = lax.all_to_all(second, 'gx', 0, 0)  4.98 us
  transfers between devices with their start and end apart: 18, of which 10 were waited for; matrix products, arithmetic and copies ran while one was open for 2% of the time, Pallas kernels for 15%

profile of v8, /device:TPU:0, one launch (start us, length us, event | category | flops | bytes accessed | tf_op | source)
XLA Modules:
  0.0 106.6 jit_solution(6459080606662865376)
XLA Ops:
  0.0 1.1 %broadcast_select_fusion.2 = (bf16[3,16,16,128]{3,2,1,0:T(8,128)(2,1)S(1)}, bf16[3,16,16,128]{3,2,1,0:T(8,128)(2,1)S(1)}) fusion(pred[]{:T(512)S(6)} %eq.25, bf16[8,16,16,128]{3,2,1,0:T(8,128)(2,1)} %own_hbm.1), kind=kLoop, calls=%fused_computation.3 | loop fusion | flops 196608 | bytes 786433 | tf_op jit(solution)/shard_map/jit(_where)/select_n | solution.py:17
  1.1 3.2 %collective-permute-start = (bf16[3,16,16,128]{3,2,1,0:T(8,128)(2,1)S(1)}, bf16[3,16,16,128]{3,2,1,0:T(8,128)(2,1)S(1)}, u32[]{:S(2)}, u32[]{:S(2)}) collective-permute-start(bf16[3,16,16,128]{3,2,1,0:T(8,128)(2,1)S(1)} %get-tuple-element.55), channel_id=1, source_target_pairs={{0,16},{16,0},{32,48},{48,32},{64,80},{80,64},{96,112},{112,96},{1... | collective-permute-start | bytes 589832 | tf_op jit(solution)/shard_map/ppermute | solution.py:12
  4.3 4.0 %collective-permute-start.1 = (bf16[3,16,16,128]{3,2,1,0:T(8,128)(2,1)S(1)}, bf16[3,16,16,128]{3,2,1,0:T(8,128)(2,1)S(1)}, u32[]{:S(2)}, u32[]{:S(2)}) collective-permute-start(bf16[3,16,16,128]{3,2,1,0:T(8,128)(2,1)S(1)} %get-tuple-element.54), channel_id=1, source_target_pairs={{0,112},{16,32},{32,16},{48,64},{64,48},{80,96},{96,80},{112,0},{1... | collective-permute-start | bytes 589832 | tf_op jit(solution)/shard_map/ppermute | solution.py:12
  8.3 4.9 %prepare.1 = (bf16[4,3,3,128,256]{4,3,2,1,0:T(8,128)(2,1)}, bf16[9,256,256]{2,1,0:T(8,128)(2,1)}, bf16[9,512,256]{2,1,0:T(8,128)(2,1)}) custom-call(bf16[3,3,3,128,128]{4,3,2,1,0:T(8,128)(2,1)} %full_hbm.1, bf16[3,3,3,64,256]{4,3,2,1,0:T(8,128)(2,1)} %bitcast.20, bf16[3,3,3,64,512]{4,3,2,1,0:T(8,128)(2,1)} %bitcast.19), custom_call_target="tpu_custom_call" | custom-call | tf_op jit(solution)/shard_map/prepare/pallas_call | solution.py:286
  13.2 0.1 pad_add_fusion.place_ref
  13.3 3.8 %collective-permute-done.1.x_out_ref = bf16[3,16,16,128]{3,2,1,0:T(8,128)(2,1)S(1)} collective-permute-done((bf16[3,16,16,128]{3,2,1,0:T(8,128)(2,1)S(1)}, bf16[3,16,16,128]{3,2,1,0:T(8,128)(2,1)S(1)}, u32[]{:S(2)}, u32[]{:S(2)}) %collective-permute-start.1) | collective-permute-done | bytes 196640 | tf_op jit(solution)/shard_map/ppermute | solution.py:12
  17.1 0.9 pack_y.1
  18.0 0.1 collective-permute-start.2
  18.1 3.1 %collective-permute-start.3 = (bf16[14,3,16,128]{3,2,1,0:T(8,128)(2,1)S(1)}, bf16[14,3,16,128]{3,2,1,0:T(8,128)(2,1)S(1)}, u32[]{:S(2)}, u32[]{:S(2)}) collective-permute-start(bf16[14,3,16,128]{3,2,1,0:T(8,128)(2,1)S(1)} %get-tuple-element.34), channel_id=1, source_target_pairs={{0,14},{2,4},{4,2},{6,8},{8,6},{10,12},{12,10},{14,0},{1,15},{3,5}... | collective-permute-start | bytes 516104 | tf_op jit(solution)/shard_map/ppermute | solution.py:12
  21.2 3.1 %collective-permute-done.3.y_out_ref = bf16[14,3,16,128]{3,2,1,0:T(8,128)(2,1)S(1)} collective-permute-done((bf16[14,3,16,128]{3,2,1,0:T(8,128)(2,1)S(1)}, bf16[14,3,16,128]{3,2,1,0:T(8,128)(2,1)S(1)}, u32[]{:S(2)}, u32[]{:S(2)}) %collective-permute-start.3) | collective-permute-done | bytes 172064 | tf_op jit(solution)/shard_map/ppermute | solution.py:12
  24.3 0.6 pack_z.1
  24.9 1.6 %collective-permute-start.4 = (bf16[14,22,128]{2,1,0:T(8,128)(2,1)S(1)}, bf16[14,22,128]{2,1,0:T(8,128)(2,1)S(1)}, u32[]{:S(2)}, u32[]{:S(2)}) collective-permute-start(bf16[14,22,128]{2,1,0:T(8,128)(2,1)S(1)} %pack_z.1), channel_id=1, source_target_pairs={{0,1},{1,0},{2,3},{3,2},{4,5},{5,4},{6,7},{7,6},{8,9},{9,8},{10,11... | collective-permute-start | bytes 236552 | tf_op jit(solution)/shard_map/ppermute | solution.py:645
  26.5 2.3 %assemble.1 = (bf16[14,22,16,128]{3,2,1,0:T(8,128)(2,1)S(1)}, bf16[4,3,3,128,256]{4,3,2,1,0:T(8,128)(2,1)S(1)}) custom-call(s32[5]{0:T(128)S(1)} %pad_add_fusion.place_ref, bf16[8,16,16,128]{3,2,1,0:T(8,128)(2,1)} %own_hbm.1, bf16[3,16,16,128]{3,2,1,0:T(8,128)(2,1)S(1)} %collective-permute-done.x_in_ref, ...), custom_call_target="tpu_custom_call" | custom-call | tf_op jit(solution)/shard_map/assemble/pallas_call | solution.py:137
  28.9 0.0 copy-start.1
  28.9 0.6 collective-permute-done.4.edge_ref
  29.5 5.9 %encode.1.field_ref = bf16[6,10,8,128]{3,2,1,0:T(8,128)(2,1)S(1)} custom-call(s32[5]{0:T(128)S(1)} %pad_add_fusion.place_ref, bf16[14,22,16,128]{3,2,1,0:T(8,128)(2,1)S(1)} %get-tuple-element.36.field_ref, bf16[14,22,128]{2,1,0:T(8,128)(2,1)S(1)} %collective-permute-done.4.edge_ref, bf16[4,3,3,128,256]{4,3,2,1,0:T(8,128)(2,1)S(1)} %get-tuple-element.38.weights_ref), custom_call_target="tpu_custom_call" | custom-call | tf_op jit(solution)/shard_map/encode/pallas_call | solution.py:206
  35.5 1.6 %collective-permute-start.5 = (bf16[6,10,128]{2,1,0:T(8,128)(2,1)S(1)}, bf16[6,10,128]{2,1,0:T(8,128)(2,1)S(1)}, u32[]{:S(2)}, u32[]{:S(2)}) collective-permute-start(bf16[6,10,128]{2,1,0:T(8,128)(2,1)S(1)} %fusion.1), channel_id=1, source_target_pairs={{0,1},{1,0},{2,3},{3,2},{4,5},{5,4},{6,7},{7,6},{8,9},{9,8},{10,11... | collective-permute-start | bytes 46088 | tf_op jit(solution)/shard_map/ppermute | solution.py:638
  37.1 2.3 %collective-permute-done.5.edge_ref = bf16[6,10,128]{2,1,0:T(8,128)(2,1)S(1)} collective-permute-done((bf16[6,10,128]{2,1,0:T(8,128)(2,1)S(1)}, bf16[6,10,128]{2,1,0:T(8,128)(2,1)S(1)}, u32[]{:S(2)}, u32[]{:S(2)}) %collective-permute-start.5) | collective-permute-done | bytes 15392 | tf_op jit(solution)/shard_map/ppermute | solution.py:638
  39.4 1.4 %half_level.1 = (bf16[4,8,8,256]{3,2,1,0:T(8,128)(2,1)S(1)}, bf16[2,16,256]{2,1,0:T(8,128)(2,1)S(1)}) custom-call(s32[5]{0:T(128)S(1)} %pad_add_fusion.place_ref, bf16[6,10,8,128]{3,2,1,0:T(8,128)(2,1)S(1)} %encode.1.field_ref, bf16[6,10,128]{2,1,0:T(8,128)(2,1)S(1)} %collective-permute-done.5.edge_ref, bf16[9,3,128,256]{3,2,1,0:T(8,128)(2,1)S(1)} %bitcast.16), custom_call_target="tpu_custom_call" | custom-call | tf_op jit(solution)/shard_map/half_level/pallas_call | solution.py:75
  40.8 1.0 collective-permute-start.6
  41.9 1.8 %collective-permute-start.10 = (bf16[1,8,8,256]{3,1,0,2:T(8,128)(2,1)S(1)}, bf16[1,8,8,256]{3,1,0,2:T(8,128)(2,1)S(1)}, u32[]{:S(2)}, u32[]{:S(2)}) collective-permute-start(bf16[1,8,8,256]{3,1,0,2:T(8,128)(2,1)S(1)} %get-tuple-element.58), channel_id=1, source_target_pairs={{0,112},{16,32},{32,16},{48,64},{64,48},{80,96},{96,80},{112,0},{1... | collective-permute-start | bytes 98312 | tf_op jit(solution)/shard_map/ppermute | solution.py:12
  43.7 1.5 %collective-permute-done.6 = bf16[2,4,1,256]{3,1,0,2:T(4,128)(2,1)S(1)} collective-permute-done((bf16[2,4,1,256]{3,1,0,2:T(4,128)(2,1)S(1)}, bf16[2,4,1,256]{3,1,0,2:T(4,128)(2,1)S(1)}, u32[]{:S(2)}, u32[]{:S(2)}) %collective-permute-start.6) | collective-permute-done | bytes 4128 | tf_op jit(solution)/shard_map/ppermute | solution.py:12
  45.2 0.8 broadcast_in_dim.16.after_ref
  46.0 5.7 %all-to-all-start = ((bf16[16,2,24,256]{3,2,1,0:T(8,128)(2,1)}), bf16[16,2,24,256]{3,2,1,0:T(8,128)(2,1)S(1)}, u32[]{:S(2)}, u32[]{:S(2)}) async-start(bf16[16,2,24,256]{3,2,1,0:T(8,128)(2,1)} %broadcast_in_dim.16.after_ref), calls=%async_computation | async-start | bytes 786432 | tf_op jit(solution)/shard_map/all_to_all | solution.py:656
  51.7 0.1 broadcast_select_fusion.8
  51.8 1.3 %collective-permute-start.12 = (bf16[6,1,8,256]{3,1,0,2:T(2,128)(2,1)S(1)}, bf16[6,1,8,256]{3,1,0,2:T(2,128)(2,1)S(1)}, u32[]{:S(2)}, u32[]{:S(2)}) collective-permute-start(bf16[6,1,8,256]{3,1,0,2:T(2,128)(2,1)S(1)} %get-tuple-element.51), channel_id=1, source_target_pairs={{0,14},{2,4},{4,2},{6,8},{8,6},{10,12},{12,10},{14,0},{1,15},{3,5}... | collective-permute-start | bytes 73736 | tf_op jit(solution)/shard_map/ppermute | solution.py:12
  53.1 0.1 broadcast_select_fusion.7
  53.2 0.6 collective-permute-start.13
  53.8 1.4 %bring.2.weights_ref = bf16[9,256,256]{2,1,0:T(8,128)(2,1)S(1)} custom-call(bf16[9,256,256]{2,1,0:T(8,128)(2,1)} %get-tuple-element.40.weights_hbm, bf16[16,2,24,256]{3,2,1,0:T(8,128)(2,1)} %broadcast_in_dim.16.after_ref), custom_call_target="tpu_custom_call" | custom-call | tf_op jit(solution)/shard_map/bring/pallas_call | solution.py:232
  55.2 6.7 %all-to-all-done.field_ref = bf16[16,2,24,256]{3,2,1,0:T(8,128)(2,1)S(1)} async-done(((bf16[16,2,24,256]{3,2,1,0:T(8,128)(2,1)}), bf16[16,2,24,256]{3,2,1,0:T(8,128)(2,1)S(1)}, u32[]{:S(2)}, u32[]{:S(2)}) %all-to-all-start) | async-done | bytes 393248 | tf_op jit(solution)/shard_map/all_to_all | solution.py:656
  61.9 2.8 %bottom_in.1 = bf16[8,8,6,4,128]{4,3,2,1,0:T(4,128)(2,1)} custom-call(s32[5]{0:T(128)S(1)} %pad_add_fusion.place_ref, bf16[16,2,24,256]{3,2,1,0:T(8,128)(2,1)S(1)} %all-to-all-done.field_ref, bf16[9,256,256]{2,1,0:T(8,128)(2,1)S(1)} %bring.2.weights_ref), custom_call_target="tpu_custom_call" | custom-call | tf_op jit(solution)/shard_map/bottom_in/pallas_call | solution.py:425
  64.6 3.5 %all-to-all-start.1 = ((bf16[8,8,6,4,128]{4,3,2,1,0:T(4,128)(2,1)}), bf16[8,8,6,4,128]{4,3,2,1,0:T(4,128)(2,1)S(1)}, u32[]{:S(2)}, u32[]{:S(2)}) async-start(bf16[8,8,6,4,128]{4,3,2,1,0:T(4,128)(2,1)} %bottom_in.1), calls=%async_computation.1 | async-start | bytes 786432 | tf_op jit(solution)/shard_map/all_to_all | solution.py:658
  68.1 0.1 broadcast_select_fusion.9
  68.3 0.2 pad_maximum_fusion
  68.5 9.0 %all-to-all-done.1.after_ref.field_ref = bf16[8,8,6,4,128]{4,3,2,1,0:T(4,128)(2,1)S(1)} async-done(((bf16[8,8,6,4,128]{4,3,2,1,0:T(4,128)(2,1)}), bf16[8,8,6,4,128]{4,3,2,1,0:T(4,128)(2,1)S(1)}, u32[]{:S(2)}, u32[]{:S(2)}) %all-to-all-start.1) | async-done | bytes 393248 | tf_op jit(solution)/shard_map/all_to_all | solution.py:658
  77.5 0.5 broadcast_select_fusion
  78.0 0.1 collective-permute-start.8
  78.1 2.0 %collective-permute-start.9 = (bf16[8,8,6,2,128]{4,3,2,1,0:T(2,128)(2,1)S(1)}, bf16[8,8,6,2,128]{4,3,2,1,0:T(2,128)(2,1)S(1)}, u32[]{:S(2)}, u32[]{:S(2)}) collective-permute-start(bf16[8,8,6,2,128]{4,3,2,1,0:T(2,128)(2,1)S(1)} %get-tuple-element.56), channel_id=1, source_target_pairs={{0,14},{2,4},{4,2},{6,8},{8,6},{10,12},{12,10},{14,0},{1,15},{3,5}... | collective-permute-start | bytes 589832 | tf_op jit(solution)/shard_map/ppermute | solution.py:12
  80.1 0.7 collective-permute-start.14
  80.8 1.7 %bring.3.weights_ref = bf16[9,512,256]{2,1,0:T(8,128)(2,1)S(1)} custom-call(bf16[9,512,256]{2,1,0:T(8,128)(2,1)} %get-tuple-element.44.weights_hbm, bf16[8,8,6,4,128]{4,3,2,1,0:T(4,128)(2,1)S(1)} %all-to-all-done.1.after_ref.field_ref), custom_call_target="tpu_custom_call" | custom-call | tf_op jit(solution)/shard_map/bring/pallas_call | solution.py:232
  82.5 1.8 %collective-permute-done.14.edge_ref = bf16[6,10,256]{2,1,0:T(8,128)(2,1)S(1)} collective-permute-done((bf16[6,10,256]{2,1,0:T(8,128)(2,1)S(1)}, bf16[6,10,256]{2,1,0:T(8,128)(2,1)S(1)}, u32[]{:S(2)}, u32[]{:S(2)}) %collective-permute-start.14) | collective-permute-done | bytes 30752 | tf_op jit(solution)/shard_map/ppermute | solution.py:638
  84.3 0.2 collective-permute-done.9.y_out_ref
  84.5 4.1 %bottom_out.1 = bf16[8,2,6,8,128]{4,3,2,1,0:T(8,128)(2,1)} custom-call(s32[5]{0:T(128)S(1)} %pad_add_fusion.place_ref, bf16[8,8,6,4,128]{4,3,2,1,0:T(4,128)(2,1)S(1)} %all-to-all-done.1.after_ref.field_ref, bf16[8,8,6,2,128]{4,3,2,1,0:T(2,128)(2,1)S(1)} %collective-permute-done.8.y_in_ref, bf16[8,8,6,2,128]{4,3,2,1,0:T(2,128)(2,1)S(1)} %collective-permute-done.9.y_out_ref, ...), custom_call_target="tpu_custom_call" | custom-call | tf_op jit(solution)/shard_map/bottom_out/pallas_call | solution.py:480
  88.6 3.4 %all-to-all-start.2 = ((bf16[8,2,6,8,128]{4,3,2,1,0:T(8,128)(2,1)}), bf16[8,2,6,8,128]{4,3,2,1,0:T(8,128)(2,1)S(1)}, u32[]{:S(2)}, u32[]{:S(2)}) async-start(bf16[8,2,6,8,128]{4,3,2,1,0:T(8,128)(2,1)} %bottom_out.1), calls=%async_computation.2 | async-start | bytes 393216 | tf_op jit(solution)/shard_map/all_to_all | solution.py:666
  92.0 0.1 copy.21.skip_ref
  92.1 3.3 %decode_skip.1 = (f32[3,288,256]{2,1,0:T(8,128)S(1)}, bf16[3,512,256]{2,1,0:T(8,128)(2,1)S(1)}, bf16[3,512,256]{2,1,0:T(8,128)(2,1)S(1)}, bf16[3,512,256]{2,1,0:T(8,128)(2,1)S(1)}) custom-call(bf16[6,10,8,256]{3,2,1,0:T(8,128)(2,1)S(1)} %copy.21.skip_ref, bf16[6,10,256]{2,1,0:T(8,128)(2,1)S(1)} %collective-permute-done.14.edge_ref, ...), custom_call_target="tpu_custom_call" | custom-call | tf_op jit(solution)/shard_map/decode_skip/pallas_call | solution.py:530
  95.4 5.0 %all-to-all-done.2.bottom_ref = bf16[8,2,6,8,128]{4,3,2,1,0:T(8,128)(2,1)S(1)} async-done(((bf16[8,2,6,8,128]{4,3,2,1,0:T(8,128)(2,1)}), bf16[8,2,6,8,128]{4,3,2,1,0:T(8,128)(2,1)S(1)}, u32[]{:S(2)}, u32[]{:S(2)}) %all-to-all-start.2) | async-done | bytes 196640 | tf_op jit(solution)/shard_map/all_to_all | solution.py:666
  100.4 6.1 %decode.1 = bf16[4,8,8,256]{3,2,1,0:T(8,128)(2,1)} custom-call(s32[5]{0:T(128)S(1)} %pad_add_fusion.place_ref, bf16[8,2,6,8,128]{4,3,2,1,0:T(8,128)(2,1)S(1)} %all-to-all-done.2.bottom_ref, f32[3,288,256]{2,1,0:T(8,128)S(1)} %get-tuple-element.47.skip_ref, bf16[3,512,256]{2,1,0:T(8,128)(2,1)S(1)} %get-tuple-element.48.refs_0_, ...), custom_call_target="tpu_custom_call" | custom-call | tf_op jit(solution)/shard_map/decode/pallas_call | solution.py:610
  (25 shorter events, 0.2 us)
Async XLA Ops:
  0.0 17.1 %copy-start = (bf16[8,16,16,128]{3,2,1,0:T(8,128)(2,1)S(1)}, bf16[8,16,16,128]{3,2,1,0:T(8,128)(2,1)}, u32[]{:S(2)}) copy-start(bf16[8,16,16,128]{3,2,1,0:T(8,128)(2,1)} %own_hbm.1) | copy-start | bytes 1572868
  1.1 12.2 %collective-permute-start = (bf16[3,16,16,128]{3,2,1,0:T(8,128)(2,1)S(1)}, bf16[3,16,16,128]{3,2,1,0:T(8,128)(2,1)S(1)}, u32[]{:S(2)}, u32[]{:S(2)}) collective-permute-start(bf16[3,16,16,128]{3,2,1,0:T(8,128)(2,1)S(1)} %get-tuple-element.55), channel_id=1, source_target_pairs={{0,16},{16,0},{32,48},{48,32},{64,80},{80,64},{96,112},{112,96},{1... | collective-permute-start | bytes 589832 | tf_op jit(solution)/shard_map/ppermute | solution.py:12
  4.3 12.8 %collective-permute-start.1 = (bf16[3,16,16,128]{3,2,1,0:T(8,128)(2,1)S(1)}, bf16[3,16,16,128]{3,2,1,0:T(8,128)(2,1)S(1)}, u32[]{:S(2)}, u32[]{:S(2)}) collective-permute-start(bf16[3,16,16,128]{3,2,1,0:T(8,128)(2,1)S(1)} %get-tuple-element.54), channel_id=1, source_target_pairs={{0,112},{16,32},{32,16},{48,64},{64,48},{80,96},{96,80},{112,0},{1... | collective-permute-start | bytes 589832 | tf_op jit(solution)/shard_map/ppermute | solution.py:12
  18.0 3.2 %collective-permute-start.2 = (bf16[14,3,16,128]{3,2,1,0:T(8,128)(2,1)S(1)}, bf16[14,3,16,128]{3,2,1,0:T(8,128)(2,1)S(1)}, u32[]{:S(2)}, u32[]{:S(2)}) collective-permute-start(bf16[14,3,16,128]{3,2,1,0:T(8,128)(2,1)S(1)} %get-tuple-element.33), channel_id=1, source_target_pairs={{0,2},{2,0},{4,6},{6,4},{8,10},{10,8},{12,14},{14,12},{1,3},{3,1},... | collective-permute-start | bytes 516104 | tf_op jit(solution)/shard_map/ppermute | solution.py:12
  18.1 6.2 %collective-permute-start.3 = (bf16[14,3,16,128]{3,2,1,0:T(8,128)(2,1)S(1)}, bf16[14,3,16,128]{3,2,1,0:T(8,128)(2,1)S(1)}, u32[]{:S(2)}, u32[]{:S(2)}) collective-permute-start(bf16[14,3,16,128]{3,2,1,0:T(8,128)(2,1)S(1)} %get-tuple-element.34), channel_id=1, source_target_pairs={{0,14},{2,4},{4,2},{6,8},{8,6},{10,12},{12,10},{14,0},{1,15},{3,5}... | collective-permute-start | bytes 516104 | tf_op jit(solution)/shard_map/ppermute | solution.py:12
  24.9 4.6 %collective-permute-start.4 = (bf16[14,22,128]{2,1,0:T(8,128)(2,1)S(1)}, bf16[14,22,128]{2,1,0:T(8,128)(2,1)S(1)}, u32[]{:S(2)}, u32[]{:S(2)}) collective-permute-start(bf16[14,22,128]{2,1,0:T(8,128)(2,1)S(1)} %pack_z.1), channel_id=1, source_target_pairs={{0,1},{1,0},{2,3},{3,2},{4,5},{5,4},{6,7},{7,6},{8,9},{9,8},{10,11... | collective-permute-start | bytes 236552 | tf_op jit(solution)/shard_map/ppermute | solution.py:645
  28.9 10.5 %copy-start.1 = (bf16[3,3,3,128,256]{4,3,2,1,0:T(8,128)(2,1)S(1)}, bf16[3,3,3,128,256]{4,3,2,1,0:T(8,128)(2,1)}, u32[]{:S(2)}) copy-start(bf16[3,3,3,128,256]{4,3,2,1,0:T(8,128)(2,1)} %param.8) | copy-start | bytes 5308420
  35.5 3.9 %collective-permute-start.5 = (bf16[6,10,128]{2,1,0:T(8,128)(2,1)S(1)}, bf16[6,10,128]{2,1,0:T(8,128)(2,1)S(1)}, u32[]{:S(2)}, u32[]{:S(2)}) collective-permute-start(bf16[6,10,128]{2,1,0:T(8,128)(2,1)S(1)} %fusion.1), channel_id=1, source_target_pairs={{0,1},{1,0},{2,3},{3,2},{4,5},{5,4},{6,7},{7,6},{8,9},{9,8},{10,11... | collective-permute-start | bytes 46088 | tf_op jit(solution)/shard_map/ppermute | solution.py:638
  40.8 4.3 %collective-permute-start.6 = (bf16[2,4,1,256]{3,1,0,2:T(4,128)(2,1)S(1)}, bf16[2,4,1,256]{3,1,0,2:T(4,128)(2,1)S(1)}, u32[]{:S(2)}, u32[]{:S(2)}) collective-permute-start(bf16[2,4,1,256]{3,1,0,2:T(4,128)(2,1)S(1)} %get-tuple-element.70), channel_id=1, source_target_pairs={{0,14},{2,4},{4,2},{6,8},{8,6},{10,12},{12,10},{14,0},{1,15},{3,5}... | collective-permute-start | bytes 12296 | tf_op jit(solution)/shard_map/ppermute | solution.py:12
  41.9 3.3 %collective-permute-start.7 = (bf16[2,4,1,256]{3,1,0,2:T(4,128)(2,1)S(1)}, bf16[2,4,1,256]{3,1,0,2:T(4,128)(2,1)S(1)}, u32[]{:S(2)}, u32[]{:S(2)}) collective-permute-start(bf16[2,4,1,256]{3,1,0,2:T(4,128)(2,1)S(1)} %get-tuple-element.71), channel_id=1, source_target_pairs={{0,2},{2,0},{4,6},{6,4},{8,10},{10,8},{12,14},{14,12},{1,3},{3,1},... | collective-permute-start | bytes 12296 | tf_op jit(solution)/shard_map/ppermute | solution.py:12
  41.9 9.8 %collective-permute-start.10 = (bf16[1,8,8,256]{3,1,0,2:T(8,128)(2,1)S(1)}, bf16[1,8,8,256]{3,1,0,2:T(8,128)(2,1)S(1)}, u32[]{:S(2)}, u32[]{:S(2)}) collective-permute-start(bf16[1,8,8,256]{3,1,0,2:T(8,128)(2,1)S(1)} %get-tuple-element.58), channel_id=1, source_target_pairs={{0,112},{16,32},{32,16},{48,64},{64,48},{80,96},{96,80},{112,0},{1... | collective-permute-start | bytes 98312 | tf_op jit(solution)/shard_map/ppermute | solution.py:12
  43.7 8.0 %collective-permute-start.11 = (bf16[1,8,8,256]{3,1,0,2:T(8,128)(2,1)S(1)}, bf16[1,8,8,256]{3,1,0,2:T(8,128)(2,1)S(1)}, u32[]{:S(2)}, u32[]{:S(2)}) collective-permute-start(bf16[1,8,8,256]{3,1,0,2:T(8,128)(2,1)S(1)} %get-tuple-element.59), channel_id=1, source_target_pairs={{0,16},{16,0},{32,48},{48,32},{64,80},{80,64},{96,112},{112,96},{1... | collective-permute-start | bytes 98312 | tf_op jit(solution)/shard_map/ppermute | solution.py:12
  46.0 15.9 %all-to-all-start = ((bf16[16,2,24,256]{3,2,1,0:T(8,128)(2,1)}), bf16[16,2,24,256]{3,2,1,0:T(8,128)(2,1)S(1)}, u32[]{:S(2)}, u32[]{:S(2)}) async-start(bf16[16,2,24,256]{3,2,1,0:T(8,128)(2,1)} %broadcast_in_dim.16.after_ref), calls=%async_computation | async-start | bytes 786432 | tf_op jit(solution)/shard_map/all_to_all | solution.py:656
  51.8 16.3 %collective-permute-start.12 = (bf16[6,1,8,256]{3,1,0,2:T(2,128)(2,1)S(1)}, bf16[6,1,8,256]{3,1,0,2:T(2,128)(2,1)S(1)}, u32[]{:S(2)}, u32[]{:S(2)}) collective-permute-start(bf16[6,1,8,256]{3,1,0,2:T(2,128)(2,1)S(1)} %get-tuple-element.51), channel_id=1, source_target_pairs={{0,14},{2,4},{4,2},{6,8},{8,6},{10,12},{12,10},{14,0},{1,15},{3,5}... | collective-permute-start | bytes 73736 | tf_op jit(solution)/shard_map/ppermute | solution.py:12
  53.2 15.0 %collective-permute-start.13 = (bf16[6,1,8,256]{3,1,0,2:T(2,128)(2,1)S(1)}, bf16[6,1,8,256]{3,1,0,2:T(2,128)(2,1)S(1)}, u32[]{:S(2)}, u32[]{:S(2)}) collective-permute-start(bf16[6,1,8,256]{3,1,0,2:T(2,128)(2,1)S(1)} %broadcast_select_fusion.7), channel_id=1, source_target_pairs={{0,2},{2,0},{4,6},{6,4},{8,10},{10,8},{12,14},{14,12},{1,3},{3,1},... | collective-permute-start | bytes 73736 | tf_op jit(solution)/shard_map/ppermute | solution.py:12
  64.6 12.9 %all-to-all-start.1 = ((bf16[8,8,6,4,128]{4,3,2,1,0:T(4,128)(2,1)}), bf16[8,8,6,4,128]{4,3,2,1,0:T(4,128)(2,1)S(1)}, u32[]{:S(2)}, u32[]{:S(2)}) async-start(bf16[8,8,6,4,128]{4,3,2,1,0:T(4,128)(2,1)} %bottom_in.1), calls=%async_computation.1 | async-start | bytes 786432 | tf_op jit(solution)/shard_map/all_to_all | solution.py:658
  78.0 6.3 %collective-permute-start.8 = (bf16[8,8,6,2,128]{4,3,2,1,0:T(2,128)(2,1)S(1)}, bf16[8,8,6,2,128]{4,3,2,1,0:T(2,128)(2,1)S(1)}, u32[]{:S(2)}, u32[]{:S(2)}) collective-permute-start(bf16[8,8,6,2,128]{4,3,2,1,0:T(2,128)(2,1)S(1)} %get-tuple-element.57), channel_id=1, source_target_pairs={{0,2},{2,0},{4,6},{6,4},{8,10},{10,8},{12,14},{14,12},{1,3},{3,1},... | collective-permute-start | bytes 589832 | tf_op jit(solution)/shard_map/ppermute | solution.py:12
  78.1 6.4 %collective-permute-start.9 = (bf16[8,8,6,2,128]{4,3,2,1,0:T(2,128)(2,1)S(1)}, bf16[8,8,6,2,128]{4,3,2,1,0:T(2,128)(2,1)S(1)}, u32[]{:S(2)}, u32[]{:S(2)}) collective-permute-start(bf16[8,8,6,2,128]{4,3,2,1,0:T(2,128)(2,1)S(1)} %get-tuple-element.56), channel_id=1, source_target_pairs={{0,14},{2,4},{4,2},{6,8},{8,6},{10,12},{12,10},{14,0},{1,15},{3,5}... | collective-permute-start | bytes 589832 | tf_op jit(solution)/shard_map/ppermute | solution.py:12
  80.1 4.2 %collective-permute-start.14 = (bf16[6,10,256]{2,1,0:T(8,128)(2,1)S(1)}, bf16[6,10,256]{2,1,0:T(8,128)(2,1)S(1)}, u32[]{:S(2)}, u32[]{:S(2)}) collective-permute-start(bf16[6,10,256]{2,1,0:T(8,128)(2,1)S(1)} %fusion), channel_id=1, source_target_pairs={{0,1},{1,0},{2,3},{3,2},{4,5},{5,4},{6,7},{7,6},{8,9},{9,8},{10,11... | collective-permute-start | bytes 92168 | tf_op jit(solution)/shard_map/ppermute | solution.py:638
  88.6 11.8 %all-to-all-start.2 = ((bf16[8,2,6,8,128]{4,3,2,1,0:T(8,128)(2,1)}), bf16[8,2,6,8,128]{4,3,2,1,0:T(8,128)(2,1)S(1)}, u32[]{:S(2)}, u32[]{:S(2)}) async-start(bf16[8,2,6,8,128]{4,3,2,1,0:T(8,128)(2,1)} %bottom_out.1), calls=%async_computation.2 | async-start | bytes 393216 | tf_op jit(solution)/shard_map/all_to_all | solution.py:666

commit v9 on v7

--- a/solution.py
+++ b/solution.py
@@ -9,6 +9,8 @@
 def send(inner_block, outer_block, axis, count):
     inner = [(i, i ^ 1) for i in range(count)]
     outer = [(i, (((i + 1) ^ 1) - 1) % count) for i in range(count)]
+    if isinstance(axis, tuple):
+        inner, outer = [[(2 * i + n, 2 * j + 1 - n) for i, j in pairs for n in range(2)] for pairs in (inner, outer)]
     return lax.ppermute(inner_block, axis, inner), lax.ppermute(outer_block, axis, outer)
 
 
@@ -100,7 +102,7 @@
     return down + mid + up
 
 
-def encode(place, own, x_in, x_out, y_in, y_out, edge, weights):
+def encode(place, own, x_in, x_out, y_in, y_out, edge, edge_in, edge_out, weights):
     own_x, own_y, size_z, channels = own.shape
     reach = x_in.shape[0]
     full_x, full_y = own_x + 2 * reach, own_y + 2 * reach
@@ -111,71 +113,72 @@
 
     def body(
         place_ref,
-        own_hbm,
+        own_ref,
         x_in_ref,
         x_out_ref,
         y_in_ref,
         y_out_ref,
         edge_ref,
-        weights_hbm,
+        edge_in_ref,
+        edge_out_ref,
+        weights_ref,
         out_ref,
-        field_ref,
+        x_ref,
+        y_ref,
         side_ref,
         rows_ref,
-        weights_ref,
-        sems,
     ):
-        inner = field_ref.at[reach : reach + own_x, reach : reach + own_y]
-        copies = [pltpu.make_async_copy(own_hbm, inner, sems.at[0])]
-        for tap in range(3):
-            copies.append(pltpu.make_async_copy(weights_hbm.at[:, :, tap], weights_ref.at[tap], sems.at[1 + tap]))
-        for copy in copies:
-            copy.start()
         even_x, even_y = place_ref[0] % 2 == 0, place_ref[1] % 2 == 0
         low_x, high_x = place_ref[0] > 0, place_ref[0] < place_ref[3]
         low_y, high_y = place_ref[1] > 0, place_ref[1] < place_ref[4]
         nil = jnp.bfloat16(0)
-        inner_y = slice(reach, reach + own_y)
-        below, above = jnp.where(even_x, x_out_ref[...], x_in_ref[...]), jnp.where(even_x, x_in_ref[...], x_out_ref[...])
-        field_ref[:reach, inner_y] = jnp.where(low_x, below, nil)
-        field_ref[reach + own_x :, inner_y] = jnp.where(high_x, above, nil)
+        x_ref[0] = jnp.where(low_x, jnp.where(even_x, x_out_ref[...], x_in_ref[...]), nil)
+        x_ref[1] = jnp.where(high_x, jnp.where(even_x, x_in_ref[...], x_out_ref[...]), nil)
         for x in range(full_x):
-            here_low, here_high = low_y, high_y
+            here_low, here_high, here = low_y, high_y, None
             if x < reach:
-                here_low, here_high = low_y & low_x, high_y & low_x
+                here_low, here_high, here = low_y & low_x, high_y & low_x, low_x
             if x >= reach + own_x:
-                here_low, here_high = low_y & high_x, high_y & high_x
-            below, above = jnp.where(even_y, y_out_ref[x], y_in_ref[x]), jnp.where(even_y, y_in_ref[x], y_out_ref[x])
-            field_ref[x, :reach] = jnp.where(here_low, below, nil)
-            field_ref[x, reach + own_y :] = jnp.where(here_high, above, nil)
-            line = lax.broadcasted_iota(jnp.int32, (full_y, channels), 0)
-            inside = ((line >= reach) | low_y) & ((line < reach + own_y) | high_y)
+                here_low, here_high, here = low_y & high_x, high_y & high_x, high_x
+            y_ref[0, x] = jnp.where(here_low, jnp.where(even_y, y_out_ref[x], y_in_ref[x]), nil)
+            y_ref[1, x] = jnp.where(here_high, jnp.where(even_y, y_in_ref[x], y_out_ref[x]), nil)
+            middle = edge_ref[x].astype(jnp.float32)
+            if here is not None:
+                middle = jnp.where(here, middle, 0.0)
+            one, other = edge_in_ref[x].astype(jnp.float32), edge_out_ref[x].astype(jnp.float32)
+            below = jnp.where(here_low, jnp.where(even_y, other, one), 0.0)
+            above = jnp.where(here_high, jnp.where(even_y, one, other), 0.0)
+            for dy in range(3):
+                if dy < reach:
+                    side_ref[dy, x, : reach - dy] = below[dy:]
+                side_ref[dy, x, reach - dy : reach - dy + own_y] = middle
+                side_ref[dy, x, reach - dy + own_y : size_y] = above[: dy + 1]
+                side_ref[dy, x, size_y:] = jnp.zeros((extra - size_y, channels), jnp.float32)
+
+        def lines(x, dy):
             if x < reach:
-                inside = inside & low_x
-            if x >= reach + own_x:
-                inside = inside & high_x
-            plane = jnp.where(inside, edge_ref[x].astype(jnp.float32), 0.0)
-            for dy in range(3):
-                side_ref[dy, x, :size_y] = plane[dy : dy + size_y]
-                side_ref[dy, x, size_y:] = jnp.zeros((extra - size_y, channels), jnp.float32)
+                middle = x_ref[0, x]
+            elif x < reach + own_x:
+                middle = own_ref[x - reach]
+            else:
+                middle = x_ref[1, x - reach - own_x]
+            block = jnp.concatenate([y_ref[0, x, dy:], middle, y_ref[1, x, : dy + 1]], axis=0)
+            return block.reshape(rows, channels)
 
         first = place_ref[2] == 0
-        copies[0].wait()
         line = lax.broadcasted_iota(jnp.int32, (pool_y, pool_z, filters), 0)
         inside_y = ((line > 0) | low_y) & ((line < pool_y - 1) | high_y)
         for pair in range(size_x // 2):
             blocks = []
             for plane in range(4):
                 for dy in range(3):
-                    main = field_ref[2 * pair + plane, dy : dy + size_y].reshape(rows, channels)
+                    main = lines(2 * pair + plane, dy)
                     side = side_ref[dy, 2 * pair + plane].astype(jnp.bfloat16)
                     blocks.append(jnp.concatenate([main, side], axis=0))
             block = jnp.concatenate(blocks, axis=1)
             sums = []
             for tap in range(3):
-                if pair == 0:
-                    copies[1 + tap].wait()
-                kernel = weights_ref[tap].reshape(12 * channels, 2 * filters)
+                kernel = weights_ref[:, :, tap].reshape(12 * channels, 2 * filters)
                 sums.append(jnp.dot(block, kernel, preferred_element_type=jnp.float32))
             total = jnp.maximum(join_taps(first, sums, size_y, size_z), 0.0)
             total = jnp.maximum(total[..., :filters], total[..., filters:])
@@ -193,21 +196,45 @@
 
     return pl.pallas_call(
         body,
-        in_specs=[pl.BlockSpec(memory_space=pltpu.SMEM), pl.BlockSpec(memory_space=pltpu.HBM)]
-        + [pl.BlockSpec(memory_space=pltpu.VMEM)] * 5
-        + [pl.BlockSpec(memory_space=pltpu.HBM)],
+        in_specs=[pl.BlockSpec(memory_space=pltpu.SMEM)] + [pl.BlockSpec(memory_space=pltpu.VMEM)] * 9,
         out_specs=pl.BlockSpec(memory_space=pltpu.VMEM),
         out_shape=jax.ShapeDtypeStruct((size_x // 2, pool_y, pool_z, filters), jnp.bfloat16),
         scratch_shapes=[
-            pltpu.VMEM((full_x, full_y, size_z, channels), jnp.bfloat16),
+            pltpu.VMEM((2, reach, own_y, size_z, channels), jnp.bfloat16),
+            pltpu.VMEM((2, full_x, reach, size_z, channels), jnp.bfloat16),
             pltpu.VMEM((3, full_x, extra, channels), jnp.float32),
             pltpu.VMEM((pool_y * size_z, filters), jnp.float32),
-            pltpu.VMEM((3, 4, 3, channels, 2 * filters), weights.dtype),
-            pltpu.SemaphoreType.DMA((4,)),
         ],
-        compiler_params=pltpu.CompilerParams(vmem_limit_bytes=20 << 20),
+        compiler_params=pltpu.CompilerParams(vmem_limit_bytes=14 << 20),
         name="encode",
-    )(place, far(own), x_in, x_out, y_in, y_out, edge, far(weights))
+    )(place, near(own), x_in, x_out, y_in, y_out, edge, edge_in, edge_out, near(weights))
+
+
+def near(array):
+    return pltpu.with_memory_space_constraint(array, pltpu.VMEM)
+
+
+def bring(arrays, after):
+    pieces = [(i, n) for i, array in enumerate(arrays) for n in range(array.shape[0])]
+    count = len(arrays)
+
+    def body(*refs):
+        hbms, outs, sems = refs[:count], refs[count + 1 : -1], refs[-1]
+        copies = [pltpu.make_async_copy(hbms[i].at[n], outs[i].at[n], sems.at[k]) for k, (i, n) in enumerate(pieces)]
+        for copy in copies:
+            copy.start()
+        for copy in copies:
+            copy.wait()
+
+    return pl.pallas_call(
+        body,
+        in_specs=[pl.BlockSpec(memory_space=pltpu.HBM)] * count + [pl.BlockSpec(memory_space=pl.ANY)],
+        out_specs=[pl.BlockSpec(memory_space=pltpu.VMEM)] * count,
+        out_shape=[pltpu.VMEM(array.shape, array.dtype) for array in arrays],
+        scratch_shapes=[pltpu.SemaphoreType.DMA((len(pieces),))],
+        compiler_params=pltpu.CompilerParams(vmem_limit_bytes=4 << 20),
+        name="bring",
+    )(*map(far, arrays), after)
 
 
 def far(array):
@@ -272,7 +299,7 @@
     reach = x_in.shape[0]
     full_x = own_x + 2 * reach
 
-    def body(place_ref, own_ref, x_in_ref, x_out_ref, inner_ref, outer_ref, plane_ref, rows_ref):
+    def body(place_ref, own_ref, x_in_ref, x_out_ref, inner_ref, outer_ref, plane_ref, inner_edge_ref, outer_edge_ref, rows_ref):
         even_x, even_y, first = place_ref[0] % 2 == 0, place_ref[1] % 2 == 0, place_ref[2] == 0
         below = jnp.where(even_x, x_out_ref[...], x_in_ref[...])
         above = jnp.where(even_x, x_in_ref[...], x_out_ref[...])
@@ -287,47 +314,20 @@
                 for y in range(own_y):
                     rows_ref[start + x, y : y + 1] = edge[x, y]
         plane_ref[...] = rows_ref[...].astype(plane_ref.dtype)
+        low, high = rows_ref[:, :reach], rows_ref[:, own_y - reach :]
+        inner_edge_ref[...] = jnp.where(even_y, high, low).astype(plane_ref.dtype)
+        outer_edge_ref[...] = jnp.where(even_y, low, high).astype(plane_ref.dtype)
 
     return pl.pallas_call(
         body,
         in_specs=[pl.BlockSpec(memory_space=pltpu.SMEM)] + [pl.BlockSpec(memory_space=pltpu.VMEM)] * 3,
-        out_specs=[pl.BlockSpec(memory_space=pltpu.VMEM)] * 3,
+        out_specs=[pl.BlockSpec(memory_space=pltpu.VMEM)] * 5,
         out_shape=[jax.ShapeDtypeStruct((full_x, reach, size_z, channels), jnp.bfloat16)] * 2
-        + [jax.ShapeDtypeStruct((full_x, own_y, channels), jnp.bfloat16)],
+        + [jax.ShapeDtypeStruct((full_x, rows, channels), jnp.bfloat16) for rows in (own_y, reach, reach)],
         scratch_shapes=[pltpu.VMEM((full_x, own_y, channels), jnp.float32)],
         compiler_params=pltpu.CompilerParams(vmem_limit_bytes=8 << 20),
         name="pack_y",
     )(place, own, x_in, x_out)
-
-
-def pack_z(place, plane, y_in, y_out):
-    full_x, own_y, channels = plane.shape
-    reach, size_z = y_in.shape[1:3]
-    full_y = own_y + 2 * reach
-
-    def body(place_ref, plane_ref, y_in_ref, y_out_ref, out_ref, rows_ref):
-        even_y, first = place_ref[1] % 2 == 0, place_ref[2] == 0
-        rows_ref[:, reach : reach + own_y] = plane_ref[...].astype(jnp.float32)
-        edges = []
-        for ref in (y_in_ref, y_out_ref):
-            block = ref[...].astype(jnp.float32)
-            edges.append(jnp.where(first, block[:, :, size_z - 1 :], block[:, :, :1]))
-        below, above = jnp.where(even_y, edges[1], edges[0]), jnp.where(even_y, edges[0], edges[1])
-        for x in range(full_x):
-            for y in range(reach):
-                rows_ref[x, y : y + 1] = below[x, y]
-                rows_ref[x, reach + own_y + y : reach + own_y + y + 1] = above[x, y]
-        out_ref[...] = rows_ref[...].astype(out_ref.dtype)
-
-    return pl.pallas_call(
-        body,
-        in_specs=[pl.BlockSpec(memory_space=pltpu.SMEM)] + [pl.BlockSpec(memory_space=pltpu.VMEM)] * 3,
-        out_specs=pl.BlockSpec(memory_space=pltpu.VMEM),
-        out_shape=jax.ShapeDtypeStruct((full_x, full_y, channels), jnp.bfloat16),
-        scratch_shapes=[pltpu.VMEM((full_x, full_y, channels), jnp.float32)],
-        compiler_params=pltpu.CompilerParams(vmem_limit_bytes=8 << 20),
-        name="pack_z",
-    )(place, plane, y_in, y_out)
 
 
 def halves(pair_low, pair_high):
@@ -366,9 +366,7 @@
     own_z = size_y = 4
     size_x, all_z, size_z = devices * own_x, 2 * own_z, own_z + 2
 
-    def body(place_ref, field_ref, weights_hbm, out_ref, pad_ref, weights_ref, sem):
-        copy = pltpu.make_async_copy(weights_hbm, weights_ref, sem)
-        copy.start()
+    def body(place_ref, field_ref, weights_ref, out_ref, pad_ref):
         zero = jnp.zeros((all_z + 2, 8, channels), jnp.float32)
         pad_ref[0] = zero
         pad_ref[size_x + 1] = zero
@@ -387,7 +385,6 @@
                         pad_ref[*to, size_y + 1 : size_y + 2] = block[line : line + 1]
                         pad_ref[*to, size_y + 2 :] = zero[0, size_y + 2 :]
         start = 2 * place_ref[2]
-        copy.wait()
         for first in range(0, size_x, 4):
             total = column_product(pad_ref, weights_ref, first, start, 4, size_z)
             for pair in range(2):
@@ -397,17 +394,15 @@
 
     return pl.pallas_call(
         body,
-        in_specs=[pl.BlockSpec(memory_space=space) for space in (pltpu.SMEM, pltpu.VMEM, pltpu.HBM)],
+        in_specs=[pl.BlockSpec(memory_space=space) for space in (pltpu.SMEM, pltpu.VMEM, pltpu.VMEM)],
         out_specs=pl.BlockSpec(memory_space=pltpu.VMEM),
         out_shape=jax.ShapeDtypeStruct((devices, size_x // 2, size_z, size_y, 128), jnp.bfloat16),
         scratch_shapes=[
             pltpu.VMEM((size_x + 2, all_z + 2, 8, channels), jnp.float32),
-            pltpu.VMEM(weights.shape, weights.dtype),
-            pltpu.SemaphoreType.DMA(()),
         ],
         compiler_params=pltpu.CompilerParams(vmem_limit_bytes=12 << 20),
         name="bottom_in",
-    )(place, field, far(weights))
+    )(place, field, near(weights))
 
 
 def bottom_out(place, field, y_in, y_out, weights):
@@ -415,9 +410,7 @@
     size_x, channels = 2 * pairs, 64 * devices
     own_x = size_x // devices
 
-    def body(place_ref, field_ref, y_in_ref, y_out_ref, weights_hbm, out_ref, pad_ref, total_ref, weights_ref, sem):
-        copy = pltpu.make_async_copy(weights_hbm, weights_ref, sem)
-        copy.start()
+    def body(place_ref, field_ref, y_in_ref, y_out_ref, weights_ref, out_ref, pad_ref, total_ref):
         even_y = place_ref[1] % 2 == 0
         low_y, high_y = place_ref[1] > 0, place_ref[1] < place_ref[4]
         zero = jnp.zeros((size_z + 2, 8, channels), jnp.float32)
@@ -442,7 +435,6 @@
                     lines = slice(line, line + even.shape[1])
                     pad_ref[1 + 2 * pair, 1 : size_z + 1, lines, 128 * k : 128 * k + 128] = even
                     pad_ref[2 + 2 * pair, 1 : size_z + 1, lines, 128 * k : 128 * k + 128] = odd
-        copy.wait()
         for first in range(0, size_x, 4):
             total = column_product(pad_ref, weights_ref, first, 0, 4, size_z)
             total_ref[1 + first : 5 + first, 1 : size_z + 1] = total
@@ -458,19 +450,16 @@
     return pl.pallas_call(
         body,
         in_specs=[pl.BlockSpec(memory_space=pltpu.SMEM)]
-        + [pl.BlockSpec(memory_space=pltpu.VMEM)] * 3
-        + [pl.BlockSpec(memory_space=pltpu.HBM)],
+        + [pl.BlockSpec(memory_space=pltpu.VMEM)] * 4,
         out_specs=pl.BlockSpec(memory_space=pltpu.VMEM),
         out_shape=jax.ShapeDtypeStruct((devices, own_x, size_z, 8, 128), jnp.bfloat16),
         scratch_shapes=[
             pltpu.VMEM((size_x + 2, size_z + 2, 8, channels), jnp.float32),
             pltpu.VMEM((size_x + 2, size_z + 2, 8, 128), jnp.float32),
-            pltpu.VMEM(weights.shape, weights.dtype),
-            pltpu.SemaphoreType.DMA(()),
         ],
-        compiler_params=pltpu.CompilerParams(vmem_limit_bytes=20 << 20),
+        compiler_params=pltpu.CompilerParams(vmem_limit_bytes=16 << 20),
         name="bottom_out",
-    )(place, field, y_in, y_out, far(weights))
+    )(place, field, y_in, y_out, near(weights))
 
 
 def decode_skip(place, skip, edge, weights):
@@ -520,10 +509,6 @@
         compiler_params=pltpu.CompilerParams(vmem_limit_bytes=14 << 20),
         name="decode_skip",
     )(skip, edge, far(weights))
-
-
-def near(array):
-    return pltpu.with_memory_space_constraint(array, pltpu.VMEM)
 
 
 def decode(place, bottom, skip_sums, first_weights, weights, shape):
@@ -625,10 +610,12 @@
         x_in, x_out = swaps(volume[:3], volume[-3:], "gx", gx)
         turned = [w.transpose(0, 1, 2, 4, 3) for w in (w_bottom_in, w_bottom_out)]
         (w_pair, w_in, w_out), x_in, x_out = lax.optimization_barrier((prepare(w_full, *turned), x_in, x_out))
-        y_inner, y_outer, plane = pack_y(place, volume, x_in, x_out)
+        y_inner, y_outer, plane, edge_inner, edge_outer = pack_y(place, volume, x_in, x_out)
         y_in, y_out = send(y_inner, y_outer, "gy", gy)
-        edge = lax.ppermute(pack_z(place, plane, y_in, y_out), "gz", swap)
-        pooled = encode(place, volume, x_in, x_out, y_in, y_out, edge, w_pair)
+        edge = lax.ppermute(plane, "gz", swap)
+        edge_in, edge_out = send(edge_inner, edge_outer, ("gy", "gz"), gy)
+        own, w_pair = bring([volume, w_pair], plane)
+        pooled = encode(place, own, x_in, x_out, y_in, y_out, edge, edge_in, edge_out, w_pair)
 
         edge = edge_of(pooled[:, :, 0], pooled[:, :, -1])
         skip, coarse = half_level(place, pooled, edge, w_half.reshape(9, 3, w_half.shape[3], w_half.shape[4]))
@@ -636,9 +623,11 @@
         below, above = halo(lines, "gy", gy, 2, 1)
         column = jnp.concatenate([coarse, below[:, :, 0], above[:, :, 0]], axis=1)
         column = jnp.broadcast_to(column[None], (gx * gz,) + column.shape)
+        (w_in,) = bring([w_in], column)
         column = lax.all_to_all(column, ("gx", "gz"), 0, 0)
         first = bottom_in(place, column, w_in)
         first = lax.all_to_all(first, "gx", 0, 0)
+        (w_out,) = bring([w_out], first)
         y_in, y_out = swaps(first[:, :, :, :2], first[:, :, :, -2:], "gy", gy)
         around = extend(skip, "gx", gx, 0, 1)
         around = extend(around, "gy", gy, 1, 1)

time: 112 us -> 105 us (0.938)
  waiting for transfers between devices: 38.9 us -> 31.7 us
    ppermute x1, waiting for transfers between devices: 2.99 us -> 0.01 us  [local(): edge = lax.ppermute(plane, 'gz', swap)]
    pallas_call x2 -> x4, Pallas kernels: 8.67 us -> 11 us  [the longest x1 5.97 us: encode(): pl.pallas_call(body, in_specs=[pl.BlockSpec(memory_space=pltpu.SMEM)] + [...]
    all_to_all x1, waiting for transfers between devices: 7.35 us -> 5.16 us  [local(): column = lax.all_to_all(column, ('gx', 'gz'), 0, 0)]
    ppermute x6 -> x7, starting transfers between devices: 14.4 us -> 16.6 us  [send(): lax.ppermute(outer_block, axis, outer)]
    pallas_call x1, Pallas kernels: 6.19 us -> 4.13 us  [bottom_out(): pl.pallas_call(body, in_specs=[pl.BlockSpec(memory_space=pltpu.SMEM)] + [...]
    ppermute x6 -> x7, waiting for transfers between devices: 8.66 us -> 7.45 us  [send(): lax.ppermute(outer_block, axis, outer)]
    ppermute x6 -> x7, starting transfers between devices: 3.45 us -> 3.53 us  [send(): lax.ppermute(inner_block, axis, inner)]
  transfers between devices with their start and end apart: 18 -> 20, of which waited for: 10 -> 8; matrix products, arithmetic and copies ran while one was open for 1% -> 2% of each run, Pallas kernels for 11% -> 15%
where the time goes in v9:
time: 105 us
  starting transfers between devices  34.8 us (33%)
  Pallas kernels  34.4 us (33%)
  waiting for transfers between devices  31.7 us (30%)
  other arithmetic  2.26 us (2%)
  local copies, waits for them, and re-layouts  1.05 us (1%)
    ppermute x7, starting transfers between devices, send(): lax.ppermute(outer_block, axis, outer)  16.6 us
    all_to_all x1, waiting for transfers between devices, local(): first = lax.all_to_all(first, 'gx', 0, 0)  9.04 us
    ppermute x7, waiting for transfers between devices, send(): lax.ppermute(outer_block, axis, outer)  7.45 us
    pallas_call x1, Pallas kernels, decode(): pl.pallas_call(body, in_specs=[pl.BlockSpec(memory_space=pltpu.SMEM)] + [...  6.06 us
    pallas_call x1, Pallas kernels, encode(): pl.pallas_call(body, in_specs=[pl.BlockSpec(memory_space=pltpu.SMEM)] + [...  5.97 us
    all_to_all x1, waiting for transfers between devices, local(): column = lax.all_to_all(column, ('gx', 'gz'), 0, 0)  5.16 us
    ppermute x2, waiting for transfers between devices, edge_of(): lax.ppermute(jnp.where(place_z == 0, plane_high, plane_low), 'gz', swap)  5.08 us
    pallas_call x3, Pallas kernels, bring(): pl.pallas_call(body, in_specs=[pl.BlockSpec(memory_space=pltpu.HBM)] * co...  5.03 us
  transfers between devices with their start and end apart: 20, of which 8 were waited for; matrix products, arithmetic and copies ran while one was open for 2% of the time, Pallas kernels for 15%

profile of v9, /device:TPU:0, one launch (start us, length us, event | category | flops | bytes accessed | tf_op | source)
XLA Modules:
  0.0 104.7 jit_solution(7256269614816850655)
XLA Ops:
  0.0 1.1 %broadcast_select_fusion.2 = (bf16[3,16,16,128]{3,2,1,0:T(8,128)(2,1)S(1)}, bf16[3,16,16,128]{3,2,1,0:T(8,128)(2,1)S(1)}) fusion(pred[]{:T(512)S(6)} %eq.25, bf16[8,16,16,128]{3,2,1,0:T(8,128)(2,1)} %refs_0_.1), kind=kLoop, calls=%fused_computation.3 | loop fusion | flops 196608 | bytes 786433 | tf_op jit(solution)/shard_map/jit(_where)/select_n | solution.py:19
  1.1 3.2 %collective-permute-start = (bf16[3,16,16,128]{3,2,1,0:T(8,128)(2,1)S(1)}, bf16[3,16,16,128]{3,2,1,0:T(8,128)(2,1)S(1)}, u32[]{:S(2)}, u32[]{:S(2)}) collective-permute-start(bf16[3,16,16,128]{3,2,1,0:T(8,128)(2,1)S(1)} %get-tuple-element.59), channel_id=1, source_target_pairs={{0,16},{16,0},{32,48},{48,32},{64,80},{80,64},{96,112},{112,96},{1... | collective-permute-start | bytes 589832 | tf_op jit(solution)/shard_map/ppermute | solution.py:14
  4.3 4.0 %collective-permute-start.1 = (bf16[3,16,16,128]{3,2,1,0:T(8,128)(2,1)S(1)}, bf16[3,16,16,128]{3,2,1,0:T(8,128)(2,1)S(1)}, u32[]{:S(2)}, u32[]{:S(2)}) collective-permute-start(bf16[3,16,16,128]{3,2,1,0:T(8,128)(2,1)S(1)} %get-tuple-element.58), channel_id=1, source_target_pairs={{0,112},{16,32},{32,16},{48,64},{64,48},{80,96},{96,80},{112,0},{1... | collective-permute-start | bytes 589832 | tf_op jit(solution)/shard_map/ppermute | solution.py:14
  8.3 4.9 %prepare.1 = (bf16[4,3,3,128,256]{4,3,2,1,0:T(8,128)(2,1)}, bf16[9,256,256]{2,1,0:T(8,128)(2,1)}, bf16[9,512,256]{2,1,0:T(8,128)(2,1)}) custom-call(bf16[3,3,3,128,128]{4,3,2,1,0:T(8,128)(2,1)} %full_hbm.1, bf16[3,3,3,64,256]{4,3,2,1,0:T(8,128)(2,1)} %bitcast.20, bf16[3,3,3,64,512]{4,3,2,1,0:T(8,128)(2,1)} %bitcast.19), custom_call_target="tpu_custom_call" | custom-call | tf_op jit(solution)/shard_map/prepare/pallas_call | solution.py:283
  13.2 0.1 pad_add_fusion.place_ref
  13.3 3.8 %collective-permute-done.1.x_out_ref = bf16[3,16,16,128]{3,2,1,0:T(8,128)(2,1)S(1)} collective-permute-done((bf16[3,16,16,128]{3,2,1,0:T(8,128)(2,1)S(1)}, bf16[3,16,16,128]{3,2,1,0:T(8,128)(2,1)S(1)}, u32[]{:S(2)}, u32[]{:S(2)}) %collective-permute-start.1) | collective-permute-done | bytes 196640 | tf_op jit(solution)/shard_map/ppermute | solution.py:14
  17.1 0.9 pack_y.1
  18.0 0.1 collective-permute-start.2
  18.1 3.1 %collective-permute-start.3 = (bf16[14,3,16,128]{3,2,1,0:T(8,128)(2,1)S(1)}, bf16[14,3,16,128]{3,2,1,0:T(8,128)(2,1)S(1)}, u32[]{:S(2)}, u32[]{:S(2)}) collective-permute-start(bf16[14,3,16,128]{3,2,1,0:T(8,128)(2,1)S(1)} %get-tuple-element.39), channel_id=1, source_target_pairs={{0,14},{2,4},{4,2},{6,8},{8,6},{10,12},{12,10},{14,0},{1,15},{3,5}... | collective-permute-start | bytes 516104 | tf_op jit(solution)/shard_map/ppermute | solution.py:14
  21.2 1.5 %collective-permute-start.4 = (bf16[14,16,128]{2,1,0:T(8,128)(2,1)S(1)}, bf16[14,16,128]{2,1,0:T(8,128)(2,1)S(1)}, u32[]{:S(2)}, u32[]{:S(2)}) collective-permute-start(bf16[14,16,128]{2,1,0:T(8,128)(2,1)S(1)} %get-tuple-element.36.refs_2_), channel_id=1, source_target_pairs={{0,1},{1,0},{2,3},{3,2},{4,5},{5,4},{6,7},{7,6},{8,9},{9,8},{10,11... | collective-permute-start | bytes 172040 | tf_op jit(solution)/shard_map/ppermute | solution.py:615
  22.7 1.9 %collective-permute-start.6 = (bf16[14,3,128]{2,1,0:T(4,128)(2,1)S(1)}, bf16[14,3,128]{2,1,0:T(4,128)(2,1)S(1)}, u32[]{:S(2)}, u32[]{:S(2)}) collective-permute-start(bf16[14,3,128]{2,1,0:T(4,128)(2,1)S(1)} %get-tuple-element.41), channel_id=1, source_target_pairs={{0,15},{1,14},{2,5},{3,4},{4,3},{5,2},{6,9},{7,8},{8,7},{9,6},{10,... | collective-permute-start | bytes 32264 | tf_op jit(solution)/shard_map/ppermute | solution.py:14
  24.6 2.0 %bring.3 = (bf16[8,16,16,128]{3,2,1,0:T(8,128)(2,1)S(1)}, bf16[4,3,3,128,256]{4,3,2,1,0:T(8,128)(2,1)S(1)}) custom-call(bf16[8,16,16,128]{3,2,1,0:T(8,128)(2,1)} %refs_0_.1, bf16[4,3,3,128,256]{4,3,2,1,0:T(8,128)(2,1)} %get-tuple-element.33.refs_1_, bf16[14,16,128]{2,1,0:T(8,128)(2,1)S(1)} %get-tuple-element.36.refs_2_), custom_call_target="tpu_custom_call" | custom-call | tf_op jit(solution)/shard_map/bring/pallas_call | solution.py:229
  26.6 0.0 copy-start.1
  26.6 0.0 collective-permute-done.5.edge_in_ref
  26.6 1.3 %collective-permute-done.6.edge_out_ref = bf16[14,3,128]{2,1,0:T(4,128)(2,1)S(1)} collective-permute-done((bf16[14,3,128]{2,1,0:T(4,128)(2,1)S(1)}, bf16[14,3,128]{2,1,0:T(4,128)(2,1)S(1)}, u32[]{:S(2)}, u32[]{:S(2)}) %collective-permute-start.6) | collective-permute-done | bytes 10784 | tf_op jit(solution)/shard_map/ppermute | solution.py:14
  28.0 6.0 %encode.1.field_ref = bf16[6,10,8,128]{3,2,1,0:T(8,128)(2,1)S(1)} custom-call(s32[5]{0:T(128)S(1)} %pad_add_fusion.place_ref, bf16[8,16,16,128]{3,2,1,0:T(8,128)(2,1)S(1)} %get-tuple-element.37.own_ref, bf16[3,16,16,128]{3,2,1,0:T(8,128)(2,1)S(1)} %collective-permute-done.x_in_ref, bf16[3,16,16,128]{3,2,1,0:T(8,128)(2,1)S(1)} %collective-permute-done.1.x_out_ref, ...), custom_call_target="tpu_custom_call" | custom-call | tf_op jit(solution)/shard_map/encode/pallas_call | solution.py:197
  34.0 0.6 collective-permute-start.7
  34.7 3.3 %collective-permute-done.7.edge_ref = bf16[6,10,128]{2,1,0:T(8,128)(2,1)S(1)} collective-permute-done((bf16[6,10,128]{2,1,0:T(8,128)(2,1)S(1)}, bf16[6,10,128]{2,1,0:T(8,128)(2,1)S(1)}, u32[]{:S(2)}, u32[]{:S(2)}) %collective-permute-start.7) | collective-permute-done | bytes 15392 | tf_op jit(solution)/shard_map/ppermute | solution.py:608
  37.9 1.4 %half_level.1 = (bf16[4,8,8,256]{3,2,1,0:T(8,128)(2,1)S(1)}, bf16[2,16,256]{2,1,0:T(8,128)(2,1)S(1)}) custom-call(s32[5]{0:T(128)S(1)} %pad_add_fusion.place_ref, bf16[6,10,8,128]{3,2,1,0:T(8,128)(2,1)S(1)} %encode.1.field_ref, bf16[6,10,128]{2,1,0:T(8,128)(2,1)S(1)} %collective-permute-done.7.edge_ref, bf16[9,3,128,256]{3,2,1,0:T(8,128)(2,1)S(1)} %bitcast.16), custom_call_target="tpu_custom_call" | custom-call | tf_op jit(solution)/shard_map/half_level/pallas_call | solution.py:77
  39.4 0.1 collective-permute-start.8
  39.5 0.1 collective-permute-start.9
  39.6 1.8 %collective-permute-start.12 = (bf16[1,8,8,256]{3,1,0,2:T(8,128)(2,1)S(1)}, bf16[1,8,8,256]{3,1,0,2:T(8,128)(2,1)S(1)}, u32[]{:S(2)}, u32[]{:S(2)}) collective-permute-start(bf16[1,8,8,256]{3,1,0,2:T(8,128)(2,1)S(1)} %get-tuple-element.62), channel_id=1, source_target_pairs={{0,112},{16,32},{32,16},{48,64},{64,48},{80,96},{96,80},{112,0},{1... | collective-permute-start | bytes 98312 | tf_op jit(solution)/shard_map/ppermute | solution.py:14
  41.4 2.3 %collective-permute-done.8 = bf16[2,4,1,256]{3,1,0,2:T(4,128)(2,1)S(1)} collective-permute-done((bf16[2,4,1,256]{3,1,0,2:T(4,128)(2,1)S(1)}, bf16[2,4,1,256]{3,1,0,2:T(4,128)(2,1)S(1)}, u32[]{:S(2)}, u32[]{:S(2)}) %collective-permute-start.8) | collective-permute-done | bytes 4128 | tf_op jit(solution)/shard_map/ppermute | solution.py:14
  43.8 0.8 broadcast_in_dim.16.refs_1_
  44.6 5.0 %all-to-all-start = ((bf16[16,2,24,256]{3,2,1,0:T(8,128)(2,1)}), bf16[16,2,24,256]{3,2,1,0:T(8,128)(2,1)S(1)}, u32[]{:S(2)}, u32[]{:S(2)}) async-start(bf16[16,2,24,256]{3,2,1,0:T(8,128)(2,1)} %broadcast_in_dim.16.refs_1_), calls=%async_computation | async-start | bytes 786432 | tf_op jit(solution)/shard_map/all_to_all | solution.py:627
  49.6 0.1 broadcast_select_fusion.8
  49.7 0.1 broadcast_select_fusion.7
  49.8 0.1 collective-permute-start.15
  49.9 2.8 %collective-permute-start.14 = (bf16[6,1,8,256]{3,1,0,2:T(2,128)(2,1)S(1)}, bf16[6,1,8,256]{3,1,0,2:T(2,128)(2,1)S(1)}, u32[]{:S(2)}, u32[]{:S(2)}) collective-permute-start(bf16[6,1,8,256]{3,1,0,2:T(2,128)(2,1)S(1)} %get-tuple-element.55), channel_id=1, source_target_pairs={{0,14},{2,4},{4,2},{6,8},{8,6},{10,12},{12,10},{14,0},{1,15},{3,5}... | collective-permute-start | bytes 73736 | tf_op jit(solution)/shard_map/ppermute | solution.py:14
  52.8 1.4 %bring.4.weights_ref = bf16[9,256,256]{2,1,0:T(8,128)(2,1)S(1)} custom-call(bf16[9,256,256]{2,1,0:T(8,128)(2,1)} %get-tuple-element.44.refs_0_, bf16[16,2,24,256]{3,2,1,0:T(8,128)(2,1)} %broadcast_in_dim.16.refs_1_), custom_call_target="tpu_custom_call" | custom-call | tf_op jit(solution)/shard_map/bring/pallas_call | solution.py:229
  54.2 5.2 %all-to-all-done.field_ref = bf16[16,2,24,256]{3,2,1,0:T(8,128)(2,1)S(1)} async-done(((bf16[16,2,24,256]{3,2,1,0:T(8,128)(2,1)}), bf16[16,2,24,256]{3,2,1,0:T(8,128)(2,1)S(1)}, u32[]{:S(2)}, u32[]{:S(2)}) %all-to-all-start) | async-done | bytes 393248 | tf_op jit(solution)/shard_map/all_to_all | solution.py:627
  59.3 2.8 %bottom_in.1 = bf16[8,8,6,4,128]{4,3,2,1,0:T(4,128)(2,1)} custom-call(s32[5]{0:T(128)S(1)} %pad_add_fusion.place_ref, bf16[16,2,24,256]{3,2,1,0:T(8,128)(2,1)S(1)} %all-to-all-done.field_ref, bf16[9,256,256]{2,1,0:T(8,128)(2,1)S(1)} %bring.4.weights_ref), custom_call_target="tpu_custom_call" | custom-call | tf_op jit(solution)/shard_map/bottom_in/pallas_call | solution.py:395
  62.1 3.5 %all-to-all-start.1 = ((bf16[8,8,6,4,128]{4,3,2,1,0:T(4,128)(2,1)}), bf16[8,8,6,4,128]{4,3,2,1,0:T(4,128)(2,1)S(1)}, u32[]{:S(2)}, u32[]{:S(2)}) async-start(bf16[8,8,6,4,128]{4,3,2,1,0:T(4,128)(2,1)} %bottom_in.1), calls=%async_computation.1 | async-start | bytes 786432 | tf_op jit(solution)/shard_map/all_to_all | solution.py:629
  65.6 0.1 broadcast_select_fusion.9
  65.7 0.2 pad_maximum_fusion
  66.0 9.0 %all-to-all-done.1.refs_1_.field_ref = bf16[8,8,6,4,128]{4,3,2,1,0:T(4,128)(2,1)S(1)} async-done(((bf16[8,8,6,4,128]{4,3,2,1,0:T(4,128)(2,1)}), bf16[8,8,6,4,128]{4,3,2,1,0:T(4,128)(2,1)S(1)}, u32[]{:S(2)}, u32[]{:S(2)}) %all-to-all-start.1) | async-done | bytes 393248 | tf_op jit(solution)/shard_map/all_to_all | solution.py:629
  75.0 0.5 broadcast_select_fusion
  75.5 0.1 collective-permute-start.10
  75.5 2.8 %collective-permute-start.11 = (bf16[8,8,6,2,128]{4,3,2,1,0:T(2,128)(2,1)S(1)}, bf16[8,8,6,2,128]{4,3,2,1,0:T(2,128)(2,1)S(1)}, u32[]{:S(2)}, u32[]{:S(2)}) collective-permute-start(bf16[8,8,6,2,128]{4,3,2,1,0:T(2,128)(2,1)S(1)} %get-tuple-element.60), channel_id=1, source_target_pairs={{0,14},{2,4},{4,2},{6,8},{8,6},{10,12},{12,10},{14,0},{1,15},{3,5}... | collective-permute-start | bytes 589832 | tf_op jit(solution)/shard_map/ppermute | solution.py:14
  78.4 0.7 collective-permute-start.16
  79.1 1.7 %bring.5.weights_ref = bf16[9,512,256]{2,1,0:T(8,128)(2,1)S(1)} custom-call(bf16[9,512,256]{2,1,0:T(8,128)(2,1)} %get-tuple-element.48.refs_0_, bf16[8,8,6,4,128]{4,3,2,1,0:T(4,128)(2,1)S(1)} %all-to-all-done.1.refs_1_.field_ref), custom_call_target="tpu_custom_call" | custom-call | tf_op jit(solution)/shard_map/bring/pallas_call | solution.py:229
  80.7 1.8 %collective-permute-done.16.edge_ref = bf16[6,10,256]{2,1,0:T(8,128)(2,1)S(1)} collective-permute-done((bf16[6,10,256]{2,1,0:T(8,128)(2,1)S(1)}, bf16[6,10,256]{2,1,0:T(8,128)(2,1)S(1)}, u32[]{:S(2)}, u32[]{:S(2)}) %collective-permute-start.16) | collective-permute-done | bytes 30752 | tf_op jit(solution)/shard_map/ppermute | solution.py:608
  82.5 4.1 %bottom_out.1 = bf16[8,2,6,8,128]{4,3,2,1,0:T(8,128)(2,1)} custom-call(s32[5]{0:T(128)S(1)} %pad_add_fusion.place_ref, bf16[8,8,6,4,128]{4,3,2,1,0:T(4,128)(2,1)S(1)} %all-to-all-done.1.refs_1_.field_ref, bf16[8,8,6,2,128]{4,3,2,1,0:T(2,128)(2,1)S(1)} %collective-permute-done.10.y_in_ref, bf16[8,8,6,2,128]{4,3,2,1,0:T(2,128)(2,1)S(1)} %collective-permute-done.11.y_out_ref, ...), custom_call_target="tpu_custom_call" | custom-call | tf_op jit(solution)/shard_map/bottom_out/pallas_call | solution.py:450
  86.7 3.4 %all-to-all-start.2 = ((bf16[8,2,6,8,128]{4,3,2,1,0:T(8,128)(2,1)}), bf16[8,2,6,8,128]{4,3,2,1,0:T(8,128)(2,1)S(1)}, u32[]{:S(2)}, u32[]{:S(2)}) async-start(bf16[8,2,6,8,128]{4,3,2,1,0:T(8,128)(2,1)} %bottom_out.1), calls=%async_computation.2 | async-start | bytes 393216 | tf_op jit(solution)/shard_map/all_to_all | solution.py:637
  90.1 0.1 copy.21.skip_ref
  90.2 3.3 %decode_skip.1 = (f32[3,288,256]{2,1,0:T(8,128)S(1)}, bf16[3,512,256]{2,1,0:T(8,128)(2,1)S(1)}, bf16[3,512,256]{2,1,0:T(8,128)(2,1)S(1)}, bf16[3,512,256]{2,1,0:T(8,128)(2,1)S(1)}) custom-call(bf16[6,10,8,256]{3,2,1,0:T(8,128)(2,1)S(1)} %copy.21.skip_ref, bf16[6,10,256]{2,1,0:T(8,128)(2,1)S(1)} %collective-permute-done.16.edge_ref, ...), custom_call_target="tpu_custom_call" | custom-call | tf_op jit(solution)/shard_map/decode_skip/pallas_call | solution.py:500
  93.5 5.0 %all-to-all-done.2.bottom_ref = bf16[8,2,6,8,128]{4,3,2,1,0:T(8,128)(2,1)S(1)} async-done(((bf16[8,2,6,8,128]{4,3,2,1,0:T(8,128)(2,1)}), bf16[8,2,6,8,128]{4,3,2,1,0:T(8,128)(2,1)S(1)}, u32[]{:S(2)}, u32[]{:S(2)}) %all-to-all-start.2) | async-done | bytes 196640 | tf_op jit(solution)/shard_map/all_to_all | solution.py:637
  98.5 6.1 %decode.1 = bf16[4,8,8,256]{3,2,1,0:T(8,128)(2,1)} custom-call(s32[5]{0:T(128)S(1)} %pad_add_fusion.place_ref, bf16[8,2,6,8,128]{4,3,2,1,0:T(8,128)(2,1)S(1)} %all-to-all-done.2.bottom_ref, f32[3,288,256]{2,1,0:T(8,128)S(1)} %get-tuple-element.51.skip_ref, bf16[3,512,256]{2,1,0:T(8,128)(2,1)S(1)} %get-tuple-element.52.refs_0_, ...), custom_call_target="tpu_custom_call" | custom-call | tf_op jit(solution)/shard_map/decode/pallas_call | solution.py:580
  (28 shorter events, 0.2 us)
Async XLA Ops:
  0.0 17.1 %copy-start = (bf16[8,16,16,128]{3,2,1,0:T(8,128)(2,1)S(1)}, bf16[8,16,16,128]{3,2,1,0:T(8,128)(2,1)}, u32[]{:S(2)}) copy-start(bf16[8,16,16,128]{3,2,1,0:T(8,128)(2,1)} %refs_0_.1) | copy-start | bytes 1572868
  1.1 12.2 %collective-permute-start = (bf16[3,16,16,128]{3,2,1,0:T(8,128)(2,1)S(1)}, bf16[3,16,16,128]{3,2,1,0:T(8,128)(2,1)S(1)}, u32[]{:S(2)}, u32[]{:S(2)}) collective-permute-start(bf16[3,16,16,128]{3,2,1,0:T(8,128)(2,1)S(1)} %get-tuple-element.59), channel_id=1, source_target_pairs={{0,16},{16,0},{32,48},{48,32},{64,80},{80,64},{96,112},{112,96},{1... | collective-permute-start | bytes 589832 | tf_op jit(solution)/shard_map/ppermute | solution.py:14
  4.3 12.8 %collective-permute-start.1 = (bf16[3,16,16,128]{3,2,1,0:T(8,128)(2,1)S(1)}, bf16[3,16,16,128]{3,2,1,0:T(8,128)(2,1)S(1)}, u32[]{:S(2)}, u32[]{:S(2)}) collective-permute-start(bf16[3,16,16,128]{3,2,1,0:T(8,128)(2,1)S(1)} %get-tuple-element.58), channel_id=1, source_target_pairs={{0,112},{16,32},{32,16},{48,64},{64,48},{80,96},{96,80},{112,0},{1... | collective-permute-start | bytes 589832 | tf_op jit(solution)/shard_map/ppermute | solution.py:14
  18.0 10.0 %collective-permute-start.2 = (bf16[14,3,16,128]{3,2,1,0:T(8,128)(2,1)S(1)}, bf16[14,3,16,128]{3,2,1,0:T(8,128)(2,1)S(1)}, u32[]{:S(2)}, u32[]{:S(2)}) collective-permute-start(bf16[14,3,16,128]{3,2,1,0:T(8,128)(2,1)S(1)} %get-tuple-element.38), channel_id=1, source_target_pairs={{0,2},{2,0},{4,6},{6,4},{8,10},{10,8},{12,14},{14,12},{1,3},{3,1},... | collective-permute-start | bytes 516104 | tf_op jit(solution)/shard_map/ppermute | solution.py:14
  18.1 9.9 %collective-permute-start.3 = (bf16[14,3,16,128]{3,2,1,0:T(8,128)(2,1)S(1)}, bf16[14,3,16,128]{3,2,1,0:T(8,128)(2,1)S(1)}, u32[]{:S(2)}, u32[]{:S(2)}) collective-permute-start(bf16[14,3,16,128]{3,2,1,0:T(8,128)(2,1)S(1)} %get-tuple-element.39), channel_id=1, source_target_pairs={{0,14},{2,4},{4,2},{6,8},{8,6},{10,12},{12,10},{14,0},{1,15},{3,5}... | collective-permute-start | bytes 516104 | tf_op jit(solution)/shard_map/ppermute | solution.py:14
  21.2 6.7 %collective-permute-start.4 = (bf16[14,16,128]{2,1,0:T(8,128)(2,1)S(1)}, bf16[14,16,128]{2,1,0:T(8,128)(2,1)S(1)}, u32[]{:S(2)}, u32[]{:S(2)}) collective-permute-start(bf16[14,16,128]{2,1,0:T(8,128)(2,1)S(1)} %get-tuple-element.36.refs_2_), channel_id=1, source_target_pairs={{0,1},{1,0},{2,3},{3,2},{4,5},{5,4},{6,7},{7,6},{8,9},{9,8},{10,11... | collective-permute-start | bytes 172040 | tf_op jit(solution)/shard_map/ppermute | solution.py:615
  22.7 3.9 %collective-permute-start.5 = (bf16[14,3,128]{2,1,0:T(4,128)(2,1)S(1)}, bf16[14,3,128]{2,1,0:T(4,128)(2,1)S(1)}, u32[]{:S(2)}, u32[]{:S(2)}) collective-permute-start(bf16[14,3,128]{2,1,0:T(4,128)(2,1)S(1)} %get-tuple-element.40), channel_id=1, source_target_pairs={{0,3},{1,2},{2,1},{3,0},{4,7},{5,6},{6,5},{7,4},{8,11},{9,10},{10,... | collective-permute-start | bytes 32264 | tf_op jit(solution)/shard_map/ppermute | solution.py:14
  22.7 5.3 %collective-permute-start.6 = (bf16[14,3,128]{2,1,0:T(4,128)(2,1)S(1)}, bf16[14,3,128]{2,1,0:T(4,128)(2,1)S(1)}, u32[]{:S(2)}, u32[]{:S(2)}) collective-permute-start(bf16[14,3,128]{2,1,0:T(4,128)(2,1)S(1)} %get-tuple-element.41), channel_id=1, source_target_pairs={{0,15},{1,14},{2,5},{3,4},{4,3},{5,2},{6,9},{7,8},{8,7},{9,6},{10,... | collective-permute-start | bytes 32264 | tf_op jit(solution)/shard_map/ppermute | solution.py:14
  26.6 11.3 %copy-start.1 = (bf16[3,3,3,128,256]{4,3,2,1,0:T(8,128)(2,1)S(1)}, bf16[3,3,3,128,256]{4,3,2,1,0:T(8,128)(2,1)}, u32[]{:S(2)}) copy-start(bf16[3,3,3,128,256]{4,3,2,1,0:T(8,128)(2,1)} %param.8) | copy-start | bytes 5308420
  34.0 3.9 %collective-permute-start.7 = (bf16[6,10,128]{2,1,0:T(8,128)(2,1)S(1)}, bf16[6,10,128]{2,1,0:T(8,128)(2,1)S(1)}, u32[]{:S(2)}, u32[]{:S(2)}) collective-permute-start(bf16[6,10,128]{2,1,0:T(8,128)(2,1)S(1)} %fusion.1), channel_id=1, source_target_pairs={{0,1},{1,0},{2,3},{3,2},{4,5},{5,4},{6,7},{7,6},{8,9},{9,8},{10,11... | collective-permute-start | bytes 46088 | tf_op jit(solution)/shard_map/ppermute | solution.py:608
  39.4 4.3 %collective-permute-start.8 = (bf16[2,4,1,256]{3,1,0,2:T(4,128)(2,1)S(1)}, bf16[2,4,1,256]{3,1,0,2:T(4,128)(2,1)S(1)}, u32[]{:S(2)}, u32[]{:S(2)}) collective-permute-start(bf16[2,4,1,256]{3,1,0,2:T(4,128)(2,1)S(1)} %get-tuple-element.74), channel_id=1, source_target_pairs={{0,14},{2,4},{4,2},{6,8},{8,6},{10,12},{12,10},{14,0},{1,15},{3,5}... | collective-permute-start | bytes 12296 | tf_op jit(solution)/shard_map/ppermute | solution.py:14
  39.5 4.2 %collective-permute-start.9 = (bf16[2,4,1,256]{3,1,0,2:T(4,128)(2,1)S(1)}, bf16[2,4,1,256]{3,1,0,2:T(4,128)(2,1)S(1)}, u32[]{:S(2)}, u32[]{:S(2)}) collective-permute-start(bf16[2,4,1,256]{3,1,0,2:T(4,128)(2,1)S(1)} %get-tuple-element.75), channel_id=1, source_target_pairs={{0,2},{2,0},{4,6},{6,4},{8,10},{10,8},{12,14},{14,12},{1,3},{3,1},... | collective-permute-start | bytes 12296 | tf_op jit(solution)/shard_map/ppermute | solution.py:14
  39.6 10.0 %collective-permute-start.12 = (bf16[1,8,8,256]{3,1,0,2:T(8,128)(2,1)S(1)}, bf16[1,8,8,256]{3,1,0,2:T(8,128)(2,1)S(1)}, u32[]{:S(2)}, u32[]{:S(2)}) collective-permute-start(bf16[1,8,8,256]{3,1,0,2:T(8,128)(2,1)S(1)} %get-tuple-element.62), channel_id=1, source_target_pairs={{0,112},{16,32},{32,16},{48,64},{64,48},{80,96},{96,80},{112,0},{1... | collective-permute-start | bytes 98312 | tf_op jit(solution)/shard_map/ppermute | solution.py:14
  41.4 8.2 %collective-permute-start.13 = (bf16[1,8,8,256]{3,1,0,2:T(8,128)(2,1)S(1)}, bf16[1,8,8,256]{3,1,0,2:T(8,128)(2,1)S(1)}, u32[]{:S(2)}, u32[]{:S(2)}) collective-permute-start(bf16[1,8,8,256]{3,1,0,2:T(8,128)(2,1)S(1)} %get-tuple-element.63), channel_id=1, source_target_pairs={{0,16},{16,0},{32,48},{48,32},{64,80},{80,64},{96,112},{112,96},{1... | collective-permute-start | bytes 98312 | tf_op jit(solution)/shard_map/ppermute | solution.py:14
  44.6 14.7 %all-to-all-start = ((bf16[16,2,24,256]{3,2,1,0:T(8,128)(2,1)}), bf16[16,2,24,256]{3,2,1,0:T(8,128)(2,1)S(1)}, u32[]{:S(2)}, u32[]{:S(2)}) async-start(bf16[16,2,24,256]{3,2,1,0:T(8,128)(2,1)} %broadcast_in_dim.16.refs_1_), calls=%async_computation | async-start | bytes 786432 | tf_op jit(solution)/shard_map/all_to_all | solution.py:627
  49.8 15.7 %collective-permute-start.15 = (bf16[6,1,8,256]{3,1,0,2:T(2,128)(2,1)S(1)}, bf16[6,1,8,256]{3,1,0,2:T(2,128)(2,1)S(1)}, u32[]{:S(2)}, u32[]{:S(2)}) collective-permute-start(bf16[6,1,8,256]{3,1,0,2:T(2,128)(2,1)S(1)} %broadcast_select_fusion.7), channel_id=1, source_target_pairs={{0,2},{2,0},{4,6},{6,4},{8,10},{10,8},{12,14},{14,12},{1,3},{3,1},... | collective-permute-start | bytes 73736 | tf_op jit(solution)/shard_map/ppermute | solution.py:14
  49.9 15.7 %collective-permute-start.14 = (bf16[6,1,8,256]{3,1,0,2:T(2,128)(2,1)S(1)}, bf16[6,1,8,256]{3,1,0,2:T(2,128)(2,1)S(1)}, u32[]{:S(2)}, u32[]{:S(2)}) collective-permute-start(bf16[6,1,8,256]{3,1,0,2:T(2,128)(2,1)S(1)} %get-tuple-element.55), channel_id=1, source_target_pairs={{0,14},{2,4},{4,2},{6,8},{8,6},{10,12},{12,10},{14,0},{1,15},{3,5}... | collective-permute-start | bytes 73736 | tf_op jit(solution)/shard_map/ppermute | solution.py:14
  62.1 12.9 %all-to-all-start.1 = ((bf16[8,8,6,4,128]{4,3,2,1,0:T(4,128)(2,1)}), bf16[8,8,6,4,128]{4,3,2,1,0:T(4,128)(2,1)S(1)}, u32[]{:S(2)}, u32[]{:S(2)}) async-start(bf16[8,8,6,4,128]{4,3,2,1,0:T(4,128)(2,1)} %bottom_in.1), calls=%async_computation.1 | async-start | bytes 786432 | tf_op jit(solution)/shard_map/all_to_all | solution.py:629
  75.5 7.1 %collective-permute-start.10 = (bf16[8,8,6,2,128]{4,3,2,1,0:T(2,128)(2,1)S(1)}, bf16[8,8,6,2,128]{4,3,2,1,0:T(2,128)(2,1)S(1)}, u32[]{:S(2)}, u32[]{:S(2)}) collective-permute-start(bf16[8,8,6,2,128]{4,3,2,1,0:T(2,128)(2,1)S(1)} %get-tuple-element.61), channel_id=1, source_target_pairs={{0,2},{2,0},{4,6},{6,4},{8,10},{10,8},{12,14},{14,12},{1,3},{3,1},... | collective-permute-start | bytes 589832 | tf_op jit(solution)/shard_map/ppermute | solution.py:14
  75.5 7.0 %collective-permute-start.11 = (bf16[8,8,6,2,128]{4,3,2,1,0:T(2,128)(2,1)S(1)}, bf16[8,8,6,2,128]{4,3,2,1,0:T(2,128)(2,1)S(1)}, u32[]{:S(2)}, u32[]{:S(2)}) collective-permute-start(bf16[8,8,6,2,128]{4,3,2,1,0:T(2,128)(2,1)S(1)} %get-tuple-element.60), channel_id=1, source_target_pairs={{0,14},{2,4},{4,2},{6,8},{8,6},{10,12},{12,10},{14,0},{1,15},{3,5}... | collective-permute-start | bytes 589832 | tf_op jit(solution)/shard_map/ppermute | solution.py:14
  78.4 4.2 %collective-permute-start.16 = (bf16[6,10,256]{2,1,0:T(8,128)(2,1)S(1)}, bf16[6,10,256]{2,1,0:T(8,128)(2,1)S(1)}, u32[]{:S(2)}, u32[]{:S(2)}) collective-permute-start(bf16[6,10,256]{2,1,0:T(8,128)(2,1)S(1)} %fusion), channel_id=1, source_target_pairs={{0,1},{1,0},{2,3},{3,2},{4,5},{5,4},{6,7},{7,6},{8,9},{9,8},{10,11... | collective-permute-start | bytes 92168 | tf_op jit(solution)/shard_map/ppermute | solution.py:608
  86.7 11.8 %all-to-all-start.2 = ((bf16[8,2,6,8,128]{4,3,2,1,0:T(8,128)(2,1)}), bf16[8,2,6,8,128]{4,3,2,1,0:T(8,128)(2,1)S(1)}, u32[]{:S(2)}, u32[]{:S(2)}) async-start(bf16[8,2,6,8,128]{4,3,2,1,0:T(8,128)(2,1)} %bottom_out.1), calls=%async_computation.2 | async-start | bytes 393216 | tf_op jit(solution)/shard_map/all_to_all | solution.py:637

commit v10 on v9

--- a/solution.py
+++ b/solution.py
@@ -343,21 +343,30 @@
     return jnp.where(lane < 64, even, pltpu.roll(odd, 64, even.ndim - 1))
 
 
-def column_product(pad_ref, weights_ref, first, start, planes, size_z):
-    channels = pad_ref.shape[-1]
-    rows = planes * size_z * 8
+def pair_planes(pad_ref, pair_ref):
+    pairs = pair_ref.shape[1]
+    for odd in range(2):
+        for pair in range(pairs - odd):
+            planes = [pad_ref[2 * pair + odd + n] for n in range(2)]
+            pair_ref[odd, pair] = jnp.concatenate(planes, axis=1).astype(pair_ref.dtype)
+
+
+def column_product(pair_ref, weights_ref, first, start, pairs, size_z):
+    channels = pair_ref.shape[-1]
+    rows = pairs * size_z * 16
     blocks = []
     for dx in range(3):
         for dz in range(3):
-            block = pad_ref[first + dx : first + dx + planes, pl.ds(start + dz, size_z)]
-            blocks.append(block.reshape(rows, channels).astype(jnp.bfloat16))
+            block = pair_ref[dx % 2, first + dx // 2 : first + dx // 2 + pairs, pl.ds(start + dz, size_z)]
+            blocks.append(block.reshape(rows, channels))
     block = jnp.concatenate(blocks, axis=1)
     total = jnp.dot(block, weights_ref[...].reshape(9 * channels, 256), preferred_element_type=jnp.float32)
-    low = total[:, :128].reshape(planes * size_z, 8, 128)
-    mid = pltpu.roll(total[:, :128], 64, 1).reshape(planes * size_z, 8, 128)
-    high = total[:, 128:].reshape(planes * size_z, 8, 128)
+    groups = pairs * size_z * 2
+    low = total[:, :128].reshape(groups, 8, 128)
+    mid = pltpu.roll(total[:, :128], 64, 1).reshape(groups, 8, 128)
+    high = total[:, 128:].reshape(groups, 8, 128)
     total = pltpu.roll(low, 1, 1) + mid + pltpu.roll(high, 7, 1)
-    return jnp.maximum(total, 0.0).reshape(planes, size_z, 8, 128)
+    return jnp.maximum(total, 0.0).reshape(pairs, size_z, 2, 8, 128)
 
 
 def bottom_in(place, field, weights):
@@ -366,7 +375,7 @@
     own_z = size_y = 4
     size_x, all_z, size_z = devices * own_x, 2 * own_z, own_z + 2
 
-    def body(place_ref, field_ref, weights_ref, out_ref, pad_ref):
+    def body(place_ref, field_ref, weights_ref, out_ref, pad_ref, pair_ref):
         zero = jnp.zeros((all_z + 2, 8, channels), jnp.float32)
         pad_ref[0] = zero
         pad_ref[size_x + 1] = zero
@@ -385,12 +394,13 @@
                         pad_ref[*to, size_y + 1 : size_y + 2] = block[line : line + 1]
                         pad_ref[*to, size_y + 2 :] = zero[0, size_y + 2 :]
         start = 2 * place_ref[2]
-        for first in range(0, size_x, 4):
-            total = column_product(pad_ref, weights_ref, first, start, 4, size_z)
+        pair_planes(pad_ref, pair_ref)
+        for first in range(0, size_x // 2, 2):
+            total = column_product(pair_ref, weights_ref, first, start, 2, size_z)
             for pair in range(2):
-                both = side_by_side(total[2 * pair], total[2 * pair + 1])[:, 1 : size_y + 1].astype(out_ref.dtype)
+                both = side_by_side(total[pair, :, 0], total[pair, :, 1])[:, 1 : size_y + 1].astype(out_ref.dtype)
                 for i in range(devices):
-                    out_ref[i, first // 2 + pair] = both
+                    out_ref[i, first + pair] = both
 
     return pl.pallas_call(
         body,
@@ -399,8 +409,9 @@
         out_shape=jax.ShapeDtypeStruct((devices, size_x // 2, size_z, size_y, 128), jnp.bfloat16),
         scratch_shapes=[
             pltpu.VMEM((size_x + 2, all_z + 2, 8, channels), jnp.float32),
+            pltpu.VMEM((2, size_x // 2 + 1, all_z + 2, 16, channels), jnp.bfloat16),
         ],
-        compiler_params=pltpu.CompilerParams(vmem_limit_bytes=12 << 20),
+        compiler_params=pltpu.CompilerParams(vmem_limit_bytes=16 << 20),
         name="bottom_in",
     )(place, field, near(weights))
 
@@ -410,7 +421,7 @@
     size_x, channels = 2 * pairs, 64 * devices
     own_x = size_x // devices
 
-    def body(place_ref, field_ref, y_in_ref, y_out_ref, weights_ref, out_ref, pad_ref, total_ref):
+    def body(place_ref, field_ref, y_in_ref, y_out_ref, weights_ref, out_ref, pad_ref, pair_ref, total_ref):
         even_y = place_ref[1] % 2 == 0
         low_y, high_y = place_ref[1] > 0, place_ref[1] < place_ref[4]
         zero = jnp.zeros((size_z + 2, 8, channels), jnp.float32)
@@ -435,9 +446,11 @@
                     lines = slice(line, line + even.shape[1])
                     pad_ref[1 + 2 * pair, 1 : size_z + 1, lines, 128 * k : 128 * k + 128] = even
                     pad_ref[2 + 2 * pair, 1 : size_z + 1, lines, 128 * k : 128 * k + 128] = odd
-        for first in range(0, size_x, 4):
-            total = column_product(pad_ref, weights_ref, first, 0, 4, size_z)
-            total_ref[1 + first : 5 + first, 1 : size_z + 1] = total
+        pair_planes(pad_ref, pair_ref)
+        for first in range(0, pairs, 2):
+            total = column_product(pair_ref, weights_ref, first, 0, 2, size_z)
+            for plane in range(4):
+                total_ref[1 + 2 * first + plane, 1 : size_z + 1] = total[plane // 2, :, plane % 2]
         start = 2 * place_ref[2]
         for i in range(size_x // 2 + 1):
             low, high = [total_ref[2 * i + n, pl.ds(start, size_z)] for n in range(2)]
@@ -455,9 +468,10 @@
         out_shape=jax.ShapeDtypeStruct((devices, own_x, size_z, 8, 128), jnp.bfloat16),
         scratch_shapes=[
             pltpu.VMEM((size_x + 2, size_z + 2, 8, channels), jnp.float32),
+            pltpu.VMEM((2, pairs + 1, size_z + 2, 16, channels), jnp.bfloat16),
             pltpu.VMEM((size_x + 2, size_z + 2, 8, 128), jnp.float32),
         ],
-        compiler_params=pltpu.CompilerParams(vmem_limit_bytes=16 << 20),
+        compiler_params=pltpu.CompilerParams(vmem_limit_bytes=20 << 20),
         name="bottom_out",
     )(place, field, y_in, y_out, near(weights))
 
@@ -626,13 +640,13 @@
         (w_in,) = bring([w_in], column)
         column = lax.all_to_all(column, ("gx", "gz"), 0, 0)
         first = bottom_in(place, column, w_in)
+        (w_out,) = bring([w_out], first)
         first = lax.all_to_all(first, "gx", 0, 0)
-        (w_out,) = bring([w_out], first)
-        y_in, y_out = swaps(first[:, :, :, :2], first[:, :, :, -2:], "gy", gy)
         around = extend(skip, "gx", gx, 0, 1)
         around = extend(around, "gy", gy, 1, 1)
         side = edge_of(around[:, :, 0], around[:, :, -1])
-        y_in, y_out, around, side = lax.optimization_barrier((y_in, y_out, around, side))
+        first, around, side = lax.optimization_barrier((first, around, side))
+        y_in, y_out = swaps(first[:, :, :, :2], first[:, :, :, -2:], "gy", gy)
         second = bottom_out(place, first, y_in, y_out, w_out)
         second = lax.all_to_all(second, "gx", 0, 0)
         w_up = w_up.reshape(9, 3, w_up.shape[3], w_up.shape[4])

time: 105 us -> 105 us (level)
    all_to_all x1, waiting for transfers between devices: 9.04 us -> 4.27 us  [local(): first = lax.all_to_all(first, 'gx', 0, 0)]
    ppermute x2, waiting for transfers between devices: 5.08 us -> 7.62 us  [edge_of(): lax.ppermute(jnp.where(place_z == 0, plane_high, plane_low), 'gz', swap)]
    ppermute x7, waiting for transfers between devices: 7.45 us -> 9.86 us  [send(): lax.ppermute(outer_block, axis, outer)]
  transfers between devices with their start and end apart: 20 -> 20, of which waited for: 8 -> 10; matrix products, arithmetic and copies ran while one was open for 2% -> 2% of each run, Pallas kernels for 15% -> 13%
where the time goes in v10:
time: 105 us
  starting transfers between devices  35.8 us (34%)
  Pallas kernels  34.3 us (33%)
  waiting for transfers between devices  31.1 us (30%)
  other arithmetic  2.26 us (2%)
  local copies, waits for them, and re-layouts  1.05 us (1%)
    ppermute x7, starting transfers between devices, send(): lax.ppermute(outer_block, axis, outer)  17.5 us
    ppermute x7, waiting for transfers between devices, send(): lax.ppermute(outer_block, axis, outer)  9.86 us
    ppermute x2, waiting for transfers between devices, edge_of(): lax.ppermute(jnp.where(place_z == 0, plane_high, plane_low), 'gz', swap)  7.62 us
    pallas_call x1, Pallas kernels, decode(): pl.pallas_call(body, in_specs=[pl.BlockSpec(memory_space=pltpu.SMEM)] + [...  6.06 us
    pallas_call x1, Pallas kernels, encode(): pl.pallas_call(body, in_specs=[pl.BlockSpec(memory_space=pltpu.SMEM)] + [...  5.97 us
    all_to_all x1, waiting for transfers between devices, local(): second = lax.all_to_all(second, 'gx', 0, 0)  5.06 us
    pallas_call x3, Pallas kernels, bring(): pl.pallas_call(body, in_specs=[pl.BlockSpec(memory_space=pltpu.HBM)] * co...  5.03 us
    all_to_all x1, starting transfers between devices, local(): column = lax.all_to_all(column, ('gx', 'gz'), 0, 0)  5.01 us
  transfers between devices with their start and end apart: 20, of which 10 were waited for; matrix products, arithmetic and copies ran while one was open for 2% of the time, Pallas kernels for 13%

profile of v10, /device:TPU:0, one launch (start us, length us, event | category | flops | bytes accessed | tf_op | source)
XLA Modules:
  0.0 105.0 jit_solution(4118448301920337223)
XLA Ops:
  0.0 1.1 %broadcast_select_fusion.2 = (bf16[3,16,16,128]{3,2,1,0:T(8,128)(2,1)S(1)}, bf16[3,16,16,128]{3,2,1,0:T(8,128)(2,1)S(1)}) fusion(pred[]{:T(512)S(6)} %eq.25, bf16[8,16,16,128]{3,2,1,0:T(8,128)(2,1)} %refs_0_.1), kind=kLoop, calls=%fused_computation.3 | loop fusion | flops 196608 | bytes 786433 | tf_op jit(solution)/shard_map/jit(_where)/select_n | solution.py:19
  1.1 3.2 %collective-permute-start = (bf16[3,16,16,128]{3,2,1,0:T(8,128)(2,1)S(1)}, bf16[3,16,16,128]{3,2,1,0:T(8,128)(2,1)S(1)}, u32[]{:S(2)}, u32[]{:S(2)}) collective-permute-start(bf16[3,16,16,128]{3,2,1,0:T(8,128)(2,1)S(1)} %get-tuple-element.57), channel_id=1, source_target_pairs={{0,16},{16,0},{32,48},{48,32},{64,80},{80,64},{96,112},{112,96},{1... | collective-permute-start | bytes 589832 | tf_op jit(solution)/shard_map/ppermute | solution.py:14
  4.3 4.0 %collective-permute-start.1 = (bf16[3,16,16,128]{3,2,1,0:T(8,128)(2,1)S(1)}, bf16[3,16,16,128]{3,2,1,0:T(8,128)(2,1)S(1)}, u32[]{:S(2)}, u32[]{:S(2)}) collective-permute-start(bf16[3,16,16,128]{3,2,1,0:T(8,128)(2,1)S(1)} %get-tuple-element.56), channel_id=1, source_target_pairs={{0,112},{16,32},{32,16},{48,64},{64,48},{80,96},{96,80},{112,0},{1... | collective-permute-start | bytes 589832 | tf_op jit(solution)/shard_map/ppermute | solution.py:14
  8.3 4.9 %prepare.1 = (bf16[4,3,3,128,256]{4,3,2,1,0:T(8,128)(2,1)}, bf16[9,256,256]{2,1,0:T(8,128)(2,1)}, bf16[9,512,256]{2,1,0:T(8,128)(2,1)}) custom-call(bf16[3,3,3,128,128]{4,3,2,1,0:T(8,128)(2,1)} %full_hbm.1, bf16[3,3,3,64,256]{4,3,2,1,0:T(8,128)(2,1)} %bitcast.20, bf16[3,3,3,64,512]{4,3,2,1,0:T(8,128)(2,1)} %bitcast.19), custom_call_target="tpu_custom_call" | custom-call | tf_op jit(solution)/shard_map/prepare/pallas_call | solution.py:283
  13.2 0.1 pad_add_fusion.place_ref
  13.3 3.8 %collective-permute-done.1.x_out_ref = bf16[3,16,16,128]{3,2,1,0:T(8,128)(2,1)S(1)} collective-permute-done((bf16[3,16,16,128]{3,2,1,0:T(8,128)(2,1)S(1)}, bf16[3,16,16,128]{3,2,1,0:T(8,128)(2,1)S(1)}, u32[]{:S(2)}, u32[]{:S(2)}) %collective-permute-start.1) | collective-permute-done | bytes 196640 | tf_op jit(solution)/shard_map/ppermute | solution.py:14
  17.1 0.9 pack_y.1
  18.0 0.1 collective-permute-start.2
  18.1 3.1 %collective-permute-start.3 = (bf16[14,3,16,128]{3,2,1,0:T(8,128)(2,1)S(1)}, bf16[14,3,16,128]{3,2,1,0:T(8,128)(2,1)S(1)}, u32[]{:S(2)}, u32[]{:S(2)}) collective-permute-start(bf16[14,3,16,128]{3,2,1,0:T(8,128)(2,1)S(1)} %get-tuple-element.38), channel_id=1, source_target_pairs={{0,14},{2,4},{4,2},{6,8},{8,6},{10,12},{12,10},{14,0},{1,15},{3,5}... | collective-permute-start | bytes 516104 | tf_op jit(solution)/shard_map/ppermute | solution.py:14
  21.2 1.5 %collective-permute-start.4 = (bf16[14,16,128]{2,1,0:T(8,128)(2,1)S(1)}, bf16[14,16,128]{2,1,0:T(8,128)(2,1)S(1)}, u32[]{:S(2)}, u32[]{:S(2)}) collective-permute-start(bf16[14,16,128]{2,1,0:T(8,128)(2,1)S(1)} %get-tuple-element.35.refs_2_), channel_id=1, source_target_pairs={{0,1},{1,0},{2,3},{3,2},{4,5},{5,4},{6,7},{7,6},{8,9},{9,8},{10,11... | collective-permute-start | bytes 172040 | tf_op jit(solution)/shard_map/ppermute | solution.py:629
  22.7 1.9 %collective-permute-start.6 = (bf16[14,3,128]{2,1,0:T(4,128)(2,1)S(1)}, bf16[14,3,128]{2,1,0:T(4,128)(2,1)S(1)}, u32[]{:S(2)}, u32[]{:S(2)}) collective-permute-start(bf16[14,3,128]{2,1,0:T(4,128)(2,1)S(1)} %get-tuple-element.40), channel_id=1, source_target_pairs={{0,15},{1,14},{2,5},{3,4},{4,3},{5,2},{6,9},{7,8},{8,7},{9,6},{10,... | collective-permute-start | bytes 32264 | tf_op jit(solution)/shard_map/ppermute | solution.py:14
  24.6 2.0 %bring.3 = (bf16[8,16,16,128]{3,2,1,0:T(8,128)(2,1)S(1)}, bf16[4,3,3,128,256]{4,3,2,1,0:T(8,128)(2,1)S(1)}) custom-call(bf16[8,16,16,128]{3,2,1,0:T(8,128)(2,1)} %refs_0_.1, bf16[4,3,3,128,256]{4,3,2,1,0:T(8,128)(2,1)} %get-tuple-element.32.refs_1_, bf16[14,16,128]{2,1,0:T(8,128)(2,1)S(1)} %get-tuple-element.35.refs_2_), custom_call_target="tpu_custom_call" | custom-call | tf_op jit(solution)/shard_map/bring/pallas_call | solution.py:229
  26.6 1.3 %collective-permute-done.6.edge_out_ref = bf16[14,3,128]{2,1,0:T(4,128)(2,1)S(1)} collective-permute-done((bf16[14,3,128]{2,1,0:T(4,128)(2,1)S(1)}, bf16[14,3,128]{2,1,0:T(4,128)(2,1)S(1)}, u32[]{:S(2)}, u32[]{:S(2)}) %collective-permute-start.6) | collective-permute-done | bytes 10784 | tf_op jit(solution)/shard_map/ppermute | solution.py:14
  28.0 6.0 %encode.1.field_ref = bf16[6,10,8,128]{3,2,1,0:T(8,128)(2,1)S(1)} custom-call(s32[5]{0:T(128)S(1)} %pad_add_fusion.place_ref, bf16[8,16,16,128]{3,2,1,0:T(8,128)(2,1)S(1)} %get-tuple-element.36.own_ref, bf16[3,16,16,128]{3,2,1,0:T(8,128)(2,1)S(1)} %collective-permute-done.x_in_ref, bf16[3,16,16,128]{3,2,1,0:T(8,128)(2,1)S(1)} %collective-permute-done.1.x_out_ref, ...), custom_call_target="tpu_custom_call" | custom-call | tf_op jit(solution)/shard_map/encode/pallas_call | solution.py:197
  34.0 0.6 collective-permute-start.7
  34.7 3.3 %collective-permute-done.7.edge_ref = bf16[6,10,128]{2,1,0:T(8,128)(2,1)S(1)} collective-permute-done((bf16[6,10,128]{2,1,0:T(8,128)(2,1)S(1)}, bf16[6,10,128]{2,1,0:T(8,128)(2,1)S(1)}, u32[]{:S(2)}, u32[]{:S(2)}) %collective-permute-start.7) | collective-permute-done | bytes 15392 | tf_op jit(solution)/shard_map/ppermute | solution.py:622
  37.9 1.4 %half_level.1 = (bf16[4,8,8,256]{3,2,1,0:T(8,128)(2,1)S(1)}, bf16[2,16,256]{2,1,0:T(8,128)(2,1)S(1)}) custom-call(s32[5]{0:T(128)S(1)} %pad_add_fusion.place_ref, bf16[6,10,8,128]{3,2,1,0:T(8,128)(2,1)S(1)} %encode.1.field_ref, bf16[6,10,128]{2,1,0:T(8,128)(2,1)S(1)} %collective-permute-done.7.edge_ref, bf16[9,3,128,256]{3,2,1,0:T(8,128)(2,1)S(1)} %bitcast.16), custom_call_target="tpu_custom_call" | custom-call | tf_op jit(solution)/shard_map/half_level/pallas_call | solution.py:77
  39.4 0.1 collective-permute-start.8
  39.5 0.1 collective-permute-start.9
  39.6 1.8 %collective-permute-start.10 = (bf16[1,8,8,256]{3,1,0,2:T(8,128)(2,1)S(1)}, bf16[1,8,8,256]{3,1,0,2:T(8,128)(2,1)S(1)}, u32[]{:S(2)}, u32[]{:S(2)}) collective-permute-start(bf16[1,8,8,256]{3,1,0,2:T(8,128)(2,1)S(1)} %get-tuple-element.60), channel_id=1, source_target_pairs={{0,112},{16,32},{32,16},{48,64},{64,48},{80,96},{96,80},{112,0},{1... | collective-permute-start | bytes 98312 | tf_op jit(solution)/shard_map/ppermute | solution.py:14
  41.4 2.3 %collective-permute-done.8 = bf16[2,4,1,256]{3,1,0,2:T(4,128)(2,1)S(1)} collective-permute-done((bf16[2,4,1,256]{3,1,0,2:T(4,128)(2,1)S(1)}, bf16[2,4,1,256]{3,1,0,2:T(4,128)(2,1)S(1)}, u32[]{:S(2)}, u32[]{:S(2)}) %collective-permute-start.8) | collective-permute-done | bytes 4128 | tf_op jit(solution)/shard_map/ppermute | solution.py:14
  43.8 0.8 broadcast_in_dim.16.refs_1_
  44.6 5.0 %all-to-all-start = ((bf16[16,2,24,256]{3,2,1,0:T(8,128)(2,1)}), bf16[16,2,24,256]{3,2,1,0:T(8,128)(2,1)S(1)}, u32[]{:S(2)}, u32[]{:S(2)}) async-start(bf16[16,2,24,256]{3,2,1,0:T(8,128)(2,1)} %broadcast_in_dim.16.refs_1_), calls=%async_computation | async-start | bytes 786432 | tf_op jit(solution)/shard_map/all_to_all | solution.py:641
  49.6 0.1 broadcast_select_fusion.8
  49.7 0.1 broadcast_select_fusion.7
  49.8 0.1 collective-permute-start.13
  49.9 2.8 %collective-permute-start.12 = (bf16[6,1,8,256]{3,1,0,2:T(2,128)(2,1)S(1)}, bf16[6,1,8,256]{3,1,0,2:T(2,128)(2,1)S(1)}, u32[]{:S(2)}, u32[]{:S(2)}) collective-permute-start(bf16[6,1,8,256]{3,1,0,2:T(2,128)(2,1)S(1)} %get-tuple-element.53), channel_id=1, source_target_pairs={{0,14},{2,4},{4,2},{6,8},{8,6},{10,12},{12,10},{14,0},{1,15},{3,5}... | collective-permute-start | bytes 73736 | tf_op jit(solution)/shard_map/ppermute | solution.py:14
  52.8 1.4 %bring.4.weights_ref = bf16[9,256,256]{2,1,0:T(8,128)(2,1)S(1)} custom-call(bf16[9,256,256]{2,1,0:T(8,128)(2,1)} %get-tuple-element.43.refs_0_, bf16[16,2,24,256]{3,2,1,0:T(8,128)(2,1)} %broadcast_in_dim.16.refs_1_), custom_call_target="tpu_custom_call" | custom-call | tf_op jit(solution)/shard_map/bring/pallas_call | solution.py:229
  54.2 0.7 collective-permute-done.12
  54.9 0.1 broadcast_select_fusion.9
  55.0 4.3 %all-to-all-done.field_ref = bf16[16,2,24,256]{3,2,1,0:T(8,128)(2,1)S(1)} async-done(((bf16[16,2,24,256]{3,2,1,0:T(8,128)(2,1)}), bf16[16,2,24,256]{3,2,1,0:T(8,128)(2,1)S(1)}, u32[]{:S(2)}, u32[]{:S(2)}) %all-to-all-start) | async-done | bytes 393248 | tf_op jit(solution)/shard_map/all_to_all | solution.py:641
  59.3 2.9 %bottom_in.1.refs_1_ = bf16[8,8,6,4,128]{4,3,2,1,0:T(4,128)(2,1)} custom-call(s32[5]{0:T(128)S(1)} %pad_add_fusion.place_ref, bf16[16,2,24,256]{3,2,1,0:T(8,128)(2,1)S(1)} %all-to-all-done.field_ref, bf16[9,256,256]{2,1,0:T(8,128)(2,1)S(1)} %bring.4.weights_ref), custom_call_target="tpu_custom_call" | custom-call | tf_op jit(solution)/shard_map/bottom_in/pallas_call | solution.py:405
  62.2 3.5 %all-to-all-start.1 = ((bf16[8,8,6,4,128]{4,3,2,1,0:T(4,128)(2,1)}), bf16[8,8,6,4,128]{4,3,2,1,0:T(4,128)(2,1)S(1)}, u32[]{:S(2)}, u32[]{:S(2)}) async-start(bf16[8,8,6,4,128]{4,3,2,1,0:T(4,128)(2,1)} %bottom_in.1.refs_1_), calls=%async_computation.1 | async-start | bytes 786432 | tf_op jit(solution)/shard_map/all_to_all | solution.py:644
  65.6 0.2 pad_maximum_fusion
  65.9 0.7 collective-permute-start.14
  66.6 4.4 %collective-permute-done.14.edge_ref = bf16[6,10,256]{2,1,0:T(8,128)(2,1)S(1)} collective-permute-done((bf16[6,10,256]{2,1,0:T(8,128)(2,1)S(1)}, bf16[6,10,256]{2,1,0:T(8,128)(2,1)S(1)}, u32[]{:S(2)}, u32[]{:S(2)}) %collective-permute-start.14) | collective-permute-done | bytes 30752 | tf_op jit(solution)/shard_map/ppermute | solution.py:622
  70.9 4.3 %all-to-all-done.1.field_ref = bf16[8,8,6,4,128]{4,3,2,1,0:T(4,128)(2,1)S(1)} async-done(((bf16[8,8,6,4,128]{4,3,2,1,0:T(4,128)(2,1)}), bf16[8,8,6,4,128]{4,3,2,1,0:T(4,128)(2,1)S(1)}, u32[]{:S(2)}, u32[]{:S(2)}) %all-to-all-start.1) | async-done | bytes 393248 | tf_op jit(solution)/shard_map/all_to_all | solution.py:644
  75.2 0.5 broadcast_select_fusion
  75.7 0.1 collective-permute-start.15
  75.8 3.8 %collective-permute-start.16 = (bf16[8,8,6,2,128]{4,3,2,1,0:T(2,128)(2,1)S(1)}, bf16[8,8,6,2,128]{4,3,2,1,0:T(2,128)(2,1)S(1)}, u32[]{:S(2)}, u32[]{:S(2)}) collective-permute-start(bf16[8,8,6,2,128]{4,3,2,1,0:T(2,128)(2,1)S(1)} %get-tuple-element.58), channel_id=1, source_target_pairs={{0,14},{2,4},{4,2},{6,8},{8,6},{10,12},{12,10},{14,0},{1,15},{3,5}... | collective-permute-start | bytes 589832 | tf_op jit(solution)/shard_map/ppermute | solution.py:14
  79.5 1.7 %bring.5.weights_ref = bf16[9,512,256]{2,1,0:T(8,128)(2,1)S(1)} custom-call(bf16[9,512,256]{2,1,0:T(8,128)(2,1)} %get-tuple-element.46.refs_0_, bf16[8,8,6,4,128]{4,3,2,1,0:T(4,128)(2,1)} %bottom_in.1.refs_1_), custom_call_target="tpu_custom_call" | custom-call | tf_op jit(solution)/shard_map/bring/pallas_call | solution.py:229
  81.2 1.7 %collective-permute-done.16.y_out_ref = bf16[8,8,6,2,128]{4,3,2,1,0:T(2,128)(2,1)S(1)} collective-permute-done((bf16[8,8,6,2,128]{4,3,2,1,0:T(2,128)(2,1)S(1)}, bf16[8,8,6,2,128]{4,3,2,1,0:T(2,128)(2,1)S(1)}, u32[]{:S(2)}, u32[]{:S(2)}) %collective-permute-start.16) | collective-permute-done | bytes 196640 | tf_op jit(solution)/shard_map/ppermute | solution.py:14
  82.9 4.0 %bottom_out.1 = bf16[8,2,6,8,128]{4,3,2,1,0:T(8,128)(2,1)} custom-call(s32[5]{0:T(128)S(1)} %pad_add_fusion.place_ref, bf16[8,8,6,4,128]{4,3,2,1,0:T(4,128)(2,1)S(1)} %all-to-all-done.1.field_ref, bf16[8,8,6,2,128]{4,3,2,1,0:T(2,128)(2,1)S(1)} %collective-permute-done.15.y_in_ref, bf16[8,8,6,2,128]{4,3,2,1,0:T(2,128)(2,1)S(1)} %collective-permute-done.16.y_out_ref, ...), custom_call_target="tpu_custom_call" | custom-call | tf_op jit(solution)/shard_map/bottom_out/pallas_call | solution.py:463
  86.8 3.4 %all-to-all-start.2 = ((bf16[8,2,6,8,128]{4,3,2,1,0:T(8,128)(2,1)}), bf16[8,2,6,8,128]{4,3,2,1,0:T(8,128)(2,1)S(1)}, u32[]{:S(2)}, u32[]{:S(2)}) async-start(bf16[8,2,6,8,128]{4,3,2,1,0:T(8,128)(2,1)} %bottom_out.1), calls=%async_computation.2 | async-start | bytes 393216 | tf_op jit(solution)/shard_map/all_to_all | solution.py:651
  90.3 0.1 copy.21.skip_ref
  90.4 3.3 %decode_skip.1 = (f32[3,288,256]{2,1,0:T(8,128)S(1)}, bf16[3,512,256]{2,1,0:T(8,128)(2,1)S(1)}, bf16[3,512,256]{2,1,0:T(8,128)(2,1)S(1)}, bf16[3,512,256]{2,1,0:T(8,128)(2,1)S(1)}) custom-call(bf16[6,10,8,256]{3,2,1,0:T(8,128)(2,1)S(1)} %copy.21.skip_ref, bf16[6,10,256]{2,1,0:T(8,128)(2,1)S(1)} %collective-permute-done.14.edge_ref, ...), custom_call_target="tpu_custom_call" | custom-call | tf_op jit(solution)/shard_map/decode_skip/pallas_call | solution.py:514
  93.7 5.1 %all-to-all-done.2.bottom_ref = bf16[8,2,6,8,128]{4,3,2,1,0:T(8,128)(2,1)S(1)} async-done(((bf16[8,2,6,8,128]{4,3,2,1,0:T(8,128)(2,1)}), bf16[8,2,6,8,128]{4,3,2,1,0:T(8,128)(2,1)S(1)}, u32[]{:S(2)}, u32[]{:S(2)}) %all-to-all-start.2) | async-done | bytes 196640 | tf_op jit(solution)/shard_map/all_to_all | solution.py:651
  98.7 6.1 %decode.1 = bf16[4,8,8,256]{3,2,1,0:T(8,128)(2,1)} custom-call(s32[5]{0:T(128)S(1)} %pad_add_fusion.place_ref, bf16[8,2,6,8,128]{4,3,2,1,0:T(8,128)(2,1)S(1)} %all-to-all-done.2.bottom_ref, f32[3,288,256]{2,1,0:T(8,128)S(1)} %get-tuple-element.49.skip_ref, bf16[3,512,256]{2,1,0:T(8,128)(2,1)S(1)} %get-tuple-element.50.refs_0_, ...), custom_call_target="tpu_custom_call" | custom-call | tf_op jit(solution)/shard_map/decode/pallas_call | solution.py:594
  (28 shorter events, 0.2 us)
Async XLA Ops:
  0.0 17.1 %copy-start = (bf16[8,16,16,128]{3,2,1,0:T(8,128)(2,1)S(1)}, bf16[8,16,16,128]{3,2,1,0:T(8,128)(2,1)}, u32[]{:S(2)}) copy-start(bf16[8,16,16,128]{3,2,1,0:T(8,128)(2,1)} %refs_0_.1) | copy-start | bytes 1572868
  1.1 12.2 %collective-permute-start = (bf16[3,16,16,128]{3,2,1,0:T(8,128)(2,1)S(1)}, bf16[3,16,16,128]{3,2,1,0:T(8,128)(2,1)S(1)}, u32[]{:S(2)}, u32[]{:S(2)}) collective-permute-start(bf16[3,16,16,128]{3,2,1,0:T(8,128)(2,1)S(1)} %get-tuple-element.57), channel_id=1, source_target_pairs={{0,16},{16,0},{32,48},{48,32},{64,80},{80,64},{96,112},{112,96},{1... | collective-permute-start | bytes 589832 | tf_op jit(solution)/shard_map/ppermute | solution.py:14
  4.3 12.8 %collective-permute-start.1 = (bf16[3,16,16,128]{3,2,1,0:T(8,128)(2,1)S(1)}, bf16[3,16,16,128]{3,2,1,0:T(8,128)(2,1)S(1)}, u32[]{:S(2)}, u32[]{:S(2)}) collective-permute-start(bf16[3,16,16,128]{3,2,1,0:T(8,128)(2,1)S(1)} %get-tuple-element.56), channel_id=1, source_target_pairs={{0,112},{16,32},{32,16},{48,64},{64,48},{80,96},{96,80},{112,0},{1... | collective-permute-start | bytes 589832 | tf_op jit(solution)/shard_map/ppermute | solution.py:14
  18.0 10.0 %collective-permute-start.2 = (bf16[14,3,16,128]{3,2,1,0:T(8,128)(2,1)S(1)}, bf16[14,3,16,128]{3,2,1,0:T(8,128)(2,1)S(1)}, u32[]{:S(2)}, u32[]{:S(2)}) collective-permute-start(bf16[14,3,16,128]{3,2,1,0:T(8,128)(2,1)S(1)} %get-tuple-element.37), channel_id=1, source_target_pairs={{0,2},{2,0},{4,6},{6,4},{8,10},{10,8},{12,14},{14,12},{1,3},{3,1},... | collective-permute-start | bytes 516104 | tf_op jit(solution)/shard_map/ppermute | solution.py:14
  18.1 9.9 %collective-permute-start.3 = (bf16[14,3,16,128]{3,2,1,0:T(8,128)(2,1)S(1)}, bf16[14,3,16,128]{3,2,1,0:T(8,128)(2,1)S(1)}, u32[]{:S(2)}, u32[]{:S(2)}) collective-permute-start(bf16[14,3,16,128]{3,2,1,0:T(8,128)(2,1)S(1)} %get-tuple-element.38), channel_id=1, source_target_pairs={{0,14},{2,4},{4,2},{6,8},{8,6},{10,12},{12,10},{14,0},{1,15},{3,5}... | collective-permute-start | bytes 516104 | tf_op jit(solution)/shard_map/ppermute | solution.py:14
  21.2 6.7 %collective-permute-start.4 = (bf16[14,16,128]{2,1,0:T(8,128)(2,1)S(1)}, bf16[14,16,128]{2,1,0:T(8,128)(2,1)S(1)}, u32[]{:S(2)}, u32[]{:S(2)}) collective-permute-start(bf16[14,16,128]{2,1,0:T(8,128)(2,1)S(1)} %get-tuple-element.35.refs_2_), channel_id=1, source_target_pairs={{0,1},{1,0},{2,3},{3,2},{4,5},{5,4},{6,7},{7,6},{8,9},{9,8},{10,11... | collective-permute-start | bytes 172040 | tf_op jit(solution)/shard_map/ppermute | solution.py:629
  22.7 3.9 %collective-permute-start.5 = (bf16[14,3,128]{2,1,0:T(4,128)(2,1)S(1)}, bf16[14,3,128]{2,1,0:T(4,128)(2,1)S(1)}, u32[]{:S(2)}, u32[]{:S(2)}) collective-permute-start(bf16[14,3,128]{2,1,0:T(4,128)(2,1)S(1)} %get-tuple-element.39), channel_id=1, source_target_pairs={{0,3},{1,2},{2,1},{3,0},{4,7},{5,6},{6,5},{7,4},{8,11},{9,10},{10,... | collective-permute-start | bytes 32264 | tf_op jit(solution)/shard_map/ppermute | solution.py:14
  22.7 5.3 %collective-permute-start.6 = (bf16[14,3,128]{2,1,0:T(4,128)(2,1)S(1)}, bf16[14,3,128]{2,1,0:T(4,128)(2,1)S(1)}, u32[]{:S(2)}, u32[]{:S(2)}) collective-permute-start(bf16[14,3,128]{2,1,0:T(4,128)(2,1)S(1)} %get-tuple-element.40), channel_id=1, source_target_pairs={{0,15},{1,14},{2,5},{3,4},{4,3},{5,2},{6,9},{7,8},{8,7},{9,6},{10,... | collective-permute-start | bytes 32264 | tf_op jit(solution)/shard_map/ppermute | solution.py:14
  26.6 11.3 %copy-start.1 = (bf16[3,3,3,128,256]{4,3,2,1,0:T(8,128)(2,1)S(1)}, bf16[3,3,3,128,256]{4,3,2,1,0:T(8,128)(2,1)}, u32[]{:S(2)}) copy-start(bf16[3,3,3,128,256]{4,3,2,1,0:T(8,128)(2,1)} %param.8) | copy-start | bytes 5308420
  34.0 3.9 %collective-permute-start.7 = (bf16[6,10,128]{2,1,0:T(8,128)(2,1)S(1)}, bf16[6,10,128]{2,1,0:T(8,128)(2,1)S(1)}, u32[]{:S(2)}, u32[]{:S(2)}) collective-permute-start(bf16[6,10,128]{2,1,0:T(8,128)(2,1)S(1)} %fusion.1), channel_id=1, source_target_pairs={{0,1},{1,0},{2,3},{3,2},{4,5},{5,4},{6,7},{7,6},{8,9},{9,8},{10,11... | collective-permute-start | bytes 46088 | tf_op jit(solution)/shard_map/ppermute | solution.py:622
  39.4 4.3 %collective-permute-start.8 = (bf16[2,4,1,256]{3,1,0,2:T(4,128)(2,1)S(1)}, bf16[2,4,1,256]{3,1,0,2:T(4,128)(2,1)S(1)}, u32[]{:S(2)}, u32[]{:S(2)}) collective-permute-start(bf16[2,4,1,256]{3,1,0,2:T(4,128)(2,1)S(1)} %get-tuple-element.72), channel_id=1, source_target_pairs={{0,14},{2,4},{4,2},{6,8},{8,6},{10,12},{12,10},{14,0},{1,15},{3,5}... | collective-permute-start | bytes 12296 | tf_op jit(solution)/shard_map/ppermute | solution.py:14
  39.5 4.2 %collective-permute-start.9 = (bf16[2,4,1,256]{3,1,0,2:T(4,128)(2,1)S(1)}, bf16[2,4,1,256]{3,1,0,2:T(4,128)(2,1)S(1)}, u32[]{:S(2)}, u32[]{:S(2)}) collective-permute-start(bf16[2,4,1,256]{3,1,0,2:T(4,128)(2,1)S(1)} %get-tuple-element.73), channel_id=1, source_target_pairs={{0,2},{2,0},{4,6},{6,4},{8,10},{10,8},{12,14},{14,12},{1,3},{3,1},... | collective-permute-start | bytes 12296 | tf_op jit(solution)/shard_map/ppermute | solution.py:14
  39.6 10.0 %collective-permute-start.10 = (bf16[1,8,8,256]{3,1,0,2:T(8,128)(2,1)S(1)}, bf16[1,8,8,256]{3,1,0,2:T(8,128)(2,1)S(1)}, u32[]{:S(2)}, u32[]{:S(2)}) collective-permute-start(bf16[1,8,8,256]{3,1,0,2:T(8,128)(2,1)S(1)} %get-tuple-element.60), channel_id=1, source_target_pairs={{0,112},{16,32},{32,16},{48,64},{64,48},{80,96},{96,80},{112,0},{1... | collective-permute-start | bytes 98312 | tf_op jit(solution)/shard_map/ppermute | solution.py:14
  41.4 8.2 %collective-permute-start.11 = (bf16[1,8,8,256]{3,1,0,2:T(8,128)(2,1)S(1)}, bf16[1,8,8,256]{3,1,0,2:T(8,128)(2,1)S(1)}, u32[]{:S(2)}, u32[]{:S(2)}) collective-permute-start(bf16[1,8,8,256]{3,1,0,2:T(8,128)(2,1)S(1)} %get-tuple-element.61), channel_id=1, source_target_pairs={{0,16},{16,0},{32,48},{48,32},{64,80},{80,64},{96,112},{112,96},{1... | collective-permute-start | bytes 98312 | tf_op jit(solution)/shard_map/ppermute | solution.py:14
  44.6 14.7 %all-to-all-start = ((bf16[16,2,24,256]{3,2,1,0:T(8,128)(2,1)}), bf16[16,2,24,256]{3,2,1,0:T(8,128)(2,1)S(1)}, u32[]{:S(2)}, u32[]{:S(2)}) async-start(bf16[16,2,24,256]{3,2,1,0:T(8,128)(2,1)} %broadcast_in_dim.16.refs_1_), calls=%async_computation | async-start | bytes 786432 | tf_op jit(solution)/shard_map/all_to_all | solution.py:641
  49.8 4.3 %collective-permute-start.13 = (bf16[6,1,8,256]{3,1,0,2:T(2,128)(2,1)S(1)}, bf16[6,1,8,256]{3,1,0,2:T(2,128)(2,1)S(1)}, u32[]{:S(2)}, u32[]{:S(2)}) collective-permute-start(bf16[6,1,8,256]{3,1,0,2:T(2,128)(2,1)S(1)} %broadcast_select_fusion.7), channel_id=1, source_target_pairs={{0,2},{2,0},{4,6},{6,4},{8,10},{10,8},{12,14},{14,12},{1,3},{3,1},... | collective-permute-start | bytes 73736 | tf_op jit(solution)/shard_map/ppermute | solution.py:14
  49.9 5.0 %collective-permute-start.12 = (bf16[6,1,8,256]{3,1,0,2:T(2,128)(2,1)S(1)}, bf16[6,1,8,256]{3,1,0,2:T(2,128)(2,1)S(1)}, u32[]{:S(2)}, u32[]{:S(2)}) collective-permute-start(bf16[6,1,8,256]{3,1,0,2:T(2,128)(2,1)S(1)} %get-tuple-element.53), channel_id=1, source_target_pairs={{0,14},{2,4},{4,2},{6,8},{8,6},{10,12},{12,10},{14,0},{1,15},{3,5}... | collective-permute-start | bytes 73736 | tf_op jit(solution)/shard_map/ppermute | solution.py:14
  62.2 13.0 %all-to-all-start.1 = ((bf16[8,8,6,4,128]{4,3,2,1,0:T(4,128)(2,1)}), bf16[8,8,6,4,128]{4,3,2,1,0:T(4,128)(2,1)S(1)}, u32[]{:S(2)}, u32[]{:S(2)}) async-start(bf16[8,8,6,4,128]{4,3,2,1,0:T(4,128)(2,1)} %bottom_in.1.refs_1_), calls=%async_computation.1 | async-start | bytes 786432 | tf_op jit(solution)/shard_map/all_to_all | solution.py:644
  65.9 5.0 %collective-permute-start.14 = (bf16[6,10,256]{2,1,0:T(8,128)(2,1)S(1)}, bf16[6,10,256]{2,1,0:T(8,128)(2,1)S(1)}, u32[]{:S(2)}, u32[]{:S(2)}) collective-permute-start(bf16[6,10,256]{2,1,0:T(8,128)(2,1)S(1)} %fusion), channel_id=1, source_target_pairs={{0,1},{1,0},{2,3},{3,2},{4,5},{5,4},{6,7},{7,6},{8,9},{9,8},{10,11... | collective-permute-start | bytes 92168 | tf_op jit(solution)/shard_map/ppermute | solution.py:622
  75.7 5.5 %collective-permute-start.15 = (bf16[8,8,6,2,128]{4,3,2,1,0:T(2,128)(2,1)S(1)}, bf16[8,8,6,2,128]{4,3,2,1,0:T(2,128)(2,1)S(1)}, u32[]{:S(2)}, u32[]{:S(2)}) collective-permute-start(bf16[8,8,6,2,128]{4,3,2,1,0:T(2,128)(2,1)S(1)} %get-tuple-element.59), channel_id=1, source_target_pairs={{0,2},{2,0},{4,6},{6,4},{8,10},{10,8},{12,14},{14,12},{1,3},{3,1},... | collective-permute-start | bytes 589832 | tf_op jit(solution)/shard_map/ppermute | solution.py:14
  75.8 7.1 %collective-permute-start.16 = (bf16[8,8,6,2,128]{4,3,2,1,0:T(2,128)(2,1)S(1)}, bf16[8,8,6,2,128]{4,3,2,1,0:T(2,128)(2,1)S(1)}, u32[]{:S(2)}, u32[]{:S(2)}) collective-permute-start(bf16[8,8,6,2,128]{4,3,2,1,0:T(2,128)(2,1)S(1)} %get-tuple-element.58), channel_id=1, source_target_pairs={{0,14},{2,4},{4,2},{6,8},{8,6},{10,12},{12,10},{14,0},{1,15},{3,5}... | collective-permute-start | bytes 589832 | tf_op jit(solution)/shard_map/ppermute | solution.py:14
  86.8 11.9 %all-to-all-start.2 = ((bf16[8,2,6,8,128]{4,3,2,1,0:T(8,128)(2,1)}), bf16[8,2,6,8,128]{4,3,2,1,0:T(8,128)(2,1)S(1)}, u32[]{:S(2)}, u32[]{:S(2)}) async-start(bf16[8,2,6,8,128]{4,3,2,1,0:T(8,128)(2,1)} %bottom_out.1), calls=%async_computation.2 | async-start | bytes 393216 | tf_op jit(solution)/shard_map/all_to_all | solution.py:651

commit v11 on v10

--- a/solution.py
+++ b/solution.py
@@ -483,15 +483,15 @@
     deep = weights.shape[2] - channels
     rows, extra = size_x * size_y * size_z, size_x * size_y
 
-    def body(skip_ref, edge_ref, weights_hbm, out_ref, *refs):
-        rest_refs, (weights_ref, sems) = refs[:3], refs[3:]
+    def body(place_ref, skip_ref, edge_ref, weights_hbm, out_hbm, *refs):
+        rest_refs, (weights_ref, out_ref, sems) = refs[:4], refs[4:]
         copies = [
             pltpu.make_async_copy(weights_hbm.at[step, :, pl.ds(deep, channels)], weights_ref.at[step], sems.at[step])
             for step in range(9)
         ]
         rest = [
             pltpu.make_async_copy(weights_hbm.at[step, :, pl.ds(0, deep)], rest_refs[step], sems.at[9 + step])
-            for step in range(3)
+            for step in range(4)
         ]
         for copy in copies + rest:
             copy.start()
@@ -505,27 +505,37 @@
         for copy in copies:
             copy.wait()
         block = jnp.concatenate(blocks, axis=1)
+        sums = []
         for tap in range(3):
             kernel = weights_ref[:, tap].reshape(9 * channels, filters)
-            out_ref[tap] = jnp.dot(block, kernel, preferred_element_type=jnp.float32)
+            sums.append(jnp.dot(block, kernel, preferred_element_type=jnp.float32))
+        out_ref[...] = join_taps(place_ref[2] == 0, sums, extra, size_z)
+        rest.append(pltpu.make_async_copy(out_ref, out_hbm, sems.at[13]))
+        rest[-1].start()
         for copy in rest:
             copy.wait()
 
     return pl.pallas_call(
         body,
-        in_specs=[pl.BlockSpec(memory_space=pltpu.VMEM)] * 2 + [pl.BlockSpec(memory_space=pltpu.HBM)],
-        out_specs=[pl.BlockSpec(memory_space=pltpu.VMEM)] * 4,
+        in_specs=[pl.BlockSpec(memory_space=pltpu.SMEM)]
+        + [pl.BlockSpec(memory_space=pltpu.VMEM)] * 2
+        + [pl.BlockSpec(memory_space=pltpu.HBM)],
+        out_specs=[pl.BlockSpec(memory_space=pltpu.HBM)] + [pl.BlockSpec(memory_space=pltpu.VMEM)] * 4,
         out_shape=[
-            pltpu.VMEM((3, rows + extra, filters), jnp.float32),
+            pltpu.HBM((extra, size_z, filters), jnp.float32),
         ]
-        + [pltpu.VMEM((3, deep, filters), jnp.bfloat16)] * 3,
-        scratch_shapes=[pltpu.VMEM((9, 3, channels, filters), jnp.bfloat16), pltpu.SemaphoreType.DMA((12,))],
+        + [pltpu.VMEM((3, deep, filters), jnp.bfloat16)] * 4,
+        scratch_shapes=[
+            pltpu.VMEM((9, 3, channels, filters), jnp.bfloat16),
+            pltpu.VMEM((extra, size_z, filters), jnp.float32),
+            pltpu.SemaphoreType.DMA((14,)),
+        ],
         compiler_params=pltpu.CompilerParams(vmem_limit_bytes=14 << 20),
         name="decode_skip",
-    )(skip, edge, far(weights))
-
-
-def decode(place, bottom, skip_sums, first_weights, weights, shape):
+    )(place, skip, edge, far(weights))
+
+
+def decode(place, bottom, skip_part, first_weights, weights, shape):
     devices, pairs, coarse_z, _, _ = bottom.shape
     size_x, size_y, size_z = shape
     full_x, full_y = size_x + 2, size_y + 2
@@ -533,12 +543,13 @@
     filters = weights.shape[-1]
     rows, extra = size_x * size_y * size_z, size_x * size_y
 
-    def body(place_ref, bottom_ref, skip_ref, *refs):
-        near_refs, (weights_hbm, out_ref, main_ref, side_ref, sums_ref, weights_ref, sems) = refs[:3], refs[3:]
+    def body(place_ref, bottom_ref, skip_hbm, *refs):
+        near_refs, (weights_hbm, out_ref, main_ref, side_ref, sums_ref, skip_ref, weights_ref, sems) = refs[:4], refs[4:]
         copies = [
-            pltpu.make_async_copy(weights_hbm.at[3 + step, :, pl.ds(0, channels)], weights_ref.at[step], sems.at[step])
-            for step in range(6)
+            pltpu.make_async_copy(weights_hbm.at[4 + step, :, pl.ds(0, channels)], weights_ref.at[step], sems.at[step])
+            for step in range(5)
         ]
+        copies.append(pltpu.make_async_copy(skip_hbm, skip_ref, sems.at[5]))
         for copy in copies:
             copy.start()
         first = place_ref[2] == 0
@@ -572,29 +583,29 @@
                 for dy in range(3):
                     main_ref[dy, x] = fine[8 * dy : 8 * dy + size_y * size_z].astype(jnp.bfloat16)
                     side_ref[dy, x] = fine_edge[dy : dy + size_y]
-        for dx in range(3):
-            blocks = []
-            for dy in range(3):
-                main = main_ref[dy, dx : dx + size_x].reshape(rows, channels)
-                side = side_ref[dy, dx : dx + size_x].reshape(extra, channels).astype(jnp.bfloat16)
-                blocks.append(jnp.concatenate([main, side], axis=0))
-                if dx:
-                    copies[3 * dx + dy - 3].wait()
-            block = jnp.concatenate(blocks, axis=1)
+        for step in range(9):
+            dx, dy = step // 3, step % 3
+            main = main_ref[dy, dx : dx + size_x].reshape(rows, channels)
+            side = side_ref[dy, dx : dx + size_x].reshape(extra, channels).astype(jnp.bfloat16)
+            block = jnp.concatenate([main, side], axis=0)
+            if step >= 4:
+                copies[step - 4].wait()
             for tap in range(3):
-                if dx == 0:
-                    kernel = jnp.concatenate([ref[tap] for ref in near_refs], axis=0)
-                    sums_ref[tap] = skip_ref[tap] + jnp.dot(block, kernel, preferred_element_type=jnp.float32)
+                kernel = near_refs[step][tap] if step < 4 else weights_ref[step - 4, tap]
+                product = jnp.dot(block, kernel, preferred_element_type=jnp.float32)
+                if step == 0:
+                    sums_ref[tap] = product
                 else:
-                    kernel = weights_ref[3 * dx - 3 : 3 * dx, tap].reshape(3 * channels, filters)
-                    sums_ref[tap] += jnp.dot(block, kernel, preferred_element_type=jnp.float32)
-        total = join_taps(first, [sums_ref[tap] for tap in range(3)], extra, size_z)
+                    sums_ref[tap] += product
+        copies[-1].wait()
+        total = join_taps(first, [sums_ref[tap] for tap in range(3)], extra, size_z) + skip_ref[...]
         out_ref[...] = total.reshape(size_x, size_y, size_z, filters).astype(out_ref.dtype)
 
     return pl.pallas_call(
         body,
         in_specs=[pl.BlockSpec(memory_space=pltpu.SMEM)]
-        + [pl.BlockSpec(memory_space=pltpu.VMEM)] * 5
+        + [pl.BlockSpec(memory_space=space) for space in (pltpu.VMEM, pltpu.HBM)]
+        + [pl.BlockSpec(memory_space=pltpu.VMEM)] * 4
         + [pl.BlockSpec(memory_space=pltpu.HBM)],
         out_specs=pl.BlockSpec(memory_space=pltpu.VMEM),
         out_shape=jax.ShapeDtypeStruct((size_x, size_y, size_z, filters), jnp.bfloat16),
@@ -602,12 +613,13 @@
             pltpu.VMEM((3, full_x, size_y * size_z, channels), jnp.bfloat16),
             pltpu.VMEM((3, full_x, size_y, channels), jnp.float32),
             pltpu.VMEM((3, rows + extra, filters), jnp.float32),
-            pltpu.VMEM((6, 3, channels, filters), jnp.bfloat16),
+            pltpu.VMEM((extra, size_z, filters), jnp.float32),
+            pltpu.VMEM((5, 3, channels, filters), jnp.bfloat16),
             pltpu.SemaphoreType.DMA((6,)),
         ],
         compiler_params=pltpu.CompilerParams(vmem_limit_bytes=20 << 20),
         name="decode",
-    )(place, bottom, near(skip_sums), *map(near, first_weights), far(weights))
+    )(place, bottom, far(skip_part), *map(near, first_weights), far(weights))
 
 
 def solution(mesh):
@@ -650,8 +662,8 @@
         second = bottom_out(place, first, y_in, y_out, w_out)
         second = lax.all_to_all(second, "gx", 0, 0)
         w_up = w_up.reshape(9, 3, w_up.shape[3], w_up.shape[4])
-        skip_sums, *w_near = decode_skip(place, around, side, w_up)
-        return decode(place, second, skip_sums, w_near, w_up, skip.shape[:3])
+        skip_part, *w_near = decode_skip(place, around, side, w_up)
+        return decode(place, second, skip_part, w_near, w_up, skip.shape[:3])
 
     space = P("gx", "gy", "gz", None)
     filters = P(None, None, None, None, "gx")

time: 105 us -> 105 us (level)
  waiting for transfers between devices: 31.1 us -> 29.8 us
    all_to_all x1, waiting for transfers between devices: 5.06 us -> 3.75 us  [local(): second = lax.all_to_all(second, 'gx', 0, 0)]
    pallas_call x1, Pallas kernels: 3.26 us -> 4.57 us  [decode_skip(): pl.pallas_call(body, in_specs=[pl.BlockSpec(memory_space=pltpu.SMEM)] + [...]
  transfers between devices with their start and end apart: 20 -> 20, of which waited for: 10 -> 10; matrix products, arithmetic and copies ran while one was open for 2% -> 2% of each run, Pallas kernels for 13% -> 14%
where the time goes in v11:
time: 105 us; the launch traced here: 104 us
  starting transfers between devices  35.8 us (34%)
  Pallas kernels  34.7 us (33%)
  waiting for transfers between devices  29.8 us (28%)
  other arithmetic  2.26 us (2%)
  local copies, waits for them, and re-layouts  1.05 us (1%)
    ppermute x7, starting transfers between devices, send(): lax.ppermute(outer_block, axis, outer)  17.5 us
    ppermute x7, waiting for transfers between devices, send(): lax.ppermute(outer_block, axis, outer)  9.86 us
    ppermute x2, waiting for transfers between devices, edge_of(): lax.ppermute(jnp.where(place_z == 0, plane_high, plane_low), 'gz', swap)  7.62 us
    pallas_call x1, Pallas kernels, encode(): pl.pallas_call(body, in_specs=[pl.BlockSpec(memory_space=pltpu.SMEM)] + [...  5.97 us
    pallas_call x1, Pallas kernels, decode(): pl.pallas_call(body, in_specs=[pl.BlockSpec(memory_space=pltpu.SMEM)] + [...  5.12 us
    pallas_call x3, Pallas kernels, bring(): pl.pallas_call(body, in_specs=[pl.BlockSpec(memory_space=pltpu.HBM)] * co...  5.03 us
    all_to_all x1, starting transfers between devices, local(): column = lax.all_to_all(column, ('gx', 'gz'), 0, 0)  5.01 us
    pallas_call x1, Pallas kernels, prepare(): pl.pallas_call(body, in_specs=[pl.BlockSpec(memory_space=pltpu.HBM)] * 3,...  4.89 us
  transfers between devices with their start and end apart: 20, of which 10 were waited for; matrix products, arithmetic and copies ran while one was open for 2% of the time, Pallas kernels for 14%

profile of v11, /device:TPU:0, one launch (start us, length us, event | category | flops | bytes accessed | tf_op | source)
XLA Modules:
  0.0 104.0 jit_solution(13046959608573459668)
XLA Ops:
  0.0 1.1 %broadcast_select_fusion.2 = (bf16[3,16,16,128]{3,2,1,0:T(8,128)(2,1)S(1)}, bf16[3,16,16,128]{3,2,1,0:T(8,128)(2,1)S(1)}) fusion(pred[]{:T(512)S(6)} %eq.25, bf16[8,16,16,128]{3,2,1,0:T(8,128)(2,1)} %refs_0_.1), kind=kLoop, calls=%fused_computation.3 | loop fusion | flops 196608 | bytes 786433 | tf_op jit(solution)/shard_map/jit(_where)/select_n | solution.py:19
  1.1 3.2 %collective-permute-start = (bf16[3,16,16,128]{3,2,1,0:T(8,128)(2,1)S(1)}, bf16[3,16,16,128]{3,2,1,0:T(8,128)(2,1)S(1)}, u32[]{:S(2)}, u32[]{:S(2)}) collective-permute-start(bf16[3,16,16,128]{3,2,1,0:T(8,128)(2,1)S(1)} %get-tuple-element.59), channel_id=1, source_target_pairs={{0,16},{16,0},{32,48},{48,32},{64,80},{80,64},{96,112},{112,96},{1... | collective-permute-start | bytes 589832 | tf_op jit(solution)/shard_map/ppermute | solution.py:14
  4.3 4.0 %collective-permute-start.1 = (bf16[3,16,16,128]{3,2,1,0:T(8,128)(2,1)S(1)}, bf16[3,16,16,128]{3,2,1,0:T(8,128)(2,1)S(1)}, u32[]{:S(2)}, u32[]{:S(2)}) collective-permute-start(bf16[3,16,16,128]{3,2,1,0:T(8,128)(2,1)S(1)} %get-tuple-element.58), channel_id=1, source_target_pairs={{0,112},{16,32},{32,16},{48,64},{64,48},{80,96},{96,80},{112,0},{1... | collective-permute-start | bytes 589832 | tf_op jit(solution)/shard_map/ppermute | solution.py:14
  8.3 4.9 %prepare.1 = (bf16[4,3,3,128,256]{4,3,2,1,0:T(8,128)(2,1)}, bf16[9,256,256]{2,1,0:T(8,128)(2,1)}, bf16[9,512,256]{2,1,0:T(8,128)(2,1)}) custom-call(bf16[3,3,3,128,128]{4,3,2,1,0:T(8,128)(2,1)} %full_hbm.1, bf16[3,3,3,64,256]{4,3,2,1,0:T(8,128)(2,1)} %bitcast.20, bf16[3,3,3,64,512]{4,3,2,1,0:T(8,128)(2,1)} %bitcast.19), custom_call_target="tpu_custom_call" | custom-call | tf_op jit(solution)/shard_map/prepare/pallas_call | solution.py:283
  13.2 0.1 pad_add_fusion.place_ref
  13.3 3.8 %collective-permute-done.1.x_out_ref = bf16[3,16,16,128]{3,2,1,0:T(8,128)(2,1)S(1)} collective-permute-done((bf16[3,16,16,128]{3,2,1,0:T(8,128)(2,1)S(1)}, bf16[3,16,16,128]{3,2,1,0:T(8,128)(2,1)S(1)}, u32[]{:S(2)}, u32[]{:S(2)}) %collective-permute-start.1) | collective-permute-done | bytes 196640 | tf_op jit(solution)/shard_map/ppermute | solution.py:14
  17.1 0.9 pack_y.1
  18.0 0.1 collective-permute-start.2
  18.1 3.1 %collective-permute-start.3 = (bf16[14,3,16,128]{3,2,1,0:T(8,128)(2,1)S(1)}, bf16[14,3,16,128]{3,2,1,0:T(8,128)(2,1)S(1)}, u32[]{:S(2)}, u32[]{:S(2)}) collective-permute-start(bf16[14,3,16,128]{3,2,1,0:T(8,128)(2,1)S(1)} %get-tuple-element.39), channel_id=1, source_target_pairs={{0,14},{2,4},{4,2},{6,8},{8,6},{10,12},{12,10},{14,0},{1,15},{3,5}... | collective-permute-start | bytes 516104 | tf_op jit(solution)/shard_map/ppermute | solution.py:14
  21.2 1.5 %collective-permute-start.4 = (bf16[14,16,128]{2,1,0:T(8,128)(2,1)S(1)}, bf16[14,16,128]{2,1,0:T(8,128)(2,1)S(1)}, u32[]{:S(2)}, u32[]{:S(2)}) collective-permute-start(bf16[14,16,128]{2,1,0:T(8,128)(2,1)S(1)} %get-tuple-element.36.refs_2_), channel_id=1, source_target_pairs={{0,1},{1,0},{2,3},{3,2},{4,5},{5,4},{6,7},{7,6},{8,9},{9,8},{10,11... | collective-permute-start | bytes 172040 | tf_op jit(solution)/shard_map/ppermute | solution.py:641
  22.7 1.9 %collective-permute-start.6 = (bf16[14,3,128]{2,1,0:T(4,128)(2,1)S(1)}, bf16[14,3,128]{2,1,0:T(4,128)(2,1)S(1)}, u32[]{:S(2)}, u32[]{:S(2)}) collective-permute-start(bf16[14,3,128]{2,1,0:T(4,128)(2,1)S(1)} %get-tuple-element.41), channel_id=1, source_target_pairs={{0,15},{1,14},{2,5},{3,4},{4,3},{5,2},{6,9},{7,8},{8,7},{9,6},{10,... | collective-permute-start | bytes 32264 | tf_op jit(solution)/shard_map/ppermute | solution.py:14
  24.6 2.0 %bring.3 = (bf16[8,16,16,128]{3,2,1,0:T(8,128)(2,1)S(1)}, bf16[4,3,3,128,256]{4,3,2,1,0:T(8,128)(2,1)S(1)}) custom-call(bf16[8,16,16,128]{3,2,1,0:T(8,128)(2,1)} %refs_0_.1, bf16[4,3,3,128,256]{4,3,2,1,0:T(8,128)(2,1)} %get-tuple-element.33.refs_1_, bf16[14,16,128]{2,1,0:T(8,128)(2,1)S(1)} %get-tuple-element.36.refs_2_), custom_call_target="tpu_custom_call" | custom-call | tf_op jit(solution)/shard_map/bring/pallas_call | solution.py:229
  26.6 1.3 %collective-permute-done.6.edge_out_ref = bf16[14,3,128]{2,1,0:T(4,128)(2,1)S(1)} collective-permute-done((bf16[14,3,128]{2,1,0:T(4,128)(2,1)S(1)}, bf16[14,3,128]{2,1,0:T(4,128)(2,1)S(1)}, u32[]{:S(2)}, u32[]{:S(2)}) %collective-permute-start.6) | collective-permute-done | bytes 10784 | tf_op jit(solution)/shard_map/ppermute | solution.py:14
  28.0 6.0 %encode.1.field_ref = bf16[6,10,8,128]{3,2,1,0:T(8,128)(2,1)S(1)} custom-call(s32[5]{0:T(128)S(1)} %pad_add_fusion.place_ref, bf16[8,16,16,128]{3,2,1,0:T(8,128)(2,1)S(1)} %get-tuple-element.37.own_ref, bf16[3,16,16,128]{3,2,1,0:T(8,128)(2,1)S(1)} %collective-permute-done.x_in_ref, bf16[3,16,16,128]{3,2,1,0:T(8,128)(2,1)S(1)} %collective-permute-done.1.x_out_ref, ...), custom_call_target="tpu_custom_call" | custom-call | tf_op jit(solution)/shard_map/encode/pallas_call | solution.py:197
  34.0 0.6 collective-permute-start.7
  34.7 3.3 %collective-permute-done.7.edge_ref = bf16[6,10,128]{2,1,0:T(8,128)(2,1)S(1)} collective-permute-done((bf16[6,10,128]{2,1,0:T(8,128)(2,1)S(1)}, bf16[6,10,128]{2,1,0:T(8,128)(2,1)S(1)}, u32[]{:S(2)}, u32[]{:S(2)}) %collective-permute-start.7) | collective-permute-done | bytes 15392 | tf_op jit(solution)/shard_map/ppermute | solution.py:634
  37.9 1.4 %half_level.1 = (bf16[4,8,8,256]{3,2,1,0:T(8,128)(2,1)S(1)}, bf16[2,16,256]{2,1,0:T(8,128)(2,1)S(1)}) custom-call(s32[5]{0:T(128)S(1)} %pad_add_fusion.place_ref, bf16[6,10,8,128]{3,2,1,0:T(8,128)(2,1)S(1)} %encode.1.field_ref, bf16[6,10,128]{2,1,0:T(8,128)(2,1)S(1)} %collective-permute-done.7.edge_ref, bf16[9,3,128,256]{3,2,1,0:T(8,128)(2,1)S(1)} %bitcast.16), custom_call_target="tpu_custom_call" | custom-call | tf_op jit(solution)/shard_map/half_level/pallas_call | solution.py:77
  39.4 0.1 collective-permute-start.8
  39.5 0.1 collective-permute-start.9
  39.6 1.8 %collective-permute-start.10 = (bf16[1,8,8,256]{3,1,0,2:T(8,128)(2,1)S(1)}, bf16[1,8,8,256]{3,1,0,2:T(8,128)(2,1)S(1)}, u32[]{:S(2)}, u32[]{:S(2)}) collective-permute-start(bf16[1,8,8,256]{3,1,0,2:T(8,128)(2,1)S(1)} %get-tuple-element.62), channel_id=1, source_target_pairs={{0,112},{16,32},{32,16},{48,64},{64,48},{80,96},{96,80},{112,0},{1... | collective-permute-start | bytes 98312 | tf_op jit(solution)/shard_map/ppermute | solution.py:14
  41.4 2.3 %collective-permute-done.8 = bf16[2,4,1,256]{3,1,0,2:T(4,128)(2,1)S(1)} collective-permute-done((bf16[2,4,1,256]{3,1,0,2:T(4,128)(2,1)S(1)}, bf16[2,4,1,256]{3,1,0,2:T(4,128)(2,1)S(1)}, u32[]{:S(2)}, u32[]{:S(2)}) %collective-permute-start.8) | collective-permute-done | bytes 4128 | tf_op jit(solution)/shard_map/ppermute | solution.py:14
  43.8 0.8 broadcast_in_dim.16.refs_1_
  44.6 5.0 %all-to-all-start = ((bf16[16,2,24,256]{3,2,1,0:T(8,128)(2,1)}), bf16[16,2,24,256]{3,2,1,0:T(8,128)(2,1)S(1)}, u32[]{:S(2)}, u32[]{:S(2)}) async-start(bf16[16,2,24,256]{3,2,1,0:T(8,128)(2,1)} %broadcast_in_dim.16.refs_1_), calls=%async_computation | async-start | bytes 786432 | tf_op jit(solution)/shard_map/all_to_all | solution.py:653
  49.6 0.1 broadcast_select_fusion.8
  49.7 0.1 broadcast_select_fusion.7
  49.8 0.1 collective-permute-start.13
  49.9 2.8 %collective-permute-start.12 = (bf16[6,1,8,256]{3,1,0,2:T(2,128)(2,1)S(1)}, bf16[6,1,8,256]{3,1,0,2:T(2,128)(2,1)S(1)}, u32[]{:S(2)}, u32[]{:S(2)}) collective-permute-start(bf16[6,1,8,256]{3,1,0,2:T(2,128)(2,1)S(1)} %get-tuple-element.55), channel_id=1, source_target_pairs={{0,14},{2,4},{4,2},{6,8},{8,6},{10,12},{12,10},{14,0},{1,15},{3,5}... | collective-permute-start | bytes 73736 | tf_op jit(solution)/shard_map/ppermute | solution.py:14
  52.8 1.4 %bring.4.weights_ref = bf16[9,256,256]{2,1,0:T(8,128)(2,1)S(1)} custom-call(bf16[9,256,256]{2,1,0:T(8,128)(2,1)} %get-tuple-element.44.refs_0_, bf16[16,2,24,256]{3,2,1,0:T(8,128)(2,1)} %broadcast_in_dim.16.refs_1_), custom_call_target="tpu_custom_call" | custom-call | tf_op jit(solution)/shard_map/bring/pallas_call | solution.py:229
  54.2 0.7 collective-permute-done.12
  54.9 0.1 broadcast_select_fusion.9
  55.0 4.3 %all-to-all-done.field_ref = bf16[16,2,24,256]{3,2,1,0:T(8,128)(2,1)S(1)} async-done(((bf16[16,2,24,256]{3,2,1,0:T(8,128)(2,1)}), bf16[16,2,24,256]{3,2,1,0:T(8,128)(2,1)S(1)}, u32[]{:S(2)}, u32[]{:S(2)}) %all-to-all-start) | async-done | bytes 393248 | tf_op jit(solution)/shard_map/all_to_all | solution.py:653
  59.3 2.9 %bottom_in.1.refs_1_ = bf16[8,8,6,4,128]{4,3,2,1,0:T(4,128)(2,1)} custom-call(s32[5]{0:T(128)S(1)} %pad_add_fusion.place_ref, bf16[16,2,24,256]{3,2,1,0:T(8,128)(2,1)S(1)} %all-to-all-done.field_ref, bf16[9,256,256]{2,1,0:T(8,128)(2,1)S(1)} %bring.4.weights_ref), custom_call_target="tpu_custom_call" | custom-call | tf_op jit(solution)/shard_map/bottom_in/pallas_call | solution.py:405
  62.2 3.5 %all-to-all-start.1 = ((bf16[8,8,6,4,128]{4,3,2,1,0:T(4,128)(2,1)}), bf16[8,8,6,4,128]{4,3,2,1,0:T(4,128)(2,1)S(1)}, u32[]{:S(2)}, u32[]{:S(2)}) async-start(bf16[8,8,6,4,128]{4,3,2,1,0:T(4,128)(2,1)} %bottom_in.1.refs_1_), calls=%async_computation.1 | async-start | bytes 786432 | tf_op jit(solution)/shard_map/all_to_all | solution.py:656
  65.6 0.2 pad_maximum_fusion
  65.9 0.7 collective-permute-start.14
  66.6 4.4 %collective-permute-done.14.edge_ref = bf16[6,10,256]{2,1,0:T(8,128)(2,1)S(1)} collective-permute-done((bf16[6,10,256]{2,1,0:T(8,128)(2,1)S(1)}, bf16[6,10,256]{2,1,0:T(8,128)(2,1)S(1)}, u32[]{:S(2)}, u32[]{:S(2)}) %collective-permute-start.14) | collective-permute-done | bytes 30752 | tf_op jit(solution)/shard_map/ppermute | solution.py:634
  70.9 4.3 %all-to-all-done.1.field_ref = bf16[8,8,6,4,128]{4,3,2,1,0:T(4,128)(2,1)S(1)} async-done(((bf16[8,8,6,4,128]{4,3,2,1,0:T(4,128)(2,1)}), bf16[8,8,6,4,128]{4,3,2,1,0:T(4,128)(2,1)S(1)}, u32[]{:S(2)}, u32[]{:S(2)}) %all-to-all-start.1) | async-done | bytes 393248 | tf_op jit(solution)/shard_map/all_to_all | solution.py:656
  75.2 0.5 broadcast_select_fusion
  75.7 0.1 collective-permute-start.15
  75.8 3.8 %collective-permute-start.16 = (bf16[8,8,6,2,128]{4,3,2,1,0:T(2,128)(2,1)S(1)}, bf16[8,8,6,2,128]{4,3,2,1,0:T(2,128)(2,1)S(1)}, u32[]{:S(2)}, u32[]{:S(2)}) collective-permute-start(bf16[8,8,6,2,128]{4,3,2,1,0:T(2,128)(2,1)S(1)} %get-tuple-element.60), channel_id=1, source_target_pairs={{0,14},{2,4},{4,2},{6,8},{8,6},{10,12},{12,10},{14,0},{1,15},{3,5}... | collective-permute-start | bytes 589832 | tf_op jit(solution)/shard_map/ppermute | solution.py:14
  79.5 1.7 %bring.5.weights_ref = bf16[9,512,256]{2,1,0:T(8,128)(2,1)S(1)} custom-call(bf16[9,512,256]{2,1,0:T(8,128)(2,1)} %get-tuple-element.47.refs_0_, bf16[8,8,6,4,128]{4,3,2,1,0:T(4,128)(2,1)} %bottom_in.1.refs_1_), custom_call_target="tpu_custom_call" | custom-call | tf_op jit(solution)/shard_map/bring/pallas_call | solution.py:229
  81.2 1.7 %collective-permute-done.16.y_out_ref = bf16[8,8,6,2,128]{4,3,2,1,0:T(2,128)(2,1)S(1)} collective-permute-done((bf16[8,8,6,2,128]{4,3,2,1,0:T(2,128)(2,1)S(1)}, bf16[8,8,6,2,128]{4,3,2,1,0:T(2,128)(2,1)S(1)}, u32[]{:S(2)}, u32[]{:S(2)}) %collective-permute-start.16) | collective-permute-done | bytes 196640 | tf_op jit(solution)/shard_map/ppermute | solution.py:14
  82.9 4.0 %bottom_out.1 = bf16[8,2,6,8,128]{4,3,2,1,0:T(8,128)(2,1)} custom-call(s32[5]{0:T(128)S(1)} %pad_add_fusion.place_ref, bf16[8,8,6,4,128]{4,3,2,1,0:T(4,128)(2,1)S(1)} %all-to-all-done.1.field_ref, bf16[8,8,6,2,128]{4,3,2,1,0:T(2,128)(2,1)S(1)} %collective-permute-done.15.y_in_ref, bf16[8,8,6,2,128]{4,3,2,1,0:T(2,128)(2,1)S(1)} %collective-permute-done.16.y_out_ref, ...), custom_call_target="tpu_custom_call" | custom-call | tf_op jit(solution)/shard_map/bottom_out/pallas_call | solution.py:463
  86.8 3.4 %all-to-all-start.2 = ((bf16[8,2,6,8,128]{4,3,2,1,0:T(8,128)(2,1)}), bf16[8,2,6,8,128]{4,3,2,1,0:T(8,128)(2,1)S(1)}, u32[]{:S(2)}, u32[]{:S(2)}) async-start(bf16[8,2,6,8,128]{4,3,2,1,0:T(8,128)(2,1)} %bottom_out.1), calls=%async_computation.2 | async-start | bytes 393216 | tf_op jit(solution)/shard_map/all_to_all | solution.py:663
  90.3 0.1 copy.21.skip_ref
  90.4 4.6 %decode_skip.1 = (f32[32,8,256]{2,1,0:T(8,128)}, bf16[3,512,256]{2,1,0:T(8,128)(2,1)S(1)}, bf16[3,512,256]{2,1,0:T(8,128)(2,1)S(1)}, bf16[3,512,256]{2,1,0:T(8,128)(2,1)S(1)}, bf16[3,512,256]{2,1,0:T(8,128)(2,1)S(1)}) custom-call(s32[5]{0:T(128)S(1)} %pad_add_fusion.place_ref, bf16[6,10,8,256]{3,2,1,0:T(8,128)(2,1)S(1)} %copy.21.skip_ref, ...), custom_call_target="tpu_custom_call" | custom-call | tf_op jit(solution)/shard_map/decode_skip/pallas_call | solution.py:518
  95.0 3.7 %all-to-all-done.2.bottom_ref = bf16[8,2,6,8,128]{4,3,2,1,0:T(8,128)(2,1)S(1)} async-done(((bf16[8,2,6,8,128]{4,3,2,1,0:T(8,128)(2,1)}), bf16[8,2,6,8,128]{4,3,2,1,0:T(8,128)(2,1)S(1)}, u32[]{:S(2)}, u32[]{:S(2)}) %all-to-all-start.2) | async-done | bytes 196640 | tf_op jit(solution)/shard_map/all_to_all | solution.py:663
  98.8 5.1 %decode.1 = bf16[4,8,8,256]{3,2,1,0:T(8,128)(2,1)} custom-call(s32[5]{0:T(128)S(1)} %pad_add_fusion.place_ref, bf16[8,2,6,8,128]{4,3,2,1,0:T(8,128)(2,1)S(1)} %all-to-all-done.2.bottom_ref, f32[32,8,256]{2,1,0:T(8,128)} %get-tuple-element.50.skip_hbm, bf16[3,512,256]{2,1,0:T(8,128)(2,1)S(1)} %get-tuple-element.51.refs_0_, ...), custom_call_target="tpu_custom_call" | custom-call | tf_op jit(solution)/shard_map/decode/pallas_call | solution.py:604
  (28 shorter events, 0.2 us)
Async XLA Ops:
  0.0 17.1 %copy-start = (bf16[8,16,16,128]{3,2,1,0:T(8,128)(2,1)S(1)}, bf16[8,16,16,128]{3,2,1,0:T(8,128)(2,1)}, u32[]{:S(2)}) copy-start(bf16[8,16,16,128]{3,2,1,0:T(8,128)(2,1)} %refs_0_.1) | copy-start | bytes 1572868
  1.1 12.2 %collective-permute-start = (bf16[3,16,16,128]{3,2,1,0:T(8,128)(2,1)S(1)}, bf16[3,16,16,128]{3,2,1,0:T(8,128)(2,1)S(1)}, u32[]{:S(2)}, u32[]{:S(2)}) collective-permute-start(bf16[3,16,16,128]{3,2,1,0:T(8,128)(2,1)S(1)} %get-tuple-element.59), channel_id=1, source_target_pairs={{0,16},{16,0},{32,48},{48,32},{64,80},{80,64},{96,112},{112,96},{1... | collective-permute-start | bytes 589832 | tf_op jit(solution)/shard_map/ppermute | solution.py:14
  4.3 12.8 %collective-permute-start.1 = (bf16[3,16,16,128]{3,2,1,0:T(8,128)(2,1)S(1)}, bf16[3,16,16,128]{3,2,1,0:T(8,128)(2,1)S(1)}, u32[]{:S(2)}, u32[]{:S(2)}) collective-permute-start(bf16[3,16,16,128]{3,2,1,0:T(8,128)(2,1)S(1)} %get-tuple-element.58), channel_id=1, source_target_pairs={{0,112},{16,32},{32,16},{48,64},{64,48},{80,96},{96,80},{112,0},{1... | collective-permute-start | bytes 589832 | tf_op jit(solution)/shard_map/ppermute | solution.py:14
  18.0 10.0 %collective-permute-start.2 = (bf16[14,3,16,128]{3,2,1,0:T(8,128)(2,1)S(1)}, bf16[14,3,16,128]{3,2,1,0:T(8,128)(2,1)S(1)}, u32[]{:S(2)}, u32[]{:S(2)}) collective-permute-start(bf16[14,3,16,128]{3,2,1,0:T(8,128)(2,1)S(1)} %get-tuple-element.38), channel_id=1, source_target_pairs={{0,2},{2,0},{4,6},{6,4},{8,10},{10,8},{12,14},{14,12},{1,3},{3,1},... | collective-permute-start | bytes 516104 | tf_op jit(solution)/shard_map/ppermute | solution.py:14
  18.1 9.9 %collective-permute-start.3 = (bf16[14,3,16,128]{3,2,1,0:T(8,128)(2,1)S(1)}, bf16[14,3,16,128]{3,2,1,0:T(8,128)(2,1)S(1)}, u32[]{:S(2)}, u32[]{:S(2)}) collective-permute-start(bf16[14,3,16,128]{3,2,1,0:T(8,128)(2,1)S(1)} %get-tuple-element.39), channel_id=1, source_target_pairs={{0,14},{2,4},{4,2},{6,8},{8,6},{10,12},{12,10},{14,0},{1,15},{3,5}... | collective-permute-start | bytes 516104 | tf_op jit(solution)/shard_map/ppermute | solution.py:14
  21.2 6.7 %collective-permute-start.4 = (bf16[14,16,128]{2,1,0:T(8,128)(2,1)S(1)}, bf16[14,16,128]{2,1,0:T(8,128)(2,1)S(1)}, u32[]{:S(2)}, u32[]{:S(2)}) collective-permute-start(bf16[14,16,128]{2,1,0:T(8,128)(2,1)S(1)} %get-tuple-element.36.refs_2_), channel_id=1, source_target_pairs={{0,1},{1,0},{2,3},{3,2},{4,5},{5,4},{6,7},{7,6},{8,9},{9,8},{10,11... | collective-permute-start | bytes 172040 | tf_op jit(solution)/shard_map/ppermute | solution.py:641
  22.7 3.9 %collective-permute-start.5 = (bf16[14,3,128]{2,1,0:T(4,128)(2,1)S(1)}, bf16[14,3,128]{2,1,0:T(4,128)(2,1)S(1)}, u32[]{:S(2)}, u32[]{:S(2)}) collective-permute-start(bf16[14,3,128]{2,1,0:T(4,128)(2,1)S(1)} %get-tuple-element.40), channel_id=1, source_target_pairs={{0,3},{1,2},{2,1},{3,0},{4,7},{5,6},{6,5},{7,4},{8,11},{9,10},{10,... | collective-permute-start | bytes 32264 | tf_op jit(solution)/shard_map/ppermute | solution.py:14
  22.7 5.3 %collective-permute-start.6 = (bf16[14,3,128]{2,1,0:T(4,128)(2,1)S(1)}, bf16[14,3,128]{2,1,0:T(4,128)(2,1)S(1)}, u32[]{:S(2)}, u32[]{:S(2)}) collective-permute-start(bf16[14,3,128]{2,1,0:T(4,128)(2,1)S(1)} %get-tuple-element.41), channel_id=1, source_target_pairs={{0,15},{1,14},{2,5},{3,4},{4,3},{5,2},{6,9},{7,8},{8,7},{9,6},{10,... | collective-permute-start | bytes 32264 | tf_op jit(solution)/shard_map/ppermute | solution.py:14
  26.6 11.3 %copy-start.1 = (bf16[3,3,3,128,256]{4,3,2,1,0:T(8,128)(2,1)S(1)}, bf16[3,3,3,128,256]{4,3,2,1,0:T(8,128)(2,1)}, u32[]{:S(2)}) copy-start(bf16[3,3,3,128,256]{4,3,2,1,0:T(8,128)(2,1)} %param.8) | copy-start | bytes 5308420
  34.0 3.9 %collective-permute-start.7 = (bf16[6,10,128]{2,1,0:T(8,128)(2,1)S(1)}, bf16[6,10,128]{2,1,0:T(8,128)(2,1)S(1)}, u32[]{:S(2)}, u32[]{:S(2)}) collective-permute-start(bf16[6,10,128]{2,1,0:T(8,128)(2,1)S(1)} %fusion.1), channel_id=1, source_target_pairs={{0,1},{1,0},{2,3},{3,2},{4,5},{5,4},{6,7},{7,6},{8,9},{9,8},{10,11... | collective-permute-start | bytes 46088 | tf_op jit(solution)/shard_map/ppermute | solution.py:634
  39.4 4.3 %collective-permute-start.8 = (bf16[2,4,1,256]{3,1,0,2:T(4,128)(2,1)S(1)}, bf16[2,4,1,256]{3,1,0,2:T(4,128)(2,1)S(1)}, u32[]{:S(2)}, u32[]{:S(2)}) collective-permute-start(bf16[2,4,1,256]{3,1,0,2:T(4,128)(2,1)S(1)} %get-tuple-element.74), channel_id=1, source_target_pairs={{0,14},{2,4},{4,2},{6,8},{8,6},{10,12},{12,10},{14,0},{1,15},{3,5}... | collective-permute-start | bytes 12296 | tf_op jit(solution)/shard_map/ppermute | solution.py:14
  39.5 4.2 %collective-permute-start.9 = (bf16[2,4,1,256]{3,1,0,2:T(4,128)(2,1)S(1)}, bf16[2,4,1,256]{3,1,0,2:T(4,128)(2,1)S(1)}, u32[]{:S(2)}, u32[]{:S(2)}) collective-permute-start(bf16[2,4,1,256]{3,1,0,2:T(4,128)(2,1)S(1)} %get-tuple-element.75), channel_id=1, source_target_pairs={{0,2},{2,0},{4,6},{6,4},{8,10},{10,8},{12,14},{14,12},{1,3},{3,1},... | collective-permute-start | bytes 12296 | tf_op jit(solution)/shard_map/ppermute | solution.py:14
  39.6 10.0 %collective-permute-start.10 = (bf16[1,8,8,256]{3,1,0,2:T(8,128)(2,1)S(1)}, bf16[1,8,8,256]{3,1,0,2:T(8,128)(2,1)S(1)}, u32[]{:S(2)}, u32[]{:S(2)}) collective-permute-start(bf16[1,8,8,256]{3,1,0,2:T(8,128)(2,1)S(1)} %get-tuple-element.62), channel_id=1, source_target_pairs={{0,112},{16,32},{32,16},{48,64},{64,48},{80,96},{96,80},{112,0},{1... | collective-permute-start | bytes 98312 | tf_op jit(solution)/shard_map/ppermute | solution.py:14
  41.4 8.2 %collective-permute-start.11 = (bf16[1,8,8,256]{3,1,0,2:T(8,128)(2,1)S(1)}, bf16[1,8,8,256]{3,1,0,2:T(8,128)(2,1)S(1)}, u32[]{:S(2)}, u32[]{:S(2)}) collective-permute-start(bf16[1,8,8,256]{3,1,0,2:T(8,128)(2,1)S(1)} %get-tuple-element.63), channel_id=1, source_target_pairs={{0,16},{16,0},{32,48},{48,32},{64,80},{80,64},{96,112},{112,96},{1... | collective-permute-start | bytes 98312 | tf_op jit(solution)/shard_map/ppermute | solution.py:14
  44.6 14.7 %all-to-all-start = ((bf16[16,2,24,256]{3,2,1,0:T(8,128)(2,1)}), bf16[16,2,24,256]{3,2,1,0:T(8,128)(2,1)S(1)}, u32[]{:S(2)}, u32[]{:S(2)}) async-start(bf16[16,2,24,256]{3,2,1,0:T(8,128)(2,1)} %broadcast_in_dim.16.refs_1_), calls=%async_computation | async-start | bytes 786432 | tf_op jit(solution)/shard_map/all_to_all | solution.py:653
  49.8 4.3 %collective-permute-start.13 = (bf16[6,1,8,256]{3,1,0,2:T(2,128)(2,1)S(1)}, bf16[6,1,8,256]{3,1,0,2:T(2,128)(2,1)S(1)}, u32[]{:S(2)}, u32[]{:S(2)}) collective-permute-start(bf16[6,1,8,256]{3,1,0,2:T(2,128)(2,1)S(1)} %broadcast_select_fusion.7), channel_id=1, source_target_pairs={{0,2},{2,0},{4,6},{6,4},{8,10},{10,8},{12,14},{14,12},{1,3},{3,1},... | collective-permute-start | bytes 73736 | tf_op jit(solution)/shard_map/ppermute | solution.py:14
  49.9 5.0 %collective-permute-start.12 = (bf16[6,1,8,256]{3,1,0,2:T(2,128)(2,1)S(1)}, bf16[6,1,8,256]{3,1,0,2:T(2,128)(2,1)S(1)}, u32[]{:S(2)}, u32[]{:S(2)}) collective-permute-start(bf16[6,1,8,256]{3,1,0,2:T(2,128)(2,1)S(1)} %get-tuple-element.55), channel_id=1, source_target_pairs={{0,14},{2,4},{4,2},{6,8},{8,6},{10,12},{12,10},{14,0},{1,15},{3,5}... | collective-permute-start | bytes 73736 | tf_op jit(solution)/shard_map/ppermute | solution.py:14
  62.2 13.0 %all-to-all-start.1 = ((bf16[8,8,6,4,128]{4,3,2,1,0:T(4,128)(2,1)}), bf16[8,8,6,4,128]{4,3,2,1,0:T(4,128)(2,1)S(1)}, u32[]{:S(2)}, u32[]{:S(2)}) async-start(bf16[8,8,6,4,128]{4,3,2,1,0:T(4,128)(2,1)} %bottom_in.1.refs_1_), calls=%async_computation.1 | async-start | bytes 786432 | tf_op jit(solution)/shard_map/all_to_all | solution.py:656
  65.9 5.0 %collective-permute-start.14 = (bf16[6,10,256]{2,1,0:T(8,128)(2,1)S(1)}, bf16[6,10,256]{2,1,0:T(8,128)(2,1)S(1)}, u32[]{:S(2)}, u32[]{:S(2)}) collective-permute-start(bf16[6,10,256]{2,1,0:T(8,128)(2,1)S(1)} %fusion), channel_id=1, source_target_pairs={{0,1},{1,0},{2,3},{3,2},{4,5},{5,4},{6,7},{7,6},{8,9},{9,8},{10,11... | collective-permute-start | bytes 92168 | tf_op jit(solution)/shard_map/ppermute | solution.py:634
  75.7 5.5 %collective-permute-start.15 = (bf16[8,8,6,2,128]{4,3,2,1,0:T(2,128)(2,1)S(1)}, bf16[8,8,6,2,128]{4,3,2,1,0:T(2,128)(2,1)S(1)}, u32[]{:S(2)}, u32[]{:S(2)}) collective-permute-start(bf16[8,8,6,2,128]{4,3,2,1,0:T(2,128)(2,1)S(1)} %get-tuple-element.61), channel_id=1, source_target_pairs={{0,2},{2,0},{4,6},{6,4},{8,10},{10,8},{12,14},{14,12},{1,3},{3,1},... | collective-permute-start | bytes 589832 | tf_op jit(solution)/shard_map/ppermute | solution.py:14
  75.8 7.1 %collective-permute-start.16 = (bf16[8,8,6,2,128]{4,3,2,1,0:T(2,128)(2,1)S(1)}, bf16[8,8,6,2,128]{4,3,2,1,0:T(2,128)(2,1)S(1)}, u32[]{:S(2)}, u32[]{:S(2)}) collective-permute-start(bf16[8,8,6,2,128]{4,3,2,1,0:T(2,128)(2,1)S(1)} %get-tuple-element.60), channel_id=1, source_target_pairs={{0,14},{2,4},{4,2},{6,8},{8,6},{10,12},{12,10},{14,0},{1,15},{3,5}... | collective-permute-start | bytes 589832 | tf_op jit(solution)/shard_map/ppermute | solution.py:14
  86.8 11.9 %all-to-all-start.2 = ((bf16[8,2,6,8,128]{4,3,2,1,0:T(8,128)(2,1)}), bf16[8,2,6,8,128]{4,3,2,1,0:T(8,128)(2,1)S(1)}, u32[]{:S(2)}, u32[]{:S(2)}) async-start(bf16[8,2,6,8,128]{4,3,2,1,0:T(8,128)(2,1)} %bottom_out.1), calls=%async_computation.2 | async-start | bytes 393216 | tf_op jit(solution)/shard_map/all_to_all | solution.py:663

commit v12 on v11

--- a/solution.py
+++ b/solution.py
@@ -178,7 +178,7 @@
             block = jnp.concatenate(blocks, axis=1)
             sums = []
             for tap in range(3):
-                kernel = weights_ref[:, :, tap].reshape(12 * channels, 2 * filters)
+                kernel = weights_ref[tap].reshape(12 * channels, 2 * filters)
                 sums.append(jnp.dot(block, kernel, preferred_element_type=jnp.float32))
             total = jnp.maximum(join_taps(first, sums, size_y, size_z), 0.0)
             total = jnp.maximum(total[..., :filters], total[..., filters:])
@@ -261,12 +261,13 @@
                     copies[-1].start()
             jobs.append(copies)
         first.wait()
-        zero = jnp.zeros((3, 3, channels, filters), jnp.bfloat16)
+        zero = jnp.zeros((3, channels, filters), jnp.bfloat16)
         results = []
-        for plane in range(4):
-            pair_ref[plane, :, :, :, :filters] = full_ref[plane] if plane < 3 else zero
-            pair_ref[plane, :, :, :, filters:] = full_ref[plane - 1] if plane > 0 else zero
-            results.append(pltpu.make_async_copy(pair_ref.at[plane], pair_hbm.at[plane], sems.at[55 + plane]))
+        for tap in range(3):
+            for plane in range(4):
+                pair_ref[tap, plane, :, :, :filters] = full_ref[plane, :, tap] if plane < 3 else zero
+                pair_ref[tap, plane, :, :, filters:] = full_ref[plane - 1, :, tap] if plane > 0 else zero
+            results.append(pltpu.make_async_copy(pair_ref.at[tap], pair_hbm.at[tap], sems.at[55 + tap]))
             results[-1].start()
         for order, (ref, to_ref, to_hbm) in enumerate(((in_ref, to_in_ref, to_in_hbm), (out_ref, to_out_ref, to_out_hbm))):
             for step in range(9):
@@ -279,7 +280,7 @@
         for copy in results:
             copy.wait()
 
-    shapes = [(4, 3, 3, channels, 2 * filters)] + [(9, depth, 256) for depth in depths]
+    shapes = [(3, 4, 3, channels, 2 * filters)] + [(9, depth, 256) for depth in depths]
     return pl.pallas_call(
         body,
         in_specs=[pl.BlockSpec(memory_space=pltpu.HBM)] * 3,

time: 105 us -> 105 us (level)
  no operation moved by 1% of the time
where the time goes in v12:
time: 105 us; the launch traced here: 104 us
  starting transfers between devices  35.8 us (34%)
  Pallas kernels  34.6 us (33%)
  waiting for transfers between devices  29.8 us (28%)
  other arithmetic  2.26 us (2%)
  local copies, waits for them, and re-layouts  1.05 us (1%)
    ppermute x7, starting transfers between devices, send(): lax.ppermute(outer_block, axis, outer)  17.5 us
    ppermute x7, waiting for transfers between devices, send(): lax.ppermute(outer_block, axis, outer)  9.91 us
    ppermute x2, waiting for transfers between devices, edge_of(): lax.ppermute(jnp.where(place_z == 0, plane_high, plane_low), 'gz', swap)  7.62 us
    pallas_call x1, Pallas kernels, encode(): pl.pallas_call(body, in_specs=[pl.BlockSpec(memory_space=pltpu.SMEM)] + [...  5.97 us
    pallas_call x1, Pallas kernels, decode(): pl.pallas_call(body, in_specs=[pl.BlockSpec(memory_space=pltpu.SMEM)] + [...  5.12 us
    pallas_call x3, Pallas kernels, bring(): pl.pallas_call(body, in_specs=[pl.BlockSpec(memory_space=pltpu.HBM)] * co...  5.03 us
    all_to_all x1, starting transfers between devices, local(): column = lax.all_to_all(column, ('gx', 'gz'), 0, 0)  5.01 us
    pallas_call x1, Pallas kernels, prepare(): pl.pallas_call(body, in_specs=[pl.BlockSpec(memory_space=pltpu.HBM)] * 3,...  4.84 us
  transfers between devices with their start and end apart: 20, of which 10 were waited for; matrix products, arithmetic and copies ran while one was open for 2% of the time, Pallas kernels for 14%

profile of v12, /device:TPU:0, one launch (start us, length us, event | category | flops | bytes accessed | tf_op | source)
XLA Modules:
  0.0 104.0 jit_solution(3067092999506202827)
XLA Ops:
  0.0 1.1 %broadcast_select_fusion.2 = (bf16[3,16,16,128]{3,2,1,0:T(8,128)(2,1)S(1)}, bf16[3,16,16,128]{3,2,1,0:T(8,128)(2,1)S(1)}) fusion(pred[]{:T(512)S(6)} %eq.25, bf16[8,16,16,128]{3,2,1,0:T(8,128)(2,1)} %refs_0_.1), kind=kLoop, calls=%fused_computation.3 | loop fusion | flops 196608 | bytes 786433 | tf_op jit(solution)/shard_map/jit(_where)/select_n | solution.py:19
  1.1 3.2 %collective-permute-start = (bf16[3,16,16,128]{3,2,1,0:T(8,128)(2,1)S(1)}, bf16[3,16,16,128]{3,2,1,0:T(8,128)(2,1)S(1)}, u32[]{:S(2)}, u32[]{:S(2)}) collective-permute-start(bf16[3,16,16,128]{3,2,1,0:T(8,128)(2,1)S(1)} %get-tuple-element.59), channel_id=1, source_target_pairs={{0,16},{16,0},{32,48},{48,32},{64,80},{80,64},{96,112},{112,96},{1... | collective-permute-start | bytes 589832 | tf_op jit(solution)/shard_map/ppermute | solution.py:14
  4.3 4.0 %collective-permute-start.1 = (bf16[3,16,16,128]{3,2,1,0:T(8,128)(2,1)S(1)}, bf16[3,16,16,128]{3,2,1,0:T(8,128)(2,1)S(1)}, u32[]{:S(2)}, u32[]{:S(2)}) collective-permute-start(bf16[3,16,16,128]{3,2,1,0:T(8,128)(2,1)S(1)} %get-tuple-element.58), channel_id=1, source_target_pairs={{0,112},{16,32},{32,16},{48,64},{64,48},{80,96},{96,80},{112,0},{1... | collective-permute-start | bytes 589832 | tf_op jit(solution)/shard_map/ppermute | solution.py:14
  8.3 4.8 %prepare.1 = (bf16[3,4,3,128,256]{4,3,2,1,0:T(8,128)(2,1)}, bf16[9,256,256]{2,1,0:T(8,128)(2,1)}, bf16[9,512,256]{2,1,0:T(8,128)(2,1)}) custom-call(bf16[3,3,3,128,128]{4,3,2,1,0:T(8,128)(2,1)} %full_hbm.1, bf16[3,3,3,64,256]{4,3,2,1,0:T(8,128)(2,1)} %bitcast.20, bf16[3,3,3,64,512]{4,3,2,1,0:T(8,128)(2,1)} %bitcast.19), custom_call_target="tpu_custom_call" | custom-call | tf_op jit(solution)/shard_map/prepare/pallas_call | solution.py:284
  13.1 0.1 pad_add_fusion.place_ref
  13.2 3.9 %collective-permute-done.1.x_out_ref = bf16[3,16,16,128]{3,2,1,0:T(8,128)(2,1)S(1)} collective-permute-done((bf16[3,16,16,128]{3,2,1,0:T(8,128)(2,1)S(1)}, bf16[3,16,16,128]{3,2,1,0:T(8,128)(2,1)S(1)}, u32[]{:S(2)}, u32[]{:S(2)}) %collective-permute-start.1) | collective-permute-done | bytes 196640 | tf_op jit(solution)/shard_map/ppermute | solution.py:14
  17.1 0.9 pack_y.1
  18.0 0.1 collective-permute-start.2
  18.1 3.1 %collective-permute-start.3 = (bf16[14,3,16,128]{3,2,1,0:T(8,128)(2,1)S(1)}, bf16[14,3,16,128]{3,2,1,0:T(8,128)(2,1)S(1)}, u32[]{:S(2)}, u32[]{:S(2)}) collective-permute-start(bf16[14,3,16,128]{3,2,1,0:T(8,128)(2,1)S(1)} %get-tuple-element.39), channel_id=1, source_target_pairs={{0,14},{2,4},{4,2},{6,8},{8,6},{10,12},{12,10},{14,0},{1,15},{3,5}... | collective-permute-start | bytes 516104 | tf_op jit(solution)/shard_map/ppermute | solution.py:14
  21.2 1.5 %collective-permute-start.4 = (bf16[14,16,128]{2,1,0:T(8,128)(2,1)S(1)}, bf16[14,16,128]{2,1,0:T(8,128)(2,1)S(1)}, u32[]{:S(2)}, u32[]{:S(2)}) collective-permute-start(bf16[14,16,128]{2,1,0:T(8,128)(2,1)S(1)} %get-tuple-element.36.refs_2_), channel_id=1, source_target_pairs={{0,1},{1,0},{2,3},{3,2},{4,5},{5,4},{6,7},{7,6},{8,9},{9,8},{10,11... | collective-permute-start | bytes 172040 | tf_op jit(solution)/shard_map/ppermute | solution.py:642
  22.7 1.9 %collective-permute-start.6 = (bf16[14,3,128]{2,1,0:T(4,128)(2,1)S(1)}, bf16[14,3,128]{2,1,0:T(4,128)(2,1)S(1)}, u32[]{:S(2)}, u32[]{:S(2)}) collective-permute-start(bf16[14,3,128]{2,1,0:T(4,128)(2,1)S(1)} %get-tuple-element.41), channel_id=1, source_target_pairs={{0,15},{1,14},{2,5},{3,4},{4,3},{5,2},{6,9},{7,8},{8,7},{9,6},{10,... | collective-permute-start | bytes 32264 | tf_op jit(solution)/shard_map/ppermute | solution.py:14
  24.6 2.0 %bring.3 = (bf16[8,16,16,128]{3,2,1,0:T(8,128)(2,1)S(1)}, bf16[3,4,3,128,256]{4,3,2,1,0:T(8,128)(2,1)S(1)}) custom-call(bf16[8,16,16,128]{3,2,1,0:T(8,128)(2,1)} %refs_0_.1, bf16[3,4,3,128,256]{4,3,2,1,0:T(8,128)(2,1)} %get-tuple-element.33.refs_1_, bf16[14,16,128]{2,1,0:T(8,128)(2,1)S(1)} %get-tuple-element.36.refs_2_), custom_call_target="tpu_custom_call" | custom-call | tf_op jit(solution)/shard_map/bring/pallas_call | solution.py:229
  26.6 1.3 %collective-permute-done.6.edge_out_ref = bf16[14,3,128]{2,1,0:T(4,128)(2,1)S(1)} collective-permute-done((bf16[14,3,128]{2,1,0:T(4,128)(2,1)S(1)}, bf16[14,3,128]{2,1,0:T(4,128)(2,1)S(1)}, u32[]{:S(2)}, u32[]{:S(2)}) %collective-permute-start.6) | collective-permute-done | bytes 10784 | tf_op jit(solution)/shard_map/ppermute | solution.py:14
  28.0 6.0 %encode.1.field_ref = bf16[6,10,8,128]{3,2,1,0:T(8,128)(2,1)S(1)} custom-call(s32[5]{0:T(128)S(1)} %pad_add_fusion.place_ref, bf16[8,16,16,128]{3,2,1,0:T(8,128)(2,1)S(1)} %get-tuple-element.37.own_ref, bf16[3,16,16,128]{3,2,1,0:T(8,128)(2,1)S(1)} %collective-permute-done.x_in_ref, bf16[3,16,16,128]{3,2,1,0:T(8,128)(2,1)S(1)} %collective-permute-done.1.x_out_ref, ...), custom_call_target="tpu_custom_call" | custom-call | tf_op jit(solution)/shard_map/encode/pallas_call | solution.py:197
  34.0 0.6 collective-permute-start.7
  34.7 3.3 %collective-permute-done.7.edge_ref = bf16[6,10,128]{2,1,0:T(8,128)(2,1)S(1)} collective-permute-done((bf16[6,10,128]{2,1,0:T(8,128)(2,1)S(1)}, bf16[6,10,128]{2,1,0:T(8,128)(2,1)S(1)}, u32[]{:S(2)}, u32[]{:S(2)}) %collective-permute-start.7) | collective-permute-done | bytes 15392 | tf_op jit(solution)/shard_map/ppermute | solution.py:635
  37.9 1.4 %half_level.1 = (bf16[4,8,8,256]{3,2,1,0:T(8,128)(2,1)S(1)}, bf16[2,16,256]{2,1,0:T(8,128)(2,1)S(1)}) custom-call(s32[5]{0:T(128)S(1)} %pad_add_fusion.place_ref, bf16[6,10,8,128]{3,2,1,0:T(8,128)(2,1)S(1)} %encode.1.field_ref, bf16[6,10,128]{2,1,0:T(8,128)(2,1)S(1)} %collective-permute-done.7.edge_ref, bf16[9,3,128,256]{3,2,1,0:T(8,128)(2,1)S(1)} %bitcast.16), custom_call_target="tpu_custom_call" | custom-call | tf_op jit(solution)/shard_map/half_level/pallas_call | solution.py:77
  39.4 0.1 collective-permute-start.8
  39.5 0.1 collective-permute-start.9
  39.6 1.8 %collective-permute-start.10 = (bf16[1,8,8,256]{3,1,0,2:T(8,128)(2,1)S(1)}, bf16[1,8,8,256]{3,1,0,2:T(8,128)(2,1)S(1)}, u32[]{:S(2)}, u32[]{:S(2)}) collective-permute-start(bf16[1,8,8,256]{3,1,0,2:T(8,128)(2,1)S(1)} %get-tuple-element.62), channel_id=1, source_target_pairs={{0,112},{16,32},{32,16},{48,64},{64,48},{80,96},{96,80},{112,0},{1... | collective-permute-start | bytes 98312 | tf_op jit(solution)/shard_map/ppermute | solution.py:14
  41.4 2.3 %collective-permute-done.8 = bf16[2,4,1,256]{3,1,0,2:T(4,128)(2,1)S(1)} collective-permute-done((bf16[2,4,1,256]{3,1,0,2:T(4,128)(2,1)S(1)}, bf16[2,4,1,256]{3,1,0,2:T(4,128)(2,1)S(1)}, u32[]{:S(2)}, u32[]{:S(2)}) %collective-permute-start.8) | collective-permute-done | bytes 4128 | tf_op jit(solution)/shard_map/ppermute | solution.py:14
  43.8 0.8 broadcast_in_dim.16.refs_1_
  44.6 5.0 %all-to-all-start = ((bf16[16,2,24,256]{3,2,1,0:T(8,128)(2,1)}), bf16[16,2,24,256]{3,2,1,0:T(8,128)(2,1)S(1)}, u32[]{:S(2)}, u32[]{:S(2)}) async-start(bf16[16,2,24,256]{3,2,1,0:T(8,128)(2,1)} %broadcast_in_dim.16.refs_1_), calls=%async_computation | async-start | bytes 786432 | tf_op jit(solution)/shard_map/all_to_all | solution.py:654
  49.6 0.1 broadcast_select_fusion.8
  49.7 0.1 broadcast_select_fusion.7
  49.8 0.1 collective-permute-start.13
  49.9 2.8 %collective-permute-start.12 = (bf16[6,1,8,256]{3,1,0,2:T(2,128)(2,1)S(1)}, bf16[6,1,8,256]{3,1,0,2:T(2,128)(2,1)S(1)}, u32[]{:S(2)}, u32[]{:S(2)}) collective-permute-start(bf16[6,1,8,256]{3,1,0,2:T(2,128)(2,1)S(1)} %get-tuple-element.55), channel_id=1, source_target_pairs={{0,14},{2,4},{4,2},{6,8},{8,6},{10,12},{12,10},{14,0},{1,15},{3,5}... | collective-permute-start | bytes 73736 | tf_op jit(solution)/shard_map/ppermute | solution.py:14
  52.8 1.4 %bring.4.weights_ref = bf16[9,256,256]{2,1,0:T(8,128)(2,1)S(1)} custom-call(bf16[9,256,256]{2,1,0:T(8,128)(2,1)} %get-tuple-element.44.refs_0_, bf16[16,2,24,256]{3,2,1,0:T(8,128)(2,1)} %broadcast_in_dim.16.refs_1_), custom_call_target="tpu_custom_call" | custom-call | tf_op jit(solution)/shard_map/bring/pallas_call | solution.py:229
  54.2 0.7 collective-permute-done.12
  54.9 0.1 broadcast_select_fusion.9
  55.0 4.3 %all-to-all-done.field_ref = bf16[16,2,24,256]{3,2,1,0:T(8,128)(2,1)S(1)} async-done(((bf16[16,2,24,256]{3,2,1,0:T(8,128)(2,1)}), bf16[16,2,24,256]{3,2,1,0:T(8,128)(2,1)S(1)}, u32[]{:S(2)}, u32[]{:S(2)}) %all-to-all-start) | async-done | bytes 393248 | tf_op jit(solution)/shard_map/all_to_all | solution.py:654
  59.3 2.9 %bottom_in.1.refs_1_ = bf16[8,8,6,4,128]{4,3,2,1,0:T(4,128)(2,1)} custom-call(s32[5]{0:T(128)S(1)} %pad_add_fusion.place_ref, bf16[16,2,24,256]{3,2,1,0:T(8,128)(2,1)S(1)} %all-to-all-done.field_ref, bf16[9,256,256]{2,1,0:T(8,128)(2,1)S(1)} %bring.4.weights_ref), custom_call_target="tpu_custom_call" | custom-call | tf_op jit(solution)/shard_map/bottom_in/pallas_call | solution.py:406
  62.2 3.5 %all-to-all-start.1 = ((bf16[8,8,6,4,128]{4,3,2,1,0:T(4,128)(2,1)}), bf16[8,8,6,4,128]{4,3,2,1,0:T(4,128)(2,1)S(1)}, u32[]{:S(2)}, u32[]{:S(2)}) async-start(bf16[8,8,6,4,128]{4,3,2,1,0:T(4,128)(2,1)} %bottom_in.1.refs_1_), calls=%async_computation.1 | async-start | bytes 786432 | tf_op jit(solution)/shard_map/all_to_all | solution.py:657
  65.6 0.2 pad_maximum_fusion
  65.9 0.7 collective-permute-start.14
  66.6 4.4 %collective-permute-done.14.edge_ref = bf16[6,10,256]{2,1,0:T(8,128)(2,1)S(1)} collective-permute-done((bf16[6,10,256]{2,1,0:T(8,128)(2,1)S(1)}, bf16[6,10,256]{2,1,0:T(8,128)(2,1)S(1)}, u32[]{:S(2)}, u32[]{:S(2)}) %collective-permute-start.14) | collective-permute-done | bytes 30752 | tf_op jit(solution)/shard_map/ppermute | solution.py:635
  70.9 4.3 %all-to-all-done.1.field_ref = bf16[8,8,6,4,128]{4,3,2,1,0:T(4,128)(2,1)S(1)} async-done(((bf16[8,8,6,4,128]{4,3,2,1,0:T(4,128)(2,1)}), bf16[8,8,6,4,128]{4,3,2,1,0:T(4,128)(2,1)S(1)}, u32[]{:S(2)}, u32[]{:S(2)}) %all-to-all-start.1) | async-done | bytes 393248 | tf_op jit(solution)/shard_map/all_to_all | solution.py:657
  75.2 0.5 broadcast_select_fusion
  75.7 0.1 collective-permute-start.15
  75.8 3.8 %collective-permute-start.16 = (bf16[8,8,6,2,128]{4,3,2,1,0:T(2,128)(2,1)S(1)}, bf16[8,8,6,2,128]{4,3,2,1,0:T(2,128)(2,1)S(1)}, u32[]{:S(2)}, u32[]{:S(2)}) collective-permute-start(bf16[8,8,6,2,128]{4,3,2,1,0:T(2,128)(2,1)S(1)} %get-tuple-element.60), channel_id=1, source_target_pairs={{0,14},{2,4},{4,2},{6,8},{8,6},{10,12},{12,10},{14,0},{1,15},{3,5}... | collective-permute-start | bytes 589832 | tf_op jit(solution)/shard_map/ppermute | solution.py:14
  79.5 1.7 %bring.5.weights_ref = bf16[9,512,256]{2,1,0:T(8,128)(2,1)S(1)} custom-call(bf16[9,512,256]{2,1,0:T(8,128)(2,1)} %get-tuple-element.47.refs_0_, bf16[8,8,6,4,128]{4,3,2,1,0:T(4,128)(2,1)} %bottom_in.1.refs_1_), custom_call_target="tpu_custom_call" | custom-call | tf_op jit(solution)/shard_map/bring/pallas_call | solution.py:229
  81.2 1.7 %collective-permute-done.16.y_out_ref = bf16[8,8,6,2,128]{4,3,2,1,0:T(2,128)(2,1)S(1)} collective-permute-done((bf16[8,8,6,2,128]{4,3,2,1,0:T(2,128)(2,1)S(1)}, bf16[8,8,6,2,128]{4,3,2,1,0:T(2,128)(2,1)S(1)}, u32[]{:S(2)}, u32[]{:S(2)}) %collective-permute-start.16) | collective-permute-done | bytes 196640 | tf_op jit(solution)/shard_map/ppermute | solution.py:14
  82.9 4.0 %bottom_out.1 = bf16[8,2,6,8,128]{4,3,2,1,0:T(8,128)(2,1)} custom-call(s32[5]{0:T(128)S(1)} %pad_add_fusion.place_ref, bf16[8,8,6,4,128]{4,3,2,1,0:T(4,128)(2,1)S(1)} %all-to-all-done.1.field_ref, bf16[8,8,6,2,128]{4,3,2,1,0:T(2,128)(2,1)S(1)} %collective-permute-done.15.y_in_ref, bf16[8,8,6,2,128]{4,3,2,1,0:T(2,128)(2,1)S(1)} %collective-permute-done.16.y_out_ref, ...), custom_call_target="tpu_custom_call" | custom-call | tf_op jit(solution)/shard_map/bottom_out/pallas_call | solution.py:464
  86.8 3.4 %all-to-all-start.2 = ((bf16[8,2,6,8,128]{4,3,2,1,0:T(8,128)(2,1)}), bf16[8,2,6,8,128]{4,3,2,1,0:T(8,128)(2,1)S(1)}, u32[]{:S(2)}, u32[]{:S(2)}) async-start(bf16[8,2,6,8,128]{4,3,2,1,0:T(8,128)(2,1)} %bottom_out.1), calls=%async_computation.2 | async-start | bytes 393216 | tf_op jit(solution)/shard_map/all_to_all | solution.py:664
  90.3 0.1 copy.21.skip_ref
  90.4 4.6 %decode_skip.1 = (f32[32,8,256]{2,1,0:T(8,128)}, bf16[3,512,256]{2,1,0:T(8,128)(2,1)S(1)}, bf16[3,512,256]{2,1,0:T(8,128)(2,1)S(1)}, bf16[3,512,256]{2,1,0:T(8,128)(2,1)S(1)}, bf16[3,512,256]{2,1,0:T(8,128)(2,1)S(1)}) custom-call(s32[5]{0:T(128)S(1)} %pad_add_fusion.place_ref, bf16[6,10,8,256]{3,2,1,0:T(8,128)(2,1)S(1)} %copy.21.skip_ref, ...), custom_call_target="tpu_custom_call" | custom-call | tf_op jit(solution)/shard_map/decode_skip/pallas_call | solution.py:519
  95.0 3.7 %all-to-all-done.2.bottom_ref = bf16[8,2,6,8,128]{4,3,2,1,0:T(8,128)(2,1)S(1)} async-done(((bf16[8,2,6,8,128]{4,3,2,1,0:T(8,128)(2,1)}), bf16[8,2,6,8,128]{4,3,2,1,0:T(8,128)(2,1)S(1)}, u32[]{:S(2)}, u32[]{:S(2)}) %all-to-all-start.2) | async-done | bytes 196640 | tf_op jit(solution)/shard_map/all_to_all | solution.py:664
  98.8 5.1 %decode.1 = bf16[4,8,8,256]{3,2,1,0:T(8,128)(2,1)} custom-call(s32[5]{0:T(128)S(1)} %pad_add_fusion.place_ref, bf16[8,2,6,8,128]{4,3,2,1,0:T(8,128)(2,1)S(1)} %all-to-all-done.2.bottom_ref, f32[32,8,256]{2,1,0:T(8,128)} %get-tuple-element.50.skip_hbm, bf16[3,512,256]{2,1,0:T(8,128)(2,1)S(1)} %get-tuple-element.51.refs_0_, ...), custom_call_target="tpu_custom_call" | custom-call | tf_op jit(solution)/shard_map/decode/pallas_call | solution.py:605
  (28 shorter events, 0.2 us)
Async XLA Ops:
  0.0 17.1 %copy-start = (bf16[8,16,16,128]{3,2,1,0:T(8,128)(2,1)S(1)}, bf16[8,16,16,128]{3,2,1,0:T(8,128)(2,1)}, u32[]{:S(2)}) copy-start(bf16[8,16,16,128]{3,2,1,0:T(8,128)(2,1)} %refs_0_.1) | copy-start | bytes 1572868
  1.1 12.1 %collective-permute-start = (bf16[3,16,16,128]{3,2,1,0:T(8,128)(2,1)S(1)}, bf16[3,16,16,128]{3,2,1,0:T(8,128)(2,1)S(1)}, u32[]{:S(2)}, u32[]{:S(2)}) collective-permute-start(bf16[3,16,16,128]{3,2,1,0:T(8,128)(2,1)S(1)} %get-tuple-element.59), channel_id=1, source_target_pairs={{0,16},{16,0},{32,48},{48,32},{64,80},{80,64},{96,112},{112,96},{1... | collective-permute-start | bytes 589832 | tf_op jit(solution)/shard_map/ppermute | solution.py:14
  4.3 12.8 %collective-permute-start.1 = (bf16[3,16,16,128]{3,2,1,0:T(8,128)(2,1)S(1)}, bf16[3,16,16,128]{3,2,1,0:T(8,128)(2,1)S(1)}, u32[]{:S(2)}, u32[]{:S(2)}) collective-permute-start(bf16[3,16,16,128]{3,2,1,0:T(8,128)(2,1)S(1)} %get-tuple-element.58), channel_id=1, source_target_pairs={{0,112},{16,32},{32,16},{48,64},{64,48},{80,96},{96,80},{112,0},{1... | collective-permute-start | bytes 589832 | tf_op jit(solution)/shard_map/ppermute | solution.py:14
  18.0 10.0 %collective-permute-start.2 = (bf16[14,3,16,128]{3,2,1,0:T(8,128)(2,1)S(1)}, bf16[14,3,16,128]{3,2,1,0:T(8,128)(2,1)S(1)}, u32[]{:S(2)}, u32[]{:S(2)}) collective-permute-start(bf16[14,3,16,128]{3,2,1,0:T(8,128)(2,1)S(1)} %get-tuple-element.38), channel_id=1, source_target_pairs={{0,2},{2,0},{4,6},{6,4},{8,10},{10,8},{12,14},{14,12},{1,3},{3,1},... | collective-permute-start | bytes 516104 | tf_op jit(solution)/shard_map/ppermute | solution.py:14
  18.1 9.9 %collective-permute-start.3 = (bf16[14,3,16,128]{3,2,1,0:T(8,128)(2,1)S(1)}, bf16[14,3,16,128]{3,2,1,0:T(8,128)(2,1)S(1)}, u32[]{:S(2)}, u32[]{:S(2)}) collective-permute-start(bf16[14,3,16,128]{3,2,1,0:T(8,128)(2,1)S(1)} %get-tuple-element.39), channel_id=1, source_target_pairs={{0,14},{2,4},{4,2},{6,8},{8,6},{10,12},{12,10},{14,0},{1,15},{3,5}... | collective-permute-start | bytes 516104 | tf_op jit(solution)/shard_map/ppermute | solution.py:14
  21.2 6.7 %collective-permute-start.4 = (bf16[14,16,128]{2,1,0:T(8,128)(2,1)S(1)}, bf16[14,16,128]{2,1,0:T(8,128)(2,1)S(1)}, u32[]{:S(2)}, u32[]{:S(2)}) collective-permute-start(bf16[14,16,128]{2,1,0:T(8,128)(2,1)S(1)} %get-tuple-element.36.refs_2_), channel_id=1, source_target_pairs={{0,1},{1,0},{2,3},{3,2},{4,5},{5,4},{6,7},{7,6},{8,9},{9,8},{10,11... | collective-permute-start | bytes 172040 | tf_op jit(solution)/shard_map/ppermute | solution.py:642
  22.7 3.9 %collective-permute-start.5 = (bf16[14,3,128]{2,1,0:T(4,128)(2,1)S(1)}, bf16[14,3,128]{2,1,0:T(4,128)(2,1)S(1)}, u32[]{:S(2)}, u32[]{:S(2)}) collective-permute-start(bf16[14,3,128]{2,1,0:T(4,128)(2,1)S(1)} %get-tuple-element.40), channel_id=1, source_target_pairs={{0,3},{1,2},{2,1},{3,0},{4,7},{5,6},{6,5},{7,4},{8,11},{9,10},{10,... | collective-permute-start | bytes 32264 | tf_op jit(solution)/shard_map/ppermute | solution.py:14
  22.7 5.3 %collective-permute-start.6 = (bf16[14,3,128]{2,1,0:T(4,128)(2,1)S(1)}, bf16[14,3,128]{2,1,0:T(4,128)(2,1)S(1)}, u32[]{:S(2)}, u32[]{:S(2)}) collective-permute-start(bf16[14,3,128]{2,1,0:T(4,128)(2,1)S(1)} %get-tuple-element.41), channel_id=1, source_target_pairs={{0,15},{1,14},{2,5},{3,4},{4,3},{5,2},{6,9},{7,8},{8,7},{9,6},{10,... | collective-permute-start | bytes 32264 | tf_op jit(solution)/shard_map/ppermute | solution.py:14
  26.6 11.3 %copy-start.1 = (bf16[3,3,3,128,256]{4,3,2,1,0:T(8,128)(2,1)S(1)}, bf16[3,3,3,128,256]{4,3,2,1,0:T(8,128)(2,1)}, u32[]{:S(2)}) copy-start(bf16[3,3,3,128,256]{4,3,2,1,0:T(8,128)(2,1)} %param.8) | copy-start | bytes 5308420
  34.0 3.9 %collective-permute-start.7 = (bf16[6,10,128]{2,1,0:T(8,128)(2,1)S(1)}, bf16[6,10,128]{2,1,0:T(8,128)(2,1)S(1)}, u32[]{:S(2)}, u32[]{:S(2)}) collective-permute-start(bf16[6,10,128]{2,1,0:T(8,128)(2,1)S(1)} %fusion.1), channel_id=1, source_target_pairs={{0,1},{1,0},{2,3},{3,2},{4,5},{5,4},{6,7},{7,6},{8,9},{9,8},{10,11... | collective-permute-start | bytes 46088 | tf_op jit(solution)/shard_map/ppermute | solution.py:635
  39.4 4.3 %collective-permute-start.8 = (bf16[2,4,1,256]{3,1,0,2:T(4,128)(2,1)S(1)}, bf16[2,4,1,256]{3,1,0,2:T(4,128)(2,1)S(1)}, u32[]{:S(2)}, u32[]{:S(2)}) collective-permute-start(bf16[2,4,1,256]{3,1,0,2:T(4,128)(2,1)S(1)} %get-tuple-element.74), channel_id=1, source_target_pairs={{0,14},{2,4},{4,2},{6,8},{8,6},{10,12},{12,10},{14,0},{1,15},{3,5}... | collective-permute-start | bytes 12296 | tf_op jit(solution)/shard_map/ppermute | solution.py:14
  39.5 4.2 %collective-permute-start.9 = (bf16[2,4,1,256]{3,1,0,2:T(4,128)(2,1)S(1)}, bf16[2,4,1,256]{3,1,0,2:T(4,128)(2,1)S(1)}, u32[]{:S(2)}, u32[]{:S(2)}) collective-permute-start(bf16[2,4,1,256]{3,1,0,2:T(4,128)(2,1)S(1)} %get-tuple-element.75), channel_id=1, source_target_pairs={{0,2},{2,0},{4,6},{6,4},{8,10},{10,8},{12,14},{14,12},{1,3},{3,1},... | collective-permute-start | bytes 12296 | tf_op jit(solution)/shard_map/ppermute | solution.py:14
  39.6 10.0 %collective-permute-start.10 = (bf16[1,8,8,256]{3,1,0,2:T(8,128)(2,1)S(1)}, bf16[1,8,8,256]{3,1,0,2:T(8,128)(2,1)S(1)}, u32[]{:S(2)}, u32[]{:S(2)}) collective-permute-start(bf16[1,8,8,256]{3,1,0,2:T(8,128)(2,1)S(1)} %get-tuple-element.62), channel_id=1, source_target_pairs={{0,112},{16,32},{32,16},{48,64},{64,48},{80,96},{96,80},{112,0},{1... | collective-permute-start | bytes 98312 | tf_op jit(solution)/shard_map/ppermute | solution.py:14
  41.4 8.2 %collective-permute-start.11 = (bf16[1,8,8,256]{3,1,0,2:T(8,128)(2,1)S(1)}, bf16[1,8,8,256]{3,1,0,2:T(8,128)(2,1)S(1)}, u32[]{:S(2)}, u32[]{:S(2)}) collective-permute-start(bf16[1,8,8,256]{3,1,0,2:T(8,128)(2,1)S(1)} %get-tuple-element.63), channel_id=1, source_target_pairs={{0,16},{16,0},{32,48},{48,32},{64,80},{80,64},{96,112},{112,96},{1... | collective-permute-start | bytes 98312 | tf_op jit(solution)/shard_map/ppermute | solution.py:14
  44.6 14.7 %all-to-all-start = ((bf16[16,2,24,256]{3,2,1,0:T(8,128)(2,1)}), bf16[16,2,24,256]{3,2,1,0:T(8,128)(2,1)S(1)}, u32[]{:S(2)}, u32[]{:S(2)}) async-start(bf16[16,2,24,256]{3,2,1,0:T(8,128)(2,1)} %broadcast_in_dim.16.refs_1_), calls=%async_computation | async-start | bytes 786432 | tf_op jit(solution)/shard_map/all_to_all | solution.py:654
  49.8 4.3 %collective-permute-start.13 = (bf16[6,1,8,256]{3,1,0,2:T(2,128)(2,1)S(1)}, bf16[6,1,8,256]{3,1,0,2:T(2,128)(2,1)S(1)}, u32[]{:S(2)}, u32[]{:S(2)}) collective-permute-start(bf16[6,1,8,256]{3,1,0,2:T(2,128)(2,1)S(1)} %broadcast_select_fusion.7), channel_id=1, source_target_pairs={{0,2},{2,0},{4,6},{6,4},{8,10},{10,8},{12,14},{14,12},{1,3},{3,1},... | collective-permute-start | bytes 73736 | tf_op jit(solution)/shard_map/ppermute | solution.py:14
  49.9 5.0 %collective-permute-start.12 = (bf16[6,1,8,256]{3,1,0,2:T(2,128)(2,1)S(1)}, bf16[6,1,8,256]{3,1,0,2:T(2,128)(2,1)S(1)}, u32[]{:S(2)}, u32[]{:S(2)}) collective-permute-start(bf16[6,1,8,256]{3,1,0,2:T(2,128)(2,1)S(1)} %get-tuple-element.55), channel_id=1, source_target_pairs={{0,14},{2,4},{4,2},{6,8},{8,6},{10,12},{12,10},{14,0},{1,15},{3,5}... | collective-permute-start | bytes 73736 | tf_op jit(solution)/shard_map/ppermute | solution.py:14
  62.2 13.0 %all-to-all-start.1 = ((bf16[8,8,6,4,128]{4,3,2,1,0:T(4,128)(2,1)}), bf16[8,8,6,4,128]{4,3,2,1,0:T(4,128)(2,1)S(1)}, u32[]{:S(2)}, u32[]{:S(2)}) async-start(bf16[8,8,6,4,128]{4,3,2,1,0:T(4,128)(2,1)} %bottom_in.1.refs_1_), calls=%async_computation.1 | async-start | bytes 786432 | tf_op jit(solution)/shard_map/all_to_all | solution.py:657
  65.9 5.0 %collective-permute-start.14 = (bf16[6,10,256]{2,1,0:T(8,128)(2,1)S(1)}, bf16[6,10,256]{2,1,0:T(8,128)(2,1)S(1)}, u32[]{:S(2)}, u32[]{:S(2)}) collective-permute-start(bf16[6,10,256]{2,1,0:T(8,128)(2,1)S(1)} %fusion), channel_id=1, source_target_pairs={{0,1},{1,0},{2,3},{3,2},{4,5},{5,4},{6,7},{7,6},{8,9},{9,8},{10,11... | collective-permute-start | bytes 92168 | tf_op jit(solution)/shard_map/ppermute | solution.py:635
  75.7 5.5 %collective-permute-start.15 = (bf16[8,8,6,2,128]{4,3,2,1,0:T(2,128)(2,1)S(1)}, bf16[8,8,6,2,128]{4,3,2,1,0:T(2,128)(2,1)S(1)}, u32[]{:S(2)}, u32[]{:S(2)}) collective-permute-start(bf16[8,8,6,2,128]{4,3,2,1,0:T(2,128)(2,1)S(1)} %get-tuple-element.61), channel_id=1, source_target_pairs={{0,2},{2,0},{4,6},{6,4},{8,10},{10,8},{12,14},{14,12},{1,3},{3,1},... | collective-permute-start | bytes 589832 | tf_op jit(solution)/shard_map/ppermute | solution.py:14
  75.8 7.1 %collective-permute-start.16 = (bf16[8,8,6,2,128]{4,3,2,1,0:T(2,128)(2,1)S(1)}, bf16[8,8,6,2,128]{4,3,2,1,0:T(2,128)(2,1)S(1)}, u32[]{:S(2)}, u32[]{:S(2)}) collective-permute-start(bf16[8,8,6,2,128]{4,3,2,1,0:T(2,128)(2,1)S(1)} %get-tuple-element.60), channel_id=1, source_target_pairs={{0,14},{2,4},{4,2},{6,8},{8,6},{10,12},{12,10},{14,0},{1,15},{3,5}... | collective-permute-start | bytes 589832 | tf_op jit(solution)/shard_map/ppermute | solution.py:14
  86.8 11.9 %all-to-all-start.2 = ((bf16[8,2,6,8,128]{4,3,2,1,0:T(8,128)(2,1)}), bf16[8,2,6,8,128]{4,3,2,1,0:T(8,128)(2,1)S(1)}, u32[]{:S(2)}, u32[]{:S(2)}) async-start(bf16[8,2,6,8,128]{4,3,2,1,0:T(8,128)(2,1)} %bottom_out.1), calls=%async_computation.2 | async-start | bytes 393216 | tf_op jit(solution)/shard_map/all_to_all | solution.py:664

commit v13 on v12

--- a/solution.py
+++ b/solution.py
@@ -64,7 +64,7 @@
         total = jnp.max(total.reshape(size_x // 2, 2, size_y // 2, 2, size_z, filters), axis=(1, 3))
         count = size_y // 2
         for part in range(filters // 128):
-            rows_ref[...] = total[..., 128 * part : 128 * part + 128].reshape(rows // 4, 128)
+            rows_ref[: rows // 4] = total[..., 128 * part : 128 * part + 128].reshape(rows // 4, 128)
             for x in range(size_x // 2):
                 for z in range(size_z // 2):
                     start = x * count * size_z + 2 * z
@@ -83,7 +83,7 @@
             jax.ShapeDtypeStruct((size_x // 2, size_z * size_y // 4, filters), jnp.bfloat16),
         ],
         scratch_shapes=[
-            pltpu.VMEM((rows // 4, 128), jnp.float32),
+            pltpu.VMEM((rows // 4 + 16, 128), jnp.float32),
             pltpu.VMEM((size_x // 2, size_z * size_y // 4, filters), jnp.float32),
         ],
         compiler_params=pltpu.CompilerParams(vmem_limit_bytes=12 << 20),
@@ -183,7 +183,7 @@
             total = jnp.maximum(join_taps(first, sums, size_y, size_z), 0.0)
             total = jnp.maximum(total[..., :filters], total[..., filters:])
             total = jnp.max(total.reshape(pool_y, 2, size_z, filters), axis=1)
-            rows_ref[...] = total.reshape(pool_y * size_z, filters)
+            rows_ref[: pool_y * size_z] = total.reshape(pool_y * size_z, filters)
             total = jnp.maximum(
                 rows_ref[pl.ds(0, pool_y * pool_z, stride=2), :], rows_ref[pl.ds(1, pool_y * pool_z, stride=2), :]
             ).reshape(pool_y, pool_z, filters)
@@ -203,7 +203,7 @@
             pltpu.VMEM((2, reach, own_y, size_z, channels), jnp.bfloat16),
             pltpu.VMEM((2, full_x, reach, size_z, channels), jnp.bfloat16),
             pltpu.VMEM((3, full_x, extra, channels), jnp.float32),
-            pltpu.VMEM((pool_y * size_z, filters), jnp.float32),
+            pltpu.VMEM((pool_y * size_z + 16, filters), jnp.float32),
         ],
         compiler_params=pltpu.CompilerParams(vmem_limit_bytes=14 << 20),
         name="encode",

time: 105 us -> 105 us (level)
  no operation moved by 1% of the time
where the time goes in v13:
time: 105 us; the launch traced here: 104 us
  starting transfers between devices  35.8 us (34%)
  Pallas kernels  34.6 us (33%)
  waiting for transfers between devices  29.8 us (28%)
  other arithmetic  2.26 us (2%)
  local copies, waits for them, and re-layouts  1.05 us (1%)
    ppermute x7, starting transfers between devices, send(): lax.ppermute(outer_block, axis, outer)  17.5 us
    ppermute x7, waiting for transfers between devices, send(): lax.ppermute(outer_block, axis, outer)  9.9 us
    ppermute x2, waiting for transfers between devices, edge_of(): lax.ppermute(jnp.where(place_z == 0, plane_high, plane_low), 'gz', swap)  7.62 us
    pallas_call x1, Pallas kernels, encode(): pl.pallas_call(body, in_specs=[pl.BlockSpec(memory_space=pltpu.SMEM)] + [...  5.98 us
    pallas_call x1, Pallas kernels, decode(): pl.pallas_call(body, in_specs=[pl.BlockSpec(memory_space=pltpu.SMEM)] + [...  5.12 us
    pallas_call x3, Pallas kernels, bring(): pl.pallas_call(body, in_specs=[pl.BlockSpec(memory_space=pltpu.HBM)] * co...  5.03 us
    all_to_all x1, starting transfers between devices, local(): column = lax.all_to_all(column, ('gx', 'gz'), 0, 0)  5.01 us
    pallas_call x1, Pallas kernels, prepare(): pl.pallas_call(body, in_specs=[pl.BlockSpec(memory_space=pltpu.HBM)] * 3,...  4.84 us
  transfers between devices with their start and end apart: 20, of which 10 were waited for; matrix products, arithmetic and copies ran while one was open for 2% of the time, Pallas kernels for 14%

profile of v13, /device:TPU:0, one launch (start us, length us, event | category | flops | bytes accessed | tf_op | source)
XLA Modules:
  0.0 104.0 jit_solution(602562704727480770)
XLA Ops:
  0.0 1.1 %broadcast_select_fusion.2 = (bf16[3,16,16,128]{3,2,1,0:T(8,128)(2,1)S(1)}, bf16[3,16,16,128]{3,2,1,0:T(8,128)(2,1)S(1)}) fusion(pred[]{:T(512)S(6)} %eq.25, bf16[8,16,16,128]{3,2,1,0:T(8,128)(2,1)} %refs_0_.1), kind=kLoop, calls=%fused_computation.3 | loop fusion | flops 196608 | bytes 786433 | tf_op jit(solution)/shard_map/jit(_where)/select_n | solution.py:19
  1.1 3.2 %collective-permute-start = (bf16[3,16,16,128]{3,2,1,0:T(8,128)(2,1)S(1)}, bf16[3,16,16,128]{3,2,1,0:T(8,128)(2,1)S(1)}, u32[]{:S(2)}, u32[]{:S(2)}) collective-permute-start(bf16[3,16,16,128]{3,2,1,0:T(8,128)(2,1)S(1)} %get-tuple-element.59), channel_id=1, source_target_pairs={{0,16},{16,0},{32,48},{48,32},{64,80},{80,64},{96,112},{112,96},{1... | collective-permute-start | bytes 589832 | tf_op jit(solution)/shard_map/ppermute | solution.py:14
  4.3 4.0 %collective-permute-start.1 = (bf16[3,16,16,128]{3,2,1,0:T(8,128)(2,1)S(1)}, bf16[3,16,16,128]{3,2,1,0:T(8,128)(2,1)S(1)}, u32[]{:S(2)}, u32[]{:S(2)}) collective-permute-start(bf16[3,16,16,128]{3,2,1,0:T(8,128)(2,1)S(1)} %get-tuple-element.58), channel_id=1, source_target_pairs={{0,112},{16,32},{32,16},{48,64},{64,48},{80,96},{96,80},{112,0},{1... | collective-permute-start | bytes 589832 | tf_op jit(solution)/shard_map/ppermute | solution.py:14
  8.3 4.8 %prepare.1 = (bf16[3,4,3,128,256]{4,3,2,1,0:T(8,128)(2,1)}, bf16[9,256,256]{2,1,0:T(8,128)(2,1)}, bf16[9,512,256]{2,1,0:T(8,128)(2,1)}) custom-call(bf16[3,3,3,128,128]{4,3,2,1,0:T(8,128)(2,1)} %full_hbm.1, bf16[3,3,3,64,256]{4,3,2,1,0:T(8,128)(2,1)} %bitcast.20, bf16[3,3,3,64,512]{4,3,2,1,0:T(8,128)(2,1)} %bitcast.19), custom_call_target="tpu_custom_call" | custom-call | tf_op jit(solution)/shard_map/prepare/pallas_call | solution.py:284
  13.1 0.1 pad_add_fusion.place_ref
  13.2 3.9 %collective-permute-done.1.x_out_ref = bf16[3,16,16,128]{3,2,1,0:T(8,128)(2,1)S(1)} collective-permute-done((bf16[3,16,16,128]{3,2,1,0:T(8,128)(2,1)S(1)}, bf16[3,16,16,128]{3,2,1,0:T(8,128)(2,1)S(1)}, u32[]{:S(2)}, u32[]{:S(2)}) %collective-permute-start.1) | collective-permute-done | bytes 196640 | tf_op jit(solution)/shard_map/ppermute | solution.py:14
  17.1 0.9 pack_y.1
  18.0 0.1 collective-permute-start.2
  18.1 3.1 %collective-permute-start.3 = (bf16[14,3,16,128]{3,2,1,0:T(8,128)(2,1)S(1)}, bf16[14,3,16,128]{3,2,1,0:T(8,128)(2,1)S(1)}, u32[]{:S(2)}, u32[]{:S(2)}) collective-permute-start(bf16[14,3,16,128]{3,2,1,0:T(8,128)(2,1)S(1)} %get-tuple-element.39), channel_id=1, source_target_pairs={{0,14},{2,4},{4,2},{6,8},{8,6},{10,12},{12,10},{14,0},{1,15},{3,5}... | collective-permute-start | bytes 516104 | tf_op jit(solution)/shard_map/ppermute | solution.py:14
  21.2 1.5 %collective-permute-start.4 = (bf16[14,16,128]{2,1,0:T(8,128)(2,1)S(1)}, bf16[14,16,128]{2,1,0:T(8,128)(2,1)S(1)}, u32[]{:S(2)}, u32[]{:S(2)}) collective-permute-start(bf16[14,16,128]{2,1,0:T(8,128)(2,1)S(1)} %get-tuple-element.36.refs_2_), channel_id=1, source_target_pairs={{0,1},{1,0},{2,3},{3,2},{4,5},{5,4},{6,7},{7,6},{8,9},{9,8},{10,11... | collective-permute-start | bytes 172040 | tf_op jit(solution)/shard_map/ppermute | solution.py:642
  22.7 1.9 %collective-permute-start.6 = (bf16[14,3,128]{2,1,0:T(4,128)(2,1)S(1)}, bf16[14,3,128]{2,1,0:T(4,128)(2,1)S(1)}, u32[]{:S(2)}, u32[]{:S(2)}) collective-permute-start(bf16[14,3,128]{2,1,0:T(4,128)(2,1)S(1)} %get-tuple-element.41), channel_id=1, source_target_pairs={{0,15},{1,14},{2,5},{3,4},{4,3},{5,2},{6,9},{7,8},{8,7},{9,6},{10,... | collective-permute-start | bytes 32264 | tf_op jit(solution)/shard_map/ppermute | solution.py:14
  24.6 2.0 %bring.3 = (bf16[8,16,16,128]{3,2,1,0:T(8,128)(2,1)S(1)}, bf16[3,4,3,128,256]{4,3,2,1,0:T(8,128)(2,1)S(1)}) custom-call(bf16[8,16,16,128]{3,2,1,0:T(8,128)(2,1)} %refs_0_.1, bf16[3,4,3,128,256]{4,3,2,1,0:T(8,128)(2,1)} %get-tuple-element.33.refs_1_, bf16[14,16,128]{2,1,0:T(8,128)(2,1)S(1)} %get-tuple-element.36.refs_2_), custom_call_target="tpu_custom_call" | custom-call | tf_op jit(solution)/shard_map/bring/pallas_call | solution.py:229
  26.6 1.3 %collective-permute-done.6.edge_out_ref = bf16[14,3,128]{2,1,0:T(4,128)(2,1)S(1)} collective-permute-done((bf16[14,3,128]{2,1,0:T(4,128)(2,1)S(1)}, bf16[14,3,128]{2,1,0:T(4,128)(2,1)S(1)}, u32[]{:S(2)}, u32[]{:S(2)}) %collective-permute-start.6) | collective-permute-done | bytes 10784 | tf_op jit(solution)/shard_map/ppermute | solution.py:14
  28.0 6.0 %encode.1.field_ref = bf16[6,10,8,128]{3,2,1,0:T(8,128)(2,1)S(1)} custom-call(s32[5]{0:T(128)S(1)} %pad_add_fusion.place_ref, bf16[8,16,16,128]{3,2,1,0:T(8,128)(2,1)S(1)} %get-tuple-element.37.own_ref, bf16[3,16,16,128]{3,2,1,0:T(8,128)(2,1)S(1)} %collective-permute-done.x_in_ref, bf16[3,16,16,128]{3,2,1,0:T(8,128)(2,1)S(1)} %collective-permute-done.1.x_out_ref, ...), custom_call_target="tpu_custom_call" | custom-call | tf_op jit(solution)/shard_map/encode/pallas_call | solution.py:197
  34.0 0.6 collective-permute-start.7
  34.7 3.3 %collective-permute-done.7.edge_ref = bf16[6,10,128]{2,1,0:T(8,128)(2,1)S(1)} collective-permute-done((bf16[6,10,128]{2,1,0:T(8,128)(2,1)S(1)}, bf16[6,10,128]{2,1,0:T(8,128)(2,1)S(1)}, u32[]{:S(2)}, u32[]{:S(2)}) %collective-permute-start.7) | collective-permute-done | bytes 15392 | tf_op jit(solution)/shard_map/ppermute | solution.py:635
  37.9 1.4 %half_level.1 = (bf16[4,8,8,256]{3,2,1,0:T(8,128)(2,1)S(1)}, bf16[2,16,256]{2,1,0:T(8,128)(2,1)S(1)}) custom-call(s32[5]{0:T(128)S(1)} %pad_add_fusion.place_ref, bf16[6,10,8,128]{3,2,1,0:T(8,128)(2,1)S(1)} %encode.1.field_ref, bf16[6,10,128]{2,1,0:T(8,128)(2,1)S(1)} %collective-permute-done.7.edge_ref, bf16[9,3,128,256]{3,2,1,0:T(8,128)(2,1)S(1)} %bitcast.16), custom_call_target="tpu_custom_call" | custom-call | tf_op jit(solution)/shard_map/half_level/pallas_call | solution.py:77
  39.4 0.1 collective-permute-start.8
  39.5 0.1 collective-permute-start.9
  39.6 1.8 %collective-permute-start.10 = (bf16[1,8,8,256]{3,1,0,2:T(8,128)(2,1)S(1)}, bf16[1,8,8,256]{3,1,0,2:T(8,128)(2,1)S(1)}, u32[]{:S(2)}, u32[]{:S(2)}) collective-permute-start(bf16[1,8,8,256]{3,1,0,2:T(8,128)(2,1)S(1)} %get-tuple-element.62), channel_id=1, source_target_pairs={{0,112},{16,32},{32,16},{48,64},{64,48},{80,96},{96,80},{112,0},{1... | collective-permute-start | bytes 98312 | tf_op jit(solution)/shard_map/ppermute | solution.py:14
  41.5 2.3 %collective-permute-done.8 = bf16[2,4,1,256]{3,1,0,2:T(4,128)(2,1)S(1)} collective-permute-done((bf16[2,4,1,256]{3,1,0,2:T(4,128)(2,1)S(1)}, bf16[2,4,1,256]{3,1,0,2:T(4,128)(2,1)S(1)}, u32[]{:S(2)}, u32[]{:S(2)}) %collective-permute-start.8) | collective-permute-done | bytes 4128 | tf_op jit(solution)/shard_map/ppermute | solution.py:14
  43.8 0.8 broadcast_in_dim.16.refs_1_
  44.6 5.0 %all-to-all-start = ((bf16[16,2,24,256]{3,2,1,0:T(8,128)(2,1)}), bf16[16,2,24,256]{3,2,1,0:T(8,128)(2,1)S(1)}, u32[]{:S(2)}, u32[]{:S(2)}) async-start(bf16[16,2,24,256]{3,2,1,0:T(8,128)(2,1)} %broadcast_in_dim.16.refs_1_), calls=%async_computation | async-start | bytes 786432 | tf_op jit(solution)/shard_map/all_to_all | solution.py:654
  49.6 0.1 broadcast_select_fusion.8
  49.7 0.1 broadcast_select_fusion.7
  49.8 0.1 collective-permute-start.13
  49.9 2.8 %collective-permute-start.12 = (bf16[6,1,8,256]{3,1,0,2:T(2,128)(2,1)S(1)}, bf16[6,1,8,256]{3,1,0,2:T(2,128)(2,1)S(1)}, u32[]{:S(2)}, u32[]{:S(2)}) collective-permute-start(bf16[6,1,8,256]{3,1,0,2:T(2,128)(2,1)S(1)} %get-tuple-element.55), channel_id=1, source_target_pairs={{0,14},{2,4},{4,2},{6,8},{8,6},{10,12},{12,10},{14,0},{1,15},{3,5}... | collective-permute-start | bytes 73736 | tf_op jit(solution)/shard_map/ppermute | solution.py:14
  52.8 1.4 %bring.4.weights_ref = bf16[9,256,256]{2,1,0:T(8,128)(2,1)S(1)} custom-call(bf16[9,256,256]{2,1,0:T(8,128)(2,1)} %get-tuple-element.44.refs_0_, bf16[16,2,24,256]{3,2,1,0:T(8,128)(2,1)} %broadcast_in_dim.16.refs_1_), custom_call_target="tpu_custom_call" | custom-call | tf_op jit(solution)/shard_map/bring/pallas_call | solution.py:229
  54.2 0.7 collective-permute-done.12
  54.9 0.1 broadcast_select_fusion.9
  55.0 4.3 %all-to-all-done.field_ref = bf16[16,2,24,256]{3,2,1,0:T(8,128)(2,1)S(1)} async-done(((bf16[16,2,24,256]{3,2,1,0:T(8,128)(2,1)}), bf16[16,2,24,256]{3,2,1,0:T(8,128)(2,1)S(1)}, u32[]{:S(2)}, u32[]{:S(2)}) %all-to-all-start) | async-done | bytes 393248 | tf_op jit(solution)/shard_map/all_to_all | solution.py:654
  59.3 2.9 %bottom_in.1.refs_1_ = bf16[8,8,6,4,128]{4,3,2,1,0:T(4,128)(2,1)} custom-call(s32[5]{0:T(128)S(1)} %pad_add_fusion.place_ref, bf16[16,2,24,256]{3,2,1,0:T(8,128)(2,1)S(1)} %all-to-all-done.field_ref, bf16[9,256,256]{2,1,0:T(8,128)(2,1)S(1)} %bring.4.weights_ref), custom_call_target="tpu_custom_call" | custom-call | tf_op jit(solution)/shard_map/bottom_in/pallas_call | solution.py:406
  62.2 3.5 %all-to-all-start.1 = ((bf16[8,8,6,4,128]{4,3,2,1,0:T(4,128)(2,1)}), bf16[8,8,6,4,128]{4,3,2,1,0:T(4,128)(2,1)S(1)}, u32[]{:S(2)}, u32[]{:S(2)}) async-start(bf16[8,8,6,4,128]{4,3,2,1,0:T(4,128)(2,1)} %bottom_in.1.refs_1_), calls=%async_computation.1 | async-start | bytes 786432 | tf_op jit(solution)/shard_map/all_to_all | solution.py:657
  65.6 0.2 pad_maximum_fusion
  65.9 0.7 collective-permute-start.14
  66.6 4.4 %collective-permute-done.14.edge_ref = bf16[6,10,256]{2,1,0:T(8,128)(2,1)S(1)} collective-permute-done((bf16[6,10,256]{2,1,0:T(8,128)(2,1)S(1)}, bf16[6,10,256]{2,1,0:T(8,128)(2,1)S(1)}, u32[]{:S(2)}, u32[]{:S(2)}) %collective-permute-start.14) | collective-permute-done | bytes 30752 | tf_op jit(solution)/shard_map/ppermute | solution.py:635
  70.9 4.3 %all-to-all-done.1.field_ref = bf16[8,8,6,4,128]{4,3,2,1,0:T(4,128)(2,1)S(1)} async-done(((bf16[8,8,6,4,128]{4,3,2,1,0:T(4,128)(2,1)}), bf16[8,8,6,4,128]{4,3,2,1,0:T(4,128)(2,1)S(1)}, u32[]{:S(2)}, u32[]{:S(2)}) %all-to-all-start.1) | async-done | bytes 393248 | tf_op jit(solution)/shard_map/all_to_all | solution.py:657
  75.2 0.5 broadcast_select_fusion
  75.7 0.1 collective-permute-start.15
  75.8 3.8 %collective-permute-start.16 = (bf16[8,8,6,2,128]{4,3,2,1,0:T(2,128)(2,1)S(1)}, bf16[8,8,6,2,128]{4,3,2,1,0:T(2,128)(2,1)S(1)}, u32[]{:S(2)}, u32[]{:S(2)}) collective-permute-start(bf16[8,8,6,2,128]{4,3,2,1,0:T(2,128)(2,1)S(1)} %get-tuple-element.60), channel_id=1, source_target_pairs={{0,14},{2,4},{4,2},{6,8},{8,6},{10,12},{12,10},{14,0},{1,15},{3,5}... | collective-permute-start | bytes 589832 | tf_op jit(solution)/shard_map/ppermute | solution.py:14
  79.5 1.7 %bring.5.weights_ref = bf16[9,512,256]{2,1,0:T(8,128)(2,1)S(1)} custom-call(bf16[9,512,256]{2,1,0:T(8,128)(2,1)} %get-tuple-element.47.refs_0_, bf16[8,8,6,4,128]{4,3,2,1,0:T(4,128)(2,1)} %bottom_in.1.refs_1_), custom_call_target="tpu_custom_call" | custom-call | tf_op jit(solution)/shard_map/bring/pallas_call | solution.py:229
  81.2 1.7 %collective-permute-done.16.y_out_ref = bf16[8,8,6,2,128]{4,3,2,1,0:T(2,128)(2,1)S(1)} collective-permute-done((bf16[8,8,6,2,128]{4,3,2,1,0:T(2,128)(2,1)S(1)}, bf16[8,8,6,2,128]{4,3,2,1,0:T(2,128)(2,1)S(1)}, u32[]{:S(2)}, u32[]{:S(2)}) %collective-permute-start.16) | collective-permute-done | bytes 196640 | tf_op jit(solution)/shard_map/ppermute | solution.py:14
  82.9 4.0 %bottom_out.1 = bf16[8,2,6,8,128]{4,3,2,1,0:T(8,128)(2,1)} custom-call(s32[5]{0:T(128)S(1)} %pad_add_fusion.place_ref, bf16[8,8,6,4,128]{4,3,2,1,0:T(4,128)(2,1)S(1)} %all-to-all-done.1.field_ref, bf16[8,8,6,2,128]{4,3,2,1,0:T(2,128)(2,1)S(1)} %collective-permute-done.15.y_in_ref, bf16[8,8,6,2,128]{4,3,2,1,0:T(2,128)(2,1)S(1)} %collective-permute-done.16.y_out_ref, ...), custom_call_target="tpu_custom_call" | custom-call | tf_op jit(solution)/shard_map/bottom_out/pallas_call | solution.py:464
  86.8 3.4 %all-to-all-start.2 = ((bf16[8,2,6,8,128]{4,3,2,1,0:T(8,128)(2,1)}), bf16[8,2,6,8,128]{4,3,2,1,0:T(8,128)(2,1)S(1)}, u32[]{:S(2)}, u32[]{:S(2)}) async-start(bf16[8,2,6,8,128]{4,3,2,1,0:T(8,128)(2,1)} %bottom_out.1), calls=%async_computation.2 | async-start | bytes 393216 | tf_op jit(solution)/shard_map/all_to_all | solution.py:664
  90.3 0.1 copy.21.skip_ref
  90.4 4.6 %decode_skip.1 = (f32[32,8,256]{2,1,0:T(8,128)}, bf16[3,512,256]{2,1,0:T(8,128)(2,1)S(1)}, bf16[3,512,256]{2,1,0:T(8,128)(2,1)S(1)}, bf16[3,512,256]{2,1,0:T(8,128)(2,1)S(1)}, bf16[3,512,256]{2,1,0:T(8,128)(2,1)S(1)}) custom-call(s32[5]{0:T(128)S(1)} %pad_add_fusion.place_ref, bf16[6,10,8,256]{3,2,1,0:T(8,128)(2,1)S(1)} %copy.21.skip_ref, ...), custom_call_target="tpu_custom_call" | custom-call | tf_op jit(solution)/shard_map/decode_skip/pallas_call | solution.py:519
  95.0 3.7 %all-to-all-done.2.bottom_ref = bf16[8,2,6,8,128]{4,3,2,1,0:T(8,128)(2,1)S(1)} async-done(((bf16[8,2,6,8,128]{4,3,2,1,0:T(8,128)(2,1)}), bf16[8,2,6,8,128]{4,3,2,1,0:T(8,128)(2,1)S(1)}, u32[]{:S(2)}, u32[]{:S(2)}) %all-to-all-start.2) | async-done | bytes 196640 | tf_op jit(solution)/shard_map/all_to_all | solution.py:664
  98.8 5.1 %decode.1 = bf16[4,8,8,256]{3,2,1,0:T(8,128)(2,1)} custom-call(s32[5]{0:T(128)S(1)} %pad_add_fusion.place_ref, bf16[8,2,6,8,128]{4,3,2,1,0:T(8,128)(2,1)S(1)} %all-to-all-done.2.bottom_ref, f32[32,8,256]{2,1,0:T(8,128)} %get-tuple-element.50.skip_hbm, bf16[3,512,256]{2,1,0:T(8,128)(2,1)S(1)} %get-tuple-element.51.refs_0_, ...), custom_call_target="tpu_custom_call" | custom-call | tf_op jit(solution)/shard_map/decode/pallas_call | solution.py:605
  (28 shorter events, 0.2 us)
Async XLA Ops:
  0.0 17.1 %copy-start = (bf16[8,16,16,128]{3,2,1,0:T(8,128)(2,1)S(1)}, bf16[8,16,16,128]{3,2,1,0:T(8,128)(2,1)}, u32[]{:S(2)}) copy-start(bf16[8,16,16,128]{3,2,1,0:T(8,128)(2,1)} %refs_0_.1) | copy-start | bytes 1572868
  1.1 12.1 %collective-permute-start = (bf16[3,16,16,128]{3,2,1,0:T(8,128)(2,1)S(1)}, bf16[3,16,16,128]{3,2,1,0:T(8,128)(2,1)S(1)}, u32[]{:S(2)}, u32[]{:S(2)}) collective-permute-start(bf16[3,16,16,128]{3,2,1,0:T(8,128)(2,1)S(1)} %get-tuple-element.59), channel_id=1, source_target_pairs={{0,16},{16,0},{32,48},{48,32},{64,80},{80,64},{96,112},{112,96},{1... | collective-permute-start | bytes 589832 | tf_op jit(solution)/shard_map/ppermute | solution.py:14
  4.3 12.8 %collective-permute-start.1 = (bf16[3,16,16,128]{3,2,1,0:T(8,128)(2,1)S(1)}, bf16[3,16,16,128]{3,2,1,0:T(8,128)(2,1)S(1)}, u32[]{:S(2)}, u32[]{:S(2)}) collective-permute-start(bf16[3,16,16,128]{3,2,1,0:T(8,128)(2,1)S(1)} %get-tuple-element.58), channel_id=1, source_target_pairs={{0,112},{16,32},{32,16},{48,64},{64,48},{80,96},{96,80},{112,0},{1... | collective-permute-start | bytes 589832 | tf_op jit(solution)/shard_map/ppermute | solution.py:14
  18.0 10.0 %collective-permute-start.2 = (bf16[14,3,16,128]{3,2,1,0:T(8,128)(2,1)S(1)}, bf16[14,3,16,128]{3,2,1,0:T(8,128)(2,1)S(1)}, u32[]{:S(2)}, u32[]{:S(2)}) collective-permute-start(bf16[14,3,16,128]{3,2,1,0:T(8,128)(2,1)S(1)} %get-tuple-element.38), channel_id=1, source_target_pairs={{0,2},{2,0},{4,6},{6,4},{8,10},{10,8},{12,14},{14,12},{1,3},{3,1},... | collective-permute-start | bytes 516104 | tf_op jit(solution)/shard_map/ppermute | solution.py:14
  18.1 9.9 %collective-permute-start.3 = (bf16[14,3,16,128]{3,2,1,0:T(8,128)(2,1)S(1)}, bf16[14,3,16,128]{3,2,1,0:T(8,128)(2,1)S(1)}, u32[]{:S(2)}, u32[]{:S(2)}) collective-permute-start(bf16[14,3,16,128]{3,2,1,0:T(8,128)(2,1)S(1)} %get-tuple-element.39), channel_id=1, source_target_pairs={{0,14},{2,4},{4,2},{6,8},{8,6},{10,12},{12,10},{14,0},{1,15},{3,5}... | collective-permute-start | bytes 516104 | tf_op jit(solution)/shard_map/ppermute | solution.py:14
  21.2 6.7 %collective-permute-start.4 = (bf16[14,16,128]{2,1,0:T(8,128)(2,1)S(1)}, bf16[14,16,128]{2,1,0:T(8,128)(2,1)S(1)}, u32[]{:S(2)}, u32[]{:S(2)}) collective-permute-start(bf16[14,16,128]{2,1,0:T(8,128)(2,1)S(1)} %get-tuple-element.36.refs_2_), channel_id=1, source_target_pairs={{0,1},{1,0},{2,3},{3,2},{4,5},{5,4},{6,7},{7,6},{8,9},{9,8},{10,11... | collective-permute-start | bytes 172040 | tf_op jit(solution)/shard_map/ppermute | solution.py:642
  22.7 3.9 %collective-permute-start.5 = (bf16[14,3,128]{2,1,0:T(4,128)(2,1)S(1)}, bf16[14,3,128]{2,1,0:T(4,128)(2,1)S(1)}, u32[]{:S(2)}, u32[]{:S(2)}) collective-permute-start(bf16[14,3,128]{2,1,0:T(4,128)(2,1)S(1)} %get-tuple-element.40), channel_id=1, source_target_pairs={{0,3},{1,2},{2,1},{3,0},{4,7},{5,6},{6,5},{7,4},{8,11},{9,10},{10,... | collective-permute-start | bytes 32264 | tf_op jit(solution)/shard_map/ppermute | solution.py:14
  22.7 5.3 %collective-permute-start.6 = (bf16[14,3,128]{2,1,0:T(4,128)(2,1)S(1)}, bf16[14,3,128]{2,1,0:T(4,128)(2,1)S(1)}, u32[]{:S(2)}, u32[]{:S(2)}) collective-permute-start(bf16[14,3,128]{2,1,0:T(4,128)(2,1)S(1)} %get-tuple-element.41), channel_id=1, source_target_pairs={{0,15},{1,14},{2,5},{3,4},{4,3},{5,2},{6,9},{7,8},{8,7},{9,6},{10,... | collective-permute-start | bytes 32264 | tf_op jit(solution)/shard_map/ppermute | solution.py:14
  26.6 11.3 %copy-start.1 = (bf16[3,3,3,128,256]{4,3,2,1,0:T(8,128)(2,1)S(1)}, bf16[3,3,3,128,256]{4,3,2,1,0:T(8,128)(2,1)}, u32[]{:S(2)}) copy-start(bf16[3,3,3,128,256]{4,3,2,1,0:T(8,128)(2,1)} %param.8) | copy-start | bytes 5308420
  34.0 3.9 %collective-permute-start.7 = (bf16[6,10,128]{2,1,0:T(8,128)(2,1)S(1)}, bf16[6,10,128]{2,1,0:T(8,128)(2,1)S(1)}, u32[]{:S(2)}, u32[]{:S(2)}) collective-permute-start(bf16[6,10,128]{2,1,0:T(8,128)(2,1)S(1)} %fusion.1), channel_id=1, source_target_pairs={{0,1},{1,0},{2,3},{3,2},{4,5},{5,4},{6,7},{7,6},{8,9},{9,8},{10,11... | collective-permute-start | bytes 46088 | tf_op jit(solution)/shard_map/ppermute | solution.py:635
  39.4 4.3 %collective-permute-start.8 = (bf16[2,4,1,256]{3,1,0,2:T(4,128)(2,1)S(1)}, bf16[2,4,1,256]{3,1,0,2:T(4,128)(2,1)S(1)}, u32[]{:S(2)}, u32[]{:S(2)}) collective-permute-start(bf16[2,4,1,256]{3,1,0,2:T(4,128)(2,1)S(1)} %get-tuple-element.74), channel_id=1, source_target_pairs={{0,14},{2,4},{4,2},{6,8},{8,6},{10,12},{12,10},{14,0},{1,15},{3,5}... | collective-permute-start | bytes 12296 | tf_op jit(solution)/shard_map/ppermute | solution.py:14
  39.5 4.2 %collective-permute-start.9 = (bf16[2,4,1,256]{3,1,0,2:T(4,128)(2,1)S(1)}, bf16[2,4,1,256]{3,1,0,2:T(4,128)(2,1)S(1)}, u32[]{:S(2)}, u32[]{:S(2)}) collective-permute-start(bf16[2,4,1,256]{3,1,0,2:T(4,128)(2,1)S(1)} %get-tuple-element.75), channel_id=1, source_target_pairs={{0,2},{2,0},{4,6},{6,4},{8,10},{10,8},{12,14},{14,12},{1,3},{3,1},... | collective-permute-start | bytes 12296 | tf_op jit(solution)/shard_map/ppermute | solution.py:14
  39.6 10.0 %collective-permute-start.10 = (bf16[1,8,8,256]{3,1,0,2:T(8,128)(2,1)S(1)}, bf16[1,8,8,256]{3,1,0,2:T(8,128)(2,1)S(1)}, u32[]{:S(2)}, u32[]{:S(2)}) collective-permute-start(bf16[1,8,8,256]{3,1,0,2:T(8,128)(2,1)S(1)} %get-tuple-element.62), channel_id=1, source_target_pairs={{0,112},{16,32},{32,16},{48,64},{64,48},{80,96},{96,80},{112,0},{1... | collective-permute-start | bytes 98312 | tf_op jit(solution)/shard_map/ppermute | solution.py:14
  41.5 8.2 %collective-permute-start.11 = (bf16[1,8,8,256]{3,1,0,2:T(8,128)(2,1)S(1)}, bf16[1,8,8,256]{3,1,0,2:T(8,128)(2,1)S(1)}, u32[]{:S(2)}, u32[]{:S(2)}) collective-permute-start(bf16[1,8,8,256]{3,1,0,2:T(8,128)(2,1)S(1)} %get-tuple-element.63), channel_id=1, source_target_pairs={{0,16},{16,0},{32,48},{48,32},{64,80},{80,64},{96,112},{112,96},{1... | collective-permute-start | bytes 98312 | tf_op jit(solution)/shard_map/ppermute | solution.py:14
  44.6 14.7 %all-to-all-start = ((bf16[16,2,24,256]{3,2,1,0:T(8,128)(2,1)}), bf16[16,2,24,256]{3,2,1,0:T(8,128)(2,1)S(1)}, u32[]{:S(2)}, u32[]{:S(2)}) async-start(bf16[16,2,24,256]{3,2,1,0:T(8,128)(2,1)} %broadcast_in_dim.16.refs_1_), calls=%async_computation | async-start | bytes 786432 | tf_op jit(solution)/shard_map/all_to_all | solution.py:654
  49.8 4.3 %collective-permute-start.13 = (bf16[6,1,8,256]{3,1,0,2:T(2,128)(2,1)S(1)}, bf16[6,1,8,256]{3,1,0,2:T(2,128)(2,1)S(1)}, u32[]{:S(2)}, u32[]{:S(2)}) collective-permute-start(bf16[6,1,8,256]{3,1,0,2:T(2,128)(2,1)S(1)} %broadcast_select_fusion.7), channel_id=1, source_target_pairs={{0,2},{2,0},{4,6},{6,4},{8,10},{10,8},{12,14},{14,12},{1,3},{3,1},... | collective-permute-start | bytes 73736 | tf_op jit(solution)/shard_map/ppermute | solution.py:14
  49.9 5.0 %collective-permute-start.12 = (bf16[6,1,8,256]{3,1,0,2:T(2,128)(2,1)S(1)}, bf16[6,1,8,256]{3,1,0,2:T(2,128)(2,1)S(1)}, u32[]{:S(2)}, u32[]{:S(2)}) collective-permute-start(bf16[6,1,8,256]{3,1,0,2:T(2,128)(2,1)S(1)} %get-tuple-element.55), channel_id=1, source_target_pairs={{0,14},{2,4},{4,2},{6,8},{8,6},{10,12},{12,10},{14,0},{1,15},{3,5}... | collective-permute-start | bytes 73736 | tf_op jit(solution)/shard_map/ppermute | solution.py:14
  62.2 13.0 %all-to-all-start.1 = ((bf16[8,8,6,4,128]{4,3,2,1,0:T(4,128)(2,1)}), bf16[8,8,6,4,128]{4,3,2,1,0:T(4,128)(2,1)S(1)}, u32[]{:S(2)}, u32[]{:S(2)}) async-start(bf16[8,8,6,4,128]{4,3,2,1,0:T(4,128)(2,1)} %bottom_in.1.refs_1_), calls=%async_computation.1 | async-start | bytes 786432 | tf_op jit(solution)/shard_map/all_to_all | solution.py:657
  65.9 5.0 %collective-permute-start.14 = (bf16[6,10,256]{2,1,0:T(8,128)(2,1)S(1)}, bf16[6,10,256]{2,1,0:T(8,128)(2,1)S(1)}, u32[]{:S(2)}, u32[]{:S(2)}) collective-permute-start(bf16[6,10,256]{2,1,0:T(8,128)(2,1)S(1)} %fusion), channel_id=1, source_target_pairs={{0,1},{1,0},{2,3},{3,2},{4,5},{5,4},{6,7},{7,6},{8,9},{9,8},{10,11... | collective-permute-start | bytes 92168 | tf_op jit(solution)/shard_map/ppermute | solution.py:635
  75.7 5.5 %collective-permute-start.15 = (bf16[8,8,6,2,128]{4,3,2,1,0:T(2,128)(2,1)S(1)}, bf16[8,8,6,2,128]{4,3,2,1,0:T(2,128)(2,1)S(1)}, u32[]{:S(2)}, u32[]{:S(2)}) collective-permute-start(bf16[8,8,6,2,128]{4,3,2,1,0:T(2,128)(2,1)S(1)} %get-tuple-element.61), channel_id=1, source_target_pairs={{0,2},{2,0},{4,6},{6,4},{8,10},{10,8},{12,14},{14,12},{1,3},{3,1},... | collective-permute-start | bytes 589832 | tf_op jit(solution)/shard_map/ppermute | solution.py:14
  75.8 7.1 %collective-permute-start.16 = (bf16[8,8,6,2,128]{4,3,2,1,0:T(2,128)(2,1)S(1)}, bf16[8,8,6,2,128]{4,3,2,1,0:T(2,128)(2,1)S(1)}, u32[]{:S(2)}, u32[]{:S(2)}) collective-permute-start(bf16[8,8,6,2,128]{4,3,2,1,0:T(2,128)(2,1)S(1)} %get-tuple-element.60), channel_id=1, source_target_pairs={{0,14},{2,4},{4,2},{6,8},{8,6},{10,12},{12,10},{14,0},{1,15},{3,5}... | collective-permute-start | bytes 589832 | tf_op jit(solution)/shard_map/ppermute | solution.py:14
  86.8 11.9 %all-to-all-start.2 = ((bf16[8,2,6,8,128]{4,3,2,1,0:T(8,128)(2,1)}), bf16[8,2,6,8,128]{4,3,2,1,0:T(8,128)(2,1)S(1)}, u32[]{:S(2)}, u32[]{:S(2)}) async-start(bf16[8,2,6,8,128]{4,3,2,1,0:T(8,128)(2,1)} %bottom_out.1), calls=%async_computation.2 | async-start | bytes 393216 | tf_op jit(solution)/shard_map/all_to_all | solution.py:664
